TPU v7x, 32 devices: a whole 2x2x4 slice. The times are simulated.
32 devices in a mesh: heads: 4 (over y, x), seq: 8 (over z, core).
Axes of the slice: x: 2, y: 2, z: 4, core: 2. Of those that a mesh axis runs over, the one named last changes fastest.
Arguments:
- tokens: bfloat16 [7168, 2048], P('seq'), may hold values from -6 to 6
- w_qkv: bfloat16 [2048, 3, 2048], P(None, None, 'heads'), may hold values from -0.1875 to 0.1875
- w_out: bfloat16 [2048, 2048], P('heads'), may hold values from -0.75 to 0.75
- w_up: bfloat16 [2048, 8192], P('seq', 'heads'), may hold values from -0.125 to 0.125
- w_down: bfloat16 [8192, 2048], P('heads', 'seq'), may hold values from -0.0625 to 0.0625
- gain_attn: float32 [2048], replicated, may hold values from 0.1 to 1.9
- gain_ffn: float32 [2048], replicated, may hold values from 0.1 to 1.9
- w_router: float32 [2048, 8], replicated, may hold values from -0.25 to 0.25
- head_quarters: int32 [5], replicated, may hold values from 1 to 4, as said below
- ffn_quarters: int32 [5], replicated, may hold values from 1 to 4, as said below
- router_targets: int32 [5, 2], replicated, may hold values from 0 to 3
- cotangent: bfloat16 [7168, 2048], P('seq'), may hold values from -6 to 6
Outputs:
- output: bfloat16 [7168, 2048], P('seq')
- grad_tokens: float32 [7168, 2048], P('seq')
- grad_qkv: float32 [2048, 3, 2048], P(None, None, 'heads')
- grad_out: float32 [2048, 2048], P('heads')
- grad_up: float32 [2048, 8192], P('seq', 'heads')
- grad_down: float32 [8192, 2048], P('heads', 'seq')
- grad_gain_attn: float32 [2048], replicated
- grad_gain_ffn: float32 [2048], replicated
- grad_router: float32 [2048, 8], replicated
Inputs may be any that keep to these rules, and one draw needn't show every extreme that they name: Sequence s uses the first head_quarters[s] * 4 heads; some sequence uses all heads and some a quarter of them. Sequence s uses the first ffn_quarters[s] * 2048 hidden units; some sequence uses all and some a quarter.
All inputs are finite; a program needn't handle non-finite values.
Results may differ from a plain program's by a relative error of at most 0.023.
Values may be sent and summed in bfloat16 or wider, within the bound.
No kernel may reach another device: no remote copies, remote signals or barrier semaphores. Data moves between devices by JAX's collectives and lax.ppermute only.
A program may use at most 256 MiB of HBM per device.

v0:
```python
import jax
import jax.numpy as jnp
from jax import lax
from jax.sharding import PartitionSpec as P

D = 2048
H = 16
HD = 128
FF = 8192
SHORT_DEV = 128
NSHORT = 3
NLONG = 2
LEVELS = 4
SEQS = 5


epsilon = 1e-05
highest = lax.Precision.HIGHEST


def normalize_parts(values):
    centered = values - jnp.mean(values, axis=-1, keepdims=True)
    inverse = lax.rsqrt(jnp.mean(centered * centered, axis=-1, keepdims=True) + epsilon)
    return (centered * inverse, inverse)


def normalize_back(grad_normed, normed_hat, inverse, gain):
    grad_hat = grad_normed * gain
    middle = (
        grad_hat
        - jnp.mean(grad_hat, axis=-1, keepdims=True)
        - normed_hat * jnp.mean(grad_hat * normed_hat, axis=-1, keepdims=True)
    )
    return (inverse * middle, jnp.sum(grad_normed * normed_hat, axis=0))


def rotate(values, cosine, sine, inverse_turn):
    row_count = values.shape[0]
    shaped = values.reshape(row_count, -1, HD)
    half_dim = HD // 2
    former = shaped[..., :half_dim]
    latter = shaped[..., half_dim:]
    if inverse_turn:
        turned = [former * cosine + latter * sine, latter * cosine - former * sine]
    else:
        turned = [former * cosine - latter * sine, latter * cosine + former * sine]
    return jnp.concatenate(turned, axis=-1).reshape(row_count, -1)


def gather_rows(keys, values):
    return (
        lax.all_gather(keys, "seq", axis=1, tiled=True),
        lax.all_gather(values, "seq", axis=1, tiled=True),
    )


def masked_scores(query, keys, first_pos):
    seq_number, seq_size = (query.shape[0], query.shape[1])
    length = keys.shape[1]
    query_heads = query.reshape(seq_number, seq_size, -1, HD)
    key_heads = keys.reshape(seq_number, length, -1, HD)
    scores = jnp.einsum(
        "cqhd,ckhd->chqk", query_heads, key_heads, preferred_element_type=jnp.float32
    ) * HD ** (-0.5)
    allowed = jnp.arange(length)[None, :] <= (first_pos + jnp.arange(seq_size))[:, None]
    return (jnp.where(allowed[None, None], scores, -1e30), query_heads, key_heads)


def attend_forward(query, keys, values, first_pos):
    seq_number, seq_size = (query.shape[0], query.shape[1])
    scores, query_heads, key_heads = masked_scores(query, keys, first_pos)
    largest = jnp.max(scores, axis=-1, keepdims=True)
    raised = jnp.exp(scores - largest)
    total = jnp.sum(raised, axis=-1, keepdims=True)
    probs = (raised / total).astype(jnp.bfloat16)
    value_heads = values.reshape(seq_number, values.shape[1], -1, HD)
    mixed = jnp.einsum("chqk,ckhd->cqhd", probs, value_heads, preferred_element_type=jnp.float32)
    return (mixed.reshape(seq_number, seq_size, -1), largest + jnp.log(total))


def attend_backward(query, keys, values, grad_mixed, log_total, first_pos):
    seq_number, seq_size = (query.shape[0], query.shape[1])
    length = keys.shape[1]
    scores, query_heads, key_heads = masked_scores(query, keys, first_pos)
    probs = jnp.exp(scores - log_total)
    value_heads = values.reshape(seq_number, length, -1, HD)
    grad_heads = grad_mixed.reshape(seq_number, seq_size, -1, HD)
    grad_probs = jnp.einsum(
        "cqhd,ckhd->chqk", grad_heads, value_heads, preferred_element_type=jnp.float32
    )
    delta = jnp.sum(probs * grad_probs, axis=-1)
    grad_scores = (probs * (grad_probs - delta[..., None])).astype(jnp.bfloat16)
    grad_query = jnp.einsum(
        "chqk,ckhd->cqhd", grad_scores, key_heads, preferred_element_type=jnp.float32
    ) * HD ** (-0.5)
    grad_query = grad_query.reshape(seq_number, seq_size, -1)
    return (grad_query, delta)


def attend_key_side(query_all, keys, values, grad_all, total_all, delta_all, key_first):
    seq_number, length = (query_all.shape[0], query_all.shape[1])
    key_count = keys.shape[1]
    query_heads = query_all.reshape(seq_number, length, -1, HD)
    key_heads = keys.reshape(seq_number, key_count, -1, HD)
    value_heads = values.reshape(seq_number, key_count, -1, HD)
    grad_heads = grad_all.reshape(seq_number, length, -1, HD)
    scores = jnp.einsum(
        "cqhd,ckhd->chqk", query_heads, key_heads, preferred_element_type=jnp.float32
    ) * HD ** (-0.5)
    allowed = (key_first + jnp.arange(key_count))[None, :] <= jnp.arange(length)[:, None]
    scores = jnp.where(allowed[None, None], scores, -1e30)
    probs = jnp.exp(scores - total_all[..., None])
    probs_low = probs.astype(jnp.bfloat16)
    grad_probs = jnp.einsum(
        "cqhd,ckhd->chqk", grad_heads, value_heads, preferred_element_type=jnp.float32
    )
    grad_scores = (probs * (grad_probs - delta_all[..., None])).astype(jnp.bfloat16)
    grad_values = jnp.einsum(
        "chqk,cqhd->ckhd", probs_low, grad_heads, preferred_element_type=jnp.float32
    )
    grad_keys = jnp.einsum(
        "chqk,cqhd->ckhd", grad_scores, query_heads, preferred_element_type=jnp.float32
    ) * HD ** (-0.5)
    return (
        grad_keys.reshape(seq_number, key_count, -1),
        grad_values.reshape(seq_number, key_count, -1),
    )


def local(
    tokens,
    w_qkv,
    w_out,
    w_up,
    w_down,
    gain_attn,
    gain_ffn,
    w_router,
    head_quarters,
    ffn_quarters,
    router_targets,
    cotangent,
):
    row_count = tokens.shape[0]
    seq_rank = lax.axis_index("seq")
    seq_count = lax.axis_size("seq")
    head_rank = lax.axis_index("heads")
    head_width = w_out.shape[0]
    ffn_width = w_up.shape[1]
    short_rows = NSHORT * SHORT_DEV
    column = jnp.arange(row_count)
    is_short = column < short_rows
    offset = column - short_rows
    seq_id = jnp.where(is_short, column // SHORT_DEV, NSHORT + offset // (2 * SHORT_DEV))
    position = jnp.where(
        is_short,
        seq_rank * SHORT_DEV + column % SHORT_DEV,
        seq_rank * 2 * SHORT_DEV + offset % (2 * SHORT_DEV),
    )
    in_seq = seq_id[:, None] == jnp.arange(SEQS)[None, :]
    member = in_seq.astype(jnp.float32)
    seq_length = jnp.where(
        jnp.arange(SEQS) < NSHORT, SHORT_DEV * seq_count, 2 * SHORT_DEV * seq_count
    ).astype(jnp.float32)
    head_level = jnp.sum(jnp.where(in_seq, head_quarters[None, :], 0), axis=1)
    ffn_level = jnp.sum(jnp.where(in_seq, ffn_quarters[None, :], 0), axis=1)
    head_index = head_rank * (head_width // HD) + jnp.arange(head_width) // HD
    head_live = (head_index[None, :] < (head_level * (H // LEVELS))[:, None]).astype(jnp.bfloat16)
    unit_index = head_rank * ffn_width + jnp.arange(ffn_width)
    ffn_live = (unit_index[None, :] < (ffn_level * (FF // LEVELS))[:, None]).astype(jnp.float32)
    half_dim = HD // 2
    frequency = 10000.0 ** (-jnp.arange(half_dim, dtype=jnp.float32) * 2.0 / HD)
    angle = position.astype(jnp.float32)[:, None] * frequency[None, :]
    cosine = jnp.cos(angle)[:, None, :]
    sine = jnp.sin(angle)[:, None, :]
    tokens_wide = tokens.astype(jnp.float32)
    hat_one, inverse_one = normalize_parts(tokens_wide)
    normed_one = hat_one * gain_attn
    normed_low = normed_one.astype(jnp.bfloat16)
    flat_qkv = w_qkv.reshape(D, -1)
    projected = jnp.dot(normed_low, flat_qkv, preferred_element_type=jnp.float32).reshape(
        row_count, 3, head_width
    )
    query = rotate(projected[:, 0], cosine, sine, False).astype(jnp.bfloat16)
    keys = rotate(projected[:, 1], cosine, sine, False).astype(jnp.bfloat16)
    values = projected[:, 2].astype(jnp.bfloat16)
    partial_pool = jnp.dot(
        member.T, normed_one, precision=highest, preferred_element_type=jnp.float32
    )
    pooled = (
        lax.psum(partial_pool.astype(jnp.bfloat16), "seq").astype(jnp.float32)
        * lax.rsqrt(seq_length)[:, None]
    )
    shape_list = ((0, NSHORT, SHORT_DEV), (short_rows, NLONG, 2 * SHORT_DEV))
    saved_parts = []
    mixed_parts = []
    for row_start, seq_number, seq_size in shape_list:
        row_stop = row_start + seq_number * seq_size
        piece_query = query[row_start:row_stop].reshape(seq_number, seq_size, head_width)
        piece_keys = keys[row_start:row_stop].reshape(seq_number, seq_size, head_width)
        piece_values = values[row_start:row_stop].reshape(seq_number, seq_size, head_width)
        gathered_keys, gathered_values = gather_rows(piece_keys, piece_values)
        mixed, log_total = attend_forward(
            piece_query, gathered_keys, gathered_values, seq_rank * seq_size
        )
        saved_parts.append(
            (piece_query, piece_keys, piece_values, gathered_keys, gathered_values, log_total)
        )
        mixed_parts.append(mixed.reshape(seq_number * seq_size, head_width))
    heads_out = (jnp.concatenate(mixed_parts, axis=0) * head_live).astype(jnp.bfloat16)
    attn_part = jnp.dot(heads_out, w_out, preferred_element_type=jnp.float32)
    hidden = tokens_wide + lax.psum(attn_part, "heads")
    hat_two, inverse_two = normalize_parts(hidden)
    normed_two = (hat_two * gain_ffn).astype(jnp.bfloat16)
    full_up, full_down = (
        lax.all_gather(w_up, "seq", axis=0, tiled=True),
        lax.all_gather(w_down, "seq", axis=1, tiled=True),
    )
    upward = jnp.dot(normed_two, full_up, preferred_element_type=jnp.float32)
    active = (jnp.square(jnp.maximum(upward, 0.0)) * ffn_live).astype(jnp.bfloat16)
    ffn_part = jnp.dot(active, full_down, preferred_element_type=jnp.float32)
    output = (hidden + lax.psum(ffn_part.astype(jnp.bfloat16), "heads").astype(jnp.float32)).astype(
        jnp.bfloat16
    )
    back_up, back_down = (
        lax.all_gather(w_up, "seq", axis=0, tiled=True),
        lax.all_gather(w_down, "seq", axis=1, tiled=True),
    )
    upward_again = jnp.dot(normed_two, back_up, preferred_element_type=jnp.float32)
    active_again = (jnp.square(jnp.maximum(upward_again, 0.0)) * ffn_live).astype(jnp.bfloat16)
    grad_active = jnp.dot(cotangent, back_down.T, preferred_element_type=jnp.float32).astype(
        jnp.bfloat16
    )
    grad_upward = (
        grad_active.astype(jnp.float32) * ffn_live * 2.0 * jnp.maximum(upward_again, 0.0)
    ).astype(jnp.bfloat16)
    grad_down_part = jnp.dot(active_again.T, cotangent, preferred_element_type=jnp.float32)
    grad_up_part = jnp.dot(normed_two.T, grad_upward, preferred_element_type=jnp.float32)
    grad_two = lax.psum(
        jnp.dot(grad_upward, back_up.T, preferred_element_type=jnp.float32), "heads"
    )
    grad_up, grad_down = (
        lax.psum_scatter(
            grad_up_part.astype(jnp.bfloat16), "seq", scatter_dimension=0, tiled=True
        ).astype(jnp.float32),
        lax.psum_scatter(
            grad_down_part.astype(jnp.bfloat16), "seq", scatter_dimension=1, tiled=True
        ).astype(jnp.float32),
    )
    back_two, grad_gain_two = normalize_back(grad_two, hat_two, inverse_two, gain_ffn)
    grad_hidden = cotangent.astype(jnp.float32) + back_two
    grad_attn = grad_hidden.astype(jnp.bfloat16)
    grad_out_part = jnp.dot(heads_out.T, grad_attn, preferred_element_type=jnp.float32)
    grad_heads = (
        jnp.dot(grad_attn, w_out.T, preferred_element_type=jnp.float32).astype(jnp.bfloat16)
        * head_live
    )
    query_grads = []
    key_grads = []
    value_grads = []
    for shape_entry, saved in zip(shape_list, saved_parts):
        row_start, seq_number, seq_size = shape_entry
        piece_query, piece_keys, piece_values, gathered_keys, gathered_values, log_total = saved
        piece_grad = grad_heads[row_start : row_start + seq_number * seq_size].reshape(
            seq_number, seq_size, head_width
        )
        grad_query, delta = attend_backward(
            piece_query, gathered_keys, gathered_values, piece_grad, log_total, seq_rank * seq_size
        )
        query_all, grad_all = (
            lax.all_gather(piece_query, "seq", axis=1, tiled=True),
            lax.all_gather(piece_grad, "seq", axis=1, tiled=True),
        )
        total_all, delta_all = (
            lax.all_gather(log_total[..., 0], "seq", axis=2, tiled=True),
            lax.all_gather(delta, "seq", axis=2, tiled=True),
        )
        local_keys, local_values = attend_key_side(
            query_all, piece_keys, piece_values, grad_all, total_all, delta_all, seq_rank * seq_size
        )
        query_grads.append(grad_query.reshape(seq_number * seq_size, head_width))
        key_grads.append(local_keys.reshape(seq_number * seq_size, head_width))
        value_grads.append(local_values.reshape(seq_number * seq_size, head_width))
    grad_query_all = rotate(jnp.concatenate(query_grads, axis=0), cosine, sine, True)
    grad_key_all = rotate(jnp.concatenate(key_grads, axis=0), cosine, sine, True)
    grad_value_all = jnp.concatenate(value_grads, axis=0)
    grad_projected = (
        jnp.stack([grad_query_all, grad_key_all, grad_value_all], axis=1)
        .astype(jnp.bfloat16)
        .reshape(row_count, -1)
    )
    grad_qkv_part = jnp.dot(
        normed_low.T, grad_projected, preferred_element_type=jnp.float32
    ).reshape(D, 3, head_width)
    grad_one = lax.psum(
        jnp.dot(grad_projected, flat_qkv.T, preferred_element_type=jnp.float32).astype(
            jnp.bfloat16
        ),
        "heads",
    ).astype(jnp.float32)
    logits = jnp.dot(pooled, w_router, precision=highest, preferred_element_type=jnp.float32)
    logit_grads = []
    for group in range(2):
        group_logits = logits[:, LEVELS * group : LEVELS * (group + 1)]
        raised = jnp.exp(group_logits - jnp.max(group_logits, axis=1, keepdims=True))
        chosen = (jnp.arange(LEVELS)[None, :] == router_targets[:, group][:, None]).astype(
            jnp.float32
        )
        logit_grads.append(raised / jnp.sum(raised, axis=1, keepdims=True) - chosen)
    grad_logits = jnp.concatenate(logit_grads, axis=1)
    grad_router = jnp.dot(
        pooled.T, grad_logits, precision=highest, preferred_element_type=jnp.float32
    )
    grad_pooled = (
        jnp.dot(grad_logits, w_router.T, precision=highest, preferred_element_type=jnp.float32)
        * lax.rsqrt(seq_length)[:, None]
    )
    grad_one = grad_one + jnp.dot(
        member, grad_pooled, precision=highest, preferred_element_type=jnp.float32
    )
    back_one, grad_gain_one = normalize_back(grad_one, hat_one, inverse_one, gain_attn)
    grad_tokens = grad_hidden + back_one
    grad_qkv, grad_out, grad_gain_attn, grad_gain_ffn = (
        lax.psum(grad_qkv_part.astype(jnp.bfloat16), "seq").astype(jnp.float32),
        lax.psum(grad_out_part.astype(jnp.bfloat16), "seq").astype(jnp.float32),
        lax.psum(grad_gain_one.astype(jnp.bfloat16), "seq").astype(jnp.float32),
        lax.psum(grad_gain_two.astype(jnp.bfloat16), "seq").astype(jnp.float32),
    )
    return (
        output,
        grad_tokens,
        grad_qkv,
        grad_out,
        grad_up,
        grad_down,
        grad_gain_attn,
        grad_gain_ffn,
        grad_router,
    )


def solution(mesh):
    return jax.shard_map(
        local,
        mesh=mesh,
        in_specs=(
            P("seq", None),
            P(None, None, "heads"),
            P("heads", None),
            P("seq", "heads"),
            P("heads", "seq"),
            P(),
            P(),
            P(),
            P(),
            P(),
            P(),
            P("seq", None),
        ),
        out_specs=(
            P("seq", None),
            P("seq", None),
            P(None, None, "heads"),
            P("heads", None),
            P("seq", "heads"),
            P("heads", "seq"),
            P(),
            P(),
            P(),
        ),
        check_vma=False,
    )
```

profile of v0, /device:TPU:0, one launch (start us, length us, event | category | flops | bytes accessed | tf_op | source)
XLA Modules:
  0.0 1484.3 jit_solution(1231842556310068782)
XLA Ops:
  21.9 11.1 fusion.159
  81.1 34.7 %all-gather.13.cloned.1.call-done = bf16[3,1024,512]{2,1,0:T(8,128)(2,1)} async-done(((bf16[3,128,512]{2,1,0:T(8,128)(2,1)}), bf16[3,1024,512]{2,1,0:T(8,128)(2,1)}) %all-gather.13.cloned.1.call-update) | async-done | bytes 3145744 | tf_op jit(solution)/shard_map/all_gather | solution.py:52
  134.2 29.6 %all-gather.17.cloned.1.call-done = bf16[2,2048,512]{2,1,0:T(8,128)(2,1)} async-done(((bf16[2,256,512]{2,1,0:T(8,128)(2,1)}), bf16[2,2048,512]{2,1,0:T(8,128)(2,1)}) %all-gather.17.cloned.1.call-update) | async-done | bytes 4194320 | tf_op jit(solution)/shard_map/all_gather | solution.py:52
  185.7 25.3 %all-gather.15.cloned.1.call-done = bf16[2,2048,512]{2,1,0:T(8,128)(2,1)} async-done(((bf16[2,256,512]{2,1,0:T(8,128)(2,1)}), bf16[2,2048,512]{2,1,0:T(8,128)(2,1)}) %all-gather.15.cloned.1.call-update) | async-done | bytes 4194320 | tf_op jit(solution)/shard_map/all_gather | solution.py:53
  217.1 10.8 fusion.70
  240.5 153.0 %all-reduce.8.cloned.1.call-done = f32[896,2048]{1,0:T(8,128)} async-done(((f32[896,2048]{1,0:T(8,128)}), f32[896,2048]{1,0:T(8,128)}) %all-reduce.8.cloned.1.call-update) | async-done | bytes 7340048 | tf_op jit(solution)/shard_map/psum | solution.py:212
  402.2 74.7 %all-gather.19.cloned.1.call-done = bf16[2048,2048]{1,0:T(8,128)(2,1)} async-done(((bf16[256,2048]{1,0:T(8,128)(2,1)}), bf16[2048,2048]{1,0:T(8,128)(2,1)}) %all-gather.19.cloned.1.call-update) | async-done | bytes 8388624 | tf_op jit(solution)/shard_map/all_gather | solution.py:216
  476.9 14.6 fusion.154
  491.6 67.9 %all-gather.21.cloned.1.call-done = bf16[2048,2048]{1,0:T(8,128)(2,1)} async-done(((bf16[2048,256]{1,0:T(8,128)(2,1)}), bf16[2048,2048]{1,0:T(8,128)(2,1)}) %all-gather.21.cloned.1.call-update) | async-done | bytes 8388624 | tf_op jit(solution)/shard_map/all_gather | solution.py:217
  559.5 15.0 %fusion.29 = bf16[896,2048]{1,0:T(8,128)(2,1)} fusion(f32[896,2048]{1,0:T(8,128)} %fusion.154, s32[2048]{0:T(1024)S(1)} %iota_add_fusion, s32[896]{0:T(1024)S(1)} %broadcast_multiply_fusion, bf16[896,2048]{1,0:T(8,128)(2,1)} %param.23, bf16[2048,2048]{1,0:T(8,128)(2,1)} %all-gather.21.cloned.1.call-done), kind=kOutput, calls=%fused_computation.42 | convolution fusion | flops 7530872832 | bytes 23080448 | tf_op jit(solution)/shard_map/dot_general | solution.py:231
  574.5 11.3 fusion.160
  593.2 146.5 %all-reduce.10.cloned.1.call-done = f32[896,2048]{1,0:T(8,128)} async-done(((f32[896,2048]{1,0:T(8,128)}), f32[896,2048]{1,0:T(8,128)}) %all-reduce.10.cloned.1.call-update) | async-done | bytes 7340048 | tf_op jit(solution)/shard_map/psum | solution.py:239
  760.4 15.4 %convolution_convert_fusion = bf16[2048,2048]{1,0:T(8,128)(2,1)} fusion(bf16[896,2048]{1,0:T(8,128)(2,1)} %param.23, f32[896,2048]{1,0:T(8,128)} %fusion.154, s32[2048]{0:T(1024)S(1)} %copy-done.58, s32[896]{0:T(1024)S(1)} %copy-done.63), kind=kOutput, calls=%fused_computation.31 | convolution fusion | flops 7529562112 | bytes 19410432 | tf_op jit(solution)/shard_map/dot_general | solution.py:237
  775.9 15.1 %convolution_convert_fusion.1 = bf16[2048,2048]{1,0:T(8,128)(2,1)} fusion(bf16[896,2048]{1,0:T(8,128)(2,1)} %fusion.29, f32[896,2048]{1,0:T(8,128)} %copy-done.3, f32[2048]{0:T(1024)S(1)} %copy-done.45, f32[896]{0:T(1024)S(1)} %add_rsqrt_fusion, f32[896]{0:T(1024)S(1)} %broadcast_multiply_fusion.6), kind=kOutput, calls=%fused_computation.32 | convolution fusion | flops 7527727104 | bytes 19414016 | tf_op jit(solution)/shard_map/dot_general | solution.py:238
  799.7 14.8 all_gather.51
  833.4 15.8 %all_gather.55 = f32[2,4,2048]{2,1,0:T(4,128)} all-gather(f32[2,4,256]{2,1,0:T(4,128)S(1)} %bitcast.162), channel_id=1, replica_groups=mesh['heads'=4,'seq'=8] {'seq'}, dimensions={2}, use_global_device_ids=true | all-gather | bytes 73728 | tf_op jit(solution)/shard_map/all_gather | solution.py:275
  849.2 10.4 fusion.87
  872.1 13.7 multiply_reduce_fusion
  885.8 14.8 fusion.74
  901.0 15.5 %all_gather.53 = f32[3,4,1024]{2,1,0:T(4,128)S(1)} all-gather(f32[3,4,128]{2,1,0:T(4,128)S(1)} %get-tuple-element.61), channel_id=1, replica_groups=mesh['heads'=4,'seq'=8] {'seq'}, dimensions={2}, use_global_device_ids=true | all-gather | bytes 55296 | tf_op jit(solution)/shard_map/all_gather | solution.py:276
  916.4 15.4 %all_gather.57 = f32[2,4,2048]{2,1,0:T(4,128)} all-gather(f32[2,4,256]{2,1,0:T(4,128)S(1)} %get-tuple-element.59), channel_id=1, replica_groups=mesh['heads'=4,'seq'=8] {'seq'}, dimensions={2}, use_global_device_ids=true | all-gather | bytes 73728 | tf_op jit(solution)/shard_map/all_gather | solution.py:276
  956.0 9.5 fusion.67
  966.0 13.0 fusion.72
  997.3 12.3 convolution_convert_fusion.2
  1010.3 14.9 %convolution_convert_fusion.3 = bf16[896,2048]{1,0:T(8,128)(2,1)} fusion(bf16[2048,2048]{1,0:T(8,128)(2,1)} %all-gather.21.cloned.1.call-done, f32[896,2048]{1,0:T(8,128)} %fusion.154, s32[2048]{0:T(1024)S(1)} %copy-done.59, s32[896]{0:T(1024)S(1)} %copy-done.64), kind=kOutput, calls=%fused_computation.73 | convolution fusion | flops 7527202816 | bytes 19410432 | tf_op jit(solution)/shard_map/dot_general | solution.py:221
  1025.2 10.2 bitcast_convert_fusion
  1041.6 28.2 %psum.67 = bf16[5,2048]{1,0:T(8,128)(2,1)S(1)} all-reduce(bf16[5,2048]{1,0:T(8,128)(2,1)S(1)} %fusion.55), channel_id=1, replica_groups=mesh['heads'=4,'seq'=8] {'seq'}, use_global_device_ids=true, to_apply=%region_18.19 | all-reduce | flops 10240 | bytes 40960 | tf_op jit(solution)/shard_map/psum | solution.py:191
  1074.6 22.2 %reduce-scatter.3.cloned.1.call-done = bf16[256,2048]{1,0:T(8,128)(2,1)} async-done(((bf16[2048,2048]{1,0:T(8,128)(2,1)}), bf16[256,2048]{1,0:T(8,128)(2,1)}) %reduce-scatter.3.cloned.1.call-update) | async-done | bytes 1048592 | tf_op jit(solution)/shard_map/reduce_scatter | solution.py:243
  1099.6 173.5 %all-reduce.12.cloned.1.call-done = (bf16[2048,3,512]{2,0,1:T(8,128)(2,1)}, bf16[512,2048]{1,0:T(8,128)(2,1)}) async-done(((bf16[2048,3,512]{2,0,1:T(8,128)(2,1)}, bf16[512,2048]{1,0:T(8,128)(2,1)}), (bf16[2048,3,512]{2,0,1:T(8,128)(2,1)}, bf16[512,2048]{1,0:T(8,128)(2,1)})) %all-reduce.12.cloned.1.call-update) | async-done | bytes 8388624 | tf_op jit(solution)/shard_map/psum | solution.py:324
  1284.6 148.0 %all-reduce.14.cloned.1.call-done = (bf16[896,2048]{1,0:T(8,128)(2,1)}, bf16[896,2048]{1,0:T(8,128)(2,1)}) async-done(((bf16[896,2048]{1,0:T(8,128)(2,1)}, bf16[896,2048]{1,0:T(8,128)(2,1)}), (bf16[896,2048]{1,0:T(8,128)(2,1)}, bf16[896,2048]{1,0:T(8,128)(2,1)})) %all-reduce.14.cloned.1.call-update) | async-done | bytes 7340048 | tf_op jit(solution)/shard_map/psum | solution.py:222
  1449.4 16.5 %all-reduce = (bf16[2048]{0:T(1024)(128)(2,1)S(1)}, bf16[2048]{0:T(1024)(128)(2,1)S(1)}) all-reduce(bf16[2048]{0:T(1024)(128)(2,1)S(1)} %get-tuple-element.11, bf16[2048]{0:T(1024)(128)(2,1)S(1)} %copy-done.52), channel_id=1, replica_groups=mesh['heads'=4,'seq'=8] {'seq'}, use_global_device_ids=true, to_apply=%region_30.31 | all-reduce | flops 4096 | bytes 16384 | tf_op jit(solution)/shard_map/psum | solution.py:326
  1467.1 10.4 fusion.23
  (303 shorter events, 285.3 us)
Async XLA Ops:
  7.2 225.5 %copy-start = (bf16[512,2048]{1,0:T(8,128)(2,1)S(1)}, bf16[512,2048]{1,0:T(8,128)(2,1)}, u32[]{:S(2)}) copy-start(bf16[512,2048]{1,0:T(8,128)(2,1)} %param.14) | copy-start | bytes 6291460
  7.2 69.3 %all-gather.11.cloned.1.call-start = ((), (), s32[]{:S(2)}) async-start(), calls=%async_computation.2 | async-start | bytes 3538944 | tf_op jit(solution)/shard_map/all_gather | solution.py:53
  35.4 80.4 %all-gather.13.cloned.1.call-start = ((), (), s32[]{:S(2)}) async-start(), calls=%async_computation.3 | async-start | bytes 3538944 | tf_op jit(solution)/shard_map/all_gather | solution.py:52
  58.0 105.8 %all-gather.17.cloned.1.call-start = ((), (), s32[]{:S(2)}) async-start(), calls=%async_computation.5 | async-start | bytes 4718592 | tf_op jit(solution)/shard_map/all_gather | solution.py:52
  61.8 149.2 %all-gather.15.cloned.1.call-start = ((), (), s32[]{:S(2)}) async-start(), calls=%async_computation.4 | async-start | bytes 4718592 | tf_op jit(solution)/shard_map/all_gather | solution.py:53
  63.7 329.7 %all-reduce.8.cloned.1.call-start = ((), (), s32[]{:S(2)}) async-start(), calls=%async_computation.6 | async-start | bytes 14680064 | tf_op jit(solution)/shard_map/psum | solution.py:212
  64.3 56.1 %copy-start.60 = (s32[256]{0:T(256)}, s32[256]{0:T(256)S(1)}, u32[]{:S(2)}) copy-start(s32[256]{0:T(256)S(1)} %iota_add_fusion.2) | copy-start | bytes 3076
  64.4 167.4 %copy-start.69 = (s32[512]{0:T(512)}, s32[512]{0:T(512)S(1)}, u32[]{:S(2)}) copy-start(s32[512]{0:T(512)S(1)} %fusion.125) | copy-start | bytes 6148
  69.1 162.7 %copy-start.65 = (s32[896]{0:T(1024)}, s32[896]{0:T(1024)S(1)}, u32[]{:S(2)}) copy-start(s32[896]{0:T(1024)S(1)} %broadcast_multiply_fusion.1) | copy-start | bytes 10756
  69.3 56.6 %copy-start.11 = (pred[128,1024]{1,0:T(8,128)(4,1)}, pred[128,1024]{1,0:T(8,128)(4,1)S(1)}, u32[]{:S(2)}) copy-start(pred[128,1024]{1,0:T(8,128)(4,1)S(1)} %iota_compare_fusion.3) | copy-start | bytes 393220
  185.6 42.3 %copy-start.46 = (f32[2,4,256]{2,1,0:T(4,128)}, f32[2,4,256]{2,1,0:T(4,128)S(1)}, u32[]{:S(2)}) copy-start(f32[2,4,256]{2,1,0:T(4,128)S(1)} %fusion) | copy-start | bytes 24580
  239.0 237.9 %all-gather.19.cloned.1.call-start = ((), (), s32[]{:S(2)}) async-start(), calls=%async_computation.7 | async-start | bytes 9437184 | tf_op jit(solution)/shard_map/all_gather | solution.py:216
  239.6 319.9 %all-gather.21.cloned.1.call-start = ((), (), s32[]{:S(2)}) async-start(), calls=%async_computation.8 | async-start | bytes 9437184 | tf_op jit(solution)/shard_map/all_gather | solution.py:217
  240.4 499.3 %all-reduce.10.cloned.1.call-start = ((), (), s32[]{:S(2)}) async-start(), calls=%async_computation.9 | async-start | bytes 14680064 | tf_op jit(solution)/shard_map/psum | solution.py:239
  240.4 319.1 %copy-start.57 = (s32[2048]{0:T(1024)}, s32[2048]{0:T(1024)S(1)}, u32[]{:S(2)}) copy-start(s32[2048]{0:T(1024)S(1)} %iota_add_fusion) | copy-start | bytes 24580
  240.5 319.1 %copy-start.62 = (s32[896]{0:T(1024)}, s32[896]{0:T(1024)S(1)}, u32[]{:S(2)}) copy-start(s32[896]{0:T(1024)S(1)} %broadcast_multiply_fusion) | copy-start | bytes 10756
  398.3 78.6 %copy-start.44 = (f32[2048]{0:T(1024)S(1)}, f32[2048]{0:T(1024)}, u32[]{:S(2)}) copy-start(f32[2048]{0:T(1024)} %param.18) | copy-start | bytes 24580
  585.9 209.1 %all-gather.23.cloned.1.call-start = ((), (), s32[]{:S(2)}) async-start(), calls=%async_computation.10 | async-start | bytes 3538944 | tf_op jit(solution)/shard_map/all_gather | solution.py:271
  589.8 237.3 %all-gather.27.cloned.1.call-start = ((), (), s32[]{:S(2)}) async-start(), calls=%async_computation.12 | async-start | bytes 4718592 | tf_op jit(solution)/shard_map/all_gather | solution.py:271
  593.1 154.2 %copy-start.45 = (f32[2048]{0:T(1024)S(1)}, f32[2048]{0:T(1024)}, u32[]{:S(2)}) copy-start(f32[2048]{0:T(1024)} %param.18) | copy-start | bytes 24580
  593.1 346.1 %all-gather.25.cloned.1.call-start = ((), (), s32[]{:S(2)}) async-start(), calls=%async_computation.11 | async-start | bytes 3538944 | tf_op jit(solution)/shard_map/all_gather | solution.py:272
  758.2 197.9 %all-gather.29.cloned.1.call-start = ((), (), s32[]{:S(2)}) async-start(), calls=%async_computation.13 | async-start | bytes 4718592 | tf_op jit(solution)/shard_map/all_gather | solution.py:272
  760.3 311.6 %reduce-scatter.5.cloned.1.call-start = ((), (), s32[]{:S(2)}) async-start(), calls=%async_computation.15 | async-start | bytes 9437184 | tf_op jit(solution)/shard_map/reduce_scatter | solution.py:246
  775.8 321.0 %reduce-scatter.3.cloned.1.call-start = ((), (), s32[]{:S(2)}) async-start(), calls=%async_computation.14 | async-start | bytes 9437184 | tf_op jit(solution)/shard_map/reduce_scatter | solution.py:243
  791.0 23.5 %copy-start.20 = (bf16[384,4,128]{2,0,1:T(8,128)(2,1)S(1)}, bf16[384,4,128]{2,0,1:T(8,128)(2,1)}, u32[]{:S(2)}) copy-start(bf16[384,4,128]{2,0,1:T(8,128)(2,1)} %copy-done.19) | copy-start | bytes 1179652
  791.0 482.2 %all-reduce.12.cloned.1.call-start = ((), (), s32[]{:S(2)}) async-start(), calls=%async_computation.16 | async-start | bytes 16777216 | tf_op jit(solution)/shard_map/psum | solution.py:324
  820.1 29.1 %copy-start.18 = (bf16[512,4,128]{2,0,1:T(8,128)(2,1)S(1)}, bf16[512,4,128]{2,0,1:T(8,128)(2,1)}, u32[]{:S(2)}) copy-start(bf16[512,4,128]{2,0,1:T(8,128)(2,1)} %copy-done.17) | copy-start | bytes 1572868
  885.8 46.0 %copy-start.31 = (f32[48,8,4,128]{3,1,2,0:T(8,128)S(1)}, f32[48,8,4,128]{3,1,2,0:T(8,128)}, u32[]{:S(2)}) copy-start(f32[48,8,4,128]{3,1,2,0:T(8,128)} %copy.273) | copy-start | bytes 2359300
  900.9 38.2 %copy-start.41 = (f32[3,4,1024]{2,1,0:T(4,128)S(1)}, f32[3,4,1024]{2,1,0:T(4,128)}, u32[]{:S(2)}) copy-start(f32[3,4,1024]{2,1,0:T(4,128)} %all_gather.51) | copy-start | bytes 147460
  1009.6 423.0 %all-reduce.14.cloned.1.call-start = ((), (), s32[]{:S(2)}) async-start(), calls=%async_computation.17 | async-start | bytes 14680064 | tf_op jit(solution)/shard_map/psum | solution.py:222
  1035.4 34.4 %copy-start.37 = (f32[2048,8]{0,1:T(8,128)S(1)}, f32[2048,8]{0,1:T(8,128)}, u32[]{:S(2)}) copy-start(f32[2048,8]{0,1:T(8,128)} %param.19) | copy-start | bytes 196612
  1035.4 35.1 %copy-start.71 = (s32[5,2]{0,1:T(2,128)S(1)}, s32[5,2]{0,1:T(2,128)}, u32[]{:S(2)}) copy-start(s32[5,2]{0,1:T(2,128)} %param.22) | copy-start | bytes 124
  (58 other events, 343.5 us)
Sparse Core Ops, SparseCore 0:
  35.5 40.9 all-gather.10
  78.6 37.1 all-gather.12
  118.0 45.7 all-gather.16
  165.2 45.6 all-gather.14
  239.2 154.2 all-reduce.7
  394.9 82.0 all-gather.18
  478.5 80.9 all-gather.20
  586.0 153.5 all-reduce.9
  741.2 38.1 all-gather.22
  780.9 46.1 all-gather.26
  828.7 40.0 all-gather.24
  870.9 44.4 all-gather.28
  917.7 87.9 reduce-scatter.4
  1008.4 88.4 reduce-scatter.2
  1099.1 174.0 all-reduce.11
  1277.1 155.5 all-reduce.13
where the time goes:
time: 1490 us; the launch traced here: 1480 us
  waiting for transfers between devices  891 us (60%)
  matrix products  268 us (18%)
  local copies, waits for them, and re-layouts  114 us (8%)
  blocking collectives  106 us (7%)
  other arithmetic  88.7 us (6%)
  between operations  15.2 us (1%)
    psum x1, waiting for transfers between devices, local(): lax.psum(grad_qkv_part.astype(jnp.bfloat16), 'seq').astype(jnp.float32)  174 us
    psum x1, waiting for transfers between devices, local(): hidden = tokens_wide + lax.psum(attn_part, 'heads')  153 us
    psum x1, waiting for transfers between devices, local(): lax.psum(ffn_part.astype(jnp.bfloat16), 'heads').astype(jnp.float32)  148 us
    psum x1, waiting for transfers between devices, local(): lax.psum(jnp.dot(grad_upward, back_up.T, preferred_element_type=jnp.float...  146 us
    all_gather x1, waiting for transfers between devices, local(): lax.all_gather(w_up, 'seq', axis=0, tiled=True)  74.7 us
    all_gather x1, waiting for transfers between devices, local(): lax.all_gather(w_down, 'seq', axis=1, tiled=True)  67.9 us
    all_gather x2, waiting for transfers between devices, gather_rows(): lax.all_gather(keys, 'seq', axis=1, tiled=True)  64.2 us
    unnamed x153, local copies, waits for them, and re-layouts  34 us
  transfers between devices with their start and end apart: 16, of which 12 were waited for; matrix products, arithmetic and copies ran while one was open for 23% of the time, Pallas kernels for 0%

commit v1 on v0

v1 whole, which is shorter than its diff:
```python
import functools

import jax
import jax.numpy as jnp
from jax import lax
from jax.experimental import pallas as pl
from jax.experimental.pallas import tpu as pltpu
from jax.sharding import PartitionSpec as P

D = 2048
H = 16
HD = 128
FF = 8192
SHORT_DEV = 128
NSHORT = 3
NLONG = 2
LEVELS = 4
SEQS = 5
CHUNKS = NSHORT + 2 * NLONG

epsilon = 1e-05
highest = lax.Precision.HIGHEST
f32 = jnp.float32
bf16 = jnp.bfloat16
SCALE = HD ** (-0.5)


def dot(left, right):
    return jnp.dot(left, right, preferred_element_type=f32)


def contract(left, right, left_dim, right_dim):
    return lax.dot_general(
        left, right, (((left_dim,), (right_dim,)), ((), ())), preferred_element_type=f32
    )


def normalize_parts(values):
    centered = values - jnp.mean(values, axis=-1, keepdims=True)
    inverse = lax.rsqrt(jnp.mean(centered * centered, axis=-1, keepdims=True) + epsilon)
    return (centered * inverse, inverse)


def normalize_back(grad_normed, normed_hat, inverse, gain):
    grad_hat = grad_normed * gain
    middle = (
        grad_hat
        - jnp.mean(grad_hat, axis=-1, keepdims=True)
        - normed_hat * jnp.mean(grad_hat * normed_hat, axis=-1, keepdims=True)
    )
    return (inverse * middle, jnp.sum(grad_normed * normed_hat, axis=0))


def flip(values, axis, size, bit):
    return lax.ppermute(values, axis, [(i, i ^ bit) for i in range(size)])


def butterfly(values, axis, size):
    bit = 1
    while bit < size:
        values = values + flip(values, axis, size, bit)
        bit *= 2
    return values


def key_copies(scal, own, others, keys_short, keys_long, sems, members, heads):
    head, member = scal[0], scal[1]
    copies = []
    for part in range(members):
        source = own if part == 0 else others[(part - 1) * heads : part * heads]
        whose = lax.rem(member + part, members)
        for slot in range(heads):
            block = (head ^ slot) * members + whose
            number = len(copies)
            copies.append(
                pltpu.make_async_copy(
                    source[slot].at[0:NSHORT], keys_short.at[:, block], sems.at[number]
                )
            )
            for index in range(NLONG):
                first = NSHORT + 2 * index
                number = len(copies)
                copies.append(
                    pltpu.make_async_copy(
                        source[slot].at[first : first + 2],
                        keys_long.at[index, block],
                        sems.at[number],
                    )
                )
    return copies


def row_copies(scal, slots, held, sems, heads, outward):
    head = scal[0]
    copies = []
    for slot in range(heads):
        ends = (slots[slot], held.at[head ^ slot])
        if outward:
            ends = ends[::-1]
        copies.append(pltpu.make_async_copy(ends[0], ends[1], sems.at[slot]))
    return copies


def sequence_loop(work):
    def short(index, carry):
        work(0, index, index, 1, index)
        return carry

    def long(index, carry):
        work(1, index, NSHORT + 2 * index, 2, NSHORT + index)
        return carry

    lax.fori_loop(0, NSHORT, short, 0)
    lax.fori_loop(0, NLONG, long, 0)


def allowed_mask(member, members, size):
    key_at = lax.broadcasted_iota(jnp.int32, (members * size, size), 0)
    query_at = lax.broadcasted_iota(jnp.int32, (members * size, size), 1) + member * size
    return key_at <= query_at


def attend_kernel(heads, members, scal, *refs):
    count = heads
    query_slots = refs[:count]
    own = refs[count : 2 * count]
    others = refs[2 * count : (1 + members) * count]
    rest = refs[(1 + members) * count :]
    out_slots = rest[:count]
    log_ref = rest[count]
    queries, keys_short, keys_long, mixed, row_sems, key_sems = rest[count + 1 :]
    copies = row_copies(scal, query_slots, queries, row_sems, heads, False)
    copies += key_copies(scal, own, others, keys_short, keys_long, key_sems, members, heads)
    for copy in copies:
        copy.start()
    for copy in copies:
        copy.wait()

    def work(kind, index, first, chunks, live_at):
        size = chunks * SHORT_DEV
        live = scal[2 + live_at].astype(f32)
        mask = allowed_mask(scal[1], members, size)
        for place in range(heads):
            span = (place + 1) * members
            if kind == 0:
                block = keys_short[index, 0:span]
            else:
                block = keys_long[index, 0:span]
            block = block.reshape(span * size, 2 * HD)
            keys, values = block[:, :HD], block[:, HD:]
            query = queries[place, pl.ds(first, chunks)].reshape(size, HD)
            scores = contract(keys, query, 1, 1) * SCALE
            edge = place * members * size
            last = jnp.where(mask, scores[edge:], -1e30)
            largest = jnp.max(last, axis=0, keepdims=True)
            if place:
                early = scores[:edge]
                largest = jnp.maximum(largest, jnp.max(early, axis=0, keepdims=True))
            raised = jnp.exp(last - largest)
            total = jnp.sum(raised, axis=0, keepdims=True)
            low = raised.astype(bf16)
            turned = contract(values[edge:], low, 0, 0)
            if place:
                raised = jnp.exp(early - largest)
                total = total + jnp.sum(raised, axis=0, keepdims=True)
                turned = turned + contract(values[:edge], raised.astype(bf16), 0, 0)
            turned = turned * (live / total)
            mixed[place, pl.ds(first, chunks)] = (
                turned.T.astype(bf16).reshape(chunks, SHORT_DEV, HD)
            )
            logs = largest + jnp.log(total)
            for chunk in range(chunks):
                log_ref[place, first + chunk] = logs[:, chunk * SHORT_DEV : (chunk + 1) * SHORT_DEV]

    sequence_loop(work)
    copies = row_copies(scal, out_slots, mixed, row_sems, heads, True)
    for copy in copies:
        copy.start()
    for copy in copies:
        copy.wait()


def attend_forward(scal, query_slots, own, others, heads, members):
    blocks = heads * members
    anywhere = pl.BlockSpec(memory_space=pl.ANY)
    result = pl.pallas_call(
        functools.partial(attend_kernel, heads, members),
        out_shape=[jax.ShapeDtypeStruct((CHUNKS, SHORT_DEV, HD), bf16)] * heads
        + [jax.ShapeDtypeStruct((heads, CHUNKS, 1, SHORT_DEV), f32)],
        in_specs=[pl.BlockSpec(memory_space=pltpu.SMEM)]
        + [anywhere] * (len(query_slots) + len(own) + len(others)),
        out_specs=[anywhere] * heads + [pl.BlockSpec(memory_space=pltpu.VMEM)],
        scratch_shapes=[
            pltpu.VMEM((heads, CHUNKS, SHORT_DEV, HD), bf16),
            pltpu.VMEM((NSHORT, blocks, SHORT_DEV, 2 * HD), bf16),
            pltpu.VMEM((NLONG, blocks, 2, SHORT_DEV, 2 * HD), bf16),
            pltpu.VMEM((heads, CHUNKS, SHORT_DEV, HD), bf16),
            pltpu.SemaphoreType.DMA((heads,)),
            pltpu.SemaphoreType.DMA((3 * blocks,)),
        ],
        compiler_params=pltpu.CompilerParams(vmem_limit_bytes=56 << 20),
        cost_estimate=pl.CostEstimate(
            flops=4 * 10**9, bytes_accessed=7 << 20, transcendentals=4 * 10**6
        ),
        name="attend_forward",
    )(scal, *query_slots, *own, *others)
    return (result[:heads], result[heads])


def back_kernel(heads, members, scal, *refs):
    count = heads
    query_slots = refs[:count]
    own = refs[count : 2 * count]
    others = refs[2 * count : (1 + members) * count]
    rest = refs[(1 + members) * count :]
    grad_slots = rest[:count]
    log_ref = rest[count]
    rest = rest[count + 1 :]
    query_out = rest[:count]
    pair_out = rest[count : (1 + members) * count]
    scratch = rest[(1 + members) * count :]
    queries, keys_short, keys_long, grads, sum_short, sum_long = scratch[:6]
    low_short, low_long, row_sems, grad_sems, key_sems = scratch[6:]
    copies = row_copies(scal, query_slots, queries, row_sems, heads, False)
    copies += row_copies(scal, grad_slots, grads, grad_sems, heads, False)
    copies += key_copies(scal, own, others, keys_short, keys_long, key_sems, members, heads)
    for copy in copies:
        copy.start()
    for copy in copies:
        copy.wait()

    def work(kind, index, first, chunks, live_at):
        size = chunks * SHORT_DEV
        live = scal[2 + live_at].astype(bf16)
        mask = allowed_mask(scal[1], members, size)
        if kind == 0:
            keys_ref, sum_ref, low_ref = keys_short, sum_short, low_short
        else:
            keys_ref, sum_ref, low_ref = keys_long, sum_long, low_long
        for place in reversed(range(heads)):
            span = (place + 1) * members
            block = keys_ref[index, 0:span].reshape(span * size, 2 * HD)
            keys, values = block[:, :HD], block[:, HD:]
            query = queries[place, pl.ds(first, chunks)].reshape(size, HD)
            grad = grads[place, pl.ds(first, chunks)].reshape(size, HD) * live
            logs = jnp.concatenate(
                [log_ref[place, first + chunk] for chunk in range(chunks)], axis=1
            )
            probs = jnp.exp(contract(keys, query, 1, 1) * SCALE - logs)
            edge = place * members * size
            last = jnp.where(mask, probs[edge:], 0.0)
            probs = jnp.concatenate([probs[:edge], last], axis=0) if place else last
            grad_probs = contract(values, grad, 1, 1)
            delta = jnp.sum(probs * grad_probs, axis=0, keepdims=True)
            grad_scores = (probs * (grad_probs - delta)).astype(bf16)
            grad_value = dot(probs.astype(bf16), grad)
            grad_key = dot(grad_scores, query) * SCALE
            turned = contract(keys, grad_scores, 0, 0) * SCALE
            queries[place, pl.ds(first, chunks)] = (
                turned.T.astype(bf16).reshape(chunks, SHORT_DEV, HD)
            )
            pair = jnp.concatenate([grad_key, grad_value], axis=1)
            if place == heads - 1:
                sum_ref[...] = pair
            else:
                sum_ref[0 : span * size] += pair
        low_ref[index] = sum_ref[...].astype(bf16).reshape(low_ref.shape[1:])

    sequence_loop(work)
    copies = row_copies(scal, query_out, queries, row_sems, heads, True)
    head, member = scal[0], scal[1]
    number = 0
    for part in range(members):
        whose = lax.rem(member + part, members)
        for slot in range(heads):
            block = (head ^ slot) * members + whose
            target = pair_out[part * heads + slot]
            copies.append(
                pltpu.make_async_copy(
                    low_short.at[:, block], target.at[0:NSHORT], key_sems.at[number]
                )
            )
            number += 1
            for index in range(NLONG):
                first = NSHORT + 2 * index
                copies.append(
                    pltpu.make_async_copy(
                        low_long.at[index, block],
                        target.at[first : first + 2],
                        key_sems.at[number],
                    )
                )
                number += 1
    for copy in copies:
        copy.start()
    for copy in copies:
        copy.wait()


def attend_backward(scal, query_slots, own, others, grad_slots, logs, heads, members):
    blocks = heads * members
    anywhere = pl.BlockSpec(memory_space=pl.ANY)
    result = pl.pallas_call(
        functools.partial(back_kernel, heads, members),
        out_shape=[jax.ShapeDtypeStruct((CHUNKS, SHORT_DEV, HD), bf16)] * heads
        + [jax.ShapeDtypeStruct((CHUNKS, SHORT_DEV, 2 * HD), bf16)] * blocks,
        in_specs=[pl.BlockSpec(memory_space=pltpu.SMEM)]
        + [anywhere] * (2 * heads + blocks)
        + [pl.BlockSpec(memory_space=pltpu.VMEM)],
        out_specs=[anywhere] * (heads + blocks),
        scratch_shapes=[
            pltpu.VMEM((heads, CHUNKS, SHORT_DEV, HD), bf16),
            pltpu.VMEM((NSHORT, blocks, SHORT_DEV, 2 * HD), bf16),
            pltpu.VMEM((NLONG, blocks, 2, SHORT_DEV, 2 * HD), bf16),
            pltpu.VMEM((heads, CHUNKS, SHORT_DEV, HD), bf16),
            pltpu.VMEM((blocks * SHORT_DEV, 2 * HD), f32),
            pltpu.VMEM((2 * blocks * SHORT_DEV, 2 * HD), f32),
            pltpu.VMEM((NSHORT, blocks, SHORT_DEV, 2 * HD), bf16),
            pltpu.VMEM((NLONG, blocks, 2, SHORT_DEV, 2 * HD), bf16),
            pltpu.SemaphoreType.DMA((heads,)),
            pltpu.SemaphoreType.DMA((heads,)),
            pltpu.SemaphoreType.DMA((3 * blocks,)),
        ],
        compiler_params=pltpu.CompilerParams(vmem_limit_bytes=60 << 20),
        cost_estimate=pl.CostEstimate(
            flops=10**10, bytes_accessed=12 << 20, transcendentals=4 * 10**6
        ),
        name="attend_backward",
    )(scal, *query_slots, *own, *others, *grad_slots, logs)
    return (result[:heads], result[heads:])


def local(
    tokens,
    w_qkv,
    w_out,
    w_up,
    w_down,
    gain_attn,
    gain_ffn,
    w_router,
    head_quarters,
    ffn_quarters,
    router_targets,
    cotangent,
):
    rows = tokens.shape[0]
    seq_rank = lax.axis_index("seq")
    seq_count = lax.axis_size("seq")
    head_rank = lax.axis_index("heads")
    head_count = lax.axis_size("heads")
    head_width = w_out.shape[0]
    ffn_width = w_up.shape[1]
    heads = head_width // HD
    members = seq_count // heads
    place, member = seq_rank // members, seq_rank % members
    share = rows // head_count
    short_rows = NSHORT * SHORT_DEV

    def across(values, slot):
        pairs = [
            (h * members + m, (h ^ slot) * members + m)
            for h in range(heads)
            for m in range(members)
        ]
        return lax.ppermute(values, "seq", pairs)

    def among(values, step):
        pairs = [
            (h * members + (m + step) % members, h * members + m)
            for h in range(heads)
            for m in range(members)
        ]
        return lax.ppermute(values, "seq", pairs)

    def swap(values, slot):
        return flip(values, "heads", head_count, slot)

    def own_rows(values, slot):
        return lax.dynamic_slice_in_dim(values, (head_rank ^ slot) * share, share, 0)

    def scatter_heads(parts):
        return [parts[0]] + [
            swap(parts[slot].astype(bf16), slot).astype(f32) for slot in range(1, head_count)
        ]

    def gather_heads(values):
        return [values] + [swap(values, slot) for slot in range(1, head_count)]

    def in_order(slots, kind):
        full = jnp.zeros((rows,) + slots[0].shape[1:], kind)
        for slot in range(head_count):
            full = lax.dynamic_update_slice_in_dim(
                full, slots[slot].astype(kind), (head_rank ^ slot) * share, 0
            )
        return full

    full_up = lax.all_gather(w_up, "seq", axis=0, tiled=True)
    full_down = lax.all_gather(w_down, "seq", axis=1, tiled=True)

    column = jnp.arange(rows)
    is_short = column < short_rows
    offset = column - short_rows
    seq_id = jnp.where(is_short, column // SHORT_DEV, NSHORT + offset // (2 * SHORT_DEV))
    position = jnp.where(
        is_short,
        seq_rank * SHORT_DEV + column % SHORT_DEV,
        seq_rank * 2 * SHORT_DEV + offset % (2 * SHORT_DEV),
    )
    in_seq = seq_id[:, None] == jnp.arange(SEQS)[None, :]
    seq_length = jnp.where(
        jnp.arange(SEQS) < NSHORT, SHORT_DEV * seq_count, 2 * SHORT_DEV * seq_count
    ).astype(f32)
    ffn_level = jnp.sum(jnp.where(in_seq, ffn_quarters[None, :], 0), axis=1)
    half_dim = HD // 2
    frequency = 10000.0 ** (-jnp.arange(half_dim, dtype=f32) * 2.0 / HD)
    angle = position.astype(f32)[:, None] * frequency[None, :]
    cosine = jnp.cos(angle)
    sine = jnp.sin(angle)
    my_head = head_rank * heads + place
    head_live = (my_head < head_quarters * (H // LEVELS)).astype(jnp.int32)
    scal = jnp.concatenate([jnp.stack([place, member]).astype(jnp.int32), head_live])

    tokens_wide = tokens.astype(f32)
    hat_one, _ = normalize_parts(tokens_wide)
    normed_one = hat_one * gain_attn
    normed_low = normed_one.astype(bf16)
    pool_short = jnp.sum(normed_one[:short_rows].reshape(NSHORT, SHORT_DEV, D), axis=1)
    pool_long = jnp.sum(normed_one[short_rows:].reshape(NLONG, 2 * SHORT_DEV, D), axis=1)
    flat_qkv = w_qkv.reshape(D, -1)
    projected = dot(normed_low, flat_qkv).reshape(rows, 3, head_width)

    def turn(values, back):
        former, latter = values[..., :half_dim], values[..., half_dim:]
        spin = -sine if back else sine
        return jnp.concatenate(
            [former * cosine - latter * spin, latter * cosine + former * spin], axis=-1
        )

    query_slots, pair_slots = [], []
    for slot in range(heads):
        start = (place ^ slot) * HD
        piece = lax.dynamic_slice_in_dim(projected, start, HD, 2)
        query = turn(piece[:, 0], False).astype(bf16)
        pair = jnp.concatenate([turn(piece[:, 1], False), piece[:, 2]], axis=1).astype(bf16)
        query = query.reshape(CHUNKS, SHORT_DEV, HD)
        pair = pair.reshape(CHUNKS, SHORT_DEV, 2 * HD)
        query_slots.append(across(query, slot) if slot else query)
        pair_slots.append(across(pair, slot) if slot else pair)
    other_slots = [
        among(pair_slots[slot], step) for step in range(1, members) for slot in range(heads)
    ]
    mixed_slots, logs = attend_forward(
        scal, query_slots, pair_slots, other_slots, heads, members
    )
    mixed_slots = [across(v, slot) if slot else v for slot, v in enumerate(mixed_slots)]
    mixed_slots = [v.reshape(rows, HD) for v in mixed_slots]
    heads_out = jnp.zeros((rows, head_width), bf16)
    for slot in range(heads):
        heads_out = lax.dynamic_update_slice_in_dim(
            heads_out, mixed_slots[slot], (place ^ slot) * HD, 1
        )

    pooled_sum = jnp.concatenate([pool_short, pool_long], axis=0)
    pooled = butterfly(pooled_sum, "seq", seq_count) * lax.rsqrt(seq_length)[:, None]

    heads_rel = [own_rows(heads_out, slot) for slot in range(head_count)]
    attn_parts = scatter_heads([dot(v, w_out) for v in heads_rel])
    tokens_own = own_rows(tokens, 0).astype(f32)
    hidden = tokens_own + sum(attn_parts[1:], attn_parts[0])
    hat_two, inverse_two = normalize_parts(hidden)
    normed_two = jnp.concatenate(gather_heads((hat_two * gain_ffn).astype(bf16)), axis=0)

    cotangent_rel = jnp.concatenate(
        [own_rows(cotangent, slot) for slot in range(head_count)], axis=0
    )
    level_rel = jnp.concatenate([own_rows(ffn_level, slot) for slot in range(head_count)])
    unit_index = head_rank * ffn_width + jnp.arange(ffn_width)
    ffn_live = (unit_index[None, :] < (level_rel * (FF // LEVELS))[:, None]).astype(f32)
    upward = dot(normed_two, full_up)
    kept = jnp.maximum(upward, 0.0)
    active = (jnp.square(kept) * ffn_live).astype(bf16)
    grad_active = contract(cotangent_rel, full_down, 1, 1).astype(bf16).astype(f32)
    grad_upward = (grad_active * ffn_live * 2.0 * kept).astype(bf16)
    two_parts = scatter_heads(
        [
            contract(grad_upward[slot * share : (slot + 1) * share], full_up, 1, 1)
            for slot in range(head_count)
        ]
    )
    ffn_parts = scatter_heads(
        [
            dot(active[slot * share : (slot + 1) * share], full_down)
            for slot in range(head_count)
        ]
    )
    grad_up_part = contract(normed_two, grad_upward, 0, 0).astype(bf16)
    grad_down_part = contract(active, cotangent_rel, 0, 0).astype(bf16)
    grad_up = lax.psum_scatter(grad_up_part, "seq", scatter_dimension=0, tiled=True).astype(f32)
    grad_down = lax.psum_scatter(
        grad_down_part, "seq", scatter_dimension=1, tiled=True
    ).astype(f32)

    grad_two = sum(two_parts[1:], two_parts[0])
    back_two, gain_two = normalize_back(grad_two, hat_two, inverse_two, gain_ffn)
    grad_hidden = own_rows(cotangent, 0).astype(f32) + back_two
    grad_attn = gather_heads(grad_hidden.astype(bf16))
    grad_heads = in_order([contract(v, w_out, 1, 1).astype(bf16) for v in grad_attn], bf16)
    grad_slots = []
    for slot in range(heads):
        piece = lax.dynamic_slice_in_dim(grad_heads, (place ^ slot) * HD, HD, 1)
        piece = piece.reshape(CHUNKS, SHORT_DEV, HD)
        grad_slots.append(across(piece, slot) if slot else piece)
    grad_out_part = contract(
        jnp.concatenate(heads_rel, axis=0), jnp.concatenate(grad_attn, axis=0), 0, 0
    ).astype(bf16)
    output_own = (hidden + sum(ffn_parts[1:], ffn_parts[0])).astype(bf16)
    output = in_order(gather_heads(output_own), bf16)

    grad_query_slots, grad_pair_slots = attend_backward(
        scal, query_slots, pair_slots, other_slots, grad_slots, logs, heads, members
    )
    grad_query_slots = [across(v, slot) if slot else v for slot, v in enumerate(grad_query_slots)]
    pair_sums = []
    for slot in range(heads):
        total = grad_pair_slots[slot].astype(f32)
        for step in range(1, members):
            sent = grad_pair_slots[step * heads + slot]
            total = total + among(sent, members - step).astype(f32)
        total = total.astype(bf16)
        pair_sums.append(across(total, slot) if slot else total)
    grad_projected = jnp.zeros((rows, 3, head_width), bf16)
    for slot in range(heads):
        start = (place ^ slot) * HD
        grad_query = turn(grad_query_slots[slot].reshape(rows, HD).astype(f32), True)
        pair = pair_sums[slot].reshape(rows, 2 * HD)
        grad_key = turn(pair[:, :HD].astype(f32), True)
        piece = jnp.stack([grad_query.astype(bf16), grad_key.astype(bf16), pair[:, HD:]], axis=1)
        grad_projected = lax.dynamic_update_slice_in_dim(grad_projected, piece, start, 2)
    grad_projected = grad_projected.reshape(rows, 3 * head_width)
    one_parts = scatter_heads(
        [contract(own_rows(grad_projected, slot), flat_qkv, 1, 1) for slot in range(head_count)]
    )
    grad_qkv_part = contract(normed_low, grad_projected, 0, 0).astype(bf16)

    logits = jnp.dot(pooled, w_router, precision=highest, preferred_element_type=f32)
    logit_grads = []
    for group in range(2):
        group_logits = logits[:, LEVELS * group : LEVELS * (group + 1)]
        raised = jnp.exp(group_logits - jnp.max(group_logits, axis=1, keepdims=True))
        chosen = (jnp.arange(LEVELS)[None, :] == router_targets[:, group][:, None]).astype(f32)
        logit_grads.append(raised / jnp.sum(raised, axis=1, keepdims=True) - chosen)
    grad_logits = jnp.concatenate(logit_grads, axis=1)
    grad_router = jnp.dot(pooled.T, grad_logits, precision=highest, preferred_element_type=f32)
    grad_pooled = (
        jnp.dot(grad_logits, w_router.T, precision=highest, preferred_element_type=f32)
        * lax.rsqrt(seq_length)[:, None]
    )

    member_own = own_rows(in_seq.astype(f32), 0)
    grad_one = sum(one_parts[1:], one_parts[0]) + jnp.dot(
        member_own, grad_pooled, precision=highest, preferred_element_type=f32
    )
    hat_own, inverse_own = normalize_parts(tokens_own)
    back_one, gain_one = normalize_back(grad_one, hat_own, inverse_own, gain_attn)
    grad_tokens = in_order(gather_heads((grad_hidden + back_one).astype(bf16)), f32)
    gains = jnp.stack([gain_one, gain_two])
    gains = butterfly(butterfly(gains, "heads", head_count), "seq", seq_count)
    grad_qkv = lax.psum(grad_qkv_part, "seq").astype(f32).reshape(D, 3, head_width)
    grad_out = lax.psum(grad_out_part, "seq").astype(f32)
    return (
        output,
        grad_tokens,
        grad_qkv,
        grad_out,
        grad_up,
        grad_down,
        gains[0],
        gains[1],
        grad_router,
    )


def solution(mesh):
    return jax.shard_map(
        local,
        mesh=mesh,
        in_specs=(
            P("seq", None),
            P(None, None, "heads"),
            P("heads", None),
            P("seq", "heads"),
            P("heads", "seq"),
            P(),
            P(),
            P(),
            P(),
            P(),
            P(),
            P("seq", None),
        ),
        out_specs=(
            P("seq", None),
            P("seq", None),
            P(None, None, "heads"),
            P("heads", None),
            P("seq", "heads"),
            P("heads", "seq"),
            P(),
            P(),
            P(),
        ),
        check_vma=False,
    )
```

time: 1490 us -> 993 us (0.67)
  waiting for transfers between devices: 891 us -> 534 us
  matrix products: 268 us -> 129 us
  blocking collectives: 106 us -> 0 us
  starting transfers between devices: 1.47 us -> 102 us
  Pallas kernels: 0 us -> 36.2 us
  local copies, waits for them, and re-layouts: 114 us -> 92.6 us
    psum x4 -> x1, waiting for transfers between devices: 621 us -> 0.01 us  [local(): lax.psum(grad_qkv_part, 'seq').astype(f32).reshape(D, 3, head_width)]
    ppermute x0 -> x58, waiting for transfers between devices: none -> 434 us  [the longest x32 278 us: flip(): return lax.ppermute(values, axis, [(i, i ^ bit) for i in range(size)])]
    all_gather x10 -> x2, waiting for transfers between devices: 246 us -> 0.01 us  [the longest x1 0.01 us: local(): full_up = lax.all_gather(w_up, 'seq', axis=0, tiled=True)]
    dot_general x29, matrix products: 267 us -> 127 us  [the longest x17 83.4 us: contract(): lax.dot_general(left, right, (((left_dim,), (right_dim,)), ((), ())), pre...]
    ppermute x0 -> x58, starting transfers between devices: none -> 101 us  [the longest x18 52.4 us: across(): return lax.ppermute(values, 'seq', pairs)]
    reduce_scatter x2, waiting for transfers between devices: 22.2 us -> 98.9 us  [the longest x1 87.4 us: local(): lax.psum_scatter(grad_down_part, 'seq', scatter_dimension=1, tiled=True)]
    all_gather x4 -> x0, blocking collectives: 61.4 us -> none  [the longest x2 30.8 us: local(): lax.all_gather(delta, 'seq', axis=2, tiled=True)]
    psum x2 -> x0, blocking collectives: 44.7 us -> none  [the longest x1 28.2 us: local(): lax.psum(partial_pool.astype(jnp.bfloat16), 'seq').astype(jnp.float32)]
  transfers between devices with their start and end apart: 16 -> 63, of which waited for: 12 -> 33; matrix products, arithmetic and copies ran while one was open for 23% -> 23% of each run, Pallas kernels for 0% -> 2%
where the time goes in v1:
time: 993 us; the launch traced here: 983 us
  waiting for transfers between devices  534 us (54%)
  matrix products  129 us (13%)
  starting transfers between devices  102 us (10%)
  local copies, waits for them, and re-layouts  92.6 us (9%)
  other arithmetic  74.4 us (7%)
  Pallas kernels  36.2 us (4%)
  between operations  15.4 us (2%)
    ppermute x32, waiting for transfers between devices, flip(): return lax.ppermute(values, axis, [(i, i ^ bit) for i in range(size)])  278 us
    ppermute x18, waiting for transfers between devices, across(): return lax.ppermute(values, 'seq', pairs)  156 us
    reduce_scatter x1, waiting for transfers between devices, local(): lax.psum_scatter(grad_down_part, 'seq', scatter_dimension=1, tiled=True)  87.4 us
    dot_general x17, matrix products, contract(): lax.dot_general(left, right, (((left_dim,), (right_dim,)), ((), ())), pre...  83.4 us
    ppermute x18, starting transfers between devices, across(): return lax.ppermute(values, 'seq', pairs)  52.4 us
    ppermute x32, starting transfers between devices, flip(): return lax.ppermute(values, axis, [(i, i ^ bit) for i in range(size)])  47.7 us
    dot_general x10, matrix products, dot(): return jnp.dot(left, right, preferred_element_type=f32)  42.6 us
    unnamed x105, local copies, waits for them, and re-layouts  30.9 us
  transfers between devices with their start and end apart: 63, of which 33 were waited for; matrix products, arithmetic and copies ran while one was open for 23% of the time, Pallas kernels for 2%

profile of v1, /device:TPU:0, one launch (start us, length us, event | category | flops | bytes accessed | tf_op | source)
XLA Modules:
  0.0 982.7 jit_solution(3784251016665751764)
XLA Ops:
  25.1 9.1 fusion.8
  86.3 37.5 %collective-permute-done.2.refs_3_ = bf16[7,128,128]{2,1,0:T(8,128)(2,1)} collective-permute-done((bf16[7,128,128]{2,1,0:T(8,128)(2,1)}, bf16[7,128,128]{2,1,0:T(8,128)(2,1)}, u32[]{:S(2)}, u32[]{:S(2)}) %collective-permute-start.2) | collective-permute-done | bytes 229408 | tf_op jit(solution)/shard_map/ppermute | solution.py:366
  123.8 17.7 %collective-permute-start.1 = (bf16[7,128,128]{2,1,0:T(8,128)(2,1)}, bf16[7,128,128]{2,1,0:T(8,128)(2,1)S(1)}, u32[]{:S(2)}, u32[]{:S(2)}) collective-permute-start(bf16[7,128,128]{2,1,0:T(8,128)(2,1)} %pad_maximum_fusion.12), channel_id=1, source_target_pairs={{0,4},{1,5},{2,6},{3,7},{4,0},{5,1},{6,2},{7,3},{8,12},{9,13},{10,... | collective-permute-start | bytes 688136 | tf_op jit(solution)/shard_map/ppermute | solution.py:366
  144.4 21.8 %collective-permute-done.1.refs_2_ = bf16[7,128,128]{2,1,0:T(8,128)(2,1)S(1)} collective-permute-done((bf16[7,128,128]{2,1,0:T(8,128)(2,1)}, bf16[7,128,128]{2,1,0:T(8,128)(2,1)S(1)}, u32[]{:S(2)}, u32[]{:S(2)}) %collective-permute-start.1) | collective-permute-done | bytes 229408 | tf_op jit(solution)/shard_map/ppermute | solution.py:366
  170.5 17.7 %collective-permute-done.refs_1_ = bf16[7,128,128]{2,1,0:T(8,128)(2,1)S(1)} collective-permute-done((bf16[7,128,128]{2,1,0:T(8,128)(2,1)S(1)}, bf16[7,128,128]{2,1,0:T(8,128)(2,1)S(1)}, u32[]{:S(2)}, u32[]{:S(2)}) %collective-permute-start) | collective-permute-done | bytes 229408 | tf_op jit(solution)/shard_map/ppermute | solution.py:366
  188.8 15.3 %attend_forward.1 = (bf16[7,128,128]{2,1,0:T(8,128)(2,1)}, bf16[7,128,128]{2,1,0:T(8,128)(2,1)}, bf16[7,128,128]{2,1,0:T(8,128)(2,1)}, bf16[7,128,128]{2,1,0:T(8,128)(2,1)}, f32[4,7,1,128]{3,2,1,0:T(1,128)}) custom-call(s32[7]{0:T(128)} %pad_add_fusion.scal, bf16[7,128,128]{2,1,0:T(8,128)(2,1)} %pad_maximum_fusion.10.refs_0_, ...), custom_call_target="tpu_custom_call" | custom-call | flops 4000000000 | bytes 7340032 | tf_op jit(solution)/shard_map/attend_forward/pallas_call | solution.py:186
  209.7 16.7 %collective-permute-done.10 = bf16[7,128,128]{2,1,0:T(8,128)(2,1)S(1)} collective-permute-done((bf16[7,128,128]{2,1,0:T(8,128)(2,1)}, bf16[7,128,128]{2,1,0:T(8,128)(2,1)S(1)}, u32[]{:S(2)}, u32[]{:S(2)}) %collective-permute-start.10) | collective-permute-done | bytes 229408 | tf_op jit(solution)/shard_map/ppermute | solution.py:366
  226.4 12.5 %collective-permute-done.11 = bf16[7,128,128]{2,1,0:T(8,128)(2,1)S(1)} collective-permute-done((bf16[7,128,128]{2,1,0:T(8,128)(2,1)}, bf16[7,128,128]{2,1,0:T(8,128)(2,1)S(1)}, u32[]{:S(2)}, u32[]{:S(2)}) %collective-permute-start.11) | collective-permute-done | bytes 229408 | tf_op jit(solution)/shard_map/ppermute | solution.py:366
  245.5 18.3 %collective-permute-done.13 = bf16[224,2048]{1,0:T(8,128)(2,1)S(1)} collective-permute-done((bf16[224,2048]{1,0:T(8,128)(2,1)S(1)}, bf16[224,2048]{1,0:T(8,128)(2,1)S(1)}, u32[]{:S(2)}, u32[]{:S(2)}) %collective-permute-start.13) | collective-permute-done | bytes 917536 | tf_op jit(solution)/shard_map/ppermute | solution.py:55
  263.7 20.7 %collective-permute-done.14 = bf16[224,2048]{1,0:T(8,128)(2,1)S(1)} collective-permute-done((bf16[224,2048]{1,0:T(8,128)(2,1)S(1)}, bf16[224,2048]{1,0:T(8,128)(2,1)S(1)}, u32[]{:S(2)}, u32[]{:S(2)}) %collective-permute-start.14) | collective-permute-done | bytes 917536 | tf_op jit(solution)/shard_map/ppermute | solution.py:55
  296.7 16.1 %collective-permute-done.16 = bf16[224,2048]{1,0:T(8,128)(2,1)} collective-permute-done((bf16[224,2048]{1,0:T(8,128)(2,1)}, bf16[224,2048]{1,0:T(8,128)(2,1)}, u32[]{:S(2)}, u32[]{:S(2)}) %collective-permute-start.16) | collective-permute-done | bytes 917536 | tf_op jit(solution)/shard_map/ppermute | solution.py:55
  312.9 16.2 %collective-permute-done.17 = bf16[224,2048]{1,0:T(8,128)(2,1)} collective-permute-done((bf16[224,2048]{1,0:T(8,128)(2,1)}, bf16[224,2048]{1,0:T(8,128)(2,1)}, u32[]{:S(2)}, u32[]{:S(2)}) %collective-permute-start.17) | collective-permute-done | bytes 917536 | tf_op jit(solution)/shard_map/ppermute | solution.py:55
  330.9 15.9 %fusion.4 = (bf16[896,2048]{1,0:T(8,128)(2,1)}, f32[896,2048]{1,0:T(8,128)}) fusion(s32[2048]{0:T(1024)S(1)} %iota_add_fusion, s32[896]{0:T(1024)S(1)} %add_multiply_fusion.3, bf16[2048,2048]{1,0:T(8,128)(2,1)} %all-gather.3.cloned.1.call-done, bf16[224,2048]{1,0:T(8,128)(2,1)} %collective-permute-done.18, bf16[224,2048]{1,0:T(8,128)(2,1)} %collective-permute-done.17, ...), kind=kOutput, calls=%fused_computation.11 | convolution fusion | flops 7540047872 | bytes 23080448 | tf_op jit(solution)/shard_map/dot_general | solution.py:29
  346.8 15.7 %fusion.7 = bf16[896,2048]{1,0:T(8,128)(2,1)} fusion(f32[896,2048]{1,0:T(8,128)} %get-tuple-element.168, s32[2048]{0:T(1024)S(1)} %iota_add_fusion, s32[896]{0:T(1024)S(1)} %add_multiply_fusion.3, bf16[2048,2048]{1,0:T(8,128)(2,1)} %all-gather.5.cloned.1.call-done, bf16[224,2048]{1,0:T(8,128)(2,1)} %get-tuple-element.73, ...), kind=kOutput, calls=%fused_computation.14 | convolution fusion | flops 7545552896 | bytes 23080448 | tf_op jit(solution)/shard_map/dot_general | solution.py:33
  378.0 14.3 %collective-permute-done.25 = bf16[224,2048]{1,0:T(8,128)(2,1)S(1)} collective-permute-done((bf16[224,2048]{1,0:T(8,128)(2,1)S(1)}, bf16[224,2048]{1,0:T(8,128)(2,1)S(1)}, u32[]{:S(2)}, u32[]{:S(2)}) %collective-permute-start.25) | collective-permute-done | bytes 917536 | tf_op jit(solution)/shard_map/ppermute | solution.py:55
  392.3 19.6 %collective-permute-done.26 = bf16[224,2048]{1,0:T(8,128)(2,1)S(1)} collective-permute-done((bf16[224,2048]{1,0:T(8,128)(2,1)S(1)}, bf16[224,2048]{1,0:T(8,128)(2,1)S(1)}, u32[]{:S(2)}, u32[]{:S(2)}) %collective-permute-start.26) | collective-permute-done | bytes 917536 | tf_op jit(solution)/shard_map/ppermute | solution.py:55
  423.1 18.9 %collective-permute-done.28 = bf16[224,2048]{1,0:T(8,128)(2,1)S(1)} collective-permute-done((bf16[224,2048]{1,0:T(8,128)(2,1)S(1)}, bf16[224,2048]{1,0:T(8,128)(2,1)S(1)}, u32[]{:S(2)}, u32[]{:S(2)}) %collective-permute-start.28) | collective-permute-done | bytes 917536 | tf_op jit(solution)/shard_map/ppermute | solution.py:55
  442.7 14.5 %collective-permute-done.29 = bf16[224,2048]{1,0:T(8,128)(2,1)S(1)} collective-permute-done((bf16[224,2048]{1,0:T(8,128)(2,1)S(1)}, bf16[224,2048]{1,0:T(8,128)(2,1)S(1)}, u32[]{:S(2)}, u32[]{:S(2)}) %collective-permute-start.29) | collective-permute-done | bytes 917536 | tf_op jit(solution)/shard_map/ppermute | solution.py:55
  481.7 20.9 %attend_backward.1 = (bf16[7,128,128]{2,1,0:T(8,128)(2,1)}, bf16[7,128,128]{2,1,0:T(8,128)(2,1)}, bf16[7,128,128]{2,1,0:T(8,128)(2,1)}, bf16[7,128,128]{2,1,0:T(...) custom-call(s32[7]{0:T(128)} %pad_add_fusion.scal, ...), custom_call_target="tpu_custom_call" | custom-call | flops 10000000000 | bytes 12582912 | tf_op jit(solution)/shard_map/attend_backward/pallas_call | solution.py:303
  555.7 16.1 %collective-permute-done.40 = bf16[7,128,256]{2,1,0:T(8,128)(2,1)S(1)} collective-permute-done((bf16[7,128,256]{2,1,0:T(8,128)(2,1)}, bf16[7,128,256]{2,1,0:T(8,128)(2,1)S(1)}, u32[]{:S(2)}, u32[]{:S(2)}) %collective-permute-start.40) | collective-permute-done | bytes 458784 | tf_op jit(solution)/shard_map/ppermute | solution.py:366
  587.0 9.1 convolution_convert_fusion
  604.7 14.0 %convolution_convert_fusion.2 = bf16[2048,2048]{1,0:T(8,128)(2,1)} fusion(bf16[896,2048]{1,0:T(8,128)(2,1)} %fusion.7, bf16[224,2048]{1,0:T(8,128)(2,1)} %collective-permute-done.18, bf16[224,2048]{1,0:T(8,128)(2,1)} %collective-permute-done.17, bf16[224,2048]{1,0:T(8,128)(2,1)} %collective-permute-done.16, bf16[224,2048]{1,0:T(8,128)(2,1)} %multiply_convert_fusion), kind=kOutput, calls=%fused_computation.8 | convolution fusion | flops 7535067136 | bytes 15728640 | tf_op jit(solution)/shard_map/dot_general | solution.py:33
  620.1 13.1 %convolution_convert_fusion.1 = bf16[2048,2048]{1,0:T(8,128)(2,1)} fusion(bf16[896,2048]{1,0:T(8,128)(2,1)} %get-tuple-element.167, bf16[224,2048]{1,0:T(8,128)(2,1)S(1)} %copy-done.21, bf16[224,2048]{1,0:T(8,128)(2,1)} %get-tuple-element.74, bf16[224,2048]{1,0:T(8,128)(2,1)S(1)} %copy-done.20, bf16[224,2048]{1,0:T(8,128)(2,1)S(1)} %get-tuple-element.71), kind=kOutput, calls=%fused_computation.7 | convolution fusion | flops 7535067136 | bytes 15728640 | tf_op jit(solution)/shard_map/dot_general | solution.py:33
  683.9 22.8 %collective-permute-done.20 = bf16[224,2048]{1,0:T(8,128)(2,1)S(1)} collective-permute-done((bf16[224,2048]{1,0:T(8,128)(2,1)S(1)}, bf16[224,2048]{1,0:T(8,128)(2,1)S(1)}, u32[]{:S(2)}, u32[]{:S(2)}) %collective-permute-start.20) | collective-permute-done | bytes 917536 | tf_op jit(solution)/shard_map/ppermute | solution.py:55
  739.1 16.3 %collective-permute-done.44 = bf16[224,2048]{1,0:T(8,128)(2,1)S(1)} collective-permute-done((bf16[224,2048]{1,0:T(8,128)(2,1)S(1)}, bf16[224,2048]{1,0:T(8,128)(2,1)S(1)}, u32[]{:S(2)}, u32[]{:S(2)}) %collective-permute-start.44) | collective-permute-done | bytes 917536 | tf_op jit(solution)/shard_map/ppermute | solution.py:55
  755.4 20.9 %collective-permute-done.46 = bf16[224,2048]{1,0:T(8,128)(2,1)S(1)} collective-permute-done((bf16[224,2048]{1,0:T(8,128)(2,1)S(1)}, bf16[224,2048]{1,0:T(8,128)(2,1)S(1)}, u32[]{:S(2)}, u32[]{:S(2)}) %collective-permute-start.46) | collective-permute-done | bytes 917536 | tf_op jit(solution)/shard_map/ppermute | solution.py:55
  780.3 12.8 %collective-permute-done.53 = f32[2,2048]{1,0:T(2,128)S(1)} collective-permute-done((f32[2,2048]{1,0:T(2,128)S(1)}, f32[2,2048]{1,0:T(2,128)S(1)}, u32[]{:S(2)}, u32[]{:S(2)}) %collective-permute-start.53) | collective-permute-done | bytes 16416 | tf_op jit(solution)/shard_map/ppermute | solution.py:55
  818.5 10.8 %collective-permute-done.50 = bf16[224,2048]{1,0:T(8,128)(2,1)S(1)} collective-permute-done((bf16[224,2048]{1,0:T(8,128)(2,1)S(1)}, bf16[224,2048]{1,0:T(8,128)(2,1)S(1)}, u32[]{:S(2)}, u32[]{:S(2)}) %collective-permute-start.50) | collective-permute-done | bytes 917536 | tf_op jit(solution)/shard_map/ppermute | solution.py:55
  830.7 25.6 %collective-permute-done.51 = bf16[224,2048]{1,0:T(8,128)(2,1)S(1)} collective-permute-done((bf16[224,2048]{1,0:T(8,128)(2,1)S(1)}, bf16[224,2048]{1,0:T(8,128)(2,1)S(1)}, u32[]{:S(2)}, u32[]{:S(2)}) %collective-permute-start.51) | collective-permute-done | bytes 917536 | tf_op jit(solution)/shard_map/ppermute | solution.py:55
  859.2 9.6 reshape.567
  871.3 11.5 %reduce-scatter.3.cloned.1.call-done = bf16[256,2048]{1,0:T(8,128)(2,1)} async-done(((bf16[2048,2048]{1,0:T(8,128)(2,1)}), bf16[256,2048]{1,0:T(8,128)(2,1)}) %reduce-scatter.3.cloned.1.call-update) | async-done | bytes 1048592 | tf_op jit(solution)/shard_map/reduce_scatter | solution.py:499
  885.6 87.4 %reduce-scatter.5.cloned.1.call-done = bf16[2048,256]{1,0:T(8,128)(2,1)} async-done(((bf16[2048,2048]{1,0:T(8,128)(2,1)}), bf16[2048,256]{1,0:T(8,128)(2,1)}) %reduce-scatter.5.cloned.1.call-update) | async-done | bytes 1048592 | tf_op jit(solution)/shard_map/reduce_scatter | solution.py:500
  (366 shorter events, 358.2 us)
Async XLA Ops:
  7.2 323.7 %all-gather.3.cloned.1.call-start = ((), (), s32[]{:S(2)}) async-start(), calls=%async_computation.2 | async-start | bytes 9437184 | tf_op jit(solution)/shard_map/all_gather | solution.py:398
  7.9 338.9 %all-gather.5.cloned.1.call-start = ((), (), s32[]{:S(2)}) async-start(), calls=%async_computation.3 | async-start | bytes 9437184 | tf_op jit(solution)/shard_map/all_gather | solution.py:399
  8.7 850.5 %all-reduce.3.cloned.1.call-start = ((), (), s32[]{:S(2)}) async-start(), calls=%async_computation.6 | async-start | bytes 16777216 | tf_op jit(solution)/shard_map/psum | solution.py:569
  48.5 93.0 %collective-permute-start.5 = (bf16[7,128,256]{2,1,0:T(8,128)(2,1)}, bf16[7,128,256]{2,1,0:T(8,128)(2,1)}, u32[]{:S(2)}, u32[]{:S(2)}) collective-permute-start(bf16[7,128,256]{2,1,0:T(8,128)(2,1)} %pad_maximum_fusion.9), channel_id=1, source_target_pairs={{0,6},{1,7},{2,4},{3,5},{4,2},{5,3},{6,0},{7,1},{8,14},{9,15},{10,... | collective-permute-start | bytes 1376264 | tf_op jit(solution)/shard_map/ppermute | solution.py:366
  60.7 80.8 %collective-permute-start.4 = (bf16[7,128,256]{2,1,0:T(8,128)(2,1)}, bf16[7,128,256]{2,1,0:T(8,128)(2,1)}, u32[]{:S(2)}, u32[]{:S(2)}) collective-permute-start(bf16[7,128,256]{2,1,0:T(8,128)(2,1)} %pad_maximum_fusion.8), channel_id=1, source_target_pairs={{0,4},{1,5},{2,6},{3,7},{4,0},{5,1},{6,2},{7,3},{8,12},{9,13},{10,... | collective-permute-start | bytes 1376264 | tf_op jit(solution)/shard_map/ppermute | solution.py:366
  68.0 74.0 %collective-permute-start.3 = (bf16[7,128,256]{2,1,0:T(8,128)(2,1)}, bf16[7,128,256]{2,1,0:T(8,128)(2,1)}, u32[]{:S(2)}, u32[]{:S(2)}) collective-permute-start(bf16[7,128,256]{2,1,0:T(8,128)(2,1)} %pad_maximum_fusion.7), channel_id=1, source_target_pairs={{0,2},{1,3},{2,0},{3,1},{4,6},{5,7},{6,4},{7,5},{8,10},{9,11},{10,... | collective-permute-start | bytes 1376264 | tf_op jit(solution)/shard_map/ppermute | solution.py:366
  74.7 49.1 %collective-permute-start.2 = (bf16[7,128,128]{2,1,0:T(8,128)(2,1)}, bf16[7,128,128]{2,1,0:T(8,128)(2,1)}, u32[]{:S(2)}, u32[]{:S(2)}) collective-permute-start(bf16[7,128,128]{2,1,0:T(8,128)(2,1)} %pad_maximum_fusion.13), channel_id=1, source_target_pairs={{0,6},{1,7},{2,4},{3,5},{4,2},{5,3},{6,0},{7,1},{8,14},{9,15},{10,... | collective-permute-start | bytes 688136 | tf_op jit(solution)/shard_map/ppermute | solution.py:366
  82.0 106.1 %collective-permute-start.6 = (bf16[7,128,256]{2,1,0:T(8,128)(2,1)S(1)}, bf16[7,128,256]{2,1,0:T(8,128)(2,1)}, u32[]{:S(2)}, u32[]{:S(2)}) collective-permute-start(bf16[7,128,256]{2,1,0:T(8,128)(2,1)S(1)} %pad_maximum_fusion.6.refs_4_), channel_id=1, source_target_pairs={{1,0},{0,1},{3,2},{2,3},{5,4},{4,5},{7,6},{6,7},{9,8},{8,9},{11,10... | collective-permute-start | bytes 1376264 | tf_op jit(solution)/shard_map/ppermute | solution.py:374
  123.8 42.4 %collective-permute-start.1 = (bf16[7,128,128]{2,1,0:T(8,128)(2,1)}, bf16[7,128,128]{2,1,0:T(8,128)(2,1)S(1)}, u32[]{:S(2)}, u32[]{:S(2)}) collective-permute-start(bf16[7,128,128]{2,1,0:T(8,128)(2,1)} %pad_maximum_fusion.12), channel_id=1, source_target_pairs={{0,4},{1,5},{2,6},{3,7},{4,0},{5,1},{6,2},{7,3},{8,12},{9,13},{10,... | collective-permute-start | bytes 688136 | tf_op jit(solution)/shard_map/ppermute | solution.py:366
  141.4 46.7 %collective-permute-start.9 = (bf16[7,128,256]{2,1,0:T(8,128)(2,1)}, bf16[7,128,256]{2,1,0:T(8,128)(2,1)}, u32[]{:S(2)}, u32[]{:S(2)}) collective-permute-start(bf16[7,128,256]{2,1,0:T(8,128)(2,1)} %collective-permute-done.5.refs_7_), channel_id=1, source_target_pairs={{1,0},{0,1},{3,2},{2,3},{5,4},{4,5},{7,6},{6,7},{9,8},{8,9},{11,10... | collective-permute-start | bytes 1376264 | tf_op jit(solution)/shard_map/ppermute | solution.py:374
  141.5 46.7 %collective-permute-start.8 = (bf16[7,128,256]{2,1,0:T(8,128)(2,1)}, bf16[7,128,256]{2,1,0:T(8,128)(2,1)}, u32[]{:S(2)}, u32[]{:S(2)}) collective-permute-start(bf16[7,128,256]{2,1,0:T(8,128)(2,1)} %collective-permute-done.4.refs_6_), channel_id=1, source_target_pairs={{1,0},{0,1},{3,2},{2,3},{5,4},{4,5},{7,6},{6,7},{9,8},{8,9},{11,10... | collective-permute-start | bytes 1376264 | tf_op jit(solution)/shard_map/ppermute | solution.py:374
  142.0 46.2 %collective-permute-start.7 = (bf16[7,128,256]{2,1,0:T(8,128)(2,1)}, bf16[7,128,256]{2,1,0:T(8,128)(2,1)}, u32[]{:S(2)}, u32[]{:S(2)}) collective-permute-start(bf16[7,128,256]{2,1,0:T(8,128)(2,1)} %collective-permute-done.3.refs_5_), channel_id=1, source_target_pairs={{1,0},{0,1},{3,2},{2,3},{5,4},{4,5},{7,6},{6,7},{9,8},{8,9},{11,10... | collective-permute-start | bytes 1376264 | tf_op jit(solution)/shard_map/ppermute | solution.py:374
  204.3 34.6 %collective-permute-start.11 = (bf16[7,128,128]{2,1,0:T(8,128)(2,1)}, bf16[7,128,128]{2,1,0:T(8,128)(2,1)S(1)}, u32[]{:S(2)}, u32[]{:S(2)}) collective-permute-start(bf16[7,128,128]{2,1,0:T(8,128)(2,1)} %get-tuple-element.28), channel_id=1, source_target_pairs={{0,4},{1,5},{2,6},{3,7},{4,0},{5,1},{6,2},{7,3},{8,12},{9,13},{10,... | collective-permute-start | bytes 688136 | tf_op jit(solution)/shard_map/ppermute | solution.py:366
  243.1 41.3 %collective-permute-start.14 = (bf16[224,2048]{1,0:T(8,128)(2,1)S(1)}, bf16[224,2048]{1,0:T(8,128)(2,1)S(1)}, u32[]{:S(2)}, u32[]{:S(2)}) collective-permute-start(bf16[224,2048]{1,0:T(8,128)(2,1)S(1)} %convolution_convert_fusion.4), channel_id=1, source_target_pairs={{0,16},{8,24},{16,0},{24,8},{1,17},{9,25},{17,1},{25,9},{2,18},{10... | collective-permute-start | bytes 2752520 | tf_op jit(solution)/shard_map/ppermute | solution.py:55
  245.3 39.1 %collective-permute-start.15 = (bf16[224,2048]{1,0:T(8,128)(2,1)S(1)}, bf16[224,2048]{1,0:T(8,128)(2,1)S(1)}, u32[]{:S(2)}, u32[]{:S(2)}) collective-permute-start(bf16[224,2048]{1,0:T(8,128)(2,1)S(1)} %convolution_convert_fusion.3), channel_id=1, source_target_pairs={{0,24},{8,16},{16,8},{24,0},{1,25},{9,17},{17,9},{25,1},{2,26},{10... | collective-permute-start | bytes 2752520 | tf_op jit(solution)/shard_map/ppermute | solution.py:55
  289.8 39.3 %collective-permute-start.17 = (bf16[224,2048]{1,0:T(8,128)(2,1)}, bf16[224,2048]{1,0:T(8,128)(2,1)}, u32[]{:S(2)}, u32[]{:S(2)}) collective-permute-start(bf16[224,2048]{1,0:T(8,128)(2,1)} %multiply_convert_fusion), channel_id=1, source_target_pairs={{0,16},{8,24},{16,0},{24,8},{1,17},{9,25},{17,1},{25,9},{2,18},{10... | collective-permute-start | bytes 2752520 | tf_op jit(solution)/shard_map/ppermute | solution.py:55
  291.3 39.6 %collective-permute-start.18 = (bf16[224,2048]{1,0:T(8,128)(2,1)}, bf16[224,2048]{1,0:T(8,128)(2,1)}, u32[]{:S(2)}, u32[]{:S(2)}) collective-permute-start(bf16[224,2048]{1,0:T(8,128)(2,1)} %multiply_convert_fusion), channel_id=1, source_target_pairs={{0,24},{8,16},{16,8},{24,0},{1,25},{9,17},{17,9},{25,1},{2,26},{10... | collective-permute-start | bytes 2752520 | tf_op jit(solution)/shard_map/ppermute | solution.py:55
  372.3 39.5 %collective-permute-start.26 = (bf16[224,2048]{1,0:T(8,128)(2,1)S(1)}, bf16[224,2048]{1,0:T(8,128)(2,1)S(1)}, u32[]{:S(2)}, u32[]{:S(2)}) collective-permute-start(bf16[224,2048]{1,0:T(8,128)(2,1)S(1)} %convolution_convert_fusion.10), channel_id=1, source_target_pairs={{0,16},{8,24},{16,0},{24,8},{1,17},{9,25},{17,1},{25,9},{2,18},{10... | collective-permute-start | bytes 2752520 | tf_op jit(solution)/shard_map/ppermute | solution.py:55
  376.8 35.1 %collective-permute-start.27 = (bf16[224,2048]{1,0:T(8,128)(2,1)S(1)}, bf16[224,2048]{1,0:T(8,128)(2,1)S(1)}, u32[]{:S(2)}, u32[]{:S(2)}) collective-permute-start(bf16[224,2048]{1,0:T(8,128)(2,1)S(1)} %convolution_convert_fusion.9), channel_id=1, source_target_pairs={{0,24},{8,16},{16,8},{24,0},{1,25},{9,17},{17,9},{25,1},{2,26},{10... | collective-permute-start | bytes 2752520 | tf_op jit(solution)/shard_map/ppermute | solution.py:55
  419.9 37.4 %collective-permute-start.29 = (bf16[224,2048]{1,0:T(8,128)(2,1)S(1)}, bf16[224,2048]{1,0:T(8,128)(2,1)S(1)}, u32[]{:S(2)}, u32[]{:S(2)}) collective-permute-start(bf16[224,2048]{1,0:T(8,128)(2,1)S(1)} %get-tuple-element.57), channel_id=1, source_target_pairs={{0,16},{8,24},{16,0},{24,8},{1,17},{9,25},{17,1},{25,9},{2,18},{10... | collective-permute-start | bytes 2752520 | tf_op jit(solution)/shard_map/ppermute | solution.py:55
  420.3 38.0 %collective-permute-start.30 = (bf16[224,2048]{1,0:T(8,128)(2,1)S(1)}, bf16[224,2048]{1,0:T(8,128)(2,1)S(1)}, u32[]{:S(2)}, u32[]{:S(2)}) collective-permute-start(bf16[224,2048]{1,0:T(8,128)(2,1)S(1)} %get-tuple-element.57), channel_id=1, source_target_pairs={{0,24},{8,16},{16,8},{24,0},{1,25},{9,17},{17,9},{25,1},{2,26},{10... | collective-permute-start | bytes 2752520 | tf_op jit(solution)/shard_map/ppermute | solution.py:55
  604.6 278.2 %reduce-scatter.3.cloned.1.call-start = ((), (), s32[]{:S(2)}) async-start(), calls=%async_computation.4 | async-start | bytes 9437184 | tf_op jit(solution)/shard_map/reduce_scatter | solution.py:499
  618.7 354.3 %reduce-scatter.5.cloned.1.call-start = ((), (), s32[]{:S(2)}) async-start(), calls=%async_computation.5 | async-start | bytes 9437184 | tf_op jit(solution)/shard_map/reduce_scatter | solution.py:500
  664.0 42.7 %collective-permute-start.20 = (bf16[224,2048]{1,0:T(8,128)(2,1)S(1)}, bf16[224,2048]{1,0:T(8,128)(2,1)S(1)}, u32[]{:S(2)}, u32[]{:S(2)}) collective-permute-start(bf16[224,2048]{1,0:T(8,128)(2,1)S(1)} %convolution_convert_fusion.13), channel_id=1, source_target_pairs={{0,16},{8,24},{16,0},{24,8},{1,17},{9,25},{17,1},{25,9},{2,18},{10... | collective-permute-start | bytes 2752520 | tf_op jit(solution)/shard_map/ppermute | solution.py:55
  669.1 37.6 %collective-permute-start.21 = (bf16[224,2048]{1,0:T(8,128)(2,1)S(1)}, bf16[224,2048]{1,0:T(8,128)(2,1)S(1)}, u32[]{:S(2)}, u32[]{:S(2)}) collective-permute-start(bf16[224,2048]{1,0:T(8,128)(2,1)S(1)} %convolution_convert_fusion.12), channel_id=1, source_target_pairs={{0,24},{8,16},{16,8},{24,0},{1,25},{9,17},{17,9},{25,1},{2,26},{10... | collective-permute-start | bytes 2752520 | tf_op jit(solution)/shard_map/ppermute | solution.py:55
  719.2 36.2 %collective-permute-start.44 = (bf16[224,2048]{1,0:T(8,128)(2,1)S(1)}, bf16[224,2048]{1,0:T(8,128)(2,1)S(1)}, u32[]{:S(2)}, u32[]{:S(2)}) collective-permute-start(bf16[224,2048]{1,0:T(8,128)(2,1)S(1)} %convolution_convert_fusion.8), channel_id=1, source_target_pairs={{0,8},{8,0},{16,24},{24,16},{1,9},{9,1},{17,25},{25,17},{2,10},{10... | collective-permute-start | bytes 2752520 | tf_op jit(solution)/shard_map/ppermute | solution.py:55
  720.0 35.3 %collective-permute-start.45 = (bf16[224,2048]{1,0:T(8,128)(2,1)S(1)}, bf16[224,2048]{1,0:T(8,128)(2,1)S(1)}, u32[]{:S(2)}, u32[]{:S(2)}) collective-permute-start(bf16[224,2048]{1,0:T(8,128)(2,1)S(1)} %convolution_convert_fusion.7), channel_id=1, source_target_pairs={{0,16},{8,24},{16,0},{24,8},{1,17},{9,25},{17,1},{25,9},{2,18},{10... | collective-permute-start | bytes 2752520 | tf_op jit(solution)/shard_map/ppermute | solution.py:55
  721.8 54.5 %collective-permute-start.46 = (bf16[224,2048]{1,0:T(8,128)(2,1)S(1)}, bf16[224,2048]{1,0:T(8,128)(2,1)S(1)}, u32[]{:S(2)}, u32[]{:S(2)}) collective-permute-start(bf16[224,2048]{1,0:T(8,128)(2,1)S(1)} %convolution_convert_fusion.6), channel_id=1, source_target_pairs={{0,24},{8,16},{16,8},{24,0},{1,25},{9,17},{17,9},{25,1},{2,26},{10... | collective-permute-start | bytes 2752520 | tf_op jit(solution)/shard_map/ppermute | solution.py:55
  725.0 83.5 %collective-permute-start.23 = (bf16[224,2048]{1,0:T(8,128)(2,1)S(1)}, bf16[224,2048]{1,0:T(8,128)(2,1)S(1)}, u32[]{:S(2)}, u32[]{:S(2)}) collective-permute-start(bf16[224,2048]{1,0:T(8,128)(2,1)S(1)} %get-tuple-element.170), channel_id=1, source_target_pairs={{0,16},{8,24},{16,0},{24,8},{1,17},{9,25},{17,1},{25,9},{2,18},{10... | collective-permute-start | bytes 2752520 | tf_op jit(solution)/shard_map/ppermute | solution.py:55
  735.7 78.5 %collective-permute-start.24 = (bf16[224,2048]{1,0:T(8,128)(2,1)S(1)}, bf16[224,2048]{1,0:T(8,128)(2,1)S(1)}, u32[]{:S(2)}, u32[]{:S(2)}) collective-permute-start(bf16[224,2048]{1,0:T(8,128)(2,1)S(1)} %get-tuple-element.170), channel_id=1, source_target_pairs={{0,24},{8,16},{16,8},{24,0},{1,25},{9,17},{17,9},{25,1},{2,26},{10... | collective-permute-start | bytes 2752520 | tf_op jit(solution)/shard_map/ppermute | solution.py:55
  815.2 41.1 %collective-permute-start.51 = (bf16[224,2048]{1,0:T(8,128)(2,1)S(1)}, bf16[224,2048]{1,0:T(8,128)(2,1)S(1)}, u32[]{:S(2)}, u32[]{:S(2)}) collective-permute-start(bf16[224,2048]{1,0:T(8,128)(2,1)S(1)} %get-tuple-element.56), channel_id=1, source_target_pairs={{0,16},{8,24},{16,0},{24,8},{1,17},{9,25},{17,1},{25,9},{2,18},{10... | collective-permute-start | bytes 2752520 | tf_op jit(solution)/shard_map/ppermute | solution.py:55
  816.7 41.1 %collective-permute-start.52 = (bf16[224,2048]{1,0:T(8,128)(2,1)S(1)}, bf16[224,2048]{1,0:T(8,128)(2,1)S(1)}, u32[]{:S(2)}, u32[]{:S(2)}) collective-permute-start(bf16[224,2048]{1,0:T(8,128)(2,1)S(1)} %get-tuple-element.56), channel_id=1, source_target_pairs={{0,24},{8,16},{16,8},{24,0},{1,25},{9,17},{17,9},{25,1},{2,26},{10... | collective-permute-start | bytes 2752520 | tf_op jit(solution)/shard_map/ppermute | solution.py:55
  (75 other events, 1593.4 us)
Sparse Core Ops, SparseCore 0:
  9.6 128.7 all-gather.2
  139.9 102.4 all-gather.4
  604.7 185.5 all-reduce.2
  792.5 90.3 reduce-scatter.2
  885.0 87.9 reduce-scatter.4

commit v2 on v1

--- a/solution.py
+++ b/solution.py
@@ -330,6 +330,153 @@
     return (result[:heads], result[heads:])
 
 
+def rotate_rows(values, cosine, sine):
+    return values * cosine + pltpu.roll(values, HD // 2, 1) * sine
+
+
+def project_kernel(heads, scal, tokens, gain, cosine, sine, weights, *refs):
+    query_slots, pair_slots = refs[:heads], refs[heads : 2 * heads]
+    normed, pooled = refs[2 * heads : 2 * heads + 2]
+    held_weights, acc, queries, pairs, in_sems, out_sems = refs[2 * heads + 2 :]
+    head = scal[0]
+    loads = [
+        pltpu.make_async_copy(weights.at[part], held_weights.at[part], in_sems.at[part])
+        for part in range(3)
+    ]
+    for load in loads:
+        load.start()
+    pooled[...] = jnp.zeros(pooled.shape, f32)
+
+    def norm(chunk, carry):
+        here = pl.ds(pl.multiple_of(chunk * SHORT_DEV, SHORT_DEV), SHORT_DEV)
+        hat, _ = normalize_parts(tokens[here, :].astype(f32))
+        values = hat * gain[...]
+        normed[here, :] = values.astype(bf16)
+        at = jnp.where(chunk < NSHORT, chunk, NSHORT + (chunk - NSHORT) // 2)
+        rows = lax.broadcasted_iota(jnp.int32, pooled.shape, 0)
+        added = jnp.sum(values, axis=0, keepdims=True)
+        pooled[...] += jnp.where(rows == at, added, 0.0)
+        return carry
+
+    lax.fori_loop(0, CHUNKS, norm, 0)
+    stores = []
+    for part in range(3):
+        loads[part].wait()
+        acc[...] = dot(normed[...], held_weights[part])
+
+        def spread(chunk, carry):
+            here = pl.ds(pl.multiple_of(chunk * SHORT_DEV, SHORT_DEV), SHORT_DEV)
+            for index in range(heads):
+                values = acc[here, index * HD : (index + 1) * HD]
+                if part < 2:
+                    values = rotate_rows(values, cosine[here, :], sine[here, :])
+                if part == 0:
+                    queries[index, chunk] = values.astype(bf16)
+                elif part == 1:
+                    pairs[index, chunk, :, :HD] = values.astype(bf16)
+                else:
+                    pairs[index, chunk, :, HD:] = values.astype(bf16)
+            return carry
+
+        lax.fori_loop(0, CHUNKS, spread, 0)
+        if part != 1:
+            held, outs = (queries, query_slots) if part == 0 else (pairs, pair_slots)
+            for slot in range(heads):
+                copy = pltpu.make_async_copy(
+                    held.at[head ^ slot], outs[slot], out_sems.at[len(stores)]
+                )
+                copy.start()
+                stores.append(copy)
+    for store in stores:
+        store.wait()
+
+
+def project(scal, tokens, gain, cosine, sine, weights):
+    rows = tokens.shape[0]
+    width = weights.shape[2]
+    heads = width // HD
+    anywhere = pl.BlockSpec(memory_space=pl.ANY)
+    inside = pl.BlockSpec(memory_space=pltpu.VMEM)
+    result = pl.pallas_call(
+        functools.partial(project_kernel, heads),
+        out_shape=[jax.ShapeDtypeStruct((CHUNKS, SHORT_DEV, HD), bf16)] * heads
+        + [jax.ShapeDtypeStruct((CHUNKS, SHORT_DEV, 2 * HD), bf16)] * heads
+        + [jax.ShapeDtypeStruct((rows, D), bf16), jax.ShapeDtypeStruct((8, D), f32)],
+        in_specs=[pl.BlockSpec(memory_space=pltpu.SMEM)] + [inside] * 4 + [anywhere],
+        out_specs=[anywhere] * (2 * heads) + [inside] * 2,
+        scratch_shapes=[
+            pltpu.VMEM((3, D, width), bf16),
+            pltpu.VMEM((rows, width), f32),
+            pltpu.VMEM((heads, CHUNKS, SHORT_DEV, HD), bf16),
+            pltpu.VMEM((heads, CHUNKS, SHORT_DEV, 2 * HD), bf16),
+            pltpu.SemaphoreType.DMA((3,)),
+            pltpu.SemaphoreType.DMA((2 * heads,)),
+        ],
+        compiler_params=pltpu.CompilerParams(vmem_limit_bytes=50 << 20),
+        cost_estimate=pl.CostEstimate(
+            flops=6 * rows * D * width, bytes_accessed=16 << 20, transcendentals=rows
+        ),
+        name="project",
+    )(scal, tokens, gain, cosine, sine, weights)
+    return (result[:heads], result[heads : 2 * heads], result[2 * heads], result[2 * heads + 1])
+
+
+def gather_kernel(heads, scal, cosine, sine, *refs):
+    query_slots, pair_slots = refs[:heads], refs[heads : 2 * heads]
+    out_query, out_key, out_value = refs[2 * heads : 2 * heads + 3]
+    queries, pairs, sems = refs[2 * heads + 3 :]
+    copies = []
+    for held, slots in ((queries, query_slots), (pairs, pair_slots)):
+        for slot in range(heads):
+            copy = pltpu.make_async_copy(
+                slots[slot], held.at[scal[0] ^ slot], sems.at[len(copies)]
+            )
+            copy.start()
+            copies.append(copy)
+    for copy in copies:
+        copy.wait()
+
+    def spread(chunk, carry):
+        here = pl.ds(pl.multiple_of(chunk * SHORT_DEV, SHORT_DEV), SHORT_DEV)
+        for index in range(heads):
+            there = slice(index * HD, (index + 1) * HD)
+            values = queries[index, chunk].astype(f32)
+            values = rotate_rows(values, cosine[here, :], sine[here, :])
+            out_query[here, there] = values.astype(bf16)
+            values = pairs[index, chunk, :, :HD].astype(f32)
+            values = rotate_rows(values, cosine[here, :], sine[here, :])
+            out_key[here, there] = values.astype(bf16)
+            out_value[here, there] = pairs[index, chunk, :, HD:]
+        return carry
+
+    lax.fori_loop(0, CHUNKS, spread, 0)
+
+
+def gather_grads(scal, cosine, sine, query_slots, pair_slots):
+    heads = len(query_slots)
+    rows = CHUNKS * SHORT_DEV
+    anywhere = pl.BlockSpec(memory_space=pl.ANY)
+    inside = pl.BlockSpec(memory_space=pltpu.VMEM)
+    return pl.pallas_call(
+        functools.partial(gather_kernel, heads),
+        out_shape=[jax.ShapeDtypeStruct((rows, heads * HD), bf16)] * 3,
+        in_specs=[pl.BlockSpec(memory_space=pltpu.SMEM)]
+        + [inside] * 2
+        + [anywhere] * (2 * heads),
+        out_specs=[inside] * 3,
+        scratch_shapes=[
+            pltpu.VMEM((heads, CHUNKS, SHORT_DEV, HD), bf16),
+            pltpu.VMEM((heads, CHUNKS, SHORT_DEV, 2 * HD), bf16),
+            pltpu.SemaphoreType.DMA((2 * heads,)),
+        ],
+        compiler_params=pltpu.CompilerParams(vmem_limit_bytes=24 << 20),
+        cost_estimate=pl.CostEstimate(
+            flops=10 * rows * heads * HD, bytes_accessed=6 << 20, transcendentals=0
+        ),
+        name="gather_grads",
+    )(scal, cosine, sine, *query_slots, *pair_slots)
+
+
 def local(
     tokens,
     w_qkv,
@@ -395,8 +542,21 @@
             )
         return full
 
+    def placed(slots, key, axis):
+        size = slots[0].shape[axis]
+        shape = list(slots[0].shape)
+        shape[axis] = size * len(slots)
+        full = jnp.zeros(shape, slots[0].dtype)
+        for slot, values in enumerate(slots):
+            full = lax.dynamic_update_slice_in_dim(full, values, (key ^ slot) * size, axis)
+        return full
+
+    def after(values, *others):
+        return lax.optimization_barrier((values,) + others)[0]
+
+    full_down = lax.all_gather(w_down, "seq", axis=1, tiled=True)
     full_up = lax.all_gather(w_up, "seq", axis=0, tiled=True)
-    full_down = lax.all_gather(w_down, "seq", axis=1, tiled=True)
+    all_out = jnp.concatenate(gather_heads(w_out), axis=0)
 
     column = jnp.arange(rows)
     is_short = column < short_rows
@@ -417,131 +577,22 @@
     angle = position.astype(f32)[:, None] * frequency[None, :]
     cosine = jnp.cos(angle)
     sine = jnp.sin(angle)
+    cosine = jnp.concatenate([cosine, cosine], axis=1)
+    sine = jnp.concatenate([-sine, sine], axis=1)
     my_head = head_rank * heads + place
     head_live = (my_head < head_quarters * (H // LEVELS)).astype(jnp.int32)
     scal = jnp.concatenate([jnp.stack([place, member]).astype(jnp.int32), head_live])
 
-    tokens_wide = tokens.astype(f32)
-    hat_one, _ = normalize_parts(tokens_wide)
-    normed_one = hat_one * gain_attn
-    normed_low = normed_one.astype(bf16)
-    pool_short = jnp.sum(normed_one[:short_rows].reshape(NSHORT, SHORT_DEV, D), axis=1)
-    pool_long = jnp.sum(normed_one[short_rows:].reshape(NLONG, 2 * SHORT_DEV, D), axis=1)
-    flat_qkv = w_qkv.reshape(D, -1)
-    projected = dot(normed_low, flat_qkv).reshape(rows, 3, head_width)
-
-    def turn(values, back):
-        former, latter = values[..., :half_dim], values[..., half_dim:]
-        spin = -sine if back else sine
-        return jnp.concatenate(
-            [former * cosine - latter * spin, latter * cosine + former * spin], axis=-1
-        )
-
-    query_slots, pair_slots = [], []
-    for slot in range(heads):
-        start = (place ^ slot) * HD
-        piece = lax.dynamic_slice_in_dim(projected, start, HD, 2)
-        query = turn(piece[:, 0], False).astype(bf16)
-        pair = jnp.concatenate([turn(piece[:, 1], False), piece[:, 2]], axis=1).astype(bf16)
-        query = query.reshape(CHUNKS, SHORT_DEV, HD)
-        pair = pair.reshape(CHUNKS, SHORT_DEV, 2 * HD)
-        query_slots.append(across(query, slot) if slot else query)
-        pair_slots.append(across(pair, slot) if slot else pair)
+    sent_queries, sent_pairs, normed_low, pooled_sum = project(
+        scal, tokens, gain_attn[None, :], cosine, sine, w_qkv.transpose(1, 0, 2)
+    )
+    pooled_sum = pooled_sum[:SEQS]
+    query_slots = [across(v, slot) if slot else v for slot, v in enumerate(sent_queries)]
+    pair_slots = [across(v, slot) if slot else v for slot, v in enumerate(sent_pairs)]
     other_slots = [
         among(pair_slots[slot], step) for step in range(1, members) for slot in range(heads)
     ]
-    mixed_slots, logs = attend_forward(
-        scal, query_slots, pair_slots, other_slots, heads, members
-    )
-    mixed_slots = [across(v, slot) if slot else v for slot, v in enumerate(mixed_slots)]
-    mixed_slots = [v.reshape(rows, HD) for v in mixed_slots]
-    heads_out = jnp.zeros((rows, head_width), bf16)
-    for slot in range(heads):
-        heads_out = lax.dynamic_update_slice_in_dim(
-            heads_out, mixed_slots[slot], (place ^ slot) * HD, 1
-        )
-
-    pooled_sum = jnp.concatenate([pool_short, pool_long], axis=0)
     pooled = butterfly(pooled_sum, "seq", seq_count) * lax.rsqrt(seq_length)[:, None]
-
-    heads_rel = [own_rows(heads_out, slot) for slot in range(head_count)]
-    attn_parts = scatter_heads([dot(v, w_out) for v in heads_rel])
-    tokens_own = own_rows(tokens, 0).astype(f32)
-    hidden = tokens_own + sum(attn_parts[1:], attn_parts[0])
-    hat_two, inverse_two = normalize_parts(hidden)
-    normed_two = jnp.concatenate(gather_heads((hat_two * gain_ffn).astype(bf16)), axis=0)
-
-    cotangent_rel = jnp.concatenate(
-        [own_rows(cotangent, slot) for slot in range(head_count)], axis=0
-    )
-    level_rel = jnp.concatenate([own_rows(ffn_level, slot) for slot in range(head_count)])
-    unit_index = head_rank * ffn_width + jnp.arange(ffn_width)
-    ffn_live = (unit_index[None, :] < (level_rel * (FF // LEVELS))[:, None]).astype(f32)
-    upward = dot(normed_two, full_up)
-    kept = jnp.maximum(upward, 0.0)
-    active = (jnp.square(kept) * ffn_live).astype(bf16)
-    grad_active = contract(cotangent_rel, full_down, 1, 1).astype(bf16).astype(f32)
-    grad_upward = (grad_active * ffn_live * 2.0 * kept).astype(bf16)
-    two_parts = scatter_heads(
-        [
-            contract(grad_upward[slot * share : (slot + 1) * share], full_up, 1, 1)
-            for slot in range(head_count)
-        ]
-    )
-    ffn_parts = scatter_heads(
-        [
-            dot(active[slot * share : (slot + 1) * share], full_down)
-            for slot in range(head_count)
-        ]
-    )
-    grad_up_part = contract(normed_two, grad_upward, 0, 0).astype(bf16)
-    grad_down_part = contract(active, cotangent_rel, 0, 0).astype(bf16)
-    grad_up = lax.psum_scatter(grad_up_part, "seq", scatter_dimension=0, tiled=True).astype(f32)
-    grad_down = lax.psum_scatter(
-        grad_down_part, "seq", scatter_dimension=1, tiled=True
-    ).astype(f32)
-
-    grad_two = sum(two_parts[1:], two_parts[0])
-    back_two, gain_two = normalize_back(grad_two, hat_two, inverse_two, gain_ffn)
-    grad_hidden = own_rows(cotangent, 0).astype(f32) + back_two
-    grad_attn = gather_heads(grad_hidden.astype(bf16))
-    grad_heads = in_order([contract(v, w_out, 1, 1).astype(bf16) for v in grad_attn], bf16)
-    grad_slots = []
-    for slot in range(heads):
-        piece = lax.dynamic_slice_in_dim(grad_heads, (place ^ slot) * HD, HD, 1)
-        piece = piece.reshape(CHUNKS, SHORT_DEV, HD)
-        grad_slots.append(across(piece, slot) if slot else piece)
-    grad_out_part = contract(
-        jnp.concatenate(heads_rel, axis=0), jnp.concatenate(grad_attn, axis=0), 0, 0
-    ).astype(bf16)
-    output_own = (hidden + sum(ffn_parts[1:], ffn_parts[0])).astype(bf16)
-    output = in_order(gather_heads(output_own), bf16)
-
-    grad_query_slots, grad_pair_slots = attend_backward(
-        scal, query_slots, pair_slots, other_slots, grad_slots, logs, heads, members
-    )
-    grad_query_slots = [across(v, slot) if slot else v for slot, v in enumerate(grad_query_slots)]
-    pair_sums = []
-    for slot in range(heads):
-        total = grad_pair_slots[slot].astype(f32)
-        for step in range(1, members):
-            sent = grad_pair_slots[step * heads + slot]
-            total = total + among(sent, members - step).astype(f32)
-        total = total.astype(bf16)
-        pair_sums.append(across(total, slot) if slot else total)
-    grad_projected = jnp.zeros((rows, 3, head_width), bf16)
-    for slot in range(heads):
-        start = (place ^ slot) * HD
-        grad_query = turn(grad_query_slots[slot].reshape(rows, HD).astype(f32), True)
-        pair = pair_sums[slot].reshape(rows, 2 * HD)
-        grad_key = turn(pair[:, :HD].astype(f32), True)
-        piece = jnp.stack([grad_query.astype(bf16), grad_key.astype(bf16), pair[:, HD:]], axis=1)
-        grad_projected = lax.dynamic_update_slice_in_dim(grad_projected, piece, start, 2)
-    grad_projected = grad_projected.reshape(rows, 3 * head_width)
-    one_parts = scatter_heads(
-        [contract(own_rows(grad_projected, slot), flat_qkv, 1, 1) for slot in range(head_count)]
-    )
-    grad_qkv_part = contract(normed_low, grad_projected, 0, 0).astype(bf16)
 
     logits = jnp.dot(pooled, w_router, precision=highest, preferred_element_type=f32)
     logit_grads = []
@@ -558,16 +609,124 @@
     )
 
     member_own = own_rows(in_seq.astype(f32), 0)
-    grad_one = sum(one_parts[1:], one_parts[0]) + jnp.dot(
+    grad_pooled_own = jnp.dot(
         member_own, grad_pooled, precision=highest, preferred_element_type=f32
     )
+    tokens_own = own_rows(tokens, 0).astype(f32)
     hat_own, inverse_own = normalize_parts(tokens_own)
+
+    mixed_slots, logs = attend_forward(
+        scal, query_slots, pair_slots, other_slots, heads, members
+    )
+    mixed_slots = [across(v, slot) if slot else v for slot, v in enumerate(mixed_slots)]
+    mixed_slots, grad_router, grad_pooled_own, hat_own, inverse_own = lax.optimization_barrier(
+        (mixed_slots, grad_router, grad_pooled_own, hat_own, inverse_own)
+    )
+    mixed_slots = [v.reshape(rows, HD) for v in mixed_slots]
+    heads_out = placed(mixed_slots, place, 1)
+
+    heads_rel = [own_rows(heads_out, slot) for slot in range(head_count)]
+    heads_own = jnp.concatenate(
+        [heads_rel[0]] + [swap(heads_rel[slot], slot) for slot in range(1, head_count)], axis=1
+    )
+    hidden = tokens_own + dot(heads_own, all_out)
+    hat_two, inverse_two = normalize_parts(hidden)
+    normed_two = gather_heads((hat_two * gain_ffn).astype(bf16))
+
+    cotangent_rel = jnp.concatenate(
+        [own_rows(cotangent, slot) for slot in range(head_count)], axis=0
+    )
+    level_rel = jnp.concatenate([own_rows(ffn_level, slot) for slot in range(head_count)])
+    unit_index = head_rank * ffn_width + jnp.arange(ffn_width)
+    ffn_live = (unit_index[None, :] < (level_rel * (FF // LEVELS))[:, None]).astype(f32)
+    grad_active = contract(cotangent_rel, full_down, 1, 1).astype(bf16)
+    normed_two, grad_active = lax.optimization_barrier((normed_two, grad_active))
+    normed_two = jnp.concatenate(normed_two, axis=0)
+    upward = dot(normed_two, full_up)
+    kept = jnp.maximum(upward, 0.0)
+    active = (jnp.square(kept) * ffn_live).astype(bf16)
+    grad_upward = (grad_active.astype(f32) * ffn_live * 2.0 * kept).astype(bf16)
+    grad_down_part = contract(active, cotangent_rel, 0, 0).astype(bf16)
+    grad_upward, grad_down_part = lax.optimization_barrier((grad_upward, grad_down_part))
+    grad_down = lax.psum_scatter(
+        grad_down_part, "seq", scatter_dimension=1, tiled=True
+    ).astype(f32)
+    two_parts = [
+        contract(grad_upward[slot * share : (slot + 1) * share], full_up, 1, 1)
+        for slot in range(head_count)
+    ]
+    two_parts = scatter_heads(two_parts)
+    grad_up_part = contract(normed_two, grad_upward, 0, 0).astype(bf16)
+    two_parts, grad_up_part = lax.optimization_barrier((two_parts, grad_up_part))
+    grad_up = lax.psum_scatter(grad_up_part, "seq", scatter_dimension=0, tiled=True).astype(f32)
+
+    grad_two = sum(two_parts[1:], two_parts[0])
+    back_two, gain_two = normalize_back(grad_two, hat_two, inverse_two, gain_ffn)
+    grad_hidden = own_rows(cotangent, 0).astype(f32) + back_two
+    grad_attn_own = grad_hidden.astype(bf16)
+    grad_mixed = contract(grad_attn_own, all_out, 1, 1).astype(bf16)
+    grad_mixed = [
+        grad_mixed[:, slot * head_width : (slot + 1) * head_width] for slot in range(head_count)
+    ]
+    grad_mixed = [grad_mixed[0]] + [
+        swap(grad_mixed[slot], slot) for slot in range(1, head_count)
+    ]
+    grad_heads = placed(grad_mixed, head_rank, 0)
+    grad_slots = []
+    for slot in range(heads):
+        piece = lax.dynamic_slice_in_dim(grad_heads, (place ^ slot) * HD, HD, 1)
+        piece = piece.reshape(CHUNKS, SHORT_DEV, HD)
+        grad_slots.append(across(piece, slot) if slot else piece)
+    grad_attn = gather_heads(after(grad_attn_own, grad_heads))
+    grad_attn = jnp.concatenate(grad_attn, axis=0)
+    grad_out_part = contract(jnp.concatenate(heads_rel, axis=0), grad_attn, 0, 0).astype(bf16)
+    ffn_parts = [
+        dot(active[slot * share : (slot + 1) * share], full_down) for slot in range(head_count)
+    ]
+    ffn_parts = [ffn_parts[0]] + [v.astype(bf16) for v in ffn_parts[1:]]
+    grad_slots, ffn_parts = lax.optimization_barrier((grad_slots, ffn_parts))
+
+    grad_query_slots, grad_pair_slots = attend_backward(
+        scal, query_slots, pair_slots, other_slots, grad_slots, logs, heads, members
+    )
+    grad_query_slots = [across(v, slot) if slot else v for slot, v in enumerate(grad_query_slots)]
+    pair_sums = []
+    for slot in range(heads):
+        total = grad_pair_slots[slot].astype(f32)
+        for step in range(1, members):
+            sent = grad_pair_slots[step * heads + slot]
+            total = total + among(sent, members - step).astype(f32)
+        total = total.astype(bf16)
+        pair_sums.append(across(total, slot) if slot else total)
+    grad_query_slots, pair_sums, grad_out_part = lax.optimization_barrier(
+        (grad_query_slots, pair_sums, grad_out_part)
+    )
+    grad_projected = gather_grads(scal, cosine, -sine, grad_query_slots, pair_sums)
+    one_parts = scatter_heads(
+        [
+            sum(
+                contract(own_rows(grad_projected[part], slot), w_qkv[:, part], 1, 1)
+                for part in range(3)
+            )
+            for slot in range(head_count)
+        ]
+    )
+    grad_parts = [contract(normed_low, v, 0, 0).astype(bf16) for v in grad_projected]
+    grad_parts = [after(v, grad_down, grad_up) for v in grad_parts + [grad_out_part]]
+    grad_parts = [v.astype(f32) for v in lax.psum(grad_parts, "seq")]
+    grad_qkv = jnp.stack(grad_parts[:3], axis=1)
+    grad_out = grad_parts[3]
+    ffn_parts = [ffn_parts[0]] + [
+        swap(ffn_parts[slot], slot).astype(f32) for slot in range(1, head_count)
+    ]
+    output_own = (hidden + sum(ffn_parts[1:], ffn_parts[0])).astype(bf16)
+    output = in_order(gather_heads(output_own), bf16)
+
+    grad_one = sum(one_parts[1:], one_parts[0]) + grad_pooled_own
     back_one, gain_one = normalize_back(grad_one, hat_own, inverse_own, gain_attn)
     grad_tokens = in_order(gather_heads((grad_hidden + back_one).astype(bf16)), f32)
     gains = jnp.stack([gain_one, gain_two])
     gains = butterfly(butterfly(gains, "heads", head_count), "seq", seq_count)
-    grad_qkv = lax.psum(grad_qkv_part, "seq").astype(f32).reshape(D, 3, head_width)
-    grad_out = lax.psum(grad_out_part, "seq").astype(f32)
     return (
         output,
         grad_tokens,

time: 993 us -> 847 us (0.85)
  waiting for transfers between devices: 534 us -> 433 us
  local copies, waits for them, and re-layouts: 92.6 us -> 38.3 us
  other arithmetic: 74.4 us -> 48.5 us
  Pallas kernels: 36.2 us -> 59.1 us
  starting transfers between devices: 102 us -> 112 us
    psum x1, waiting for transfers between devices: 0.01 us -> 108 us  [local(): grad_parts = [v.astype(f32) for v in lax.psum(grad_parts, 'seq')]]
    reduce_scatter x1, waiting for transfers between devices: 87.4 us -> 0.01 us  [local(): lax.psum_scatter(grad_down_part, 'seq', scatter_dimension=1, tiled=True)]
    ppermute x32 -> x38, waiting for transfers between devices: 278 us -> 201 us  [flip(): return lax.ppermute(values, axis, [(i, i ^ bit) for i in range(size)])]
    ppermute x18, waiting for transfers between devices: 156 us -> 123 us  [across(): return lax.ppermute(values, 'seq', pairs)]
    pallas_call x0 -> x2, Pallas kernels: none -> 22.6 us  [the longest x1 18.1 us: project(): pl.pallas_call(functools.partial(project_kernel, heads), out_shape=[jax.S...]
    another operation x20 -> x3, local copies, waits for them, and re-layouts: 26.6 us -> 4.09 us
    unnamed x105 -> x134, local copies, waits for them, and re-layouts: 30.9 us -> 16.7 us
    concatenate x11 -> x1, other arithmetic: 13.8 us -> 0.19 us  [local(): cosine = jnp.concatenate([cosine, cosine], axis=1)]
  transfers between devices with their start and end apart: 63 -> 69, of which waited for: 33 -> 27; matrix products, arithmetic and copies ran while one was open for 23% -> 22% of each run, Pallas kernels for 2% -> 7%
where the time goes in v2:
time: 847 us; the launch traced here: 843 us
  waiting for transfers between devices  433 us (51%)
  matrix products  137 us (16%)
  starting transfers between devices  112 us (13%)
  Pallas kernels  59.1 us (7%)
  other arithmetic  48.5 us (6%)
  local copies, waits for them, and re-layouts  38.3 us (5%)
  between operations  14.9 us (2%)
    ppermute x38, waiting for transfers between devices, flip(): return lax.ppermute(values, axis, [(i, i ^ bit) for i in range(size)])  201 us
    ppermute x18, waiting for transfers between devices, across(): return lax.ppermute(values, 'seq', pairs)  123 us
    psum x1, waiting for transfers between devices, local(): grad_parts = [v.astype(f32) for v in lax.psum(grad_parts, 'seq')]  108 us
    dot_general x24, matrix products, contract(): lax.dot_general(left, right, (((left_dim,), (right_dim,)), ((), ())), pre...  91.4 us
    ppermute x38, starting transfers between devices, flip(): return lax.ppermute(values, axis, [(i, i ^ bit) for i in range(size)])  59.5 us
    ppermute x18, starting transfers between devices, across(): return lax.ppermute(values, 'seq', pairs)  49.8 us
    dot_general x6, matrix products, dot(): return jnp.dot(left, right, preferred_element_type=f32)  41.9 us
    pallas_call x1, Pallas kernels, attend_backward(): pl.pallas_call(functools.partial(back_kernel, heads, members), out_shape=...  20.9 us
  transfers between devices with their start and end apart: 69, of which 27 were waited for; matrix products, arithmetic and copies ran while one was open for 22% of the time, Pallas kernels for 7%

profile of v2, /device:TPU:0, one launch (start us, length us, event | category | flops | bytes accessed | tf_op | source)
XLA Modules:
  0.0 843.4 jit_solution(15543035350587414212)
XLA Ops:
  11.6 18.1 %project.1 = (bf16[7,128,128]{2,1,0:T(8,128)(2,1)S(1)}, bf16[7,128,128]{2,1,0:T(8,128)(2,1)S(1)}, bf16[7,128,128]{2,1,0:T(8,128)(2,1)S(1)}, bf16[7,128,128]{2,1,...) custom-call(s32[7]{0:T(128)S(1)} %pad_add_fusion.scal, ...), custom_call_target="tpu_custom_call" | custom-call | flops 5637144576 | bytes 16777216 | tf_op jit(solution)/shard_map/project/pallas_call | solution.py:400
  49.4 56.4 %collective-permute-done.14 = f32[5,2048]{1,0:T(8,128)S(1)} collective-permute-done((f32[5,2048]{1,0:T(8,128)S(1)}, f32[5,2048]{1,0:T(8,128)S(1)}, u32[]{:S(2)}, u32[]{:S(2)}) %collective-permute-start.14) | collective-permute-done | bytes 40992 | tf_op jit(solution)/shard_map/ppermute | solution.py:55
  109.2 12.3 %collective-permute-done.15 = f32[5,2048]{1,0:T(8,128)S(1)} collective-permute-done((f32[5,2048]{1,0:T(8,128)S(1)}, f32[5,2048]{1,0:T(8,128)S(1)}, u32[]{:S(2)}, u32[]{:S(2)}) %collective-permute-start.15) | collective-permute-done | bytes 40992 | tf_op jit(solution)/shard_map/ppermute | solution.py:55
  122.7 15.4 %collective-permute-done.1.refs_2_ = bf16[7,128,128]{2,1,0:T(8,128)(2,1)} collective-permute-done((bf16[7,128,128]{2,1,0:T(8,128)(2,1)S(1)}, bf16[7,128,128]{2,1,0:T(8,128)(2,1)}, u32[]{:S(2)}, u32[]{:S(2)}) %collective-permute-start.1) | collective-permute-done | bytes 229408 | tf_op jit(solution)/shard_map/ppermute | solution.py:513
  151.7 15.6 %attend_forward.1 = (bf16[7,128,128]{2,1,0:T(8,128)(2,1)}, bf16[7,128,128]{2,1,0:T(8,128)(2,1)}, bf16[7,128,128]{2,1,0:T(8,128)(2,1)}, bf16[7,128,128]{2,1,0:T(8,128)(2,1)}, f32[4,7,1,128]{3,2,1,0:T(1,128)}) custom-call(s32[7]{0:T(128)} %copy-done.6, bf16[7,128,128]{2,1,0:T(8,128)(2,1)} %copy-done.9, bf16[7,128,128]{2,1,0:T(8,128)(2,1)} %copy-done.45, ...), custom_call_target="tpu_custom_call" | custom-call | flops 4000000000 | bytes 7340032 | tf_op jit(solution)/shard_map/attend_forward/pallas_call | solution.py:186
  174.9 21.0 %collective-permute-done.10 = bf16[7,128,128]{2,1,0:T(8,128)(2,1)S(1)} collective-permute-done((bf16[7,128,128]{2,1,0:T(8,128)(2,1)}, bf16[7,128,128]{2,1,0:T(8,128)(2,1)S(1)}, u32[]{:S(2)}, u32[]{:S(2)}) %collective-permute-start.10) | collective-permute-done | bytes 229408 | tf_op jit(solution)/shard_map/ppermute | solution.py:513
  200.1 10.5 %collective-permute-done.12 = bf16[7,128,128]{2,1,0:T(8,128)(2,1)S(1)} collective-permute-done((bf16[7,128,128]{2,1,0:T(8,128)(2,1)}, bf16[7,128,128]{2,1,0:T(8,128)(2,1)S(1)}, u32[]{:S(2)}, u32[]{:S(2)}) %collective-permute-start.12) | collective-permute-done | bytes 229408 | tf_op jit(solution)/shard_map/ppermute | solution.py:513
  217.2 29.4 %collective-permute-done.20 = bf16[512,2048]{1,0:T(8,128)(2,1)S(1)} collective-permute-done((bf16[512,2048]{1,0:T(8,128)(2,1)}, bf16[512,2048]{1,0:T(8,128)(2,1)S(1)}, u32[]{:S(2)}, u32[]{:S(2)}) %collective-permute-start.20) | collective-permute-done | bytes 2097184 | tf_op jit(solution)/shard_map/ppermute | solution.py:55
  260.9 12.5 %convolution_convert_fusion.2 = bf16[896,2048]{1,0:T(8,128)(2,1)} fusion(bf16[2048,2048]{1,0:T(8,128)(2,1)} %all-gather.3.cloned.1.call-done, bf16[224,2048]{1,0:T(8,128)(2,1)} %get-tuple-element.181, bf16[224,2048]{1,0:T(8,128)(2,1)} %get-tuple-element.182, bf16[224,2048]{1,0:T(8,128)(2,1)} %get-tuple-element.180, bf16[224,2048]{1,0:T(8,128)(2,1)} %get-tuple-element.179), kind=kOutput, calls=%fused_computation.18 | convolution fusion | flops 7532707840 | bytes 15728640 | tf_op jit(solution)/shard_map/dot_general | solution.py:33
  273.4 7.4 collective-permute-done.22
  280.7 19.3 %collective-permute-done.23 = bf16[224,2048]{1,0:T(8,128)(2,1)} collective-permute-done((bf16[224,2048]{1,0:T(8,128)(2,1)S(1)}, bf16[224,2048]{1,0:T(8,128)(2,1)}, u32[]{:S(2)}, u32[]{:S(2)}) %collective-permute-start.23) | collective-permute-done | bytes 917536 | tf_op jit(solution)/shard_map/ppermute | solution.py:55
  307.6 15.1 %fusion.3 = (bf16[896,2048]{1,0:T(8,128)(2,1)S(1)}, bf16[896,2048]{1,0:T(8,128)(2,1)}) fusion(s32[2048]{0:T(1024)S(1)} %iota_add_fusion, s32[896]{0:T(1024)S(1)} %add_multiply_fusion.3, bf16[896,2048]{1,0:T(8,128)(2,1)} %convolution_convert_fusion.2, bf16[896,2048]{1,0:T(8,128)(2,1)} %constant_dynamic-update-slice_fusion.4, ...), kind=kOutput, calls=%fused_computation.7 | convolution fusion | flops 7534542848 | bytes 23080448 | tf_op jit(solution)/shard_map/dot_general | solution.py:29
  324.6 11.4 %convolution_convert_fusion.1 = bf16[2048,2048]{1,0:T(8,128)(2,1)} fusion(bf16[896,2048]{1,0:T(8,128)(2,1)S(1)} %get-tuple-element.177, bf16[224,2048]{1,0:T(8,128)(2,1)S(1)} %copy-done.25, bf16[224,2048]{1,0:T(8,128)(2,1)S(1)} %copy-done.26, bf16[224,2048]{1,0:T(8,128)(2,1)S(1)} %copy-done.24, bf16[224,2048]{1,0:T(8,128)(2,1)S(1)} %copy-done.18), kind=kOutput, calls=%fused_computation.3 | convolution fusion | flops 7535067136 | bytes 15728640 | tf_op jit(solution)/shard_map/dot_general | solution.py:33
  336.2 7.4 convolution_convert_fusion.12
  344.3 8.1 convolution_convert_fusion.11
  358.4 13.7 %convolution_convert_fusion = bf16[2048,2048]{1,0:T(8,128)(2,1)} fusion(bf16[896,2048]{1,0:T(8,128)(2,1)} %constant_dynamic-update-slice_fusion.4, bf16[896,2048]{1,0:T(8,128)(2,1)S(1)} %copy-done.52), kind=kOutput, calls=%fused_computation.2 | convolution fusion | flops 7520387072 | bytes 15728640 | tf_op jit(solution)/shard_map/dot_general | solution.py:33
  372.1 7.7 fusion.71
  382.4 9.3 %collective-permute-done.26 = bf16[224,2048]{1,0:T(8,128)(2,1)} collective-permute-done((bf16[224,2048]{1,0:T(8,128)(2,1)}, bf16[224,2048]{1,0:T(8,128)(2,1)}, u32[]{:S(2)}, u32[]{:S(2)}) %collective-permute-start.26) | collective-permute-done | bytes 917536 | tf_op jit(solution)/shard_map/ppermute | solution.py:55
  397.3 7.2 fusion.52
  430.2 7.3 collective-permute-start.31
  449.3 12.8 %collective-permute-done.32.refs_14_ = bf16[7,128,128]{2,1,0:T(8,128)(2,1)S(1)} collective-permute-done((bf16[7,128,128]{2,1,0:T(8,128)(2,1)S(1)}, bf16[7,128,128]{2,1,0:T(8,128)(2,1)S(1)}, u32[]{:S(2)}, u32[]{:S(2)}) %collective-permute-start.32) | collective-permute-done | bytes 229408 | tf_op jit(solution)/shard_map/ppermute | solution.py:513
  467.6 20.9 %attend_backward.1 = (bf16[7,128,128]{2,1,0:T(8,128)(2,1)}, bf16[7,128,128]{2,1,0:T(8,128)(2,1)}, bf16[7,128,128]{2,1,0:T(8,128)(2,1)}, bf16[7,128,128]{2,1,0:T(...) custom-call(s32[7]{0:T(128)} %copy-done.6, ...), custom_call_target="tpu_custom_call" | custom-call | flops 10000000000 | bytes 12582912 | tf_op jit(solution)/shard_map/attend_backward/pallas_call | solution.py:303
  495.5 8.2 collective-permute-start.40
  506.0 16.3 %collective-permute-done.40.refs_1_ = bf16[7,128,128]{2,1,0:T(8,128)(2,1)S(1)} collective-permute-done((bf16[7,128,128]{2,1,0:T(8,128)(2,1)}, bf16[7,128,128]{2,1,0:T(8,128)(2,1)S(1)}, u32[]{:S(2)}, u32[]{:S(2)}) %collective-permute-start.40) | collective-permute-done | bytes 229408 | tf_op jit(solution)/shard_map/ppermute | solution.py:513
  531.2 9.1 %collective-permute-start.47 = (bf16[7,128,256]{2,1,0:T(8,128)(2,1)S(1)}, bf16[7,128,256]{2,1,0:T(8,128)(2,1)S(1)}, u32[]{:S(2)}, u32[]{:S(2)}) collective-permute-start(bf16[7,128,256]{2,1,0:T(8,128)(2,1)S(1)} %add_convert_fusion.3), channel_id=1, source_target_pairs={{0,4},{1,5},{2,6},{3,7},{4,0},{5,1},{6,2},{7,3},{8,12},{9,13},{10,... | collective-permute-start | bytes 1376264 | tf_op jit(solution)/shard_map/ppermute | solution.py:513
  548.3 11.7 %collective-permute-done.45.refs_5_ = bf16[7,128,256]{2,1,0:T(8,128)(2,1)S(1)} collective-permute-done((bf16[7,128,256]{2,1,0:T(8,128)(2,1)S(1)}, bf16[7,128,256]{2,1,0:T(8,128)(2,1)S(1)}, u32[]{:S(2)}, u32[]{:S(2)}) %collective-permute-start.45) | collective-permute-done | bytes 458784 | tf_op jit(solution)/shard_map/ppermute | solution.py:513
  560.4 19.4 %collective-permute-done.47.refs_6_ = bf16[7,128,256]{2,1,0:T(8,128)(2,1)S(1)} collective-permute-done((bf16[7,128,256]{2,1,0:T(8,128)(2,1)S(1)}, bf16[7,128,256]{2,1,0:T(8,128)(2,1)S(1)}, u32[]{:S(2)}, u32[]{:S(2)}) %collective-permute-start.47) | collective-permute-done | bytes 458784 | tf_op jit(solution)/shard_map/ppermute | solution.py:513
  617.6 11.8 %collective-permute-done.54 = bf16[224,2048]{1,0:T(8,128)(2,1)S(1)} collective-permute-done((bf16[224,2048]{1,0:T(8,128)(2,1)S(1)}, bf16[224,2048]{1,0:T(8,128)(2,1)S(1)}, u32[]{:S(2)}, u32[]{:S(2)}) %collective-permute-start.54) | collective-permute-done | bytes 917536 | tf_op jit(solution)/shard_map/ppermute | solution.py:55
  639.6 29.0 %collective-permute-done.59 = f32[2,2048]{1,0:T(2,128)S(1)} collective-permute-done((f32[2,2048]{1,0:T(2,128)S(1)}, f32[2,2048]{1,0:T(2,128)S(1)}, u32[]{:S(2)}, u32[]{:S(2)}) %collective-permute-start.59) | collective-permute-done | bytes 16416 | tf_op jit(solution)/shard_map/ppermute | solution.py:55
  681.4 15.4 %collective-permute-start.62 = (f32[2,2048]{1,0:T(2,128)S(1)}, f32[2,2048]{1,0:T(2,128)S(1)}, u32[]{:S(2)}, u32[]{:S(2)}) collective-permute-start(f32[2,2048]{1,0:T(2,128)S(1)} %add.337), channel_id=1, source_target_pairs={{0,2},{1,3},{2,0},{3,1},{4,6},{5,7},{6,4},{7,5},{8,10},{9,11},{10,... | collective-permute-start | bytes 49160 | tf_op jit(solution)/shard_map/ppermute | solution.py:55
  706.4 10.1 %collective-permute-done.57 = bf16[224,2048]{1,0:T(8,128)(2,1)S(1)} collective-permute-done((bf16[224,2048]{1,0:T(8,128)(2,1)S(1)}, bf16[224,2048]{1,0:T(8,128)(2,1)S(1)}, u32[]{:S(2)}, u32[]{:S(2)}) %collective-permute-start.57) | collective-permute-done | bytes 917536 | tf_op jit(solution)/shard_map/ppermute | solution.py:55
  719.3 108.0 %all-reduce.3.cloned.1.call-done = (bf16[2048,1,512]{2,0,1:T(8,128)(2,1)}, bf16[2048,1,512]{2,0,1:T(8,128)(2,1)}, bf16[2048,1,512]{2,0,1:T(8,128)(2,1)}, bf16[512,2048]{1,0:T(8,128)(2,1)}) async-done(((bf16[2048,1,512]{2,0,1:T(8,128)(2,1)}, bf16[2048,1,512]{2,0,1:T(8,128)(2,1)}, bf16[2048,1,512]{2,0,1:T(8,128)(2,1)}, bf16[512,2048]{1,0:T(8,128)(2,1)}), (bf16[2048,1,512]{2,0,1:T(8,128)(2,1)}, ...) | async-done | bytes 8388624 | tf_op jit(solution)/shard_map/psum | solution.py:716
  (365 shorter events, 250.6 us)
Async XLA Ops:
  7.2 253.7 %all-gather.3.cloned.1.call-start = ((), (), s32[]{:S(2)}) async-start(), calls=%async_computation.2 | async-start | bytes 9437184 | tf_op jit(solution)/shard_map/all_gather | solution.py:557
  7.9 299.7 %all-gather.5.cloned.1.call-start = ((), (), s32[]{:S(2)}) async-start(), calls=%async_computation.3 | async-start | bytes 9437184 | tf_op jit(solution)/shard_map/all_gather | solution.py:558
  8.7 625.4 %reduce-scatter.3.cloned.1.call-start = ((), (), s32[]{:S(2)}) async-start(), calls=%async_computation.4 | async-start | bytes 9437184 | tf_op jit(solution)/shard_map/reduce_scatter | solution.py:651
  30.4 91.2 %collective-permute-start = (bf16[7,128,128]{2,1,0:T(8,128)(2,1)S(1)}, bf16[7,128,128]{2,1,0:T(8,128)(2,1)S(1)}, u32[]{:S(2)}, u32[]{:S(2)}) collective-permute-start(bf16[7,128,128]{2,1,0:T(8,128)(2,1)S(1)} %get-tuple-element.82), channel_id=1, source_target_pairs={{0,2},{1,3},{2,0},{3,1},{4,6},{5,7},{6,4},{7,5},{8,10},{9,11},{10,... | collective-permute-start | bytes 688136 | tf_op jit(solution)/shard_map/ppermute | solution.py:513
  33.4 88.5 %collective-permute-start.3 = (bf16[7,128,256]{2,1,0:T(8,128)(2,1)S(1)}, bf16[7,128,256]{2,1,0:T(8,128)(2,1)}, u32[]{:S(2)}, u32[]{:S(2)}) collective-permute-start(bf16[7,128,256]{2,1,0:T(8,128)(2,1)S(1)} %get-tuple-element.86), channel_id=1, source_target_pairs={{0,2},{1,3},{2,0},{3,1},{4,6},{5,7},{6,4},{7,5},{8,10},{9,11},{10,... | collective-permute-start | bytes 1376264 | tf_op jit(solution)/shard_map/ppermute | solution.py:513
  33.5 88.7 %collective-permute-start.4 = (bf16[7,128,256]{2,1,0:T(8,128)(2,1)S(1)}, bf16[7,128,256]{2,1,0:T(8,128)(2,1)}, u32[]{:S(2)}, u32[]{:S(2)}) collective-permute-start(bf16[7,128,256]{2,1,0:T(8,128)(2,1)S(1)} %get-tuple-element.87), channel_id=1, source_target_pairs={{0,4},{1,5},{2,6},{3,7},{4,0},{5,1},{6,2},{7,3},{8,12},{9,13},{10,... | collective-permute-start | bytes 1376264 | tf_op jit(solution)/shard_map/ppermute | solution.py:513
  36.5 86.0 %collective-permute-start.5 = (bf16[7,128,256]{2,1,0:T(8,128)(2,1)S(1)}, bf16[7,128,256]{2,1,0:T(8,128)(2,1)}, u32[]{:S(2)}, u32[]{:S(2)}) collective-permute-start(bf16[7,128,256]{2,1,0:T(8,128)(2,1)S(1)} %get-tuple-element.88), channel_id=1, source_target_pairs={{0,6},{1,7},{2,4},{3,5},{4,2},{5,3},{6,0},{7,1},{8,14},{9,15},{10,... | collective-permute-start | bytes 1376264 | tf_op jit(solution)/shard_map/ppermute | solution.py:513
  49.0 56.8 %collective-permute-start.14 = (f32[5,2048]{1,0:T(8,128)S(1)}, f32[5,2048]{1,0:T(8,128)S(1)}, u32[]{:S(2)}, u32[]{:S(2)}) collective-permute-start(f32[5,2048]{1,0:T(8,128)S(1)} %slice_add_fusion), channel_id=1, source_target_pairs={{0,2},{1,3},{2,0},{3,1},{4,6},{5,7},{6,4},{7,5},{8,10},{9,11},{10,... | collective-permute-start | bytes 122888 | tf_op jit(solution)/shard_map/ppermute | solution.py:55
  147.5 67.1 %collective-permute-start.19 = (bf16[512,2048]{1,0:T(8,128)(2,1)}, bf16[512,2048]{1,0:T(8,128)(2,1)S(1)}, u32[]{:S(2)}, u32[]{:S(2)}) collective-permute-start(bf16[512,2048]{1,0:T(8,128)(2,1)} %param.14), channel_id=1, source_target_pairs={{0,8},{8,0},{16,24},{24,16},{1,9},{9,1},{17,25},{25,17},{2,10},{10... | collective-permute-start | bytes 6291464 | tf_op jit(solution)/shard_map/ppermute | solution.py:55
  149.4 97.2 %collective-permute-start.20 = (bf16[512,2048]{1,0:T(8,128)(2,1)}, bf16[512,2048]{1,0:T(8,128)(2,1)S(1)}, u32[]{:S(2)}, u32[]{:S(2)}) collective-permute-start(bf16[512,2048]{1,0:T(8,128)(2,1)} %param.14), channel_id=1, source_target_pairs={{0,16},{8,24},{16,0},{24,8},{1,17},{9,25},{17,1},{25,9},{2,18},{10... | collective-permute-start | bytes 6291464 | tf_op jit(solution)/shard_map/ppermute | solution.py:55
  151.0 97.3 %collective-permute-start.21 = (bf16[512,2048]{1,0:T(8,128)(2,1)}, bf16[512,2048]{1,0:T(8,128)(2,1)S(1)}, u32[]{:S(2)}, u32[]{:S(2)}) collective-permute-start(bf16[512,2048]{1,0:T(8,128)(2,1)} %param.14), channel_id=1, source_target_pairs={{0,24},{8,16},{16,8},{24,0},{1,25},{9,17},{17,9},{25,1},{2,26},{10... | collective-permute-start | bytes 6291464 | tf_op jit(solution)/shard_map/ppermute | solution.py:55
  212.1 37.7 %collective-permute-start.18 = (bf16[224,512]{1,0:T(8,128)(2,1)S(1)}, bf16[224,512]{1,0:T(8,128)(2,1)S(1)}, u32[]{:S(2)}, u32[]{:S(2)}) collective-permute-start(bf16[224,512]{1,0:T(8,128)(2,1)S(1)} %get-tuple-element.192), channel_id=1, source_target_pairs={{0,24},{8,16},{16,8},{24,0},{1,25},{9,17},{17,9},{25,1},{2,26},{10... | collective-permute-start | bytes 688136 | tf_op jit(solution)/shard_map/ppermute | solution.py:55
  258.2 41.9 %collective-permute-start.23 = (bf16[224,2048]{1,0:T(8,128)(2,1)S(1)}, bf16[224,2048]{1,0:T(8,128)(2,1)}, u32[]{:S(2)}, u32[]{:S(2)}) collective-permute-start(bf16[224,2048]{1,0:T(8,128)(2,1)S(1)} %multiply_convert_fusion), channel_id=1, source_target_pairs={{0,16},{8,24},{16,0},{24,8},{1,17},{9,25},{17,1},{25,9},{2,18},{10... | collective-permute-start | bytes 2752520 | tf_op jit(solution)/shard_map/ppermute | solution.py:55
  259.4 40.6 %collective-permute-start.24 = (bf16[224,2048]{1,0:T(8,128)(2,1)S(1)}, bf16[224,2048]{1,0:T(8,128)(2,1)}, u32[]{:S(2)}, u32[]{:S(2)}) collective-permute-start(bf16[224,2048]{1,0:T(8,128)(2,1)S(1)} %multiply_convert_fusion), channel_id=1, source_target_pairs={{0,24},{8,16},{16,8},{24,0},{1,25},{9,17},{17,9},{25,1},{2,26},{10... | collective-permute-start | bytes 2752520 | tf_op jit(solution)/shard_map/ppermute | solution.py:55
  336.1 300.7 %reduce-scatter.5.cloned.1.call-start = ((), (), s32[]{:S(2)}) async-start(), calls=%async_computation.5 | async-start | bytes 9437184 | tf_op jit(solution)/shard_map/reduce_scatter | solution.py:661
  352.4 39.3 %collective-permute-start.26 = (bf16[224,2048]{1,0:T(8,128)(2,1)}, bf16[224,2048]{1,0:T(8,128)(2,1)}, u32[]{:S(2)}, u32[]{:S(2)}) collective-permute-start(bf16[224,2048]{1,0:T(8,128)(2,1)} %convolution_convert_fusion.11), channel_id=1, source_target_pairs={{0,16},{8,24},{16,0},{24,8},{1,17},{9,25},{17,1},{25,9},{2,18},{10... | collective-permute-start | bytes 2752520 | tf_op jit(solution)/shard_map/ppermute | solution.py:55
  356.9 37.5 %collective-permute-start.27 = (bf16[224,2048]{1,0:T(8,128)(2,1)}, bf16[224,2048]{1,0:T(8,128)(2,1)}, u32[]{:S(2)}, u32[]{:S(2)}) collective-permute-start(bf16[224,2048]{1,0:T(8,128)(2,1)} %convolution_convert_fusion.10), channel_id=1, source_target_pairs={{0,24},{8,16},{16,8},{24,0},{1,25},{9,17},{17,9},{25,1},{2,26},{10... | collective-permute-start | bytes 2752520 | tf_op jit(solution)/shard_map/ppermute | solution.py:55
  397.0 430.3 %all-reduce.3.cloned.1.call-start = ((), (), s32[]{:S(2)}) async-start(), calls=%async_computation.6 | async-start | bytes 16777216 | tf_op jit(solution)/shard_map/psum | solution.py:716
  489.2 42.0 %collective-permute-start.51 = (bf16[224,2048]{1,0:T(8,128)(2,1)S(1)}, bf16[224,2048]{1,0:T(8,128)(2,1)S(1)}, u32[]{:S(2)}, u32[]{:S(2)}) collective-permute-start(bf16[224,2048]{1,0:T(8,128)(2,1)S(1)} %copy-done.28), channel_id=1, source_target_pairs={{0,16},{8,24},{16,0},{24,8},{1,17},{9,25},{17,1},{25,9},{2,18},{10... | collective-permute-start | bytes 2752520 | tf_op jit(solution)/shard_map/ppermute | solution.py:55
  490.8 49.5 %collective-permute-start.50 = (bf16[224,2048]{1,0:T(8,128)(2,1)S(1)}, bf16[224,2048]{1,0:T(8,128)(2,1)S(1)}, u32[]{:S(2)}, u32[]{:S(2)}) collective-permute-start(bf16[224,2048]{1,0:T(8,128)(2,1)S(1)} %copy-done.28), channel_id=1, source_target_pairs={{0,8},{8,0},{16,24},{24,16},{1,9},{9,1},{17,25},{25,17},{2,10},{10... | collective-permute-start | bytes 2752520 | tf_op jit(solution)/shard_map/ppermute | solution.py:55
  504.9 40.5 %collective-permute-start.41 = (bf16[7,128,128]{2,1,0:T(8,128)(2,1)S(1)}, bf16[7,128,128]{2,1,0:T(8,128)(2,1)S(1)}, u32[]{:S(2)}, u32[]{:S(2)}) collective-permute-start(bf16[7,128,128]{2,1,0:T(8,128)(2,1)S(1)} %copy-done.48), channel_id=1, source_target_pairs={{0,4},{1,5},{2,6},{3,7},{4,0},{5,1},{6,2},{7,3},{8,12},{9,13},{10,... | collective-permute-start | bytes 688136 | tf_op jit(solution)/shard_map/ppermute | solution.py:513
  531.2 48.7 %collective-permute-start.47 = (bf16[7,128,256]{2,1,0:T(8,128)(2,1)S(1)}, bf16[7,128,256]{2,1,0:T(8,128)(2,1)S(1)}, u32[]{:S(2)}, u32[]{:S(2)}) collective-permute-start(bf16[7,128,256]{2,1,0:T(8,128)(2,1)S(1)} %add_convert_fusion.3), channel_id=1, source_target_pairs={{0,4},{1,5},{2,6},{3,7},{4,0},{5,1},{6,2},{7,3},{8,12},{9,13},{10,... | collective-permute-start | bytes 1376264 | tf_op jit(solution)/shard_map/ppermute | solution.py:513
  540.3 39.6 %collective-permute-start.49 = (bf16[7,128,256]{2,1,0:T(8,128)(2,1)S(1)}, bf16[7,128,256]{2,1,0:T(8,128)(2,1)S(1)}, u32[]{:S(2)}, u32[]{:S(2)}) collective-permute-start(bf16[7,128,256]{2,1,0:T(8,128)(2,1)S(1)} %add_convert_fusion.2), channel_id=1, source_target_pairs={{0,6},{1,7},{2,4},{3,5},{4,2},{5,3},{6,0},{7,1},{8,14},{9,15},{10,... | collective-permute-start | bytes 1376264 | tf_op jit(solution)/shard_map/ppermute | solution.py:513
  545.4 62.1 %collective-permute-start.36 = (bf16[224,2048]{1,0:T(8,128)(2,1)S(1)}, bf16[224,2048]{1,0:T(8,128)(2,1)S(1)}, u32[]{:S(2)}, u32[]{:S(2)}) collective-permute-start(bf16[224,2048]{1,0:T(8,128)(2,1)S(1)} %copy-done.43), channel_id=1, source_target_pairs={{0,24},{8,16},{16,8},{24,0},{1,25},{9,17},{17,9},{25,1},{2,26},{10... | collective-permute-start | bytes 2752520 | tf_op jit(solution)/shard_map/ppermute | solution.py:55
  546.4 63.7 %collective-permute-start.35 = (bf16[224,2048]{1,0:T(8,128)(2,1)S(1)}, bf16[224,2048]{1,0:T(8,128)(2,1)S(1)}, u32[]{:S(2)}, u32[]{:S(2)}) collective-permute-start(bf16[224,2048]{1,0:T(8,128)(2,1)S(1)} %copy-done.42), channel_id=1, source_target_pairs={{0,16},{8,24},{16,0},{24,8},{1,17},{9,25},{17,1},{25,9},{2,18},{10... | collective-permute-start | bytes 2752520 | tf_op jit(solution)/shard_map/ppermute | solution.py:55
  560.0 50.2 %collective-permute-start.34 = (bf16[224,2048]{1,0:T(8,128)(2,1)S(1)}, bf16[224,2048]{1,0:T(8,128)(2,1)S(1)}, u32[]{:S(2)}, u32[]{:S(2)}) collective-permute-start(bf16[224,2048]{1,0:T(8,128)(2,1)S(1)} %copy-done.41), channel_id=1, source_target_pairs={{0,8},{8,0},{16,24},{24,16},{1,9},{9,1},{17,25},{25,17},{2,10},{10... | collective-permute-start | bytes 2752520 | tf_op jit(solution)/shard_map/ppermute | solution.py:55
  589.5 40.0 %collective-permute-start.54 = (bf16[224,2048]{1,0:T(8,128)(2,1)S(1)}, bf16[224,2048]{1,0:T(8,128)(2,1)S(1)}, u32[]{:S(2)}, u32[]{:S(2)}) collective-permute-start(bf16[224,2048]{1,0:T(8,128)(2,1)S(1)} %fusion.16), channel_id=1, source_target_pairs={{0,16},{8,24},{16,0},{24,8},{1,17},{9,25},{17,1},{25,9},{2,18},{10... | collective-permute-start | bytes 2752520 | tf_op jit(solution)/shard_map/ppermute | solution.py:55
  614.1 64.1 %collective-permute-start.37 = (bf16[224,2048]{1,0:T(8,128)(2,1)S(1)}, bf16[224,2048]{1,0:T(8,128)(2,1)}, u32[]{:S(2)}, u32[]{:S(2)}) collective-permute-start(bf16[224,2048]{1,0:T(8,128)(2,1)S(1)} %get-tuple-element.173), channel_id=1, source_target_pairs={{0,8},{8,0},{16,24},{24,16},{1,9},{9,1},{17,25},{25,17},{2,10},{10... | collective-permute-start | bytes 2752520 | tf_op jit(solution)/shard_map/ppermute | solution.py:55
  614.3 67.1 %collective-permute-start.38 = (bf16[224,2048]{1,0:T(8,128)(2,1)S(1)}, bf16[224,2048]{1,0:T(8,128)(2,1)}, u32[]{:S(2)}, u32[]{:S(2)}) collective-permute-start(bf16[224,2048]{1,0:T(8,128)(2,1)S(1)} %get-tuple-element.173), channel_id=1, source_target_pairs={{0,16},{8,24},{16,0},{24,8},{1,17},{9,25},{17,1},{25,9},{2,18},{10... | collective-permute-start | bytes 2752520 | tf_op jit(solution)/shard_map/ppermute | solution.py:55
  614.9 86.7 %collective-permute-start.39 = (bf16[224,2048]{1,0:T(8,128)(2,1)S(1)}, bf16[224,2048]{1,0:T(8,128)(2,1)}, u32[]{:S(2)}, u32[]{:S(2)}) collective-permute-start(bf16[224,2048]{1,0:T(8,128)(2,1)S(1)} %get-tuple-element.173), channel_id=1, source_target_pairs={{0,24},{8,16},{16,8},{24,0},{1,25},{9,17},{17,9},{25,1},{2,26},{10... | collective-permute-start | bytes 2752520 | tf_op jit(solution)/shard_map/ppermute | solution.py:55
  676.5 39.9 %collective-permute-start.57 = (bf16[224,2048]{1,0:T(8,128)(2,1)S(1)}, bf16[224,2048]{1,0:T(8,128)(2,1)S(1)}, u32[]{:S(2)}, u32[]{:S(2)}) collective-permute-start(bf16[224,2048]{1,0:T(8,128)(2,1)S(1)} %get-tuple-element.168), channel_id=1, source_target_pairs={{0,16},{8,24},{16,0},{24,8},{1,17},{9,25},{17,1},{25,9},{2,18},{10... | collective-permute-start | bytes 2752520 | tf_op jit(solution)/shard_map/ppermute | solution.py:55
  680.6 37.3 %collective-permute-start.58 = (bf16[224,2048]{1,0:T(8,128)(2,1)S(1)}, bf16[224,2048]{1,0:T(8,128)(2,1)S(1)}, u32[]{:S(2)}, u32[]{:S(2)}) collective-permute-start(bf16[224,2048]{1,0:T(8,128)(2,1)S(1)} %get-tuple-element.168), channel_id=1, source_target_pairs={{0,24},{8,16},{16,8},{24,0},{1,25},{9,17},{17,9},{25,1},{2,26},{10... | collective-permute-start | bytes 2752520 | tf_op jit(solution)/shard_map/ppermute | solution.py:55
  (101 other events, 2110.2 us)
Sparse Core Ops, SparseCore 0:
  9.6 146.1 all-gather.2
  157.4 99.4 all-gather.4
  336.2 93.3 reduce-scatter.2
  431.7 123.3 reduce-scatter.4
  639.7 187.5 all-reduce.2

commit v3 on v2

--- a/solution.py
+++ b/solution.py
@@ -74,7 +74,7 @@
             number = len(copies)
             copies.append(
                 pltpu.make_async_copy(
-                    source[slot].at[0:NSHORT], keys_short.at[:, block], sems.at[number]
+                    source[slot].at[0:NSHORT, :, HD:], keys_short.at[:, block], sems.at[number]
                 )
             )
             for index in range(NLONG):
@@ -82,7 +82,7 @@
                 number = len(copies)
                 copies.append(
                     pltpu.make_async_copy(
-                        source[slot].at[first : first + 2],
+                        source[slot].at[first : first + 2, :, HD:],
                         keys_long.at[index, block],
                         sems.at[number],
                     )
@@ -94,7 +94,7 @@
     head = scal[0]
     copies = []
     for slot in range(heads):
-        ends = (slots[slot], held.at[head ^ slot])
+        ends = (slots[slot].at[:, :, 0:HD], held.at[head ^ slot])
         if outward:
             ends = ends[::-1]
         copies.append(pltpu.make_async_copy(ends[0], ends[1], sems.at[slot]))
@@ -122,14 +122,13 @@
 
 def attend_kernel(heads, members, scal, *refs):
     count = heads
-    query_slots = refs[:count]
-    own = refs[count : 2 * count]
-    others = refs[2 * count : (1 + members) * count]
-    rest = refs[(1 + members) * count :]
+    own = refs[:count]
+    others = refs[count : members * count]
+    rest = refs[members * count :]
     out_slots = rest[:count]
     log_ref = rest[count]
     queries, keys_short, keys_long, mixed, row_sems, key_sems = rest[count + 1 :]
-    copies = row_copies(scal, query_slots, queries, row_sems, heads, False)
+    copies = row_copies(scal, own, queries, row_sems, heads, False)
     copies += key_copies(scal, own, others, keys_short, keys_long, key_sems, members, heads)
     for copy in copies:
         copy.start()
@@ -180,7 +179,7 @@
         copy.wait()
 
 
-def attend_forward(scal, query_slots, own, others, heads, members):
+def attend_forward(scal, own, others, heads, members):
     blocks = heads * members
     anywhere = pl.BlockSpec(memory_space=pl.ANY)
     result = pl.pallas_call(
@@ -188,7 +187,7 @@
         out_shape=[jax.ShapeDtypeStruct((CHUNKS, SHORT_DEV, HD), bf16)] * heads
         + [jax.ShapeDtypeStruct((heads, CHUNKS, 1, SHORT_DEV), f32)],
         in_specs=[pl.BlockSpec(memory_space=pltpu.SMEM)]
-        + [anywhere] * (len(query_slots) + len(own) + len(others)),
+        + [anywhere] * (len(own) + len(others)),
         out_specs=[anywhere] * heads + [pl.BlockSpec(memory_space=pltpu.VMEM)],
         scratch_shapes=[
             pltpu.VMEM((heads, CHUNKS, SHORT_DEV, HD), bf16),
@@ -203,28 +202,37 @@
             flops=4 * 10**9, bytes_accessed=7 << 20, transcendentals=4 * 10**6
         ),
         name="attend_forward",
-    )(scal, *query_slots, *own, *others)
+    )(scal, *own, *others)
     return (result[:heads], result[heads])
 
 
 def back_kernel(heads, members, scal, *refs):
     count = heads
-    query_slots = refs[:count]
-    own = refs[count : 2 * count]
-    others = refs[2 * count : (1 + members) * count]
-    rest = refs[(1 + members) * count :]
+    own = refs[:count]
+    others = refs[count : members * count]
+    rest = refs[members * count :]
     grad_slots = rest[:count]
     log_ref = rest[count]
     rest = rest[count + 1 :]
-    query_out = rest[:count]
-    pair_out = rest[count : (1 + members) * count]
-    scratch = rest[(1 + members) * count :]
+    own_out = rest[:count]
+    other_out = rest[count : count + members - 1]
+    scratch = rest[count + members - 1 :]
     queries, keys_short, keys_long, grads, sum_short, sum_long = scratch[:6]
-    low_short, low_long, row_sems, grad_sems, key_sems = scratch[6:]
-    copies = row_copies(scal, query_slots, queries, row_sems, heads, False)
+    low_short, low_long, zeros, row_sems, grad_sems, key_sems, zero_sems = scratch[6:]
+    copies = row_copies(scal, own, queries, row_sems, heads, False)
     copies += row_copies(scal, grad_slots, grads, grad_sems, heads, False)
     copies += key_copies(scal, own, others, keys_short, keys_long, key_sems, members, heads)
     for copy in copies:
+        copy.start()
+    zeros[...] = jnp.zeros(zeros.shape, bf16)
+    blanks = [
+        pltpu.make_async_copy(
+            zeros, other_out[part].at[slot, :, :, 0:HD], zero_sems.at[part * heads + slot]
+        )
+        for part in range(members - 1)
+        for slot in range(heads)
+    ]
+    for copy in blanks:
         copy.start()
     for copy in copies:
         copy.wait()
@@ -267,17 +275,17 @@
         low_ref[index] = sum_ref[...].astype(bf16).reshape(low_ref.shape[1:])
 
     sequence_loop(work)
-    copies = row_copies(scal, query_out, queries, row_sems, heads, True)
+    copies = row_copies(scal, own_out, queries, row_sems, heads, True)
     head, member = scal[0], scal[1]
     number = 0
     for part in range(members):
         whose = lax.rem(member + part, members)
         for slot in range(heads):
             block = (head ^ slot) * members + whose
-            target = pair_out[part * heads + slot]
+            target = own_out[slot] if part == 0 else other_out[part - 1].at[slot]
             copies.append(
                 pltpu.make_async_copy(
-                    low_short.at[:, block], target.at[0:NSHORT], key_sems.at[number]
+                    low_short.at[:, block], target.at[0:NSHORT, :, HD:], key_sems.at[number]
                 )
             )
             number += 1
@@ -286,28 +294,28 @@
                 copies.append(
                     pltpu.make_async_copy(
                         low_long.at[index, block],
-                        target.at[first : first + 2],
+                        target.at[first : first + 2, :, HD:],
                         key_sems.at[number],
                     )
                 )
                 number += 1
     for copy in copies:
         copy.start()
-    for copy in copies:
+    for copy in blanks + copies:
         copy.wait()
 
 
-def attend_backward(scal, query_slots, own, others, grad_slots, logs, heads, members):
+def attend_backward(scal, own, others, grad_slots, logs, heads, members):
     blocks = heads * members
     anywhere = pl.BlockSpec(memory_space=pl.ANY)
     result = pl.pallas_call(
         functools.partial(back_kernel, heads, members),
-        out_shape=[jax.ShapeDtypeStruct((CHUNKS, SHORT_DEV, HD), bf16)] * heads
-        + [jax.ShapeDtypeStruct((CHUNKS, SHORT_DEV, 2 * HD), bf16)] * blocks,
+        out_shape=[jax.ShapeDtypeStruct((CHUNKS, SHORT_DEV, 3 * HD), bf16)] * heads
+        + [jax.ShapeDtypeStruct((heads, CHUNKS, SHORT_DEV, 3 * HD), bf16)] * (members - 1),
         in_specs=[pl.BlockSpec(memory_space=pltpu.SMEM)]
-        + [anywhere] * (2 * heads + blocks)
+        + [anywhere] * (heads + blocks)
         + [pl.BlockSpec(memory_space=pltpu.VMEM)],
-        out_specs=[anywhere] * (heads + blocks),
+        out_specs=[anywhere] * (heads + members - 1),
         scratch_shapes=[
             pltpu.VMEM((heads, CHUNKS, SHORT_DEV, HD), bf16),
             pltpu.VMEM((NSHORT, blocks, SHORT_DEV, 2 * HD), bf16),
@@ -317,16 +325,18 @@
             pltpu.VMEM((2 * blocks * SHORT_DEV, 2 * HD), f32),
             pltpu.VMEM((NSHORT, blocks, SHORT_DEV, 2 * HD), bf16),
             pltpu.VMEM((NLONG, blocks, 2, SHORT_DEV, 2 * HD), bf16),
+            pltpu.VMEM((CHUNKS, SHORT_DEV, HD), bf16),
             pltpu.SemaphoreType.DMA((heads,)),
             pltpu.SemaphoreType.DMA((heads,)),
             pltpu.SemaphoreType.DMA((3 * blocks,)),
+            pltpu.SemaphoreType.DMA(((members - 1) * heads,)),
         ],
         compiler_params=pltpu.CompilerParams(vmem_limit_bytes=60 << 20),
         cost_estimate=pl.CostEstimate(
             flops=10**10, bytes_accessed=12 << 20, transcendentals=4 * 10**6
         ),
         name="attend_backward",
-    )(scal, *query_slots, *own, *others, *grad_slots, logs)
+    )(scal, *own, *others, *grad_slots, logs)
     return (result[:heads], result[heads:])
 
 
@@ -335,9 +345,9 @@
 
 
 def project_kernel(heads, scal, tokens, gain, cosine, sine, weights, *refs):
-    query_slots, pair_slots = refs[:heads], refs[heads : 2 * heads]
-    normed, pooled = refs[2 * heads : 2 * heads + 2]
-    held_weights, acc, queries, pairs, in_sems, out_sems = refs[2 * heads + 2 :]
+    slots = refs[:heads]
+    normed, pooled = refs[heads : heads + 2]
+    held_weights, acc, held, in_sems, out_sems = refs[heads + 2 :]
     head = scal[0]
     loads = [
         pltpu.make_async_copy(weights.at[part], held_weights.at[part], in_sems.at[part])
@@ -359,7 +369,6 @@
         return carry
 
     lax.fori_loop(0, CHUNKS, norm, 0)
-    stores = []
     for part in range(3):
         loads[part].wait()
         acc[...] = dot(normed[...], held_weights[part])
@@ -370,23 +379,16 @@
                 values = acc[here, index * HD : (index + 1) * HD]
                 if part < 2:
                     values = rotate_rows(values, cosine[here, :], sine[here, :])
-                if part == 0:
-                    queries[index, chunk] = values.astype(bf16)
-                elif part == 1:
-                    pairs[index, chunk, :, :HD] = values.astype(bf16)
-                else:
-                    pairs[index, chunk, :, HD:] = values.astype(bf16)
+                held[index, chunk, :, part * HD : (part + 1) * HD] = values.astype(bf16)
             return carry
 
         lax.fori_loop(0, CHUNKS, spread, 0)
-        if part != 1:
-            held, outs = (queries, query_slots) if part == 0 else (pairs, pair_slots)
-            for slot in range(heads):
-                copy = pltpu.make_async_copy(
-                    held.at[head ^ slot], outs[slot], out_sems.at[len(stores)]
-                )
-                copy.start()
-                stores.append(copy)
+    stores = [
+        pltpu.make_async_copy(held.at[head ^ slot], slots[slot], out_sems.at[slot])
+        for slot in range(heads)
+    ]
+    for store in stores:
+        store.start()
     for store in stores:
         store.wait()
 
@@ -399,18 +401,16 @@
     inside = pl.BlockSpec(memory_space=pltpu.VMEM)
     result = pl.pallas_call(
         functools.partial(project_kernel, heads),
-        out_shape=[jax.ShapeDtypeStruct((CHUNKS, SHORT_DEV, HD), bf16)] * heads
-        + [jax.ShapeDtypeStruct((CHUNKS, SHORT_DEV, 2 * HD), bf16)] * heads
+        out_shape=[jax.ShapeDtypeStruct((CHUNKS, SHORT_DEV, 3 * HD), bf16)] * heads
         + [jax.ShapeDtypeStruct((rows, D), bf16), jax.ShapeDtypeStruct((8, D), f32)],
         in_specs=[pl.BlockSpec(memory_space=pltpu.SMEM)] + [inside] * 4 + [anywhere],
-        out_specs=[anywhere] * (2 * heads) + [inside] * 2,
+        out_specs=[anywhere] * heads + [inside] * 2,
         scratch_shapes=[
             pltpu.VMEM((3, D, width), bf16),
             pltpu.VMEM((rows, width), f32),
-            pltpu.VMEM((heads, CHUNKS, SHORT_DEV, HD), bf16),
-            pltpu.VMEM((heads, CHUNKS, SHORT_DEV, 2 * HD), bf16),
+            pltpu.VMEM((heads, CHUNKS, SHORT_DEV, 3 * HD), bf16),
             pltpu.SemaphoreType.DMA((3,)),
-            pltpu.SemaphoreType.DMA((2 * heads,)),
+            pltpu.SemaphoreType.DMA((heads,)),
         ],
         compiler_params=pltpu.CompilerParams(vmem_limit_bytes=50 << 20),
         cost_estimate=pl.CostEstimate(
@@ -418,63 +418,56 @@
         ),
         name="project",
     )(scal, tokens, gain, cosine, sine, weights)
-    return (result[:heads], result[heads : 2 * heads], result[2 * heads], result[2 * heads + 1])
+    return (result[:heads], result[heads], result[heads + 1])
 
 
 def gather_kernel(heads, scal, cosine, sine, *refs):
-    query_slots, pair_slots = refs[:heads], refs[heads : 2 * heads]
-    out_query, out_key, out_value = refs[2 * heads : 2 * heads + 3]
-    queries, pairs, sems = refs[2 * heads + 3 :]
-    copies = []
-    for held, slots in ((queries, query_slots), (pairs, pair_slots)):
-        for slot in range(heads):
-            copy = pltpu.make_async_copy(
-                slots[slot], held.at[scal[0] ^ slot], sems.at[len(copies)]
-            )
-            copy.start()
-            copies.append(copy)
+    slots = refs[:heads]
+    out, held, sems = refs[heads:]
+    copies = [
+        pltpu.make_async_copy(slots[slot], held.at[scal[0] ^ slot], sems.at[slot])
+        for slot in range(heads)
+    ]
+    for copy in copies:
+        copy.start()
     for copy in copies:
         copy.wait()
 
     def spread(chunk, carry):
         here = pl.ds(pl.multiple_of(chunk * SHORT_DEV, SHORT_DEV), SHORT_DEV)
         for index in range(heads):
-            there = slice(index * HD, (index + 1) * HD)
-            values = queries[index, chunk].astype(f32)
-            values = rotate_rows(values, cosine[here, :], sine[here, :])
-            out_query[here, there] = values.astype(bf16)
-            values = pairs[index, chunk, :, :HD].astype(f32)
-            values = rotate_rows(values, cosine[here, :], sine[here, :])
-            out_key[here, there] = values.astype(bf16)
-            out_value[here, there] = pairs[index, chunk, :, HD:]
+            for part in range(3):
+                values = held[index, chunk, :, part * HD : (part + 1) * HD]
+                if part < 2:
+                    values = rotate_rows(values.astype(f32), cosine[here, :], sine[here, :])
+                at = (part * heads + index) * HD
+                out[here, at : at + HD] = values.astype(bf16)
         return carry
 
     lax.fori_loop(0, CHUNKS, spread, 0)
 
 
-def gather_grads(scal, cosine, sine, query_slots, pair_slots):
-    heads = len(query_slots)
+def gather_grads(scal, cosine, sine, slots):
+    heads = len(slots)
     rows = CHUNKS * SHORT_DEV
-    anywhere = pl.BlockSpec(memory_space=pl.ANY)
     inside = pl.BlockSpec(memory_space=pltpu.VMEM)
     return pl.pallas_call(
         functools.partial(gather_kernel, heads),
-        out_shape=[jax.ShapeDtypeStruct((rows, heads * HD), bf16)] * 3,
+        out_shape=jax.ShapeDtypeStruct((rows, 3 * heads * HD), bf16),
         in_specs=[pl.BlockSpec(memory_space=pltpu.SMEM)]
         + [inside] * 2
-        + [anywhere] * (2 * heads),
-        out_specs=[inside] * 3,
+        + [pl.BlockSpec(memory_space=pl.ANY)] * heads,
+        out_specs=inside,
         scratch_shapes=[
-            pltpu.VMEM((heads, CHUNKS, SHORT_DEV, HD), bf16),
-            pltpu.VMEM((heads, CHUNKS, SHORT_DEV, 2 * HD), bf16),
-            pltpu.SemaphoreType.DMA((2 * heads,)),
+            pltpu.VMEM((heads, CHUNKS, SHORT_DEV, 3 * HD), bf16),
+            pltpu.SemaphoreType.DMA((heads,)),
         ],
         compiler_params=pltpu.CompilerParams(vmem_limit_bytes=24 << 20),
         cost_estimate=pl.CostEstimate(
             flops=10 * rows * heads * HD, bytes_accessed=6 << 20, transcendentals=0
         ),
         name="gather_grads",
-    )(scal, cosine, sine, *query_slots, *pair_slots)
+    )(scal, cosine, sine, *slots)
 
 
 def local(
@@ -512,6 +505,10 @@
         ]
         return lax.ppermute(values, "seq", pairs)
 
+    def exchange(slots):
+        sent = [across(slots[slot], slot) for slot in reversed(range(1, heads))]
+        return [slots[0]] + sent[::-1]
+
     def among(values, step):
         pairs = [
             (h * members + (m + step) % members, h * members + m)
@@ -528,11 +525,19 @@
 
     def scatter_heads(parts):
         return [parts[0]] + [
-            swap(parts[slot].astype(bf16), slot).astype(f32) for slot in range(1, head_count)
+            swap(parts[slot].astype(bf16), slot) for slot in range(1, head_count)
         ]
 
     def gather_heads(values):
         return [values] + [swap(values, slot) for slot in range(1, head_count)]
+
+    def gather_doubling(values):
+        slots = [values]
+        bit = 1
+        while bit < head_count:
+            slots = slots + [swap(v, bit) for v in slots]
+            bit *= 2
+        return slots
 
     def in_order(slots, kind):
         full = jnp.zeros((rows,) + slots[0].shape[1:], kind)
@@ -551,12 +556,8 @@
             full = lax.dynamic_update_slice_in_dim(full, values, (key ^ slot) * size, axis)
         return full
 
-    def after(values, *others):
-        return lax.optimization_barrier((values,) + others)[0]
-
-    full_down = lax.all_gather(w_down, "seq", axis=1, tiled=True)
     full_up = lax.all_gather(w_up, "seq", axis=0, tiled=True)
-    all_out = jnp.concatenate(gather_heads(w_out), axis=0)
+    full_out = lax.all_gather(w_out, "heads", axis=0, tiled=True)
 
     column = jnp.arange(rows)
     is_short = column < short_rows
@@ -583,17 +584,73 @@
     head_live = (my_head < head_quarters * (H // LEVELS)).astype(jnp.int32)
     scal = jnp.concatenate([jnp.stack([place, member]).astype(jnp.int32), head_live])
 
-    sent_queries, sent_pairs, normed_low, pooled_sum = project(
+    slots, normed_low, pooled = project(
         scal, tokens, gain_attn[None, :], cosine, sine, w_qkv.transpose(1, 0, 2)
     )
-    pooled_sum = pooled_sum[:SEQS]
-    query_slots = [across(v, slot) if slot else v for slot, v in enumerate(sent_queries)]
-    pair_slots = [across(v, slot) if slot else v for slot, v in enumerate(sent_pairs)]
-    other_slots = [
-        among(pair_slots[slot], step) for step in range(1, members) for slot in range(heads)
-    ]
-    pooled = butterfly(pooled_sum, "seq", seq_count) * lax.rsqrt(seq_length)[:, None]
-
+    full_down = lax.all_gather(w_down, "seq", axis=1, tiled=True)
+    slots = exchange(slots)
+    other_slots = [among(v, step) for step in range(1, members) for v in slots]
+    tokens_own = own_rows(tokens, 0).astype(f32)
+    hat_own, inverse_own = normalize_parts(tokens_own)
+    hops = []
+    bit = 1
+    while bit < seq_count:
+        hops.append(bit)
+        bit *= 2
+
+    def hop(values, bits):
+        for bit in bits:
+            values = values + flip(values, "seq", seq_count, bit)
+        return values
+
+    pooled = hop(pooled[:SEQS], hops[:-2])
+    slots, other_slots, hat_own, inverse_own, pooled = lax.optimization_barrier(
+        (slots, other_slots, hat_own, inverse_own, pooled)
+    )
+    pooled = hop(pooled, hops[-2:-1])
+    mixed_slots, logs = attend_forward(scal, slots, other_slots, heads, members)
+    mixed_slots = [across(v, slot) if slot else v for slot, v in enumerate(mixed_slots)]
+    mixed_slots, pooled = lax.optimization_barrier((mixed_slots, pooled))
+    pooled = hop(pooled, hops[-1:])
+    mixed_slots = [v.reshape(rows, HD) for v in mixed_slots]
+    heads_out = placed(mixed_slots, place, 1)
+
+    heads_rel = [own_rows(heads_out, slot) for slot in range(head_count)]
+    heads_own = placed(
+        [heads_rel[0]] + [swap(heads_rel[slot], slot) for slot in range(1, head_count)],
+        head_rank,
+        1,
+    )
+    hidden = tokens_own + dot(heads_own, full_out)
+    hat_two, inverse_two = normalize_parts(hidden)
+    normed_two = gather_heads((hat_two * gain_ffn).astype(bf16))
+
+    cotangent_rel = jnp.concatenate(
+        [own_rows(cotangent, slot) for slot in range(head_count)], axis=0
+    )
+    level_rel = jnp.concatenate([own_rows(ffn_level, slot) for slot in range(head_count)])
+    unit_index = head_rank * ffn_width + jnp.arange(ffn_width)
+    ffn_live = (unit_index[None, :] < (level_rel * (FF // LEVELS))[:, None]).astype(f32)
+    normed_two, pooled = lax.optimization_barrier((normed_two, pooled))
+    normed_two = jnp.concatenate(normed_two, axis=0)
+    upward = dot(normed_two, full_up)
+    kept = jnp.maximum(upward, 0.0)
+    active = (jnp.square(kept) * ffn_live).astype(bf16)
+    grad_down_part = contract(active, cotangent_rel, 0, 0).astype(bf16)
+    cotangent_rel, kept, grad_down_part = lax.optimization_barrier(
+        (cotangent_rel, kept, grad_down_part)
+    )
+    grad_active = contract(cotangent_rel, full_down, 1, 1).astype(bf16)
+    grad_upward = (grad_active.astype(f32) * ffn_live * 2.0 * kept).astype(bf16)
+    grad_down = lax.psum_scatter(grad_down_part, "seq", scatter_dimension=1, tiled=True)
+    two_parts = [
+        contract(grad_upward[slot * share : (slot + 1) * share], full_up, 1, 1)
+        for slot in range(head_count)
+    ]
+    two_parts = scatter_heads(two_parts)
+    grad_up_part = contract(normed_two, grad_upward, 0, 0).astype(bf16)
+
+    pooled = pooled * lax.rsqrt(seq_length)[:, None]
     logits = jnp.dot(pooled, w_router, precision=highest, preferred_element_type=f32)
     logit_grads = []
     for group in range(2):
@@ -607,67 +664,25 @@
         jnp.dot(grad_logits, w_router.T, precision=highest, preferred_element_type=f32)
         * lax.rsqrt(seq_length)[:, None]
     )
-
     member_own = own_rows(in_seq.astype(f32), 0)
     grad_pooled_own = jnp.dot(
         member_own, grad_pooled, precision=highest, preferred_element_type=f32
     )
-    tokens_own = own_rows(tokens, 0).astype(f32)
-    hat_own, inverse_own = normalize_parts(tokens_own)
-
-    mixed_slots, logs = attend_forward(
-        scal, query_slots, pair_slots, other_slots, heads, members
-    )
-    mixed_slots = [across(v, slot) if slot else v for slot, v in enumerate(mixed_slots)]
-    mixed_slots, grad_router, grad_pooled_own, hat_own, inverse_own = lax.optimization_barrier(
-        (mixed_slots, grad_router, grad_pooled_own, hat_own, inverse_own)
-    )
-    mixed_slots = [v.reshape(rows, HD) for v in mixed_slots]
-    heads_out = placed(mixed_slots, place, 1)
-
-    heads_rel = [own_rows(heads_out, slot) for slot in range(head_count)]
-    heads_own = jnp.concatenate(
-        [heads_rel[0]] + [swap(heads_rel[slot], slot) for slot in range(1, head_count)], axis=1
-    )
-    hidden = tokens_own + dot(heads_own, all_out)
-    hat_two, inverse_two = normalize_parts(hidden)
-    normed_two = gather_heads((hat_two * gain_ffn).astype(bf16))
-
-    cotangent_rel = jnp.concatenate(
-        [own_rows(cotangent, slot) for slot in range(head_count)], axis=0
-    )
-    level_rel = jnp.concatenate([own_rows(ffn_level, slot) for slot in range(head_count)])
-    unit_index = head_rank * ffn_width + jnp.arange(ffn_width)
-    ffn_live = (unit_index[None, :] < (level_rel * (FF // LEVELS))[:, None]).astype(f32)
-    grad_active = contract(cotangent_rel, full_down, 1, 1).astype(bf16)
-    normed_two, grad_active = lax.optimization_barrier((normed_two, grad_active))
-    normed_two = jnp.concatenate(normed_two, axis=0)
-    upward = dot(normed_two, full_up)
-    kept = jnp.maximum(upward, 0.0)
-    active = (jnp.square(kept) * ffn_live).astype(bf16)
-    grad_upward = (grad_active.astype(f32) * ffn_live * 2.0 * kept).astype(bf16)
-    grad_down_part = contract(active, cotangent_rel, 0, 0).astype(bf16)
-    grad_upward, grad_down_part = lax.optimization_barrier((grad_upward, grad_down_part))
-    grad_down = lax.psum_scatter(
-        grad_down_part, "seq", scatter_dimension=1, tiled=True
-    ).astype(f32)
-    two_parts = [
-        contract(grad_upward[slot * share : (slot + 1) * share], full_up, 1, 1)
-        for slot in range(head_count)
-    ]
-    two_parts = scatter_heads(two_parts)
-    grad_up_part = contract(normed_two, grad_upward, 0, 0).astype(bf16)
-    two_parts, grad_up_part = lax.optimization_barrier((two_parts, grad_up_part))
-    grad_up = lax.psum_scatter(grad_up_part, "seq", scatter_dimension=0, tiled=True).astype(f32)
-
-    grad_two = sum(two_parts[1:], two_parts[0])
+    two_parts, grad_up_part, grad_router, grad_pooled_own = lax.optimization_barrier(
+        (two_parts, grad_up_part, grad_router, grad_pooled_own)
+    )
+    grad_up = lax.psum_scatter(grad_up_part, "seq", scatter_dimension=0, tiled=True)
+
+    grad_two = sum([v.astype(f32) for v in two_parts[1:]], two_parts[0])
     back_two, gain_two = normalize_back(grad_two, hat_two, inverse_two, gain_ffn)
     grad_hidden = own_rows(cotangent, 0).astype(f32) + back_two
     grad_attn_own = grad_hidden.astype(bf16)
-    grad_mixed = contract(grad_attn_own, all_out, 1, 1).astype(bf16)
+    grad_mixed = contract(grad_attn_own, full_out, 1, 1).astype(bf16)
     grad_mixed = [
-        grad_mixed[:, slot * head_width : (slot + 1) * head_width] for slot in range(head_count)
-    ]
+        lax.dynamic_slice_in_dim(grad_mixed, (head_rank ^ slot) * head_width, head_width, 1)
+        for slot in range(head_count)
+    ]
+    active, grad_mixed = lax.optimization_barrier((active, grad_mixed))
     grad_mixed = [grad_mixed[0]] + [
         swap(grad_mixed[slot], slot) for slot in range(1, head_count)
     ]
@@ -677,55 +692,76 @@
         piece = lax.dynamic_slice_in_dim(grad_heads, (place ^ slot) * HD, HD, 1)
         piece = piece.reshape(CHUNKS, SHORT_DEV, HD)
         grad_slots.append(across(piece, slot) if slot else piece)
-    grad_attn = gather_heads(after(grad_attn_own, grad_heads))
+    ffn_parts = [
+        dot(active[slot * share : (slot + 1) * share], full_down) for slot in range(head_count)
+    ]
+    ffn_parts = scatter_heads(ffn_parts)
+
+    own_grads, other_grads = attend_backward(
+        scal, slots, other_slots, grad_slots, logs, heads, members
+    )
+    own_grads, other_grads, ffn_parts[:-1] = lax.optimization_barrier(
+        (own_grads, other_grads, ffn_parts[:-1])
+    )
+    other_grads = [
+        among(v, members - step) for step, v in zip(range(1, members), other_grads)
+    ]
+    sums = []
+    for slot in range(heads):
+        total = own_grads[slot].astype(f32)
+        sums.append(sum([v[slot].astype(f32) for v in other_grads], total).astype(bf16))
+    sums, grad_attn_own = lax.optimization_barrier((sums, grad_attn_own))
+    sums = exchange(sums)
+    grad_attn = gather_heads(grad_attn_own)
     grad_attn = jnp.concatenate(grad_attn, axis=0)
     grad_out_part = contract(jnp.concatenate(heads_rel, axis=0), grad_attn, 0, 0).astype(bf16)
-    ffn_parts = [
-        dot(active[slot * share : (slot + 1) * share], full_down) for slot in range(head_count)
-    ]
-    ffn_parts = [ffn_parts[0]] + [v.astype(bf16) for v in ffn_parts[1:]]
-    grad_slots, ffn_parts = lax.optimization_barrier((grad_slots, ffn_parts))
-
-    grad_query_slots, grad_pair_slots = attend_backward(
-        scal, query_slots, pair_slots, other_slots, grad_slots, logs, heads, members
-    )
-    grad_query_slots = [across(v, slot) if slot else v for slot, v in enumerate(grad_query_slots)]
-    pair_sums = []
-    for slot in range(heads):
-        total = grad_pair_slots[slot].astype(f32)
-        for step in range(1, members):
-            sent = grad_pair_slots[step * heads + slot]
-            total = total + among(sent, members - step).astype(f32)
-        total = total.astype(bf16)
-        pair_sums.append(across(total, slot) if slot else total)
-    grad_query_slots, pair_sums, grad_out_part = lax.optimization_barrier(
-        (grad_query_slots, pair_sums, grad_out_part)
-    )
-    grad_projected = gather_grads(scal, cosine, -sine, grad_query_slots, pair_sums)
+    sums, grad_out_part = lax.optimization_barrier((sums, grad_out_part))
+    grad_projected = gather_grads(scal, cosine, -sine, sums)
+    grad_qkv_part = contract(normed_low, grad_projected, 0, 0).astype(bf16)
+    grad_projected, grad_qkv_part, grad_out_part, grad_down, grad_up = lax.optimization_barrier(
+        (grad_projected, grad_qkv_part, grad_out_part, grad_down, grad_up)
+    )
+    totals = [
+        lax.psum_scatter(v, "seq", scatter_dimension=0, tiled=True)
+        for v in (grad_qkv_part, grad_out_part)
+    ]
+    grad_down, grad_up = grad_down.astype(f32), grad_up.astype(f32)
     one_parts = scatter_heads(
         [
             sum(
-                contract(own_rows(grad_projected[part], slot), w_qkv[:, part], 1, 1)
+                contract(
+                    own_rows(grad_projected, slot)[:, part * head_width : (part + 1) * head_width],
+                    w_qkv[:, part],
+                    1,
+                    1,
+                )
                 for part in range(3)
             )
             for slot in range(head_count)
         ]
     )
-    grad_parts = [contract(normed_low, v, 0, 0).astype(bf16) for v in grad_projected]
-    grad_parts = [after(v, grad_down, grad_up) for v in grad_parts + [grad_out_part]]
-    grad_parts = [v.astype(f32) for v in lax.psum(grad_parts, "seq")]
-    grad_qkv = jnp.stack(grad_parts[:3], axis=1)
-    grad_out = grad_parts[3]
-    ffn_parts = [ffn_parts[0]] + [
-        swap(ffn_parts[slot], slot).astype(f32) for slot in range(1, head_count)
-    ]
-    output_own = (hidden + sum(ffn_parts[1:], ffn_parts[0])).astype(bf16)
-    output = in_order(gather_heads(output_own), bf16)
-
-    grad_one = sum(one_parts[1:], one_parts[0]) + grad_pooled_own
+    one_parts, totals, ffn_parts = lax.optimization_barrier((one_parts, totals, ffn_parts))
+    totals = [lax.all_gather(v, "seq", axis=0, tiled=True) for v in totals]
+    grad_qkv = jnp.stack(
+        [
+            totals[0][:, part * head_width : (part + 1) * head_width].astype(f32)
+            for part in range(3)
+        ],
+        axis=1,
+    )
+    grad_out = totals[1].astype(f32)
+    output_own = (
+        hidden + sum([v.astype(f32) for v in ffn_parts[1:]], ffn_parts[0])
+    ).astype(bf16)
+    output = in_order(gather_doubling(output_own), bf16)
+
+    grad_one = sum([v.astype(f32) for v in one_parts[1:]], one_parts[0]) + grad_pooled_own
     back_one, gain_one = normalize_back(grad_one, hat_own, inverse_own, gain_attn)
-    grad_tokens = in_order(gather_heads((grad_hidden + back_one).astype(bf16)), f32)
-    gains = jnp.stack([gain_one, gain_two])
+    token_slots = gather_heads((grad_hidden + back_one).astype(bf16))
+    token_slots, gains = lax.optimization_barrier(
+        (token_slots, jnp.stack([gain_one, gain_two]))
+    )
+    grad_tokens = in_order(token_slots, f32)
     gains = butterfly(butterfly(gains, "heads", head_count), "seq", seq_count)
     return (
         output,

time: 847 us -> 788 us (0.930)
  starting transfers between devices: 112 us -> 77.6 us
  waiting for transfers between devices: 433 us -> 403 us
    psum x1 -> x0, waiting for transfers between devices: 108 us -> none  [local(): grad_parts = [v.astype(f32) for v in lax.psum(grad_parts, 'seq')]]
    reduce_scatter x0 -> x2, waiting for transfers between devices: none -> 56.6 us  [local(): lax.psum_scatter(v, 'seq', scatter_dimension=0, tiled=True)]
    all_gather x1, waiting for transfers between devices: 0.01 us -> 23.8 us  [local(): full_down = lax.all_gather(w_down, 'seq', axis=1, tiled=True)]
    ppermute x38 -> x35, starting transfers between devices: 59.5 us -> 39.9 us  [flip(): return lax.ppermute(values, axis, [(i, i ^ bit) for i in range(size)])]
    ppermute x18 -> x12, waiting for transfers between devices: 123 us -> 109 us  [across(): return lax.ppermute(values, 'seq', pairs)]
    ppermute x18 -> x12, starting transfers between devices: 49.8 us -> 35.7 us  [across(): return lax.ppermute(values, 'seq', pairs)]
    dot_general x24 -> x22, matrix products: 91.4 us -> 101 us  [contract(): lax.dot_general(left, right, (((left_dim,), (right_dim,)), ((), ())), pre...]
    convert_element_type x10 -> x5, other arithmetic: 21.1 us -> 11.5 us  [the longest x1 4.13 us: local(): grad_out = totals[1].astype(f32)]
  transfers between devices with their start and end apart: 69 -> 61, of which waited for: 27 -> 31; matrix products, arithmetic and copies ran while one was open for 22% -> 26% of each run, Pallas kernels for 7% -> 7%
where the time goes in v3:
time: 788 us; the launch traced here: 779 us
  waiting for transfers between devices  403 us (51%)
  matrix products  137 us (17%)
  starting transfers between devices  77.6 us (10%)
  Pallas kernels  55.8 us (7%)
  other arithmetic  48.4 us (6%)
  local copies, waits for them, and re-layouts  41.3 us (5%)
  between operations  15.4 us (2%)
    ppermute x35, waiting for transfers between devices, flip(): return lax.ppermute(values, axis, [(i, i ^ bit) for i in range(size)])  205 us
    ppermute x12, waiting for transfers between devices, across(): return lax.ppermute(values, 'seq', pairs)  109 us
    dot_general x22, matrix products, contract(): lax.dot_general(left, right, (((left_dim,), (right_dim,)), ((), ())), pre...  101 us
    reduce_scatter x2, waiting for transfers between devices, local(): lax.psum_scatter(v, 'seq', scatter_dimension=0, tiled=True)  56.6 us
    ppermute x35, starting transfers between devices, flip(): return lax.ppermute(values, axis, [(i, i ^ bit) for i in range(size)])  39.9 us
    ppermute x12, starting transfers between devices, across(): return lax.ppermute(values, 'seq', pairs)  35.7 us
    dot_general x6, matrix products, dot(): return jnp.dot(left, right, preferred_element_type=f32)  32.3 us
    all_gather x1, waiting for transfers between devices, local(): full_down = lax.all_gather(w_down, 'seq', axis=1, tiled=True)  23.8 us
  transfers between devices with their start and end apart: 61, of which 31 were waited for; matrix products, arithmetic and copies ran while one was open for 26% of the time, Pallas kernels for 7%

profile of v3, /device:TPU:0, one launch (start us, length us, event | category | flops | bytes accessed | tf_op | source)
XLA Modules:
  0.0 779.0 jit_solution(567712064608203830)
XLA Ops:
  12.5 16.2 %project.1 = (bf16[7,128,384]{2,1,0:T(8,128)(2,1)S(1)}, bf16[7,128,384]{2,1,0:T(8,128)(2,1)S(1)}, bf16[7,128,384]{2,1,0:T(8,128)(2,1)S(1)}, bf16[7,128,384]{2,1,...) custom-call(s32[7]{0:T(128)S(1)} %pad_add_fusion.scal, bf16[896,2048]{1,0:T(8,128)(2,1)} %tokens.1, ...), custom_call_target="tpu_custom_call" | custom-call | flops 5637144576 | bytes 16777216 | tf_op jit(solution)/shard_map/project/pallas_call | solution.py:402
  37.9 23.5 %collective-permute-done.refs_1_ = bf16[7,128,384]{2,1,0:T(8,128)(2,1)} collective-permute-done((bf16[7,128,384]{2,1,0:T(8,128)(2,1)S(1)}, bf16[7,128,384]{2,1,0:T(8,128)(2,1)}, u32[]{:S(2)}, u32[]{:S(2)}) %collective-permute-start) | collective-permute-done | bytes 688160 | tf_op jit(solution)/shard_map/ppermute | solution.py:506
  61.4 19.3 %collective-permute-done.1.refs_2_ = bf16[7,128,384]{2,1,0:T(8,128)(2,1)} collective-permute-done((bf16[7,128,384]{2,1,0:T(8,128)(2,1)S(1)}, bf16[7,128,384]{2,1,0:T(8,128)(2,1)}, u32[]{:S(2)}, u32[]{:S(2)}) %collective-permute-start.1) | collective-permute-done | bytes 688160 | tf_op jit(solution)/shard_map/ppermute | solution.py:506
  85.4 15.8 %attend_forward.1 = (bf16[7,128,128]{2,1,0:T(8,128)(2,1)}, bf16[7,128,128]{2,1,0:T(8,128)(2,1)}, bf16[7,128,128]{2,1,0:T(8,128)(2,1)}, bf16[7,128,128]{2,1,0:T(8,128)(2,1)}, f32[4,7,1,128]{3,2,1,0:T(1,128)}) custom-call(s32[7]{0:T(128)} %copy-done.13, bf16[7,128,384]{2,1,0:T(8,128)(2,1)} %copy-done.15, bf16[7,128,384]{2,1,0:T(8,128)(2,1)} %collective-permute-done.refs_1_, ...), custom_call_target="tpu_custom_call" | custom-call | flops 4000000000 | bytes 7340032 | tf_op jit(solution)/shard_map/attend_forward/pallas_call | solution.py:185
  103.7 12.5 %collective-permute-start.8 = (bf16[7,128,128]{2,1,0:T(8,128)(2,1)}, bf16[7,128,128]{2,1,0:T(8,128)(2,1)S(1)}, u32[]{:S(2)}, u32[]{:S(2)}) collective-permute-start(bf16[7,128,128]{2,1,0:T(8,128)(2,1)} %get-tuple-element.113), channel_id=1, source_target_pairs={{0,2},{1,3},{2,0},{3,1},{4,6},{5,7},{6,4},{7,5},{8,10},{9,11},{10,... | collective-permute-start | bytes 688136 | tf_op jit(solution)/shard_map/ppermute | solution.py:506
  118.1 21.6 %collective-permute-done.11 = f32[5,2048]{1,0:T(8,128)S(1)} collective-permute-done((f32[5,2048]{1,0:T(8,128)S(1)}, f32[5,2048]{1,0:T(8,128)S(1)}, u32[]{:S(2)}, u32[]{:S(2)}) %collective-permute-start.11) | collective-permute-done | bytes 40992 | tf_op jit(solution)/shard_map/ppermute | solution.py:55
  139.8 13.9 %collective-permute-done.9 = bf16[7,128,128]{2,1,0:T(8,128)(2,1)S(1)} collective-permute-done((bf16[7,128,128]{2,1,0:T(8,128)(2,1)}, bf16[7,128,128]{2,1,0:T(8,128)(2,1)S(1)}, u32[]{:S(2)}, u32[]{:S(2)}) %collective-permute-start.9) | collective-permute-done | bytes 229408 | tf_op jit(solution)/shard_map/ppermute | solution.py:506
  185.9 9.0 %collective-permute-done.18 = f32[5,2048]{1,0:T(8,128)S(1)} collective-permute-done((f32[5,2048]{1,0:T(8,128)S(1)}, f32[5,2048]{1,0:T(8,128)S(1)}, u32[]{:S(2)}, u32[]{:S(2)}) %collective-permute-start.18) | collective-permute-done | bytes 40992 | tf_op jit(solution)/shard_map/ppermute | solution.py:55
  200.7 18.7 %collective-permute-done.16 = bf16[224,2048]{1,0:T(8,128)(2,1)} collective-permute-done((bf16[224,2048]{1,0:T(8,128)(2,1)}, bf16[224,2048]{1,0:T(8,128)(2,1)}, u32[]{:S(2)}, u32[]{:S(2)}) %collective-permute-start.16) | collective-permute-done | bytes 917536 | tf_op jit(solution)/shard_map/ppermute | solution.py:55
  228.2 13.4 %fusion = (bf16[896,2048]{1,0:T(8,128)(2,1)S(1)}, f32[896,2048]{1,0:T(8,128)}) fusion(s32[2048]{0:T(1024)S(1)} %iota_add_fusion, s32[896]{0:T(1024)S(1)} %add_multiply_fusion, bf16[896,2048]{1,0:T(8,128)(2,1)} %constant_dynamic-update-slice_fusion.16, bf16[2048,2048]{1,0:T(8,128)(2,1)} %all-gather.8.cloned.1.call-done), kind=kOutput, calls=%fused_computation.5 | convolution fusion | flops 7525367808 | bytes 23080448 | tf_op jit(solution)/shard_map/dot_general | solution.py:29
  243.4 11.4 %convolution_convert_fusion.2 = bf16[2048,2048]{1,0:T(8,128)(2,1)} fusion(bf16[896,2048]{1,0:T(8,128)(2,1)S(1)} %get-tuple-element.143, bf16[224,2048]{1,0:T(8,128)(2,1)S(1)} %copy-done.23, bf16[224,2048]{1,0:T(8,128)(2,1)S(1)} %copy-done.25, bf16[224,2048]{1,0:T(8,128)(2,1)S(1)} %copy-done.21, bf16[224,2048]{1,0:T(8,128)(2,1)S(1)} %get-tuple-element.212), kind=kOutput, calls=%fused_computation.4 | convolution fusion | flops 7535067136 | bytes 15728640 | tf_op jit(solution)/shard_map/dot_general | solution.py:33
  259.8 23.8 %all-gather.10.cloned.1.call-done = bf16[2048,2048]{1,0:T(8,128)(2,1)} async-done(((bf16[2048,256]{1,0:T(8,128)(2,1)}), bf16[2048,2048]{1,0:T(8,128)(2,1)}) %all-gather.10.cloned.1.call-update) | async-done | bytes 8388624 | tf_op jit(solution)/shard_map/all_gather | solution.py:590
  283.7 13.4 %fusion.3 = bf16[896,2048]{1,0:T(8,128)(2,1)S(1)} fusion(f32[896,2048]{1,0:T(8,128)} %get-tuple-element.127, s32[2048]{0:T(1024)S(1)} %iota_add_fusion, s32[896]{0:T(1024)S(1)} %add_multiply_fusion, bf16[896,2048]{1,0:T(8,128)(2,1)} %pad_maximum_fusion, bf16[2048,2048]{1,0:T(8,128)(2,1)} %all-gather.10.cloned.1.call-done), kind=kOutput, calls=%fused_computation.8 | convolution fusion | flops 7529037824 | bytes 23080448 | tf_op jit(solution)/shard_map/dot_general | solution.py:33
  297.1 8.5 %convolution_convert_fusion.9 = bf16[224,2048]{1,0:T(8,128)(2,1)} fusion(bf16[2048,2048]{1,0:T(8,128)(2,1)} %all-gather.8.cloned.1.call-done, bf16[896,2048]{1,0:T(8,128)(2,1)S(1)} %fusion.3), kind=kOutput, calls=%fused_computation.41 | convolution fusion | flops 1879506944 | bytes 10223616 | tf_op jit(solution)/shard_map/dot_general | solution.py:33
  320.0 13.4 %convolution_convert_fusion.1 = bf16[2048,2048]{1,0:T(8,128)(2,1)} fusion(bf16[896,2048]{1,0:T(8,128)(2,1)} %constant_dynamic-update-slice_fusion.16, bf16[896,2048]{1,0:T(8,128)(2,1)S(1)} %fusion.3), kind=kOutput, calls=%fused_computation.3 | convolution fusion | flops 7520387072 | bytes 15728640 | tf_op jit(solution)/shard_map/dot_general | solution.py:33
  333.4 7.7 fusion.56
  341.1 15.3 %collective-permute-done.20 = bf16[224,2048]{1,0:T(8,128)(2,1)} collective-permute-done((bf16[224,2048]{1,0:T(8,128)(2,1)}, bf16[224,2048]{1,0:T(8,128)(2,1)}, u32[]{:S(2)}, u32[]{:S(2)}) %collective-permute-start.20) | collective-permute-done | bytes 917536 | tf_op jit(solution)/shard_map/ppermute | solution.py:55
  391.8 8.8 %collective-permute-done.25.refs_9_ = bf16[7,128,128]{2,1,0:T(8,128)(2,1)S(1)} collective-permute-done((bf16[7,128,128]{2,1,0:T(8,128)(2,1)S(1)}, bf16[7,128,128]{2,1,0:T(8,128)(2,1)S(1)}, u32[]{:S(2)}, u32[]{:S(2)}) %collective-permute-start.25) | collective-permute-done | bytes 229408 | tf_op jit(solution)/shard_map/ppermute | solution.py:506
  400.6 7.6 collective-permute-done.26.refs_10_
  415.9 21.1 %attend_backward.1 = (bf16[7,128,384]{2,1,0:T(8,128)(2,1)}, bf16[7,128,384]{2,1,0:T(8,128)(2,1)}, bf16[7,128,384]{2,1,0:T(8,128)(2,1)}, bf16[7,128,384]{2,1,0:T(8,128)(2,1)}, bf16[4,7,128,384]{3,2,1,0:T(8,128)(2,1)}) custom-call(s32[7]{0:T(128)} %copy-done.13, bf16[7,128,384]{2,1,0:T(8,128)(2,1)} %copy-done.15, ...), custom_call_target="tpu_custom_call" | custom-call | flops 10000000000 | bytes 12582912 | tf_op jit(solution)/shard_map/attend_backward/pallas_call | solution.py:311
  458.2 11.5 %collective-permute-done.34 = bf16[224,2048]{1,0:T(8,128)(2,1)S(1)} collective-permute-done((bf16[224,2048]{1,0:T(8,128)(2,1)S(1)}, bf16[224,2048]{1,0:T(8,128)(2,1)S(1)}, u32[]{:S(2)}, u32[]{:S(2)}) %collective-permute-start.34) | collective-permute-done | bytes 917536 | tf_op jit(solution)/shard_map/ppermute | solution.py:55
  472.0 16.8 %collective-permute-done.35 = bf16[224,2048]{1,0:T(8,128)(2,1)S(1)} collective-permute-done((bf16[224,2048]{1,0:T(8,128)(2,1)S(1)}, bf16[224,2048]{1,0:T(8,128)(2,1)S(1)}, u32[]{:S(2)}, u32[]{:S(2)}) %collective-permute-start.35) | collective-permute-done | bytes 917536 | tf_op jit(solution)/shard_map/ppermute | solution.py:55
  492.4 12.2 %collective-permute-done.31.refs_1_ = bf16[7,128,384]{2,1,0:T(8,128)(2,1)S(1)} collective-permute-done((bf16[7,128,384]{2,1,0:T(8,128)(2,1)}, bf16[7,128,384]{2,1,0:T(8,128)(2,1)S(1)}, u32[]{:S(2)}, u32[]{:S(2)}) %collective-permute-start.31) | collective-permute-done | bytes 688160 | tf_op jit(solution)/shard_map/ppermute | solution.py:506
  505.4 16.3 %collective-permute-done.32.refs_2_ = bf16[7,128,384]{2,1,0:T(8,128)(2,1)S(1)} collective-permute-done((bf16[7,128,384]{2,1,0:T(8,128)(2,1)}, bf16[7,128,384]{2,1,0:T(8,128)(2,1)S(1)}, u32[]{:S(2)}, u32[]{:S(2)}) %collective-permute-start.32) | collective-permute-done | bytes 688160 | tf_op jit(solution)/shard_map/ppermute | solution.py:506
  531.5 8.9 %convolution_convert_fusion = bf16[2048,1536]{1,0:T(8,128)(2,1)} fusion(bf16[896,2048]{1,0:T(8,128)(2,1)S(1)} %copy-done.57, bf16[896,1536]{1,0:T(8,128)(2,1)S(1)} %gather_grads.1), kind=kOutput, calls=%fused_computation.2 | convolution fusion | flops 5640290304 | bytes 12713984 | tf_op jit(solution)/shard_map/dot_general | solution.py:33
  571.4 19.6 %collective-permute-done.39 = bf16[224,2048]{1,0:T(8,128)(2,1)} collective-permute-done((bf16[224,2048]{1,0:T(8,128)(2,1)S(1)}, bf16[224,2048]{1,0:T(8,128)(2,1)}, u32[]{:S(2)}, u32[]{:S(2)}) %collective-permute-start.39) | collective-permute-done | bytes 917536 | tf_op jit(solution)/shard_map/ppermute | solution.py:55
  591.0 16.9 %collective-permute-done.38 = bf16[224,2048]{1,0:T(8,128)(2,1)} collective-permute-done((bf16[224,2048]{1,0:T(8,128)(2,1)S(1)}, bf16[224,2048]{1,0:T(8,128)(2,1)}, u32[]{:S(2)}, u32[]{:S(2)}) %collective-permute-start.38) | collective-permute-done | bytes 917536 | tf_op jit(solution)/shard_map/ppermute | solution.py:55
  608.0 56.6 %reduce-scatter.9.cloned.1.call-done = bf16[256,1536]{1,0:T(8,128)(2,1)} async-done(((bf16[2048,1536]{1,0:T(8,128)(2,1)}), bf16[256,1536]{1,0:T(8,128)(2,1)}) %reduce-scatter.9.cloned.1.call-update) | async-done | bytes 786448 | tf_op jit(solution)/shard_map/reduce_scatter | solution.py:725
  685.8 7.9 %collective-permute-done.44 = bf16[224,2048]{1,0:T(8,128)(2,1)S(1)} collective-permute-done((bf16[224,2048]{1,0:T(8,128)(2,1)S(1)}, bf16[224,2048]{1,0:T(8,128)(2,1)S(1)}, u32[]{:S(2)}, u32[]{:S(2)}) %collective-permute-start.44) | collective-permute-done | bytes 917536 | tf_op jit(solution)/shard_map/ppermute | solution.py:55
  693.8 21.1 %collective-permute-done.45 = bf16[224,2048]{1,0:T(8,128)(2,1)S(1)} collective-permute-done((bf16[224,2048]{1,0:T(8,128)(2,1)S(1)}, bf16[224,2048]{1,0:T(8,128)(2,1)S(1)}, u32[]{:S(2)}, u32[]{:S(2)}) %collective-permute-start.45) | collective-permute-done | bytes 917536 | tf_op jit(solution)/shard_map/ppermute | solution.py:55
  722.7 7.8 collective-permute-done.47
  749.8 8.8 %collective-permute-done.43 = bf16[224,2048]{1,0:T(8,128)(2,1)S(1)} collective-permute-done((bf16[224,2048]{1,0:T(8,128)(2,1)S(1)}, bf16[224,2048]{1,0:T(8,128)(2,1)S(1)}, u32[]{:S(2)}, u32[]{:S(2)}) %collective-permute-start.43) | collective-permute-done | bytes 917536 | tf_op jit(solution)/shard_map/ppermute | solution.py:55
  (349 shorter events, 264.3 us)
Async XLA Ops:
  7.2 162.5 %all-gather.6.cloned.1.call-start = ((), (), s32[]{:S(2)}) async-start(), calls=%async_computation.4 | async-start | bytes 10485760 | tf_op jit(solution)/shard_map/all_gather | solution.py:560
  7.9 220.2 %all-gather.8.cloned.1.call-start = ((), (), s32[]{:S(2)}) async-start(), calls=%async_computation.5 | async-start | bytes 9437184 | tf_op jit(solution)/shard_map/all_gather | solution.py:559
  8.7 275.0 %all-gather.10.cloned.1.call-start = ((), (), s32[]{:S(2)}) async-start(), calls=%async_computation.6 | async-start | bytes 9437184 | tf_op jit(solution)/shard_map/all_gather | solution.py:590
  9.4 531.0 %reduce-scatter.5.cloned.1.call-start = ((), (), s32[]{:S(2)}) async-start(), calls=%async_computation.7 | async-start | bytes 9437184 | tf_op jit(solution)/shard_map/reduce_scatter | solution.py:645
  31.8 48.8 %collective-permute-start.1 = (bf16[7,128,384]{2,1,0:T(8,128)(2,1)S(1)}, bf16[7,128,384]{2,1,0:T(8,128)(2,1)}, u32[]{:S(2)}, u32[]{:S(2)}) collective-permute-start(bf16[7,128,384]{2,1,0:T(8,128)(2,1)S(1)} %get-tuple-element.101), channel_id=1, source_target_pairs={{0,4},{1,5},{2,6},{3,7},{4,0},{5,1},{6,2},{7,3},{8,12},{9,13},{10,... | collective-permute-start | bytes 2064392 | tf_op jit(solution)/shard_map/ppermute | solution.py:506
  34.4 46.2 %collective-permute-start.2 = (bf16[7,128,384]{2,1,0:T(8,128)(2,1)S(1)}, bf16[7,128,384]{2,1,0:T(8,128)(2,1)}, u32[]{:S(2)}, u32[]{:S(2)}) collective-permute-start(bf16[7,128,384]{2,1,0:T(8,128)(2,1)S(1)} %get-tuple-element.102), channel_id=1, source_target_pairs={{0,6},{1,7},{2,4},{3,5},{4,2},{5,3},{6,0},{7,1},{8,14},{9,15},{10,... | collective-permute-start | bytes 2064392 | tf_op jit(solution)/shard_map/ppermute | solution.py:506
  34.4 49.6 %collective-permute-start.7 = (f32[5,2048]{1,0:T(8,128)S(1)}, f32[5,2048]{1,0:T(8,128)S(1)}, u32[]{:S(2)}, u32[]{:S(2)}) collective-permute-start(f32[5,2048]{1,0:T(8,128)S(1)} %bitcast.100), channel_id=1, source_target_pairs={{0,1},{1,0},{2,3},{3,2},{4,5},{5,4},{6,7},{7,6},{8,9},{9,8},{10,11... | collective-permute-start | bytes 122888 | tf_op jit(solution)/shard_map/ppermute | solution.py:55
  34.4 49.6 %collective-permute-start.3 = (bf16[7,128,384]{2,1,0:T(8,128)(2,1)S(1)}, bf16[7,128,384]{2,1,0:T(8,128)(2,1)}, u32[]{:S(2)}, u32[]{:S(2)}) collective-permute-start(bf16[7,128,384]{2,1,0:T(8,128)(2,1)S(1)} %get-tuple-element.104.refs_0_), channel_id=1, source_target_pairs={{1,0},{0,1},{3,2},{2,3},{5,4},{4,5},{7,6},{6,7},{9,8},{8,9},{11,10... | collective-permute-start | bytes 2064392 | tf_op jit(solution)/shard_map/ppermute | solution.py:518
  101.2 38.6 %collective-permute-start.10 = (bf16[7,128,128]{2,1,0:T(8,128)(2,1)}, bf16[7,128,128]{2,1,0:T(8,128)(2,1)S(1)}, u32[]{:S(2)}, u32[]{:S(2)}) collective-permute-start(bf16[7,128,128]{2,1,0:T(8,128)(2,1)} %get-tuple-element.115), channel_id=1, source_target_pairs={{0,6},{1,7},{2,4},{3,5},{4,2},{5,3},{6,0},{7,1},{8,14},{9,15},{10,... | collective-permute-start | bytes 688136 | tf_op jit(solution)/shard_map/ppermute | solution.py:506
  116.2 37.5 %collective-permute-start.9 = (bf16[7,128,128]{2,1,0:T(8,128)(2,1)}, bf16[7,128,128]{2,1,0:T(8,128)(2,1)S(1)}, u32[]{:S(2)}, u32[]{:S(2)}) collective-permute-start(bf16[7,128,128]{2,1,0:T(8,128)(2,1)} %get-tuple-element.114), channel_id=1, source_target_pairs={{0,4},{1,5},{2,6},{3,7},{4,0},{5,1},{6,2},{7,3},{8,12},{9,13},{10,... | collective-permute-start | bytes 688136 | tf_op jit(solution)/shard_map/ppermute | solution.py:506
  178.3 41.0 %collective-permute-start.16 = (bf16[224,2048]{1,0:T(8,128)(2,1)}, bf16[224,2048]{1,0:T(8,128)(2,1)}, u32[]{:S(2)}, u32[]{:S(2)}) collective-permute-start(bf16[224,2048]{1,0:T(8,128)(2,1)} %multiply_convert_fusion), channel_id=1, source_target_pairs={{0,16},{8,24},{16,0},{24,8},{1,17},{9,25},{17,1},{25,9},{2,18},{10... | collective-permute-start | bytes 2752520 | tf_op jit(solution)/shard_map/ppermute | solution.py:55
  179.3 40.1 %collective-permute-start.17 = (bf16[224,2048]{1,0:T(8,128)(2,1)}, bf16[224,2048]{1,0:T(8,128)(2,1)}, u32[]{:S(2)}, u32[]{:S(2)}) collective-permute-start(bf16[224,2048]{1,0:T(8,128)(2,1)} %multiply_convert_fusion), channel_id=1, source_target_pairs={{0,24},{8,16},{16,8},{24,0},{1,25},{9,17},{17,9},{25,1},{2,26},{10... | collective-permute-start | bytes 2752520 | tf_op jit(solution)/shard_map/ppermute | solution.py:55
  254.8 285.6 %reduce-scatter.7.cloned.1.call-start = ((), (), s32[]{:S(2)}) async-start(), calls=%async_computation.8 | async-start | bytes 9437184 | tf_op jit(solution)/shard_map/reduce_scatter | solution.py:674
  314.1 42.2 %collective-permute-start.20 = (bf16[224,2048]{1,0:T(8,128)(2,1)}, bf16[224,2048]{1,0:T(8,128)(2,1)}, u32[]{:S(2)}, u32[]{:S(2)}) collective-permute-start(bf16[224,2048]{1,0:T(8,128)(2,1)} %convolution_convert_fusion.8), channel_id=1, source_target_pairs={{0,16},{8,24},{16,0},{24,8},{1,17},{9,25},{17,1},{25,9},{2,18},{10... | collective-permute-start | bytes 2752520 | tf_op jit(solution)/shard_map/ppermute | solution.py:55
  319.1 37.2 %collective-permute-start.21 = (bf16[224,2048]{1,0:T(8,128)(2,1)}, bf16[224,2048]{1,0:T(8,128)(2,1)}, u32[]{:S(2)}, u32[]{:S(2)}) collective-permute-start(bf16[224,2048]{1,0:T(8,128)(2,1)} %convolution_convert_fusion.7), channel_id=1, source_target_pairs={{0,24},{8,16},{16,8},{24,0},{1,25},{9,17},{17,9},{25,1},{2,26},{10... | collective-permute-start | bytes 2752520 | tf_op jit(solution)/shard_map/ppermute | solution.py:55
  356.3 251.6 %reduce-scatter.11.cloned.1.call-start = ((), (), s32[]{:S(2)}) async-start(), calls=%async_computation.10 | async-start | bytes 2359296 | tf_op jit(solution)/shard_map/reduce_scatter | solution.py:725
  374.4 62.6 %collective-permute-start.28 = (bf16[224,2048]{1,0:T(8,128)(2,1)S(1)}, bf16[224,2048]{1,0:T(8,128)(2,1)S(1)}, u32[]{:S(2)}, u32[]{:S(2)}) collective-permute-start(bf16[224,2048]{1,0:T(8,128)(2,1)S(1)} %convolution_convert_fusion.5), channel_id=1, source_target_pairs={{0,8},{8,0},{16,24},{24,16},{1,9},{9,1},{17,25},{25,17},{2,10},{10... | collective-permute-start | bytes 2752520 | tf_op jit(solution)/shard_map/ppermute | solution.py:55
  377.2 59.8 %collective-permute-start.29 = (bf16[224,2048]{1,0:T(8,128)(2,1)S(1)}, bf16[224,2048]{1,0:T(8,128)(2,1)S(1)}, u32[]{:S(2)}, u32[]{:S(2)}) collective-permute-start(bf16[224,2048]{1,0:T(8,128)(2,1)S(1)} %convolution_convert_fusion.4), channel_id=1, source_target_pairs={{0,16},{8,24},{16,0},{24,8},{1,17},{9,25},{17,1},{25,9},{2,18},{10... | collective-permute-start | bytes 2752520 | tf_op jit(solution)/shard_map/ppermute | solution.py:55
  446.5 42.2 %collective-permute-start.35 = (bf16[224,2048]{1,0:T(8,128)(2,1)S(1)}, bf16[224,2048]{1,0:T(8,128)(2,1)S(1)}, u32[]{:S(2)}, u32[]{:S(2)}) collective-permute-start(bf16[224,2048]{1,0:T(8,128)(2,1)S(1)} %copy-done.34), channel_id=1, source_target_pairs={{0,16},{8,24},{16,0},{24,8},{1,17},{9,25},{17,1},{25,9},{2,18},{10... | collective-permute-start | bytes 2752520 | tf_op jit(solution)/shard_map/ppermute | solution.py:55
  448.4 40.4 %collective-permute-start.36 = (bf16[224,2048]{1,0:T(8,128)(2,1)S(1)}, bf16[224,2048]{1,0:T(8,128)(2,1)S(1)}, u32[]{:S(2)}, u32[]{:S(2)}) collective-permute-start(bf16[224,2048]{1,0:T(8,128)(2,1)S(1)} %copy-done.34), channel_id=1, source_target_pairs={{0,24},{8,16},{16,8},{24,0},{1,25},{9,17},{17,9},{25,1},{2,26},{10... | collective-permute-start | bytes 2752520 | tf_op jit(solution)/shard_map/ppermute | solution.py:55
  450.0 54.5 %collective-permute-start.31 = (bf16[7,128,384]{2,1,0:T(8,128)(2,1)}, bf16[7,128,384]{2,1,0:T(8,128)(2,1)S(1)}, u32[]{:S(2)}, u32[]{:S(2)}) collective-permute-start(bf16[7,128,384]{2,1,0:T(8,128)(2,1)} %get-tuple-element.150), channel_id=1, source_target_pairs={{0,2},{1,3},{2,0},{3,1},{4,6},{5,7},{6,4},{7,5},{8,10},{9,11},{10,... | collective-permute-start | bytes 2064392 | tf_op jit(solution)/shard_map/ppermute | solution.py:506
  457.7 64.0 %collective-permute-start.32 = (bf16[7,128,384]{2,1,0:T(8,128)(2,1)}, bf16[7,128,384]{2,1,0:T(8,128)(2,1)S(1)}, u32[]{:S(2)}, u32[]{:S(2)}) collective-permute-start(bf16[7,128,384]{2,1,0:T(8,128)(2,1)} %get-tuple-element.151), channel_id=1, source_target_pairs={{0,4},{1,5},{2,6},{3,7},{4,0},{5,1},{6,2},{7,3},{8,12},{9,13},{10,... | collective-permute-start | bytes 2064392 | tf_op jit(solution)/shard_map/ppermute | solution.py:506
  469.8 52.8 %collective-permute-start.33 = (bf16[7,128,384]{2,1,0:T(8,128)(2,1)S(1)}, bf16[7,128,384]{2,1,0:T(8,128)(2,1)S(1)}, u32[]{:S(2)}, u32[]{:S(2)}) collective-permute-start(bf16[7,128,384]{2,1,0:T(8,128)(2,1)S(1)} %get-tuple-element.152), channel_id=1, source_target_pairs={{0,6},{1,7},{2,4},{3,5},{4,2},{5,3},{6,0},{7,1},{8,14},{9,15},{10,... | collective-permute-start | bytes 2064392 | tf_op jit(solution)/shard_map/ppermute | solution.py:506
  540.5 124.1 %reduce-scatter.9.cloned.1.call-start = ((), (), s32[]{:S(2)}) async-start(), calls=%async_computation.9 | async-start | bytes 7077888 | tf_op jit(solution)/shard_map/reduce_scatter | solution.py:725
  541.2 218.4 %all-gather.14.cloned.1.call-start = ((), (), s32[]{:S(2)}) async-start(), calls=%async_computation.12 | async-start | bytes 2359296 | tf_op jit(solution)/shard_map/all_gather | solution.py:744
  561.6 46.4 %collective-permute-start.38 = (bf16[224,2048]{1,0:T(8,128)(2,1)S(1)}, bf16[224,2048]{1,0:T(8,128)(2,1)}, u32[]{:S(2)}, u32[]{:S(2)}) collective-permute-start(bf16[224,2048]{1,0:T(8,128)(2,1)S(1)} %fusion.16), channel_id=1, source_target_pairs={{0,16},{8,24},{16,0},{24,8},{1,17},{9,25},{17,1},{25,9},{2,18},{10... | collective-permute-start | bytes 2752520 | tf_op jit(solution)/shard_map/ppermute | solution.py:55
  564.0 43.9 %collective-permute-start.37 = (bf16[224,2048]{1,0:T(8,128)(2,1)S(1)}, bf16[224,2048]{1,0:T(8,128)(2,1)}, u32[]{:S(2)}, u32[]{:S(2)}) collective-permute-start(bf16[224,2048]{1,0:T(8,128)(2,1)S(1)} %fusion.15), channel_id=1, source_target_pairs={{0,8},{8,0},{16,24},{24,16},{1,9},{9,1},{17,25},{25,17},{2,10},{10... | collective-permute-start | bytes 2752520 | tf_op jit(solution)/shard_map/ppermute | solution.py:55
  664.6 99.2 %all-gather.12.cloned.1.call-start = ((), (), s32[]{:S(2)}) async-start(), calls=%async_computation.11 | async-start | bytes 7077888 | tf_op jit(solution)/shard_map/all_gather | solution.py:744
  672.0 42.9 %collective-permute-start.45 = (bf16[224,2048]{1,0:T(8,128)(2,1)S(1)}, bf16[224,2048]{1,0:T(8,128)(2,1)S(1)}, u32[]{:S(2)}, u32[]{:S(2)}) collective-permute-start(bf16[224,2048]{1,0:T(8,128)(2,1)S(1)} %add_convert_fusion), channel_id=1, source_target_pairs={{0,16},{8,24},{16,0},{24,8},{1,17},{9,25},{17,1},{25,9},{2,18},{10... | collective-permute-start | bytes 2752520 | tf_op jit(solution)/shard_map/ppermute | solution.py:55
  673.5 41.4 %collective-permute-start.46 = (bf16[224,2048]{1,0:T(8,128)(2,1)S(1)}, bf16[224,2048]{1,0:T(8,128)(2,1)S(1)}, u32[]{:S(2)}, u32[]{:S(2)}) collective-permute-start(bf16[224,2048]{1,0:T(8,128)(2,1)S(1)} %add_convert_fusion), channel_id=1, source_target_pairs={{0,24},{8,16},{16,8},{24,0},{1,25},{9,17},{17,9},{25,1},{2,26},{10... | collective-permute-start | bytes 2752520 | tf_op jit(solution)/shard_map/ppermute | solution.py:55
  682.9 53.0 %collective-permute-start.41 = (bf16[224,2048]{1,0:T(8,128)(2,1)S(1)}, bf16[224,2048]{1,0:T(8,128)(2,1)S(1)}, u32[]{:S(2)}, u32[]{:S(2)}) collective-permute-start(bf16[224,2048]{1,0:T(8,128)(2,1)S(1)} %get-tuple-element.201), channel_id=1, source_target_pairs={{0,8},{8,0},{16,24},{24,16},{1,9},{9,1},{17,25},{25,17},{2,10},{10... | collective-permute-start | bytes 2752520 | tf_op jit(solution)/shard_map/ppermute | solution.py:55
  684.3 60.1 %collective-permute-start.42 = (bf16[224,2048]{1,0:T(8,128)(2,1)S(1)}, bf16[224,2048]{1,0:T(8,128)(2,1)S(1)}, u32[]{:S(2)}, u32[]{:S(2)}) collective-permute-start(bf16[224,2048]{1,0:T(8,128)(2,1)S(1)} %get-tuple-element.201), channel_id=1, source_target_pairs={{0,16},{8,24},{16,0},{24,8},{1,17},{9,25},{17,1},{25,9},{2,18},{10... | collective-permute-start | bytes 2752520 | tf_op jit(solution)/shard_map/ppermute | solution.py:55
  (93 other events, 1736.0 us)
Sparse Core Ops, SparseCore 0:
  9.9 90.1 all-gather.5
  101.7 99.3 all-gather.7
  202.7 80.8 all-gather.9
  285.8 87.6 reduce-scatter.4
  376.3 118.3 reduce-scatter.6
  540.6 52.7 reduce-scatter.10
  596.2 68.2 reduce-scatter.8
  666.1 27.5 all-gather.13
  695.4 64.6 all-gather.11

commit v4 on v3

--- a/solution.py
+++ b/solution.py
@@ -557,7 +557,7 @@
         return full
 
     full_up = lax.all_gather(w_up, "seq", axis=0, tiled=True)
-    full_out = lax.all_gather(w_out, "heads", axis=0, tiled=True)
+    out_slots = gather_heads(w_out)
 
     column = jnp.arange(rows)
     is_short = column < short_rows
@@ -604,9 +604,10 @@
         return values
 
     pooled = hop(pooled[:SEQS], hops[:-2])
-    slots, other_slots, hat_own, inverse_own, pooled = lax.optimization_barrier(
-        (slots, other_slots, hat_own, inverse_own, pooled)
-    )
+    slots, other_slots, out_slots[:-1], hat_own, inverse_own, pooled = lax.optimization_barrier(
+        (slots, other_slots, out_slots[:-1], hat_own, inverse_own, pooled)
+    )
+    full_out = jnp.concatenate(out_slots, axis=0)
     pooled = hop(pooled, hops[-2:-1])
     mixed_slots, logs = attend_forward(scal, slots, other_slots, heads, members)
     mixed_slots = [across(v, slot) if slot else v for slot, v in enumerate(mixed_slots)]
@@ -616,10 +617,8 @@
     heads_out = placed(mixed_slots, place, 1)
 
     heads_rel = [own_rows(heads_out, slot) for slot in range(head_count)]
-    heads_own = placed(
-        [heads_rel[0]] + [swap(heads_rel[slot], slot) for slot in range(1, head_count)],
-        head_rank,
-        1,
+    heads_own = jnp.concatenate(
+        [heads_rel[0]] + [swap(heads_rel[slot], slot) for slot in range(1, head_count)], axis=1
     )
     hidden = tokens_own + dot(heads_own, full_out)
     hat_two, inverse_two = normalize_parts(hidden)
@@ -679,14 +678,15 @@
     grad_attn_own = grad_hidden.astype(bf16)
     grad_mixed = contract(grad_attn_own, full_out, 1, 1).astype(bf16)
     grad_mixed = [
-        lax.dynamic_slice_in_dim(grad_mixed, (head_rank ^ slot) * head_width, head_width, 1)
-        for slot in range(head_count)
+        grad_mixed[:, slot * head_width : (slot + 1) * head_width] for slot in range(head_count)
     ]
     active, grad_mixed = lax.optimization_barrier((active, grad_mixed))
     grad_mixed = [grad_mixed[0]] + [
         swap(grad_mixed[slot], slot) for slot in range(1, head_count)
     ]
     grad_heads = placed(grad_mixed, head_rank, 0)
+    grad_heads, grad_attn_own = lax.optimization_barrier((grad_heads, grad_attn_own))
+    grad_attn = gather_heads(grad_attn_own)
     grad_slots = []
     for slot in range(heads):
         piece = lax.dynamic_slice_in_dim(grad_heads, (place ^ slot) * HD, HD, 1)
@@ -695,13 +695,14 @@
     ffn_parts = [
         dot(active[slot * share : (slot + 1) * share], full_down) for slot in range(head_count)
     ]
-    ffn_parts = scatter_heads(ffn_parts)
+    ffn_parts[1:] = [v.astype(bf16) for v in ffn_parts[1:]]
+    grad_slots, ffn_parts = lax.optimization_barrier((grad_slots, ffn_parts))
 
     own_grads, other_grads = attend_backward(
         scal, slots, other_slots, grad_slots, logs, heads, members
     )
-    own_grads, other_grads, ffn_parts[:-1] = lax.optimization_barrier(
-        (own_grads, other_grads, ffn_parts[:-1])
+    own_grads, other_grads, grad_attn[:-1] = lax.optimization_barrier(
+        (own_grads, other_grads, grad_attn[:-1])
     )
     other_grads = [
         among(v, members - step) for step, v in zip(range(1, members), other_grads)
@@ -710,21 +711,21 @@
     for slot in range(heads):
         total = own_grads[slot].astype(f32)
         sums.append(sum([v[slot].astype(f32) for v in other_grads], total).astype(bf16))
-    sums, grad_attn_own = lax.optimization_barrier((sums, grad_attn_own))
+    sums, ffn_parts = lax.optimization_barrier((sums, ffn_parts))
     sums = exchange(sums)
-    grad_attn = gather_heads(grad_attn_own)
+    ffn_parts = scatter_heads(ffn_parts)
     grad_attn = jnp.concatenate(grad_attn, axis=0)
     grad_out_part = contract(jnp.concatenate(heads_rel, axis=0), grad_attn, 0, 0).astype(bf16)
-    sums, grad_out_part = lax.optimization_barrier((sums, grad_out_part))
+    grad_out_part, grad_down, grad_up, sums, ffn_parts[:-1] = lax.optimization_barrier(
+        (grad_out_part, grad_down, grad_up, sums, ffn_parts[:-1])
+    )
+    total_out = lax.psum_scatter(grad_out_part, "seq", scatter_dimension=0, tiled=True)
     grad_projected = gather_grads(scal, cosine, -sine, sums)
     grad_qkv_part = contract(normed_low, grad_projected, 0, 0).astype(bf16)
-    grad_projected, grad_qkv_part, grad_out_part, grad_down, grad_up = lax.optimization_barrier(
-        (grad_projected, grad_qkv_part, grad_out_part, grad_down, grad_up)
-    )
-    totals = [
-        lax.psum_scatter(v, "seq", scatter_dimension=0, tiled=True)
-        for v in (grad_qkv_part, grad_out_part)
-    ]
+    grad_projected, grad_qkv_part, total_out, ffn_parts = lax.optimization_barrier(
+        (grad_projected, grad_qkv_part, total_out, ffn_parts)
+    )
+    total_qkv = lax.psum_scatter(grad_qkv_part, "seq", scatter_dimension=0, tiled=True)
     grad_down, grad_up = grad_down.astype(f32), grad_up.astype(f32)
     one_parts = scatter_heads(
         [
@@ -740,8 +741,8 @@
             for slot in range(head_count)
         ]
     )
-    one_parts, totals, ffn_parts = lax.optimization_barrier((one_parts, totals, ffn_parts))
-    totals = [lax.all_gather(v, "seq", axis=0, tiled=True) for v in totals]
+    one_parts, total_qkv = lax.optimization_barrier((one_parts, total_qkv))
+    totals = [lax.all_gather(v, "seq", axis=0, tiled=True) for v in (total_qkv, total_out)]
     grad_qkv = jnp.stack(
         [
             totals[0][:, part * head_width : (part + 1) * head_width].astype(f32)

time: 788 us -> 808 us (1.025)
  starting transfers between devices: 77.6 us -> 128 us
  waiting for transfers between devices: 403 us -> 371 us
    ppermute x12, waiting for transfers between devices: 109 us -> 153 us  [across(): return lax.ppermute(values, 'seq', pairs)]
    ppermute x35 -> x38, waiting for transfers between devices: 205 us -> 162 us  [flip(): return lax.ppermute(values, axis, [(i, i ^ bit) for i in range(size)])]
    ppermute x12, starting transfers between devices: 35.7 us -> 68.3 us  [across(): return lax.ppermute(values, 'seq', pairs)]
    all_gather x1, waiting for transfers between devices: 23.8 us -> 0.01 us  [local(): full_down = lax.all_gather(w_down, 'seq', axis=1, tiled=True)]
    ppermute x35 -> x38, starting transfers between devices: 39.9 us -> 58.6 us  [flip(): return lax.ppermute(values, axis, [(i, i ^ bit) for i in range(size)])]
    unnamed x131 -> x136, local copies, waits for them, and re-layouts: 20.2 us -> 21.8 us
  transfers between devices with their start and end apart: 61 -> 63, of which waited for: 31 -> 28; matrix products, arithmetic and copies ran while one was open for 26% -> 26% of each run, Pallas kernels for 7% -> 7%
where the time goes in v4:
time: 808 us; the launch traced here: 798 us
  waiting for transfers between devices  371 us (46%)
  matrix products  138 us (17%)
  starting transfers between devices  128 us (16%)
  Pallas kernels  55.7 us (7%)
  other arithmetic  48.4 us (6%)
  local copies, waits for them, and re-layouts  41.1 us (5%)
  between operations  15.6 us (2%)
    ppermute x38, waiting for transfers between devices, flip(): return lax.ppermute(values, axis, [(i, i ^ bit) for i in range(size)])  162 us
    ppermute x12, waiting for transfers between devices, across(): return lax.ppermute(values, 'seq', pairs)  153 us
    dot_general x22, matrix products, contract(): lax.dot_general(left, right, (((left_dim,), (right_dim,)), ((), ())), pre...  105 us
    ppermute x12, starting transfers between devices, across(): return lax.ppermute(values, 'seq', pairs)  68.3 us
    ppermute x38, starting transfers between devices, flip(): return lax.ppermute(values, axis, [(i, i ^ bit) for i in range(size)])  58.6 us
    reduce_scatter x1, waiting for transfers between devices, local(): lax.psum_scatter(grad_out_part, 'seq', scatter_dimension=0, tiled=True)  29 us
    dot_general x6, matrix products, dot(): return jnp.dot(left, right, preferred_element_type=f32)  29 us
    unnamed x136, local copies, waits for them, and re-layouts  21.8 us
  transfers between devices with their start and end apart: 63, of which 28 were waited for; matrix products, arithmetic and copies ran while one was open for 26% of the time, Pallas kernels for 7%

profile of v4, /device:TPU:0, one launch (start us, length us, event | category | flops | bytes accessed | tf_op | source)
XLA Modules:
  0.0 798.0 jit_solution(8655070946585262483)
XLA Ops:
  12.4 16.2 %project.1 = (bf16[7,128,384]{2,1,0:T(8,128)(2,1)S(1)}, bf16[7,128,384]{2,1,0:T(8,128)(2,1)S(1)}, bf16[7,128,384]{2,1,0:T(8,128)(2,1)S(1)}, bf16[7,128,384]{2,1,...) custom-call(s32[7]{0:T(128)S(1)} %pad_add_fusion.scal, bf16[896,2048]{1,0:T(8,128)(2,1)} %tokens.1, ...), custom_call_target="tpu_custom_call" | custom-call | flops 5637144576 | bytes 16777216 | tf_op jit(solution)/shard_map/project/pallas_call | solution.py:402
  38.8 55.2 %collective-permute-done.refs_1_ = bf16[7,128,384]{2,1,0:T(8,128)(2,1)S(1)} collective-permute-done((bf16[7,128,384]{2,1,0:T(8,128)(2,1)S(1)}, bf16[7,128,384]{2,1,0:T(8,128)(2,1)S(1)}, u32[]{:S(2)}, u32[]{:S(2)}) %collective-permute-start) | collective-permute-done | bytes 688160 | tf_op jit(solution)/shard_map/ppermute | solution.py:506
  97.8 8.1 %collective-permute-done.1.refs_2_ = bf16[7,128,384]{2,1,0:T(8,128)(2,1)} collective-permute-done((bf16[7,128,384]{2,1,0:T(8,128)(2,1)S(1)}, bf16[7,128,384]{2,1,0:T(8,128)(2,1)}, u32[]{:S(2)}, u32[]{:S(2)}) %collective-permute-start.1) | collective-permute-done | bytes 688160 | tf_op jit(solution)/shard_map/ppermute | solution.py:506
  105.9 18.1 %collective-permute-done.2.refs_3_ = bf16[7,128,384]{2,1,0:T(8,128)(2,1)} collective-permute-done((bf16[7,128,384]{2,1,0:T(8,128)(2,1)S(1)}, bf16[7,128,384]{2,1,0:T(8,128)(2,1)}, u32[]{:S(2)}, u32[]{:S(2)}) %collective-permute-start.2) | collective-permute-done | bytes 688160 | tf_op jit(solution)/shard_map/ppermute | solution.py:506
  130.0 15.7 %attend_forward.1 = (bf16[7,128,128]{2,1,0:T(8,128)(2,1)}, bf16[7,128,128]{2,1,0:T(8,128)(2,1)}, bf16[7,128,128]{2,1,0:T(8,128)(2,1)}, bf16[7,128,128]{2,1,0:T(8,128)(2,1)}, f32[4,7,1,128]{3,2,1,0:T(1,128)}) custom-call(s32[7]{0:T(128)} %copy-done.13, bf16[7,128,384]{2,1,0:T(8,128)(2,1)} %copy-done.15, bf16[7,128,384]{2,1,0:T(8,128)(2,1)} %copy-done.50, ...), custom_call_target="tpu_custom_call" | custom-call | flops 4000000000 | bytes 7340032 | tf_op jit(solution)/shard_map/attend_forward/pallas_call | solution.py:185
  145.7 28.4 %collective-permute-start.10 = (bf16[7,128,128]{2,1,0:T(8,128)(2,1)}, bf16[7,128,128]{2,1,0:T(8,128)(2,1)S(1)}, u32[]{:S(2)}, u32[]{:S(2)}) collective-permute-start(bf16[7,128,128]{2,1,0:T(8,128)(2,1)} %get-tuple-element.131), channel_id=1, source_target_pairs={{0,2},{1,3},{2,0},{3,1},{4,6},{5,7},{6,4},{7,5},{8,10},{9,11},{10,... | collective-permute-start | bytes 688136 | tf_op jit(solution)/shard_map/ppermute | solution.py:506
  182.9 24.4 %collective-permute-done.13 = f32[5,2048]{1,0:T(8,128)S(1)} collective-permute-done((f32[5,2048]{1,0:T(8,128)S(1)}, f32[5,2048]{1,0:T(8,128)S(1)}, u32[]{:S(2)}, u32[]{:S(2)}) %collective-permute-start.13) | collective-permute-done | bytes 40992 | tf_op jit(solution)/shard_map/ppermute | solution.py:55
  232.8 11.7 %collective-permute-start.21 = (f32[5,2048]{1,0:T(8,128)S(1)}, f32[5,2048]{1,0:T(8,128)S(1)}, u32[]{:S(2)}, u32[]{:S(2)}) collective-permute-start(f32[5,2048]{1,0:T(8,128)S(1)} %add.291), channel_id=1, source_target_pairs={{0,4},{1,5},{2,6},{3,7},{4,0},{5,1},{6,2},{7,3},{8,12},{9,13},{10,... | collective-permute-start | bytes 122888 | tf_op jit(solution)/shard_map/ppermute | solution.py:55
  249.0 16.6 %collective-permute-done.20 = bf16[224,2048]{1,0:T(8,128)(2,1)} collective-permute-done((bf16[224,2048]{1,0:T(8,128)(2,1)}, bf16[224,2048]{1,0:T(8,128)(2,1)}, u32[]{:S(2)}, u32[]{:S(2)}) %collective-permute-start.20) | collective-permute-done | bytes 917536 | tf_op jit(solution)/shard_map/ppermute | solution.py:55
  274.4 13.3 %fusion = (bf16[896,2048]{1,0:T(8,128)(2,1)S(1)}, f32[896,2048]{1,0:T(8,128)}) fusion(s32[2048]{0:T(1024)S(1)} %iota_add_fusion, s32[896]{0:T(1024)S(1)} %add_multiply_fusion, bf16[896,2048]{1,0:T(8,128)(2,1)} %constant_dynamic-update-slice_fusion.4, bf16[2048,2048]{1,0:T(8,128)(2,1)} %all-gather.5.cloned.1.call-done), kind=kOutput, calls=%fused_computation.5 | convolution fusion | flops 7525367808 | bytes 23080448 | tf_op jit(solution)/shard_map/dot_general | solution.py:29
  289.6 11.4 %convolution_convert_fusion.2 = bf16[2048,2048]{1,0:T(8,128)(2,1)} fusion(bf16[896,2048]{1,0:T(8,128)(2,1)S(1)} %get-tuple-element.159, bf16[224,2048]{1,0:T(8,128)(2,1)S(1)} %copy-done.25, bf16[224,2048]{1,0:T(8,128)(2,1)S(1)} %copy-done.27, bf16[224,2048]{1,0:T(8,128)(2,1)S(1)} %copy-done.23, bf16[224,2048]{1,0:T(8,128)(2,1)S(1)} %get-tuple-element.246), kind=kOutput, calls=%fused_computation.4 | convolution fusion | flops 7535067136 | bytes 15728640 | tf_op jit(solution)/shard_map/dot_general | solution.py:33
  306.1 13.4 %fusion.3 = bf16[896,2048]{1,0:T(8,128)(2,1)S(1)} fusion(f32[896,2048]{1,0:T(8,128)} %get-tuple-element.148, s32[2048]{0:T(1024)S(1)} %iota_add_fusion, s32[896]{0:T(1024)S(1)} %add_multiply_fusion, bf16[896,2048]{1,0:T(8,128)(2,1)} %pad_maximum_fusion, bf16[2048,2048]{1,0:T(8,128)(2,1)} %all-gather.7.cloned.1.call-done), kind=kOutput, calls=%fused_computation.8 | convolution fusion | flops 7529037824 | bytes 23080448 | tf_op jit(solution)/shard_map/dot_general | solution.py:33
  319.5 8.3 %convolution_convert_fusion.9 = bf16[224,2048]{1,0:T(8,128)(2,1)} fusion(bf16[2048,2048]{1,0:T(8,128)(2,1)} %all-gather.5.cloned.1.call-done, bf16[896,2048]{1,0:T(8,128)(2,1)S(1)} %fusion.3), kind=kOutput, calls=%fused_computation.41 | convolution fusion | flops 1879506944 | bytes 10223616 | tf_op jit(solution)/shard_map/dot_general | solution.py:33
  328.5 7.4 convolution_convert_fusion.8
  342.0 13.5 %convolution_convert_fusion.1 = bf16[2048,2048]{1,0:T(8,128)(2,1)} fusion(bf16[896,2048]{1,0:T(8,128)(2,1)} %constant_dynamic-update-slice_fusion.4, bf16[896,2048]{1,0:T(8,128)(2,1)S(1)} %fusion.3), kind=kOutput, calls=%fused_computation.3 | convolution fusion | flops 7520387072 | bytes 15728640 | tf_op jit(solution)/shard_map/dot_general | solution.py:33
  355.6 7.7 fusion.56
  363.2 11.5 %collective-permute-done.23 = bf16[224,2048]{1,0:T(8,128)(2,1)} collective-permute-done((bf16[224,2048]{1,0:T(8,128)(2,1)}, bf16[224,2048]{1,0:T(8,128)(2,1)}, u32[]{:S(2)}, u32[]{:S(2)}) %collective-permute-start.23) | collective-permute-done | bytes 917536 | tf_op jit(solution)/shard_map/ppermute | solution.py:55
  401.5 14.6 %collective-permute-start.28 = (bf16[7,128,128]{2,1,0:T(8,128)(2,1)S(1)}, bf16[7,128,128]{2,1,0:T(8,128)(2,1)S(1)}, u32[]{:S(2)}, u32[]{:S(2)}) collective-permute-start(bf16[7,128,128]{2,1,0:T(8,128)(2,1)S(1)} %bitcast.111), channel_id=1, source_target_pairs={{0,2},{1,3},{2,0},{3,1},{4,6},{5,7},{6,4},{7,5},{8,10},{9,11},{10,... | collective-permute-start | bytes 688136 | tf_op jit(solution)/shard_map/ppermute | solution.py:506
  430.5 11.9 %collective-permute-done.29.refs_10_ = bf16[7,128,128]{2,1,0:T(8,128)(2,1)S(1)} collective-permute-done((bf16[7,128,128]{2,1,0:T(8,128)(2,1)S(1)}, bf16[7,128,128]{2,1,0:T(8,128)(2,1)S(1)}, u32[]{:S(2)}, u32[]{:S(2)}) %collective-permute-start.29) | collective-permute-done | bytes 229408 | tf_op jit(solution)/shard_map/ppermute | solution.py:506
  445.9 21.1 %attend_backward.1 = (bf16[7,128,384]{2,1,0:T(8,128)(2,1)}, bf16[7,128,384]{2,1,0:T(8,128)(2,1)}, bf16[7,128,384]{2,1,0:T(8,128)(2,1)}, bf16[7,128,384]{2,1,0:T(8,128)(2,1)}, bf16[4,7,128,384]{3,2,1,0:T(8,128)(2,1)}) custom-call(s32[7]{0:T(128)} %copy-done.13, bf16[7,128,384]{2,1,0:T(8,128)(2,1)} %copy-done.15, bf16[7,128,384]{2,1,0:T(8,128)(2,1)} %copy-done.50, ...), custom_call_target="tpu_custom_call" | custom-call | flops 10000000000 | bytes 12582912 | tf_op jit(solution)/shard_map/attend_backward/pallas_call | solution.py:311
  478.7 10.3 %collective-permute-start.35 = (bf16[7,128,384]{2,1,0:T(8,128)(2,1)}, bf16[7,128,384]{2,1,0:T(8,128)(2,1)S(1)}, u32[]{:S(2)}, u32[]{:S(2)}) collective-permute-start(bf16[7,128,384]{2,1,0:T(8,128)(2,1)} %get-tuple-element.186), channel_id=1, source_target_pairs={{0,2},{1,3},{2,0},{3,1},{4,6},{5,7},{6,4},{7,5},{8,10},{9,11},{10,... | collective-permute-start | bytes 2064392 | tf_op jit(solution)/shard_map/ppermute | solution.py:506
  501.3 30.0 %collective-permute-done.35.refs_1_ = bf16[7,128,384]{2,1,0:T(8,128)(2,1)S(1)} collective-permute-done((bf16[7,128,384]{2,1,0:T(8,128)(2,1)}, bf16[7,128,384]{2,1,0:T(8,128)(2,1)S(1)}, u32[]{:S(2)}, u32[]{:S(2)}) %collective-permute-start.35) | collective-permute-done | bytes 688160 | tf_op jit(solution)/shard_map/ppermute | solution.py:506
  531.3 20.2 %collective-permute-done.36.refs_2_ = bf16[7,128,384]{2,1,0:T(8,128)(2,1)S(1)} collective-permute-done((bf16[7,128,384]{2,1,0:T(8,128)(2,1)}, bf16[7,128,384]{2,1,0:T(8,128)(2,1)S(1)}, u32[]{:S(2)}, u32[]{:S(2)}) %collective-permute-start.36) | collective-permute-done | bytes 688160 | tf_op jit(solution)/shard_map/ppermute | solution.py:506
  561.8 8.7 %convolution_convert_fusion = bf16[2048,1536]{1,0:T(8,128)(2,1)} fusion(bf16[896,2048]{1,0:T(8,128)(2,1)S(1)} %copy-done.58, bf16[896,1536]{1,0:T(8,128)(2,1)S(1)} %gather_grads.1), kind=kOutput, calls=%fused_computation.2 | convolution fusion | flops 5640290304 | bytes 12713984 | tf_op jit(solution)/shard_map/dot_general | solution.py:33
  573.4 29.0 %reduce-scatter.9.cloned.1.call-done = bf16[64,2048]{1,0:T(8,128)(2,1)} async-done(((bf16[512,2048]{1,0:T(8,128)(2,1)}), bf16[64,2048]{1,0:T(8,128)(2,1)}) %reduce-scatter.9.cloned.1.call-update) | async-done | bytes 262160 | tf_op jit(solution)/shard_map/reduce_scatter | solution.py:722
  625.9 10.6 %collective-permute-done.46 = bf16[224,2048]{1,0:T(8,128)(2,1)} collective-permute-done((bf16[224,2048]{1,0:T(8,128)(2,1)S(1)}, bf16[224,2048]{1,0:T(8,128)(2,1)}, u32[]{:S(2)}, u32[]{:S(2)}) %collective-permute-start.46) | collective-permute-done | bytes 917536 | tf_op jit(solution)/shard_map/ppermute | solution.py:55
  636.5 15.4 %collective-permute-done.45 = bf16[224,2048]{1,0:T(8,128)(2,1)} collective-permute-done((bf16[224,2048]{1,0:T(8,128)(2,1)S(1)}, bf16[224,2048]{1,0:T(8,128)(2,1)}, u32[]{:S(2)}, u32[]{:S(2)}) %collective-permute-start.45) | collective-permute-done | bytes 917536 | tf_op jit(solution)/shard_map/ppermute | solution.py:55
  652.0 21.4 %reduce-scatter.11.cloned.1.call-done = bf16[256,1536]{1,0:T(8,128)(2,1)} async-done(((bf16[2048,1536]{1,0:T(8,128)(2,1)}), bf16[256,1536]{1,0:T(8,128)(2,1)}) %reduce-scatter.11.cloned.1.call-update) | async-done | bytes 786448 | tf_op jit(solution)/shard_map/reduce_scatter | solution.py:728
  689.3 13.2 %collective-permute-done.41 = bf16[224,2048]{1,0:T(8,128)(2,1)S(1)} collective-permute-done((bf16[224,2048]{1,0:T(8,128)(2,1)S(1)}, bf16[224,2048]{1,0:T(8,128)(2,1)S(1)}, u32[]{:S(2)}, u32[]{:S(2)}) %collective-permute-start.41) | collective-permute-done | bytes 917536 | tf_op jit(solution)/shard_map/ppermute | solution.py:55
  709.0 13.2 %collective-permute-done.47 = bf16[224,2048]{1,0:T(8,128)(2,1)S(1)} collective-permute-done((bf16[224,2048]{1,0:T(8,128)(2,1)S(1)}, bf16[224,2048]{1,0:T(8,128)(2,1)S(1)}, u32[]{:S(2)}, u32[]{:S(2)}) %collective-permute-start.47) | collective-permute-done | bytes 917536 | tf_op jit(solution)/shard_map/ppermute | solution.py:55
  722.1 21.1 %collective-permute-done.48 = bf16[224,2048]{1,0:T(8,128)(2,1)S(1)} collective-permute-done((bf16[224,2048]{1,0:T(8,128)(2,1)S(1)}, bf16[224,2048]{1,0:T(8,128)(2,1)S(1)}, u32[]{:S(2)}, u32[]{:S(2)}) %collective-permute-start.48) | collective-permute-done | bytes 917536 | tf_op jit(solution)/shard_map/ppermute | solution.py:55
  743.8 15.8 %collective-permute-done.43 = bf16[224,2048]{1,0:T(8,128)(2,1)S(1)} collective-permute-done((bf16[224,2048]{1,0:T(8,128)(2,1)S(1)}, bf16[224,2048]{1,0:T(8,128)(2,1)S(1)}, u32[]{:S(2)}, u32[]{:S(2)}) %collective-permute-start.43) | collective-permute-done | bytes 917536 | tf_op jit(solution)/shard_map/ppermute | solution.py:55
  (354 shorter events, 245.1 us)
Async XLA Ops:
  7.2 267.2 %all-gather.5.cloned.1.call-start = ((), (), s32[]{:S(2)}) async-start(), calls=%async_computation.4 | async-start | bytes 9437184 | tf_op jit(solution)/shard_map/all_gather | solution.py:559
  7.9 298.2 %all-gather.7.cloned.1.call-start = ((), (), s32[]{:S(2)}) async-start(), calls=%async_computation.5 | async-start | bytes 9437184 | tf_op jit(solution)/shard_map/all_gather | solution.py:590
  8.7 542.8 %reduce-scatter.5.cloned.1.call-start = ((), (), s32[]{:S(2)}) async-start(), calls=%async_computation.6 | async-start | bytes 9437184 | tf_op jit(solution)/shard_map/reduce_scatter | solution.py:644
  28.6 65.4 %collective-permute-start = (bf16[7,128,384]{2,1,0:T(8,128)(2,1)S(1)}, bf16[7,128,384]{2,1,0:T(8,128)(2,1)S(1)}, u32[]{:S(2)}, u32[]{:S(2)}) collective-permute-start(bf16[7,128,384]{2,1,0:T(8,128)(2,1)S(1)} %get-tuple-element.118), channel_id=1, source_target_pairs={{0,2},{1,3},{2,0},{3,1},{4,6},{5,7},{6,4},{7,5},{8,10},{9,11},{10,... | collective-permute-start | bytes 2064392 | tf_op jit(solution)/shard_map/ppermute | solution.py:506
  31.7 98.3 %collective-permute-start.7 = (bf16[512,2048]{1,0:T(8,128)(2,1)}, bf16[512,2048]{1,0:T(8,128)(2,1)}, u32[]{:S(2)}, u32[]{:S(2)}) collective-permute-start(bf16[512,2048]{1,0:T(8,128)(2,1)} %param.14), channel_id=1, source_target_pairs={{0,8},{8,0},{16,24},{24,16},{1,9},{9,1},{17,25},{25,17},{2,10},{10... | collective-permute-start | bytes 6291464 | tf_op jit(solution)/shard_map/ppermute | solution.py:55
  33.2 96.8 %collective-permute-start.8 = (bf16[512,2048]{1,0:T(8,128)(2,1)}, bf16[512,2048]{1,0:T(8,128)(2,1)}, u32[]{:S(2)}, u32[]{:S(2)}) collective-permute-start(bf16[512,2048]{1,0:T(8,128)(2,1)} %param.14), channel_id=1, source_target_pairs={{0,16},{8,24},{16,0},{24,8},{1,17},{9,25},{17,1},{25,9},{2,18},{10... | collective-permute-start | bytes 6291464 | tf_op jit(solution)/shard_map/ppermute | solution.py:55
  34.8 71.1 %collective-permute-start.1 = (bf16[7,128,384]{2,1,0:T(8,128)(2,1)S(1)}, bf16[7,128,384]{2,1,0:T(8,128)(2,1)}, u32[]{:S(2)}, u32[]{:S(2)}) collective-permute-start(bf16[7,128,384]{2,1,0:T(8,128)(2,1)S(1)} %get-tuple-element.119), channel_id=1, source_target_pairs={{0,4},{1,5},{2,6},{3,7},{4,0},{5,1},{6,2},{7,3},{8,12},{9,13},{10,... | collective-permute-start | bytes 2064392 | tf_op jit(solution)/shard_map/ppermute | solution.py:506
  38.6 85.4 %collective-permute-start.2 = (bf16[7,128,384]{2,1,0:T(8,128)(2,1)S(1)}, bf16[7,128,384]{2,1,0:T(8,128)(2,1)}, u32[]{:S(2)}, u32[]{:S(2)}) collective-permute-start(bf16[7,128,384]{2,1,0:T(8,128)(2,1)S(1)} %get-tuple-element.120), channel_id=1, source_target_pairs={{0,6},{1,7},{2,4},{3,5},{4,2},{5,3},{6,0},{7,1},{8,14},{9,15},{10,... | collective-permute-start | bytes 2064392 | tf_op jit(solution)/shard_map/ppermute | solution.py:506
  127.5 83.9 %collective-permute-start.17 = (bf16[512,2048]{1,0:T(8,128)(2,1)}, bf16[512,2048]{1,0:T(8,128)(2,1)S(1)}, u32[]{:S(2)}, u32[]{:S(2)}) collective-permute-start(bf16[512,2048]{1,0:T(8,128)(2,1)} %param.14), channel_id=1, source_target_pairs={{0,24},{8,16},{16,8},{24,0},{1,25},{9,17},{17,9},{25,1},{2,26},{10... | collective-permute-start | bytes 6291464 | tf_op jit(solution)/shard_map/ppermute | solution.py:55
  145.7 61.6 %collective-permute-start.10 = (bf16[7,128,128]{2,1,0:T(8,128)(2,1)}, bf16[7,128,128]{2,1,0:T(8,128)(2,1)S(1)}, u32[]{:S(2)}, u32[]{:S(2)}) collective-permute-start(bf16[7,128,128]{2,1,0:T(8,128)(2,1)} %get-tuple-element.131), channel_id=1, source_target_pairs={{0,2},{1,3},{2,0},{3,1},{4,6},{5,7},{6,4},{7,5},{8,10},{9,11},{10,... | collective-permute-start | bytes 688136 | tf_op jit(solution)/shard_map/ppermute | solution.py:506
  174.1 33.2 %collective-permute-start.11 = (bf16[7,128,128]{2,1,0:T(8,128)(2,1)}, bf16[7,128,128]{2,1,0:T(8,128)(2,1)S(1)}, u32[]{:S(2)}, u32[]{:S(2)}) collective-permute-start(bf16[7,128,128]{2,1,0:T(8,128)(2,1)} %get-tuple-element.132), channel_id=1, source_target_pairs={{0,4},{1,5},{2,6},{3,7},{4,0},{5,1},{6,2},{7,3},{8,12},{9,13},{10,... | collective-permute-start | bytes 688136 | tf_op jit(solution)/shard_map/ppermute | solution.py:506
  174.1 33.2 %collective-permute-start.12 = (bf16[7,128,128]{2,1,0:T(8,128)(2,1)}, bf16[7,128,128]{2,1,0:T(8,128)(2,1)S(1)}, u32[]{:S(2)}, u32[]{:S(2)}) collective-permute-start(bf16[7,128,128]{2,1,0:T(8,128)(2,1)} %get-tuple-element.133), channel_id=1, source_target_pairs={{0,6},{1,7},{2,4},{3,5},{4,2},{5,3},{6,0},{7,1},{8,14},{9,15},{10,... | collective-permute-start | bytes 688136 | tf_op jit(solution)/shard_map/ppermute | solution.py:506
  226.5 39.2 %collective-permute-start.20 = (bf16[224,2048]{1,0:T(8,128)(2,1)}, bf16[224,2048]{1,0:T(8,128)(2,1)}, u32[]{:S(2)}, u32[]{:S(2)}) collective-permute-start(bf16[224,2048]{1,0:T(8,128)(2,1)} %multiply_convert_fusion), channel_id=1, source_target_pairs={{0,24},{8,16},{16,8},{24,0},{1,25},{9,17},{17,9},{25,1},{2,26},{10... | collective-permute-start | bytes 2752520 | tf_op jit(solution)/shard_map/ppermute | solution.py:55
  301.1 250.4 %reduce-scatter.7.cloned.1.call-start = ((), (), s32[]{:S(2)}) async-start(), calls=%async_computation.7 | async-start | bytes 9437184 | tf_op jit(solution)/shard_map/reduce_scatter | solution.py:673
  327.9 35.3 %collective-permute-start.22 = (bf16[224,2048]{1,0:T(8,128)(2,1)}, bf16[224,2048]{1,0:T(8,128)(2,1)}, u32[]{:S(2)}, u32[]{:S(2)}) collective-permute-start(bf16[224,2048]{1,0:T(8,128)(2,1)} %convolution_convert_fusion.9), channel_id=1, source_target_pairs={{0,8},{8,0},{16,24},{24,16},{1,9},{9,1},{17,25},{25,17},{2,10},{10... | collective-permute-start | bytes 2752520 | tf_op jit(solution)/shard_map/ppermute | solution.py:55
  335.8 38.9 %collective-permute-start.23 = (bf16[224,2048]{1,0:T(8,128)(2,1)}, bf16[224,2048]{1,0:T(8,128)(2,1)}, u32[]{:S(2)}, u32[]{:S(2)}) collective-permute-start(bf16[224,2048]{1,0:T(8,128)(2,1)} %convolution_convert_fusion.8), channel_id=1, source_target_pairs={{0,16},{8,24},{16,0},{24,8},{1,17},{9,25},{17,1},{25,9},{2,18},{10... | collective-permute-start | bytes 2752520 | tf_op jit(solution)/shard_map/ppermute | solution.py:55
  340.8 33.9 %collective-permute-start.24 = (bf16[224,2048]{1,0:T(8,128)(2,1)}, bf16[224,2048]{1,0:T(8,128)(2,1)}, u32[]{:S(2)}, u32[]{:S(2)}) collective-permute-start(bf16[224,2048]{1,0:T(8,128)(2,1)} %convolution_convert_fusion.7), channel_id=1, source_target_pairs={{0,24},{8,16},{16,8},{24,0},{1,25},{9,17},{17,9},{25,1},{2,26},{10... | collective-permute-start | bytes 2752520 | tf_op jit(solution)/shard_map/ppermute | solution.py:55
  374.7 227.7 %reduce-scatter.9.cloned.1.call-start = ((), (), s32[]{:S(2)}) async-start(), calls=%async_computation.8 | async-start | bytes 2359296 | tf_op jit(solution)/shard_map/reduce_scatter | solution.py:722
  421.4 45.5 %collective-permute-start.31 = (bf16[224,2048]{1,0:T(8,128)(2,1)}, bf16[224,2048]{1,0:T(8,128)(2,1)S(1)}, u32[]{:S(2)}, u32[]{:S(2)}) collective-permute-start(bf16[224,2048]{1,0:T(8,128)(2,1)} %get-tuple-element.171), channel_id=1, source_target_pairs={{0,8},{8,0},{16,24},{24,16},{1,9},{9,1},{17,25},{25,17},{2,10},{10... | collective-permute-start | bytes 2752520 | tf_op jit(solution)/shard_map/ppermute | solution.py:55
  421.8 45.2 %collective-permute-start.32 = (bf16[224,2048]{1,0:T(8,128)(2,1)}, bf16[224,2048]{1,0:T(8,128)(2,1)S(1)}, u32[]{:S(2)}, u32[]{:S(2)}) collective-permute-start(bf16[224,2048]{1,0:T(8,128)(2,1)} %get-tuple-element.171), channel_id=1, source_target_pairs={{0,16},{8,24},{16,0},{24,8},{1,17},{9,25},{17,1},{25,9},{2,18},{10... | collective-permute-start | bytes 2752520 | tf_op jit(solution)/shard_map/ppermute | solution.py:55
  476.6 74.9 %collective-permute-start.38 = (bf16[224,2048]{1,0:T(8,128)(2,1)}, bf16[224,2048]{1,0:T(8,128)(2,1)}, u32[]{:S(2)}, u32[]{:S(2)}) collective-permute-start(bf16[224,2048]{1,0:T(8,128)(2,1)} %convolution_convert_fusion.5), channel_id=1, source_target_pairs={{0,8},{8,0},{16,24},{24,16},{1,9},{9,1},{17,25},{25,17},{2,10},{10... | collective-permute-start | bytes 2752520 | tf_op jit(solution)/shard_map/ppermute | solution.py:55
  477.1 74.4 %collective-permute-start.39 = (bf16[224,2048]{1,0:T(8,128)(2,1)}, bf16[224,2048]{1,0:T(8,128)(2,1)}, u32[]{:S(2)}, u32[]{:S(2)}) collective-permute-start(bf16[224,2048]{1,0:T(8,128)(2,1)} %convolution_convert_fusion.4), channel_id=1, source_target_pairs={{0,16},{8,24},{16,0},{24,8},{1,17},{9,25},{17,1},{25,9},{2,18},{10... | collective-permute-start | bytes 2752520 | tf_op jit(solution)/shard_map/ppermute | solution.py:55
  478.7 52.6 %collective-permute-start.35 = (bf16[7,128,384]{2,1,0:T(8,128)(2,1)}, bf16[7,128,384]{2,1,0:T(8,128)(2,1)S(1)}, u32[]{:S(2)}, u32[]{:S(2)}) collective-permute-start(bf16[7,128,384]{2,1,0:T(8,128)(2,1)} %get-tuple-element.186), channel_id=1, source_target_pairs={{0,2},{1,3},{2,0},{3,1},{4,6},{5,7},{6,4},{7,5},{8,10},{9,11},{10,... | collective-permute-start | bytes 2064392 | tf_op jit(solution)/shard_map/ppermute | solution.py:506
  489.0 62.5 %collective-permute-start.36 = (bf16[7,128,384]{2,1,0:T(8,128)(2,1)}, bf16[7,128,384]{2,1,0:T(8,128)(2,1)S(1)}, u32[]{:S(2)}, u32[]{:S(2)}) collective-permute-start(bf16[7,128,384]{2,1,0:T(8,128)(2,1)} %get-tuple-element.187), channel_id=1, source_target_pairs={{0,4},{1,5},{2,6},{3,7},{4,0},{5,1},{6,2},{7,3},{8,12},{9,13},{10,... | collective-permute-start | bytes 2064392 | tf_op jit(solution)/shard_map/ppermute | solution.py:506
  491.6 59.9 %collective-permute-start.37 = (bf16[7,128,384]{2,1,0:T(8,128)(2,1)S(1)}, bf16[7,128,384]{2,1,0:T(8,128)(2,1)S(1)}, u32[]{:S(2)}, u32[]{:S(2)}) collective-permute-start(bf16[7,128,384]{2,1,0:T(8,128)(2,1)S(1)} %get-tuple-element.188), channel_id=1, source_target_pairs={{0,6},{1,7},{2,4},{3,5},{4,2},{5,3},{6,0},{7,1},{8,14},{9,15},{10,... | collective-permute-start | bytes 2064392 | tf_op jit(solution)/shard_map/ppermute | solution.py:506
  551.6 121.8 %reduce-scatter.11.cloned.1.call-start = ((), (), s32[]{:S(2)}) async-start(), calls=%async_computation.9 | async-start | bytes 7077888 | tf_op jit(solution)/shard_map/reduce_scatter | solution.py:728
  602.5 158.1 %all-gather.11.cloned.1.call-start = ((), (), s32[]{:S(2)}) async-start(), calls=%async_computation.11 | async-start | bytes 2359296 | tf_op jit(solution)/shard_map/all_gather | solution.py:745
  606.2 176.2 %all-gather.9.cloned.1.call-start = ((), (), s32[]{:S(2)}) async-start(), calls=%async_computation.10 | async-start | bytes 7077888 | tf_op jit(solution)/shard_map/all_gather | solution.py:745
  685.7 36.4 %collective-permute-start.47 = (bf16[224,2048]{1,0:T(8,128)(2,1)S(1)}, bf16[224,2048]{1,0:T(8,128)(2,1)S(1)}, u32[]{:S(2)}, u32[]{:S(2)}) collective-permute-start(bf16[224,2048]{1,0:T(8,128)(2,1)S(1)} %add_convert_fusion), channel_id=1, source_target_pairs={{0,8},{8,0},{16,24},{24,16},{1,9},{9,1},{17,25},{25,17},{2,10},{10... | collective-permute-start | bytes 2752520 | tf_op jit(solution)/shard_map/ppermute | solution.py:55
  686.5 56.8 %collective-permute-start.48 = (bf16[224,2048]{1,0:T(8,128)(2,1)S(1)}, bf16[224,2048]{1,0:T(8,128)(2,1)S(1)}, u32[]{:S(2)}, u32[]{:S(2)}) collective-permute-start(bf16[224,2048]{1,0:T(8,128)(2,1)S(1)} %add_convert_fusion), channel_id=1, source_target_pairs={{0,16},{8,24},{16,0},{24,8},{1,17},{9,25},{17,1},{25,9},{2,18},{10... | collective-permute-start | bytes 2752520 | tf_op jit(solution)/shard_map/ppermute | solution.py:55
  687.0 56.3 %collective-permute-start.49 = (bf16[224,2048]{1,0:T(8,128)(2,1)S(1)}, bf16[224,2048]{1,0:T(8,128)(2,1)S(1)}, u32[]{:S(2)}, u32[]{:S(2)}) collective-permute-start(bf16[224,2048]{1,0:T(8,128)(2,1)S(1)} %add_convert_fusion), channel_id=1, source_target_pairs={{0,24},{8,16},{16,8},{24,0},{1,25},{9,17},{17,9},{25,1},{2,26},{10... | collective-permute-start | bytes 2752520 | tf_op jit(solution)/shard_map/ppermute | solution.py:55
  702.5 57.2 %collective-permute-start.43 = (bf16[224,2048]{1,0:T(8,128)(2,1)S(1)}, bf16[224,2048]{1,0:T(8,128)(2,1)S(1)}, u32[]{:S(2)}, u32[]{:S(2)}) collective-permute-start(bf16[224,2048]{1,0:T(8,128)(2,1)S(1)} %collective-permute-done.41), channel_id=1, source_target_pairs={{0,16},{8,24},{16,0},{24,8},{1,17},{9,25},{17,1},{25,9},{2,18},{10... | collective-permute-start | bytes 2752520 | tf_op jit(solution)/shard_map/ppermute | solution.py:55
  (96 other events, 1948.8 us)
Sparse Core Ops, SparseCore 0:
  9.6 140.6 all-gather.4
  151.9 105.5 all-gather.6
  301.2 99.3 reduce-scatter.4
  402.8 117.1 reduce-scatter.6
  551.7 50.7 reduce-scatter.8
  605.2 68.1 reduce-scatter.10
  675.0 27.5 all-gather.10
  704.2 64.0 all-gather.8

commit v5 on v4

--- a/solution.py
+++ b/solution.py
@@ -517,6 +517,36 @@
         ]
         return lax.ppermute(values, "seq", pairs)
 
+    def scatter_members(values):
+        size = values.shape[0] // members
+
+        def block(number):
+            return lax.dynamic_slice_in_dim(values, number * size, size, 0)
+
+        total = block(member).astype(f32)
+        for step in range(1, members):
+            sent = block((member + members - step) % members)
+            total = total + among(sent, step).astype(f32)
+        return total.astype(bf16)
+
+    def scatter_places(values):
+        size = values.shape[0] // heads
+        pieces = [
+            lax.dynamic_slice_in_dim(values, (place ^ slot) * size, size, 0) for slot in range(heads)
+        ]
+        pieces = [v.astype(f32) for v in exchange(pieces)]
+        return sum(pieces[1:], pieces[0]).astype(bf16)
+
+    def gather_seq(values):
+        values = placed(exchange([values] * heads), place, 0)
+        size = values.shape[0]
+        full = jnp.zeros((size * members,) + values.shape[1:], values.dtype)
+        for step in range(members):
+            piece = among(values, step) if step else values
+            at = (member + step) % members * size
+            full = lax.dynamic_update_slice_in_dim(full, piece, at, 0)
+        return full
+
     def swap(values, slot):
         return flip(values, "heads", head_count, slot)
 
@@ -556,7 +586,6 @@
             full = lax.dynamic_update_slice_in_dim(full, values, (key ^ slot) * size, axis)
         return full
 
-    full_up = lax.all_gather(w_up, "seq", axis=0, tiled=True)
     out_slots = gather_heads(w_out)
 
     column = jnp.arange(rows)
@@ -587,9 +616,13 @@
     slots, normed_low, pooled = project(
         scal, tokens, gain_attn[None, :], cosine, sine, w_qkv.transpose(1, 0, 2)
     )
-    full_down = lax.all_gather(w_down, "seq", axis=1, tiled=True)
     slots = exchange(slots)
     other_slots = [among(v, step) for step in range(1, members) for v in slots]
+    slots, out_slots[:-1], own_up, own_down = lax.optimization_barrier(
+        (slots, out_slots[:-1], w_up, w_down)
+    )
+    full_up = lax.all_gather(own_up, "seq", axis=0, tiled=True)
+    full_down = lax.all_gather(own_down, "seq", axis=1, tiled=True)
     tokens_own = own_rows(tokens, 0).astype(f32)
     hat_own, inverse_own = normalize_parts(tokens_own)
     hops = []
@@ -604,8 +637,8 @@
         return values
 
     pooled = hop(pooled[:SEQS], hops[:-2])
-    slots, other_slots, out_slots[:-1], hat_own, inverse_own, pooled = lax.optimization_barrier(
-        (slots, other_slots, out_slots[:-1], hat_own, inverse_own, pooled)
+    slots, other_slots, hat_own, inverse_own, pooled = lax.optimization_barrier(
+        (slots, other_slots, hat_own, inverse_own, pooled)
     )
     full_out = jnp.concatenate(out_slots, axis=0)
     pooled = hop(pooled, hops[-2:-1])
@@ -716,49 +749,57 @@
     ffn_parts = scatter_heads(ffn_parts)
     grad_attn = jnp.concatenate(grad_attn, axis=0)
     grad_out_part = contract(jnp.concatenate(heads_rel, axis=0), grad_attn, 0, 0).astype(bf16)
-    grad_out_part, grad_down, grad_up, sums, ffn_parts[:-1] = lax.optimization_barrier(
-        (grad_out_part, grad_down, grad_up, sums, ffn_parts[:-1])
-    )
-    total_out = lax.psum_scatter(grad_out_part, "seq", scatter_dimension=0, tiled=True)
+    grad_out_part, sums, ffn_parts[:-1] = lax.optimization_barrier(
+        (grad_out_part, sums, ffn_parts[:-1])
+    )
+    total_out = scatter_members(grad_out_part)
     grad_projected = gather_grads(scal, cosine, -sine, sums)
     grad_qkv_part = contract(normed_low, grad_projected, 0, 0).astype(bf16)
-    grad_projected, grad_qkv_part, total_out, ffn_parts = lax.optimization_barrier(
-        (grad_projected, grad_qkv_part, total_out, ffn_parts)
+    grad_projected, grad_qkv_part, ffn_parts, grad_down, grad_up = lax.optimization_barrier(
+        (grad_projected, grad_qkv_part, ffn_parts, grad_down, grad_up)
     )
     total_qkv = lax.psum_scatter(grad_qkv_part, "seq", scatter_dimension=0, tiled=True)
     grad_down, grad_up = grad_down.astype(f32), grad_up.astype(f32)
-    one_parts = scatter_heads(
-        [
-            sum(
-                contract(
-                    own_rows(grad_projected, slot)[:, part * head_width : (part + 1) * head_width],
-                    w_qkv[:, part],
-                    1,
-                    1,
-                )
-                for part in range(3)
+    output_own = (
+        hidden + sum([v.astype(f32) for v in ffn_parts[1:]], ffn_parts[0])
+    ).astype(bf16)
+    output_slots = gather_heads(output_own)
+    one_parts = [
+        sum(
+            contract(
+                own_rows(grad_projected, slot)[:, part * head_width : (part + 1) * head_width],
+                w_qkv[:, part],
+                1,
+                1,
             )
-            for slot in range(head_count)
-        ]
-    )
-    one_parts, total_qkv = lax.optimization_barrier((one_parts, total_qkv))
-    totals = [lax.all_gather(v, "seq", axis=0, tiled=True) for v in (total_qkv, total_out)]
+            for part in range(3)
+        )
+        for slot in range(head_count)
+    ]
+    one_parts[1:] = [v.astype(bf16) for v in one_parts[1:]]
+    one_parts, total_out, output_slots[1:-1] = lax.optimization_barrier(
+        (one_parts, total_out, output_slots[1:-1])
+    )
+    one_parts = scatter_heads(one_parts)
+    total_out = scatter_places(total_out)
+
+    grad_one = sum([v.astype(f32) for v in one_parts[1:]], one_parts[0]) + grad_pooled_own
+    back_one, gain_one = normalize_back(grad_one, hat_own, inverse_own, gain_attn)
+    tokens_back = (grad_hidden + back_one).astype(bf16)
+    tokens_back, total_qkv, total_out = lax.optimization_barrier(
+        (tokens_back, total_qkv, total_out)
+    )
+    total_qkv = lax.all_gather(total_qkv, "seq", axis=0, tiled=True)
+    token_slots = gather_heads(tokens_back)
+    grad_out = gather_seq(total_out).astype(f32)
     grad_qkv = jnp.stack(
         [
-            totals[0][:, part * head_width : (part + 1) * head_width].astype(f32)
+            total_qkv[:, part * head_width : (part + 1) * head_width].astype(f32)
             for part in range(3)
         ],
         axis=1,
     )
-    grad_out = totals[1].astype(f32)
-    output_own = (
-        hidden + sum([v.astype(f32) for v in ffn_parts[1:]], ffn_parts[0])
-    ).astype(bf16)
-    output = in_order(gather_doubling(output_own), bf16)
-
-    grad_one = sum([v.astype(f32) for v in one_parts[1:]], one_parts[0]) + grad_pooled_own
-    back_one, gain_one = normalize_back(grad_one, hat_own, inverse_own, gain_attn)
-    token_slots = gather_heads((grad_hidden + back_one).astype(bf16))
+    output = in_order(output_slots, bf16)
     token_slots, gains = lax.optimization_barrier(
         (token_slots, jnp.stack([gain_one, gain_two]))
     )

time: 808 us -> 753 us (0.932)
  waiting for transfers between devices: 371 us -> 317 us
  starting transfers between devices: 128 us -> 155 us
  local copies, waits for them, and re-layouts: 41.1 us -> 30.6 us
    ppermute x38, waiting for transfers between devices: 162 us -> 70.8 us  [flip(): return lax.ppermute(values, axis, [(i, i ^ bit) for i in range(size)])]
    ppermute x12 -> x18, waiting for transfers between devices: 153 us -> 211 us  [across(): return lax.ppermute(values, 'seq', pairs)]
    ppermute x38, starting transfers between devices: 58.6 us -> 92.1 us  [flip(): return lax.ppermute(values, axis, [(i, i ^ bit) for i in range(size)])]
    reduce_scatter x1 -> x0, waiting for transfers between devices: 29 us -> none  [local(): lax.psum_scatter(grad_out_part, 'seq', scatter_dimension=0, tiled=True)]
    all_gather x4 -> x3, waiting for transfers between devices: 0.01 us -> 23.3 us  [the longest x1 23.3 us: local(): full_down = lax.all_gather(own_down, 'seq', axis=1, tiled=True)]
    reduce_scatter x1, waiting for transfers between devices: 21.4 us -> 3.92 us  [local(): lax.psum_scatter(grad_qkv_part, 'seq', scatter_dimension=0, tiled=True)]
    unnamed x136 -> x148, local copies, waits for them, and re-layouts: 21.8 us -> 13.5 us
    ppermute x12 -> x18, starting transfers between devices: 68.3 us -> 60.7 us  [across(): return lax.ppermute(values, 'seq', pairs)]
  transfers between devices with their start and end apart: 63 -> 69, of which waited for: 28 -> 38; matrix products, arithmetic and copies ran while one was open for 26% -> 25% of each run, Pallas kernels for 7% -> 7%
where the time goes in v5:
time: 753 us; the launch traced here: 747 us
  waiting for transfers between devices  317 us (42%)
  starting transfers between devices  155 us (21%)
  matrix products  130 us (17%)
  Pallas kernels  55.7 us (7%)
  other arithmetic  43.6 us (6%)
  local copies, waits for them, and re-layouts  30.6 us (4%)
  between operations  15.8 us (2%)
    ppermute x18, waiting for transfers between devices, across(): return lax.ppermute(values, 'seq', pairs)  211 us
    dot_general x22, matrix products, contract(): lax.dot_general(left, right, (((left_dim,), (right_dim,)), ((), ())), pre...  98.8 us
    ppermute x38, starting transfers between devices, flip(): return lax.ppermute(values, axis, [(i, i ^ bit) for i in range(size)])  92.1 us
    ppermute x38, waiting for transfers between devices, flip(): return lax.ppermute(values, axis, [(i, i ^ bit) for i in range(size)])  70.8 us
    ppermute x18, starting transfers between devices, across(): return lax.ppermute(values, 'seq', pairs)  60.7 us
    dot_general x6, matrix products, dot(): return jnp.dot(left, right, preferred_element_type=f32)  27.3 us
    all_gather x1, waiting for transfers between devices, local(): full_down = lax.all_gather(own_down, 'seq', axis=1, tiled=True)  23.3 us
    pallas_call x1, Pallas kernels, attend_backward(): pl.pallas_call(functools.partial(back_kernel, heads, members), out_shape=...  21.4 us
  transfers between devices with their start and end apart: 69, of which 38 were waited for; matrix products, arithmetic and copies ran while one was open for 25% of the time, Pallas kernels for 7%

profile of v5, /device:TPU:0, one launch (start us, length us, event | category | flops | bytes accessed | tf_op | source)
XLA Modules:
  0.0 747.3 jit_solution(9693892579118229689)
XLA Ops:
  15.4 16.2 %project.1 = (bf16[7,128,384]{2,1,0:T(8,128)(2,1)S(1)}, bf16[7,128,384]{2,1,0:T(8,128)(2,1)S(1)}, bf16[7,128,384]{2,1,0:T(8,128)(2,1)S(1)}, bf16[7,128,384]{2,1,...) custom-call(s32[7]{0:T(128)S(1)} %pad_add_fusion.scal, bf16[896,2048]{1,0:T(8,128)(2,1)} %tokens.1, ...), custom_call_target="tpu_custom_call" | custom-call | flops 5637144576 | bytes 16777216 | tf_op jit(solution)/shard_map/project/pallas_call | solution.py:402
  36.1 26.0 %collective-permute-done.refs_1_ = bf16[7,128,384]{2,1,0:T(8,128)(2,1)S(1)} collective-permute-done((bf16[7,128,384]{2,1,0:T(8,128)(2,1)S(1)}, bf16[7,128,384]{2,1,0:T(8,128)(2,1)S(1)}, u32[]{:S(2)}, u32[]{:S(2)}) %collective-permute-start) | collective-permute-done | bytes 688160 | tf_op jit(solution)/shard_map/ppermute | solution.py:506
  62.0 19.9 %collective-permute-done.1.refs_2_ = bf16[7,128,384]{2,1,0:T(8,128)(2,1)S(1)} collective-permute-done((bf16[7,128,384]{2,1,0:T(8,128)(2,1)S(1)}, bf16[7,128,384]{2,1,0:T(8,128)(2,1)S(1)}, u32[]{:S(2)}, u32[]{:S(2)}) %collective-permute-start.1) | collective-permute-done | bytes 688160 | tf_op jit(solution)/shard_map/ppermute | solution.py:506
  93.2 14.5 %collective-permute-start.13 = (f32[5,2048]{1,0:T(8,128)S(1)}, f32[5,2048]{1,0:T(8,128)S(1)}, u32[]{:S(2)}, u32[]{:S(2)}) collective-permute-start(f32[5,2048]{1,0:T(8,128)S(1)} %slice_add_fusion), channel_id=1, source_target_pairs={{0,2},{1,3},{2,0},{3,1},{4,6},{5,7},{6,4},{7,5},{8,10},{9,11},{10,... | collective-permute-start | bytes 122888 | tf_op jit(solution)/shard_map/ppermute | solution.py:55
  107.7 15.4 %attend_forward.1 = (bf16[7,128,128]{2,1,0:T(8,128)(2,1)}, bf16[7,128,128]{2,1,0:T(8,128)(2,1)}, bf16[7,128,128]{2,1,0:T(8,128)(2,1)}, bf16[7,128,128]{2,1,0:T(8,128)(2,1)}, f32[4,7,1,128]{3,2,1,0:T(1,128)}) custom-call(s32[7]{0:T(128)} %copy-done.5, bf16[7,128,384]{2,1,0:T(8,128)(2,1)} %copy-done.7, bf16[7,128,384]{2,1,0:T(8,128)(2,1)} %copy-done.55, ...), custom_call_target="tpu_custom_call" | custom-call | flops 4000000000 | bytes 7340032 | tf_op jit(solution)/shard_map/attend_forward/pallas_call | solution.py:185
  129.8 17.1 %collective-permute-done.10 = bf16[7,128,128]{2,1,0:T(8,128)(2,1)S(1)} collective-permute-done((bf16[7,128,128]{2,1,0:T(8,128)(2,1)}, bf16[7,128,128]{2,1,0:T(8,128)(2,1)S(1)}, u32[]{:S(2)}, u32[]{:S(2)}) %collective-permute-start.10) | collective-permute-done | bytes 229408 | tf_op jit(solution)/shard_map/ppermute | solution.py:506
  146.9 9.8 %collective-permute-done.12 = bf16[7,128,128]{2,1,0:T(8,128)(2,1)S(1)} collective-permute-done((bf16[7,128,128]{2,1,0:T(8,128)(2,1)}, bf16[7,128,128]{2,1,0:T(8,128)(2,1)S(1)}, u32[]{:S(2)}, u32[]{:S(2)}) %collective-permute-start.12) | collective-permute-done | bytes 229408 | tf_op jit(solution)/shard_map/ppermute | solution.py:506
  182.3 16.5 %collective-permute-start.21 = (f32[5,2048]{1,0:T(8,128)S(1)}, f32[5,2048]{1,0:T(8,128)S(1)}, u32[]{:S(2)}, u32[]{:S(2)}) collective-permute-start(f32[5,2048]{1,0:T(8,128)S(1)} %add.339), channel_id=1, source_target_pairs={{0,4},{1,5},{2,6},{3,7},{4,0},{5,1},{6,2},{7,3},{8,12},{9,13},{10,... | collective-permute-start | bytes 122888 | tf_op jit(solution)/shard_map/ppermute | solution.py:55
  201.8 13.1 %collective-permute-done.19 = bf16[224,2048]{1,0:T(8,128)(2,1)} collective-permute-done((bf16[224,2048]{1,0:T(8,128)(2,1)S(1)}, bf16[224,2048]{1,0:T(8,128)(2,1)}, u32[]{:S(2)}, u32[]{:S(2)}) %collective-permute-start.19) | collective-permute-done | bytes 917536 | tf_op jit(solution)/shard_map/ppermute | solution.py:55
  222.6 13.5 %fusion = (bf16[896,2048]{1,0:T(8,128)(2,1)S(1)}, f32[896,2048]{1,0:T(8,128)}) fusion(s32[2048]{0:T(1024)S(1)} %iota_add_fusion, s32[896]{0:T(1024)S(1)} %add_multiply_fusion, bf16[896,2048]{1,0:T(8,128)(2,1)} %constant_dynamic-update-slice_fusion.4, bf16[2048,2048]{1,0:T(8,128)(2,1)} %all-gather.4.cloned.1.call-done), kind=kOutput, calls=%fused_computation.5 | convolution fusion | flops 7525367808 | bytes 23080448 | tf_op jit(solution)/shard_map/dot_general | solution.py:29
  238.0 11.4 %convolution_convert_fusion.2 = bf16[2048,2048]{1,0:T(8,128)(2,1)} fusion(bf16[896,2048]{1,0:T(8,128)(2,1)S(1)} %get-tuple-element.175, bf16[224,2048]{1,0:T(8,128)(2,1)S(1)} %copy-done.23, bf16[224,2048]{1,0:T(8,128)(2,1)S(1)} %copy-done.25, bf16[224,2048]{1,0:T(8,128)(2,1)S(1)} %copy-done.21, bf16[224,2048]{1,0:T(8,128)(2,1)S(1)} %copy-done.12), kind=kOutput, calls=%fused_computation.4 | convolution fusion | flops 7535067136 | bytes 15728640 | tf_op jit(solution)/shard_map/dot_general | solution.py:33
  254.4 23.3 %all-gather.6.cloned.1.call-done = bf16[2048,2048]{1,0:T(8,128)(2,1)} async-done(((bf16[2048,256]{1,0:T(8,128)(2,1)}), bf16[2048,2048]{1,0:T(8,128)(2,1)}) %all-gather.6.cloned.1.call-update) | async-done | bytes 8388624 | tf_op jit(solution)/shard_map/all_gather | solution.py:625
  277.7 13.4 %fusion.3 = bf16[896,2048]{1,0:T(8,128)(2,1)S(1)} fusion(f32[896,2048]{1,0:T(8,128)} %get-tuple-element.164, s32[2048]{0:T(1024)S(1)} %iota_add_fusion, s32[896]{0:T(1024)S(1)} %add_multiply_fusion, bf16[896,2048]{1,0:T(8,128)(2,1)} %pad_maximum_fusion, bf16[2048,2048]{1,0:T(8,128)(2,1)} %all-gather.6.cloned.1.call-done), kind=kOutput, calls=%fused_computation.8 | convolution fusion | flops 7529037824 | bytes 23080448 | tf_op jit(solution)/shard_map/dot_general | solution.py:33
  291.1 8.5 %convolution_convert_fusion.7 = bf16[224,2048]{1,0:T(8,128)(2,1)} fusion(bf16[2048,2048]{1,0:T(8,128)(2,1)} %all-gather.4.cloned.1.call-done, bf16[896,2048]{1,0:T(8,128)(2,1)S(1)} %fusion.3), kind=kOutput, calls=%fused_computation.39 | convolution fusion | flops 1879506944 | bytes 10223616 | tf_op jit(solution)/shard_map/dot_general | solution.py:33
  302.0 7.0 convolution_convert_fusion.8
  314.0 13.6 %convolution_convert_fusion.1 = bf16[2048,2048]{1,0:T(8,128)(2,1)} fusion(bf16[896,2048]{1,0:T(8,128)(2,1)} %constant_dynamic-update-slice_fusion.4, bf16[896,2048]{1,0:T(8,128)(2,1)S(1)} %fusion.3), kind=kOutput, calls=%fused_computation.3 | convolution fusion | flops 7520387072 | bytes 15728640 | tf_op jit(solution)/shard_map/dot_general | solution.py:33
  327.6 7.6 %fusion.56 = f32[224,2048]{1,0:T(8,128)} fusion(bf16[2048,2048]{1,0:T(8,128)(2,1)} %all-gather.4.cloned.1.call-done, bf16[896,2048]{1,0:T(8,128)(2,1)} %copy-done.61), kind=kOutput, calls=%fused_computation.107 | convolution fusion | flops 1879048192 | bytes 11141120 | tf_op jit(solution)/shard_map/dot_general | solution.py:33
  335.3 7.7 %collective-permute-done.23 = bf16[224,2048]{1,0:T(8,128)(2,1)} collective-permute-done((bf16[224,2048]{1,0:T(8,128)(2,1)}, bf16[224,2048]{1,0:T(8,128)(2,1)}, u32[]{:S(2)}, u32[]{:S(2)}) %collective-permute-start.23) | collective-permute-done | bytes 917536 | tf_op jit(solution)/shard_map/ppermute | solution.py:55
  385.4 7.5 %collective-permute-done.29.refs_10_ = bf16[7,128,128]{2,1,0:T(8,128)(2,1)S(1)} collective-permute-done((bf16[7,128,128]{2,1,0:T(8,128)(2,1)S(1)}, bf16[7,128,128]{2,1,0:T(8,128)(2,1)S(1)}, u32[]{:S(2)}, u32[]{:S(2)}) %collective-permute-start.29) | collective-permute-done | bytes 229408 | tf_op jit(solution)/shard_map/ppermute | solution.py:506
  396.0 21.4 %attend_backward.1 = (bf16[7,128,384]{2,1,0:T(8,128)(2,1)}, bf16[7,128,384]{2,1,0:T(8,128)(2,1)}, bf16[7,128,384]{2,1,0:T(8,128)(2,1)}, bf16[7,128,384]{2,1,0:T(8,128)(2,1)}, bf16[4,7,128,384]{3,2,1,0:T(8,128)(2,1)}) custom-call(s32[7]{0:T(128)} %copy-done.5, bf16[7,128,384]{2,1,0:T(8,128)(2,1)} %copy-done.7, bf16[7,128,384]{2,1,0:T(8,128)(2,1)} %copy-done.55, ...), custom_call_target="tpu_custom_call" | custom-call | flops 10000000000 | bytes 12582912 | tf_op jit(solution)/shard_map/attend_backward/pallas_call | solution.py:311
  428.2 10.1 %collective-permute-start.35 = (bf16[7,128,384]{2,1,0:T(8,128)(2,1)S(1)}, bf16[7,128,384]{2,1,0:T(8,128)(2,1)S(1)}, u32[]{:S(2)}, u32[]{:S(2)}) collective-permute-start(bf16[7,128,384]{2,1,0:T(8,128)(2,1)S(1)} %get-tuple-element.200), channel_id=1, source_target_pairs={{0,2},{1,3},{2,0},{3,1},{4,6},{5,7},{6,4},{7,5},{8,10},{9,11},{10,... | collective-permute-start | bytes 2064392 | tf_op jit(solution)/shard_map/ppermute | solution.py:506
  450.4 38.2 %collective-permute-done.35.refs_1_ = bf16[7,128,384]{2,1,0:T(8,128)(2,1)S(1)} collective-permute-done((bf16[7,128,384]{2,1,0:T(8,128)(2,1)S(1)}, bf16[7,128,384]{2,1,0:T(8,128)(2,1)S(1)}, u32[]{:S(2)}, u32[]{:S(2)}) %collective-permute-start.35) | collective-permute-done | bytes 688160 | tf_op jit(solution)/shard_map/ppermute | solution.py:506
  491.6 16.7 %collective-permute-done.37.refs_3_ = bf16[7,128,384]{2,1,0:T(8,128)(2,1)S(1)} collective-permute-done((bf16[7,128,384]{2,1,0:T(8,128)(2,1)S(1)}, bf16[7,128,384]{2,1,0:T(8,128)(2,1)S(1)}, u32[]{:S(2)}, u32[]{:S(2)}) %collective-permute-start.37) | collective-permute-done | bytes 688160 | tf_op jit(solution)/shard_map/ppermute | solution.py:506
  511.2 8.7 %convolution_convert_fusion = bf16[2048,1536]{1,0:T(8,128)(2,1)} fusion(bf16[896,2048]{1,0:T(8,128)(2,1)S(1)} %copy-done.64, bf16[896,1536]{1,0:T(8,128)(2,1)S(1)} %gather_grads.1), kind=kOutput, calls=%fused_computation.2 | convolution fusion | flops 5640290304 | bytes 12713984 | tf_op jit(solution)/shard_map/dot_general | solution.py:33
  555.0 19.8 %collective-permute-start.48 = (bf16[64,2048]{1,0:T(8,128)(2,1)S(1)}, bf16[64,2048]{1,0:T(8,128)(2,1)S(1)}, u32[]{:S(2)}, u32[]{:S(2)}) collective-permute-start(bf16[64,2048]{1,0:T(8,128)(2,1)S(1)} %get-tuple-element.274), channel_id=1, source_target_pairs={{0,2},{1,3},{2,0},{3,1},{4,6},{5,7},{6,4},{7,5},{8,10},{9,11},{10,... | collective-permute-start | bytes 786440 | tf_op jit(solution)/shard_map/ppermute | solution.py:506
  579.9 14.5 %collective-permute-done.48 = bf16[64,2048]{1,0:T(8,128)(2,1)S(1)} collective-permute-done((bf16[64,2048]{1,0:T(8,128)(2,1)S(1)}, bf16[64,2048]{1,0:T(8,128)(2,1)S(1)}, u32[]{:S(2)}, u32[]{:S(2)}) %collective-permute-start.48) | collective-permute-done | bytes 262176 | tf_op jit(solution)/shard_map/ppermute | solution.py:506
  602.3 10.3 %collective-permute-done.50 = bf16[64,2048]{1,0:T(8,128)(2,1)} collective-permute-done((bf16[64,2048]{1,0:T(8,128)(2,1)S(1)}, bf16[64,2048]{1,0:T(8,128)(2,1)}, u32[]{:S(2)}, u32[]{:S(2)}) %collective-permute-start.50) | collective-permute-done | bytes 262176 | tf_op jit(solution)/shard_map/ppermute | solution.py:506
  631.9 14.4 %collective-permute-done.44 = bf16[224,2048]{1,0:T(8,128)(2,1)} collective-permute-done((bf16[224,2048]{1,0:T(8,128)(2,1)}, bf16[224,2048]{1,0:T(8,128)(2,1)}, u32[]{:S(2)}, u32[]{:S(2)}) %collective-permute-start.44) | collective-permute-done | bytes 917536 | tf_op jit(solution)/shard_map/ppermute | solution.py:55
  647.6 6.8 collective-permute-start.54
  658.1 17.8 %collective-permute-done.54 = bf16[64,2048]{1,0:T(8,128)(2,1)S(1)} collective-permute-done((bf16[64,2048]{1,0:T(8,128)(2,1)S(1)}, bf16[64,2048]{1,0:T(8,128)(2,1)S(1)}, u32[]{:S(2)}, u32[]{:S(2)}) %collective-permute-start.54) | collective-permute-done | bytes 262176 | tf_op jit(solution)/shard_map/ppermute | solution.py:506
  678.2 17.1 %collective-permute-done.55 = bf16[64,2048]{1,0:T(8,128)(2,1)S(1)} collective-permute-done((bf16[64,2048]{1,0:T(8,128)(2,1)S(1)}, bf16[64,2048]{1,0:T(8,128)(2,1)S(1)}, u32[]{:S(2)}, u32[]{:S(2)}) %collective-permute-start.55) | collective-permute-done | bytes 262176 | tf_op jit(solution)/shard_map/ppermute | solution.py:506
  706.2 15.9 %collective-permute-start.61 = (f32[2,2048]{1,0:T(2,128)S(1)}, f32[2,2048]{1,0:T(2,128)S(1)}, u32[]{:S(2)}, u32[]{:S(2)}) collective-permute-start(f32[2,2048]{1,0:T(2,128)S(1)} %add.394), channel_id=1, source_target_pairs={{0,2},{1,3},{2,0},{3,1},{4,6},{5,7},{6,4},{7,5},{8,10},{9,11},{10,... | collective-permute-start | bytes 49160 | tf_op jit(solution)/shard_map/ppermute | solution.py:55
  (388 shorter events, 257.6 us)
Async XLA Ops:
  7.2 215.3 %all-gather.4.cloned.1.call-start = ((), (), s32[]{:S(2)}) async-start(), calls=%async_computation.3 | async-start | bytes 9437184 | tf_op jit(solution)/shard_map/all_gather | solution.py:624
  7.3 74.7 %collective-permute-start.3 = (bf16[512,2048]{1,0:T(8,128)(2,1)}, bf16[512,2048]{1,0:T(8,128)(2,1)S(1)}, u32[]{:S(2)}, u32[]{:S(2)}) collective-permute-start(bf16[512,2048]{1,0:T(8,128)(2,1)} %param.14), channel_id=1, source_target_pairs={{0,8},{8,0},{16,24},{24,16},{1,9},{9,1},{17,25},{25,17},{2,10},{10... | collective-permute-start | bytes 6291464 | tf_op jit(solution)/shard_map/ppermute | solution.py:55
  10.3 71.7 %collective-permute-start.4 = (bf16[512,2048]{1,0:T(8,128)(2,1)}, bf16[512,2048]{1,0:T(8,128)(2,1)}, u32[]{:S(2)}, u32[]{:S(2)}) collective-permute-start(bf16[512,2048]{1,0:T(8,128)(2,1)} %param.14), channel_id=1, source_target_pairs={{0,16},{8,24},{16,0},{24,8},{1,17},{9,25},{17,1},{25,9},{2,18},{10... | collective-permute-start | bytes 6291464 | tf_op jit(solution)/shard_map/ppermute | solution.py:55
  33.3 48.7 %collective-permute-start.1 = (bf16[7,128,384]{2,1,0:T(8,128)(2,1)S(1)}, bf16[7,128,384]{2,1,0:T(8,128)(2,1)S(1)}, u32[]{:S(2)}, u32[]{:S(2)}) collective-permute-start(bf16[7,128,384]{2,1,0:T(8,128)(2,1)S(1)} %get-tuple-element.129), channel_id=1, source_target_pairs={{0,4},{1,5},{2,6},{3,7},{4,0},{5,1},{6,2},{7,3},{8,12},{9,13},{10,... | collective-permute-start | bytes 2064392 | tf_op jit(solution)/shard_map/ppermute | solution.py:506
  35.9 46.1 %collective-permute-start.2 = (bf16[7,128,384]{2,1,0:T(8,128)(2,1)S(1)}, bf16[7,128,384]{2,1,0:T(8,128)(2,1)S(1)}, u32[]{:S(2)}, u32[]{:S(2)}) collective-permute-start(bf16[7,128,384]{2,1,0:T(8,128)(2,1)S(1)} %get-tuple-element.130), channel_id=1, source_target_pairs={{0,6},{1,7},{2,4},{3,5},{4,2},{5,3},{6,0},{7,1},{8,14},{9,15},{10,... | collective-permute-start | bytes 2064392 | tf_op jit(solution)/shard_map/ppermute | solution.py:506
  83.8 193.9 %all-gather.6.cloned.1.call-start = ((), (), s32[]{:S(2)}) async-start(), calls=%async_computation.4 | async-start | bytes 9437184 | tf_op jit(solution)/shard_map/all_gather | solution.py:625
  84.5 435.3 %reduce-scatter.4.cloned.1.call-start = ((), (), s32[]{:S(2)}) async-start(), calls=%async_computation.5 | async-start | bytes 9437184 | tf_op jit(solution)/shard_map/reduce_scatter | solution.py:677
  92.3 68.4 %collective-permute-start.17 = (bf16[512,2048]{1,0:T(8,128)(2,1)S(1)}, bf16[512,2048]{1,0:T(8,128)(2,1)S(1)}, u32[]{:S(2)}, u32[]{:S(2)}) collective-permute-start(bf16[512,2048]{1,0:T(8,128)(2,1)S(1)} %copy-done.26), channel_id=1, source_target_pairs={{0,24},{8,16},{16,8},{24,0},{1,25},{9,17},{17,9},{25,1},{2,26},{10... | collective-permute-start | bytes 6291464 | tf_op jit(solution)/shard_map/ppermute | solution.py:55
  93.2 36.6 %collective-permute-start.13 = (f32[5,2048]{1,0:T(8,128)S(1)}, f32[5,2048]{1,0:T(8,128)S(1)}, u32[]{:S(2)}, u32[]{:S(2)}) collective-permute-start(f32[5,2048]{1,0:T(8,128)S(1)} %slice_add_fusion), channel_id=1, source_target_pairs={{0,2},{1,3},{2,0},{3,1},{4,6},{5,7},{6,4},{7,5},{8,10},{9,11},{10,... | collective-permute-start | bytes 122888 | tf_op jit(solution)/shard_map/ppermute | solution.py:55
  175.0 39.9 %collective-permute-start.19 = (bf16[224,2048]{1,0:T(8,128)(2,1)S(1)}, bf16[224,2048]{1,0:T(8,128)(2,1)}, u32[]{:S(2)}, u32[]{:S(2)}) collective-permute-start(bf16[224,2048]{1,0:T(8,128)(2,1)S(1)} %multiply_convert_fusion), channel_id=1, source_target_pairs={{0,16},{8,24},{16,0},{24,8},{1,17},{9,25},{17,1},{25,9},{2,18},{10... | collective-permute-start | bytes 2752520 | tf_op jit(solution)/shard_map/ppermute | solution.py:55
  175.3 39.6 %collective-permute-start.20 = (bf16[224,2048]{1,0:T(8,128)(2,1)S(1)}, bf16[224,2048]{1,0:T(8,128)(2,1)}, u32[]{:S(2)}, u32[]{:S(2)}) collective-permute-start(bf16[224,2048]{1,0:T(8,128)(2,1)S(1)} %multiply_convert_fusion), channel_id=1, source_target_pairs={{0,24},{8,16},{16,8},{24,0},{1,25},{9,17},{17,9},{25,1},{2,26},{10... | collective-permute-start | bytes 2752520 | tf_op jit(solution)/shard_map/ppermute | solution.py:55
  249.4 270.4 %reduce-scatter.6.cloned.1.call-start = ((), (), s32[]{:S(2)}) async-start(), calls=%async_computation.6 | async-start | bytes 9437184 | tf_op jit(solution)/shard_map/reduce_scatter | solution.py:706
  299.6 35.7 %collective-permute-start.24 = (bf16[224,2048]{1,0:T(8,128)(2,1)}, bf16[224,2048]{1,0:T(8,128)(2,1)S(1)}, u32[]{:S(2)}, u32[]{:S(2)}) collective-permute-start(bf16[224,2048]{1,0:T(8,128)(2,1)} %convolution_convert_fusion.7), channel_id=1, source_target_pairs={{0,24},{8,16},{16,8},{24,0},{1,25},{9,17},{17,9},{25,1},{2,26},{10... | collective-permute-start | bytes 2752520 | tf_op jit(solution)/shard_map/ppermute | solution.py:55
  309.0 33.9 %collective-permute-start.23 = (bf16[224,2048]{1,0:T(8,128)(2,1)}, bf16[224,2048]{1,0:T(8,128)(2,1)}, u32[]{:S(2)}, u32[]{:S(2)}) collective-permute-start(bf16[224,2048]{1,0:T(8,128)(2,1)} %convolution_convert_fusion.8), channel_id=1, source_target_pairs={{0,16},{8,24},{16,0},{24,8},{1,17},{9,25},{17,1},{25,9},{2,18},{10... | collective-permute-start | bytes 2752520 | tf_op jit(solution)/shard_map/ppermute | solution.py:55
  343.0 281.7 %reduce-scatter.8.cloned.1.call-start = ((), (), s32[]{:S(2)}) async-start(), calls=%async_computation.7 | async-start | bytes 7077888 | tf_op jit(solution)/shard_map/reduce_scatter | solution.py:761
  377.1 40.3 %collective-permute-start.31 = (bf16[224,2048]{1,0:T(8,128)(2,1)S(1)}, bf16[224,2048]{1,0:T(8,128)(2,1)}, u32[]{:S(2)}, u32[]{:S(2)}) collective-permute-start(bf16[224,2048]{1,0:T(8,128)(2,1)S(1)} %get-tuple-element.187), channel_id=1, source_target_pairs={{0,8},{8,0},{16,24},{24,16},{1,9},{9,1},{17,25},{25,17},{2,10},{10... | collective-permute-start | bytes 2752520 | tf_op jit(solution)/shard_map/ppermute | solution.py:55
  378.2 39.1 %collective-permute-start.32 = (bf16[224,2048]{1,0:T(8,128)(2,1)S(1)}, bf16[224,2048]{1,0:T(8,128)(2,1)}, u32[]{:S(2)}, u32[]{:S(2)}) collective-permute-start(bf16[224,2048]{1,0:T(8,128)(2,1)S(1)} %get-tuple-element.187), channel_id=1, source_target_pairs={{0,16},{8,24},{16,0},{24,8},{1,17},{9,25},{17,1},{25,9},{2,18},{10... | collective-permute-start | bytes 2752520 | tf_op jit(solution)/shard_map/ppermute | solution.py:55
  425.8 82.5 %collective-permute-start.38 = (bf16[224,2048]{1,0:T(8,128)(2,1)S(1)}, bf16[224,2048]{1,0:T(8,128)(2,1)S(1)}, u32[]{:S(2)}, u32[]{:S(2)}) collective-permute-start(bf16[224,2048]{1,0:T(8,128)(2,1)S(1)} %convolution_convert_fusion.5), channel_id=1, source_target_pairs={{0,8},{8,0},{16,24},{24,16},{1,9},{9,1},{17,25},{25,17},{2,10},{10... | collective-permute-start | bytes 2752520 | tf_op jit(solution)/shard_map/ppermute | solution.py:55
  427.8 80.6 %collective-permute-start.39 = (bf16[224,2048]{1,0:T(8,128)(2,1)S(1)}, bf16[224,2048]{1,0:T(8,128)(2,1)S(1)}, u32[]{:S(2)}, u32[]{:S(2)}) collective-permute-start(bf16[224,2048]{1,0:T(8,128)(2,1)S(1)} %convolution_convert_fusion.4), channel_id=1, source_target_pairs={{0,16},{8,24},{16,0},{24,8},{1,17},{9,25},{17,1},{25,9},{2,18},{10... | collective-permute-start | bytes 2752520 | tf_op jit(solution)/shard_map/ppermute | solution.py:55
  428.2 60.4 %collective-permute-start.35 = (bf16[7,128,384]{2,1,0:T(8,128)(2,1)S(1)}, bf16[7,128,384]{2,1,0:T(8,128)(2,1)S(1)}, u32[]{:S(2)}, u32[]{:S(2)}) collective-permute-start(bf16[7,128,384]{2,1,0:T(8,128)(2,1)S(1)} %get-tuple-element.200), channel_id=1, source_target_pairs={{0,2},{1,3},{2,0},{3,1},{4,6},{5,7},{6,4},{7,5},{8,10},{9,11},{10,... | collective-permute-start | bytes 2064392 | tf_op jit(solution)/shard_map/ppermute | solution.py:506
  438.3 53.3 %collective-permute-start.36 = (bf16[7,128,384]{2,1,0:T(8,128)(2,1)S(1)}, bf16[7,128,384]{2,1,0:T(8,128)(2,1)S(1)}, u32[]{:S(2)}, u32[]{:S(2)}) collective-permute-start(bf16[7,128,384]{2,1,0:T(8,128)(2,1)S(1)} %get-tuple-element.201), channel_id=1, source_target_pairs={{0,4},{1,5},{2,6},{3,7},{4,0},{5,1},{6,2},{7,3},{8,12},{9,13},{10,... | collective-permute-start | bytes 2064392 | tf_op jit(solution)/shard_map/ppermute | solution.py:506
  441.7 66.6 %collective-permute-start.37 = (bf16[7,128,384]{2,1,0:T(8,128)(2,1)S(1)}, bf16[7,128,384]{2,1,0:T(8,128)(2,1)S(1)}, u32[]{:S(2)}, u32[]{:S(2)}) collective-permute-start(bf16[7,128,384]{2,1,0:T(8,128)(2,1)S(1)} %get-tuple-element.202), channel_id=1, source_target_pairs={{0,6},{1,7},{2,4},{3,5},{4,2},{5,3},{6,0},{7,1},{8,14},{9,15},{10,... | collective-permute-start | bytes 2064392 | tf_op jit(solution)/shard_map/ppermute | solution.py:506
  519.9 212.0 %all-gather.8.cloned.1.call-start = ((), (), s32[]{:S(2)}) async-start(), calls=%async_computation.8 | async-start | bytes 7077888 | tf_op jit(solution)/shard_map/all_gather | solution.py:792
  555.0 39.4 %collective-permute-start.48 = (bf16[64,2048]{1,0:T(8,128)(2,1)S(1)}, bf16[64,2048]{1,0:T(8,128)(2,1)S(1)}, u32[]{:S(2)}, u32[]{:S(2)}) collective-permute-start(bf16[64,2048]{1,0:T(8,128)(2,1)S(1)} %get-tuple-element.274), channel_id=1, source_target_pairs={{0,2},{1,3},{2,0},{3,1},{4,6},{5,7},{6,4},{7,5},{8,10},{9,11},{10,... | collective-permute-start | bytes 786440 | tf_op jit(solution)/shard_map/ppermute | solution.py:506
  574.9 39.0 %collective-permute-start.45 = (bf16[224,2048]{1,0:T(8,128)(2,1)}, bf16[224,2048]{1,0:T(8,128)(2,1)S(1)}, u32[]{:S(2)}, u32[]{:S(2)}) collective-permute-start(bf16[224,2048]{1,0:T(8,128)(2,1)} %fusion.15), channel_id=1, source_target_pairs={{0,8},{8,0},{16,24},{24,16},{1,9},{9,1},{17,25},{25,17},{2,10},{10... | collective-permute-start | bytes 2752520 | tf_op jit(solution)/shard_map/ppermute | solution.py:55
  575.4 41.1 %collective-permute-start.46 = (bf16[224,2048]{1,0:T(8,128)(2,1)}, bf16[224,2048]{1,0:T(8,128)(2,1)}, u32[]{:S(2)}, u32[]{:S(2)}) collective-permute-start(bf16[224,2048]{1,0:T(8,128)(2,1)} %fusion.16), channel_id=1, source_target_pairs={{0,16},{8,24},{16,0},{24,8},{1,17},{9,25},{17,1},{25,9},{2,18},{10... | collective-permute-start | bytes 2752520 | tf_op jit(solution)/shard_map/ppermute | solution.py:55
  577.0 39.5 %collective-permute-start.47 = (bf16[224,2048]{1,0:T(8,128)(2,1)}, bf16[224,2048]{1,0:T(8,128)(2,1)}, u32[]{:S(2)}, u32[]{:S(2)}) collective-permute-start(bf16[224,2048]{1,0:T(8,128)(2,1)} %fusion.17), channel_id=1, source_target_pairs={{0,24},{8,16},{16,8},{24,0},{1,25},{9,17},{17,9},{25,1},{2,26},{10... | collective-permute-start | bytes 2752520 | tf_op jit(solution)/shard_map/ppermute | solution.py:55
  654.4 41.0 %collective-permute-start.51 = (bf16[224,2048]{1,0:T(8,128)(2,1)S(1)}, bf16[224,2048]{1,0:T(8,128)(2,1)S(1)}, u32[]{:S(2)}, u32[]{:S(2)}) collective-permute-start(bf16[224,2048]{1,0:T(8,128)(2,1)S(1)} %add_convert_fusion.1), channel_id=1, source_target_pairs={{0,8},{8,0},{16,24},{24,16},{1,9},{9,1},{17,25},{25,17},{2,10},{10... | collective-permute-start | bytes 2752520 | tf_op jit(solution)/shard_map/ppermute | solution.py:55
  654.5 42.9 %collective-permute-start.52 = (bf16[224,2048]{1,0:T(8,128)(2,1)S(1)}, bf16[224,2048]{1,0:T(8,128)(2,1)S(1)}, u32[]{:S(2)}, u32[]{:S(2)}) collective-permute-start(bf16[224,2048]{1,0:T(8,128)(2,1)S(1)} %add_convert_fusion.1), channel_id=1, source_target_pairs={{0,16},{8,24},{16,0},{24,8},{1,17},{9,25},{17,1},{25,9},{2,18},{10... | collective-permute-start | bytes 2752520 | tf_op jit(solution)/shard_map/ppermute | solution.py:55
  656.7 40.7 %collective-permute-start.53 = (bf16[224,2048]{1,0:T(8,128)(2,1)S(1)}, bf16[224,2048]{1,0:T(8,128)(2,1)S(1)}, u32[]{:S(2)}, u32[]{:S(2)}) collective-permute-start(bf16[224,2048]{1,0:T(8,128)(2,1)S(1)} %add_convert_fusion.1), channel_id=1, source_target_pairs={{0,24},{8,16},{16,8},{24,0},{1,25},{9,17},{17,9},{25,1},{2,26},{10... | collective-permute-start | bytes 2752520 | tf_op jit(solution)/shard_map/ppermute | solution.py:55
  658.0 37.3 %collective-permute-start.55 = (bf16[64,2048]{1,0:T(8,128)(2,1)S(1)}, bf16[64,2048]{1,0:T(8,128)(2,1)S(1)}, u32[]{:S(2)}, u32[]{:S(2)}) collective-permute-start(bf16[64,2048]{1,0:T(8,128)(2,1)S(1)} %add_convert_fusion.3), channel_id=1, source_target_pairs={{0,4},{1,5},{2,6},{3,7},{4,0},{5,1},{6,2},{7,3},{8,12},{9,13},{10,... | collective-permute-start | bytes 786440 | tf_op jit(solution)/shard_map/ppermute | solution.py:506
  695.3 33.9 %collective-permute-start.57 = (bf16[256,2048]{1,0:T(8,128)(2,1)S(1)}, bf16[256,2048]{1,0:T(8,128)(2,1)S(1)}, u32[]{:S(2)}, u32[]{:S(2)}) collective-permute-start(bf16[256,2048]{1,0:T(8,128)(2,1)S(1)} %constant_dynamic-update-slice_fusion.10), channel_id=1, source_target_pairs={{1,0},{0,1},{3,2},{2,3},{5,4},{4,5},{7,6},{6,7},{9,8},{8,9},{11,10... | collective-permute-start | bytes 3145736 | tf_op jit(solution)/shard_map/ppermute | solution.py:518
  (108 other events, 2048.6 us)
Sparse Core Ops, SparseCore 0:
  83.9 111.3 all-gather.3
  196.8 80.8 all-gather.5
  280.0 87.6 reduce-scatter.3
  369.9 120.4 reduce-scatter.5
  520.0 104.7 reduce-scatter.7
  626.3 89.9 all-gather.7

commit v6 on v5

--- a/solution.py
+++ b/solution.py
@@ -586,6 +586,8 @@
             full = lax.dynamic_update_slice_in_dim(full, values, (key ^ slot) * size, axis)
         return full
 
+    half = ffn_width // 2
+    first_up = lax.all_gather(w_up[:, :half], "seq", axis=0, tiled=True)
     out_slots = gather_heads(w_out)
 
     column = jnp.arange(rows)
@@ -618,13 +620,11 @@
     )
     slots = exchange(slots)
     other_slots = [among(v, step) for step in range(1, members) for v in slots]
-    slots, out_slots[:-1], own_up, own_down = lax.optimization_barrier(
-        (slots, out_slots[:-1], w_up, w_down)
-    )
-    full_up = lax.all_gather(own_up, "seq", axis=0, tiled=True)
-    full_down = lax.all_gather(own_down, "seq", axis=1, tiled=True)
     tokens_own = own_rows(tokens, 0).astype(f32)
     hat_own, inverse_own = normalize_parts(tokens_own)
+    cotangent_rel = jnp.concatenate(
+        [own_rows(cotangent, slot) for slot in range(head_count)], axis=0
+    )
     hops = []
     bit = 1
     while bit < seq_count:
@@ -637,11 +637,15 @@
         return values
 
     pooled = hop(pooled[:SEQS], hops[:-2])
-    slots, other_slots, hat_own, inverse_own, pooled = lax.optimization_barrier(
-        (slots, other_slots, hat_own, inverse_own, pooled)
-    )
+    early = (slots, other_slots, out_slots[:-1], w_up[:, half:], w_down)
+    early = early + (hat_own, inverse_own, cotangent_rel, pooled)
+    early = lax.optimization_barrier(early)
+    slots, other_slots, out_slots[:-1], own_up, own_down = early[:5]
+    hat_own, inverse_own, cotangent_rel, pooled = early[5:]
+    second_up = lax.all_gather(own_up, "seq", axis=0, tiled=True)
+    full_down = lax.all_gather(own_down, "seq", axis=1, tiled=True)
+    pooled = hop(pooled, hops[-2:-1])
     full_out = jnp.concatenate(out_slots, axis=0)
-    pooled = hop(pooled, hops[-2:-1])
     mixed_slots, logs = attend_forward(scal, slots, other_slots, heads, members)
     mixed_slots = [across(v, slot) if slot else v for slot, v in enumerate(mixed_slots)]
     mixed_slots, pooled = lax.optimization_barrier((mixed_slots, pooled))
@@ -657,13 +661,11 @@
     hat_two, inverse_two = normalize_parts(hidden)
     normed_two = gather_heads((hat_two * gain_ffn).astype(bf16))
 
-    cotangent_rel = jnp.concatenate(
-        [own_rows(cotangent, slot) for slot in range(head_count)], axis=0
-    )
     level_rel = jnp.concatenate([own_rows(ffn_level, slot) for slot in range(head_count)])
     unit_index = head_rank * ffn_width + jnp.arange(ffn_width)
     ffn_live = (unit_index[None, :] < (level_rel * (FF // LEVELS))[:, None]).astype(f32)
-    normed_two, pooled = lax.optimization_barrier((normed_two, pooled))
+    full_up = jnp.concatenate([first_up, second_up], axis=1)
+    normed_two, pooled, full_up = lax.optimization_barrier((normed_two, pooled, full_up))
     normed_two = jnp.concatenate(normed_two, axis=0)
     upward = dot(normed_two, full_up)
     kept = jnp.maximum(upward, 0.0)
@@ -763,7 +765,9 @@
     output_own = (
         hidden + sum([v.astype(f32) for v in ffn_parts[1:]], ffn_parts[0])
     ).astype(bf16)
-    output_slots = gather_heads(output_own)
+    output_slots = [output_own] + [
+        swap(output_own, slot) for slot in range(1, head_count - 1)
+    ]
     one_parts = [
         sum(
             contract(
@@ -777,8 +781,8 @@
         for slot in range(head_count)
     ]
     one_parts[1:] = [v.astype(bf16) for v in one_parts[1:]]
-    one_parts, total_out, output_slots[1:-1] = lax.optimization_barrier(
-        (one_parts, total_out, output_slots[1:-1])
+    one_parts, total_out, output_slots = lax.optimization_barrier(
+        (one_parts, total_out, output_slots)
     )
     one_parts = scatter_heads(one_parts)
     total_out = scatter_places(total_out)
@@ -786,8 +790,9 @@
     grad_one = sum([v.astype(f32) for v in one_parts[1:]], one_parts[0]) + grad_pooled_own
     back_one, gain_one = normalize_back(grad_one, hat_own, inverse_own, gain_attn)
     tokens_back = (grad_hidden + back_one).astype(bf16)
-    tokens_back, total_qkv, total_out = lax.optimization_barrier(
-        (tokens_back, total_qkv, total_out)
+    gains = butterfly(jnp.stack([gain_one, gain_two]), "heads", head_count)
+    tokens_back, total_qkv, total_out, gains = lax.optimization_barrier(
+        (tokens_back, total_qkv, total_out, gains)
     )
     total_qkv = lax.all_gather(total_qkv, "seq", axis=0, tiled=True)
     token_slots = gather_heads(tokens_back)
@@ -799,12 +804,13 @@
         ],
         axis=1,
     )
+    token_slots, gains, output_slots = lax.optimization_barrier(
+        (token_slots, gains, output_slots)
+    )
+    output_slots.append(swap(output_slots[0], head_count - 1))
     output = in_order(output_slots, bf16)
-    token_slots, gains = lax.optimization_barrier(
-        (token_slots, jnp.stack([gain_one, gain_two]))
-    )
+    gains = butterfly(gains, "seq", seq_count)
     grad_tokens = in_order(token_slots, f32)
-    gains = butterfly(butterfly(gains, "heads", head_count), "seq", seq_count)
     return (
         output,
         grad_tokens,

time: 753 us -> 742 us (0.985)
  waiting for transfers between devices: 317 us -> 292 us
    ppermute x18, waiting for transfers between devices: 211 us -> 189 us  [across(): return lax.ppermute(values, 'seq', pairs)]
    ppermute x38, starting transfers between devices: 92.1 us -> 72.5 us  [flip(): return lax.ppermute(values, axis, [(i, i ^ bit) for i in range(size)])]
    ppermute x18, starting transfers between devices: 60.7 us -> 79.9 us  [across(): return lax.ppermute(values, 'seq', pairs)]
    all_gather x1, waiting for transfers between devices: 23.3 us -> 4.58 us  [local(): full_down = lax.all_gather(own_down, 'seq', axis=1, tiled=True)]
    ppermute x38, waiting for transfers between devices: 70.8 us -> 86.2 us  [flip(): return lax.ppermute(values, axis, [(i, i ^ bit) for i in range(size)])]
    concatenate x0 -> x1, other arithmetic: none -> 8.33 us  [local(): full_up = jnp.concatenate([first_up, second_up], axis=1)]
  transfers between devices with their start and end apart: 69 -> 70, of which waited for: 38 -> 35; matrix products, arithmetic and copies ran while one was open for 25% -> 27% of each run, Pallas kernels for 7% -> 8%
where the time goes in v6:
time: 742 us; the launch traced here: 735 us
  waiting for transfers between devices  292 us (39%)
  starting transfers between devices  155 us (21%)
  matrix products  130 us (18%)
  Pallas kernels  55.5 us (7%)
  other arithmetic  50.2 us (7%)
  local copies, waits for them, and re-layouts  37 us (5%)
  between operations  15.9 us (2%)
    ppermute x18, waiting for transfers between devices, across(): return lax.ppermute(values, 'seq', pairs)  189 us
    dot_general x22, matrix products, contract(): lax.dot_general(left, right, (((left_dim,), (right_dim,)), ((), ())), pre...  98.5 us
    ppermute x38, waiting for transfers between devices, flip(): return lax.ppermute(values, axis, [(i, i ^ bit) for i in range(size)])  86.2 us
    ppermute x18, starting transfers between devices, across(): return lax.ppermute(values, 'seq', pairs)  79.9 us
    ppermute x38, starting transfers between devices, flip(): return lax.ppermute(values, axis, [(i, i ^ bit) for i in range(size)])  72.5 us
    dot_general x6, matrix products, dot(): return jnp.dot(left, right, preferred_element_type=f32)  28 us
    pallas_call x1, Pallas kernels, attend_backward(): pl.pallas_call(functools.partial(back_kernel, heads, members), out_shape=...  21.1 us
    pallas_call x1, Pallas kernels, project(): pl.pallas_call(functools.partial(project_kernel, heads), out_shape=[jax.S...  16.3 us
  transfers between devices with their start and end apart: 70, of which 35 were waited for; matrix products, arithmetic and copies ran while one was open for 27% of the time, Pallas kernels for 8%

profile of v6, /device:TPU:0, one launch (start us, length us, event | category | flops | bytes accessed | tf_op | source)
XLA Modules:
  0.0 735.2 jit_solution(15514056062354011513)
XLA Ops:
  17.0 16.3 %project.1 = (bf16[7,128,384]{2,1,0:T(8,128)(2,1)S(1)}, bf16[7,128,384]{2,1,0:T(8,128)(2,1)}, bf16[7,128,384]{2,1,0:T(8,128)(2,1)S(1)}, bf16[7,128,384]{2,1,0:T(...) custom-call(s32[7]{0:T(128)S(1)} %pad_add_fusion.scal, bf16[896,2048]{1,0:T(8,128)(2,1)} %tokens.1, ...), custom_call_target="tpu_custom_call" | custom-call | flops 5637144576 | bytes 16777216 | tf_op jit(solution)/shard_map/project/pallas_call | solution.py:402
  42.9 43.7 %collective-permute-done.refs_1_ = bf16[7,128,384]{2,1,0:T(8,128)(2,1)} collective-permute-done((bf16[7,128,384]{2,1,0:T(8,128)(2,1)}, bf16[7,128,384]{2,1,0:T(8,128)(2,1)}, u32[]{:S(2)}, u32[]{:S(2)}) %collective-permute-start) | collective-permute-done | bytes 688160 | tf_op jit(solution)/shard_map/ppermute | solution.py:506
  88.9 14.3 %collective-permute-done.2.refs_3_ = bf16[7,128,384]{2,1,0:T(8,128)(2,1)S(1)} collective-permute-done((bf16[7,128,384]{2,1,0:T(8,128)(2,1)S(1)}, bf16[7,128,384]{2,1,0:T(8,128)(2,1)S(1)}, u32[]{:S(2)}, u32[]{:S(2)}) %collective-permute-start.2) | collective-permute-done | bytes 688160 | tf_op jit(solution)/shard_map/ppermute | solution.py:506
  111.6 15.3 %attend_forward.1 = (bf16[7,128,128]{2,1,0:T(8,128)(2,1)}, bf16[7,128,128]{2,1,0:T(8,128)(2,1)}, bf16[7,128,128]{2,1,0:T(8,128)(2,1)}, bf16[7,128,128]{2,1,0:T(8,128)(2,1)}, f32[4,7,1,128]{3,2,1,0:T(1,128)}) custom-call(s32[7]{0:T(128)} %copy-done.6, bf16[7,128,384]{2,1,0:T(8,128)(2,1)} %copy-done.8, bf16[7,128,384]{2,1,0:T(8,128)(2,1)} %collective-permute-done.refs_1_, ...), custom_call_target="tpu_custom_call" | custom-call | flops 4000000000 | bytes 7340032 | tf_op jit(solution)/shard_map/attend_forward/pallas_call | solution.py:185
  127.0 14.9 %collective-permute-start.10 = (bf16[7,128,128]{2,1,0:T(8,128)(2,1)}, bf16[7,128,128]{2,1,0:T(8,128)(2,1)S(1)}, u32[]{:S(2)}, u32[]{:S(2)}) collective-permute-start(bf16[7,128,128]{2,1,0:T(8,128)(2,1)} %get-tuple-element.144), channel_id=1, source_target_pairs={{0,2},{1,3},{2,0},{3,1},{4,6},{5,7},{6,4},{7,5},{8,10},{9,11},{10,... | collective-permute-start | bytes 688136 | tf_op jit(solution)/shard_map/ppermute | solution.py:506
  149.0 26.2 %collective-permute-done.13 = f32[5,2048]{1,0:T(8,128)S(1)} collective-permute-done((f32[5,2048]{1,0:T(8,128)S(1)}, f32[5,2048]{1,0:T(8,128)S(1)}, u32[]{:S(2)}, u32[]{:S(2)}) %collective-permute-start.13) | collective-permute-done | bytes 40992 | tf_op jit(solution)/shard_map/ppermute | solution.py:55
  195.5 11.3 %collective-permute-start.21 = (f32[5,2048]{1,0:T(8,128)S(1)}, f32[5,2048]{1,0:T(8,128)S(1)}, u32[]{:S(2)}, u32[]{:S(2)}) collective-permute-start(f32[5,2048]{1,0:T(8,128)S(1)} %add.342), channel_id=1, source_target_pairs={{0,4},{1,5},{2,6},{3,7},{4,0},{5,1},{6,2},{7,3},{8,12},{9,13},{10,... | collective-permute-start | bytes 122888 | tf_op jit(solution)/shard_map/ppermute | solution.py:55
  206.9 9.0 %collective-permute-done.21 = f32[5,2048]{1,0:T(8,128)S(1)} collective-permute-done((f32[5,2048]{1,0:T(8,128)S(1)}, f32[5,2048]{1,0:T(8,128)S(1)}, u32[]{:S(2)}, u32[]{:S(2)}) %collective-permute-start.21) | collective-permute-done | bytes 40992 | tf_op jit(solution)/shard_map/ppermute | solution.py:55
  216.0 8.3 %pad_maximum_fusion = bf16[2048,2048]{1,0:T(8,128)(2,1)} fusion(bf16[2048,1024]{1,0:T(8,128)(2,1)} %all-gather.7.cloned.1.call-done, bf16[2048,1024]{1,0:T(8,128)(2,1)} %all-gather.5.cloned.1.call-done), kind=kLoop, calls=%fused_computation.2 | loop fusion | flops 16777216 | bytes 16777216 | tf_op jit(solution)/shard_map/concatenate | solution.py:667
  224.3 7.3 collective-permute-done.19
  237.1 14.2 %fusion = (bf16[896,2048]{1,0:T(8,128)(2,1)S(1)}, f32[896,2048]{1,0:T(8,128)}) fusion(s32[2048]{0:T(1024)S(1)} %iota_add_fusion, s32[896]{0:T(1024)S(1)} %add_multiply_fusion, bf16[896,2048]{1,0:T(8,128)(2,1)S(1)} %constant_dynamic-update-slice_fusion.4, bf16[2048,2048]{1,0:T(8,128)(2,1)} %pad_maximum_fusion), kind=kOutput, calls=%fused_computation.6 | convolution fusion | flops 7525367808 | bytes 23080448 | tf_op jit(solution)/shard_map/dot_general | solution.py:29
  253.2 11.4 %convolution_convert_fusion.2 = bf16[2048,2048]{1,0:T(8,128)(2,1)} fusion(bf16[896,2048]{1,0:T(8,128)(2,1)S(1)} %get-tuple-element.177, bf16[896,2048]{1,0:T(8,128)(2,1)S(1)} %copy-done.17), kind=kOutput, calls=%fused_computation.5 | convolution fusion | flops 7520387072 | bytes 15728640 | tf_op jit(solution)/shard_map/dot_general | solution.py:33
  274.1 13.4 %fusion.3 = bf16[896,2048]{1,0:T(8,128)(2,1)S(1)} fusion(f32[896,2048]{1,0:T(8,128)} %get-tuple-element.165, s32[2048]{0:T(1024)S(1)} %iota_add_fusion, s32[896]{0:T(1024)S(1)} %add_multiply_fusion, bf16[896,2048]{1,0:T(8,128)(2,1)} %pad_maximum_fusion.1, bf16[2048,2048]{1,0:T(8,128)(2,1)} %all-gather.9.cloned.1.call-done), kind=kOutput, calls=%fused_computation.9 | convolution fusion | flops 7529037824 | bytes 23080448 | tf_op jit(solution)/shard_map/dot_general | solution.py:33
  287.5 8.4 %convolution_convert_fusion.7 = bf16[224,2048]{1,0:T(8,128)(2,1)} fusion(bf16[2048,2048]{1,0:T(8,128)(2,1)} %pad_maximum_fusion, bf16[896,2048]{1,0:T(8,128)(2,1)S(1)} %fusion.3), kind=kOutput, calls=%fused_computation.40 | convolution fusion | flops 1879506944 | bytes 10223616 | tf_op jit(solution)/shard_map/dot_general | solution.py:33
  298.6 7.0 convolution_convert_fusion.8
  310.3 11.4 %convolution_convert_fusion.1 = bf16[2048,2048]{1,0:T(8,128)(2,1)} fusion(bf16[896,2048]{1,0:T(8,128)(2,1)S(1)} %copy-done.33, bf16[896,2048]{1,0:T(8,128)(2,1)S(1)} %fusion.3), kind=kOutput, calls=%fused_computation.4 | convolution fusion | flops 7520387072 | bytes 15728640 | tf_op jit(solution)/shard_map/dot_general | solution.py:33
  321.6 7.7 %fusion.56 = f32[224,2048]{1,0:T(8,128)} fusion(bf16[2048,2048]{1,0:T(8,128)(2,1)} %pad_maximum_fusion, bf16[896,2048]{1,0:T(8,128)(2,1)} %copy-done.56), kind=kOutput, calls=%fused_computation.108 | convolution fusion | flops 1879048192 | bytes 11141120 | tf_op jit(solution)/shard_map/dot_general | solution.py:33
  329.3 10.0 %collective-permute-done.23 = bf16[224,2048]{1,0:T(8,128)(2,1)} collective-permute-done((bf16[224,2048]{1,0:T(8,128)(2,1)}, bf16[224,2048]{1,0:T(8,128)(2,1)}, u32[]{:S(2)}, u32[]{:S(2)}) %collective-permute-start.23) | collective-permute-done | bytes 917536 | tf_op jit(solution)/shard_map/ppermute | solution.py:55
  345.9 6.5 convolution_convert_fusion.6
  383.0 15.0 %collective-permute-done.29.refs_10_ = bf16[7,128,128]{2,1,0:T(8,128)(2,1)S(1)} collective-permute-done((bf16[7,128,128]{2,1,0:T(8,128)(2,1)S(1)}, bf16[7,128,128]{2,1,0:T(8,128)(2,1)S(1)}, u32[]{:S(2)}, u32[]{:S(2)}) %collective-permute-start.29) | collective-permute-done | bytes 229408 | tf_op jit(solution)/shard_map/ppermute | solution.py:506
  399.9 21.1 %attend_backward.1 = (bf16[7,128,384]{2,1,0:T(8,128)(2,1)}, bf16[7,128,384]{2,1,0:T(8,128)(2,1)}, bf16[7,128,384]{2,1,0:T(8,128)(2,1)}, bf16[7,128,384]{2,1,0:T(8,128)(2,1)}, bf16[4,7,128,384]{3,2,1,0:T(8,128)(2,1)}) custom-call(s32[7]{0:T(128)} %copy-done.6, bf16[7,128,384]{2,1,0:T(8,128)(2,1)} %copy-done.8, ...), custom_call_target="tpu_custom_call" | custom-call | flops 10000000000 | bytes 12582912 | tf_op jit(solution)/shard_map/attend_backward/pallas_call | solution.py:311
  431.5 11.2 %collective-permute-start.35 = (bf16[7,128,384]{2,1,0:T(8,128)(2,1)S(1)}, bf16[7,128,384]{2,1,0:T(8,128)(2,1)S(1)}, u32[]{:S(2)}, u32[]{:S(2)}) collective-permute-start(bf16[7,128,384]{2,1,0:T(8,128)(2,1)S(1)} %get-tuple-element.202), channel_id=1, source_target_pairs={{0,2},{1,3},{2,0},{3,1},{4,6},{5,7},{6,4},{7,5},{8,10},{9,11},{10,... | collective-permute-start | bytes 2064392 | tf_op jit(solution)/shard_map/ppermute | solution.py:506
  449.9 5.2 fusion.12
  455.1 36.1 %collective-permute-done.35.refs_1_ = bf16[7,128,384]{2,1,0:T(8,128)(2,1)S(1)} collective-permute-done((bf16[7,128,384]{2,1,0:T(8,128)(2,1)S(1)}, bf16[7,128,384]{2,1,0:T(8,128)(2,1)S(1)}, u32[]{:S(2)}, u32[]{:S(2)}) %collective-permute-start.35) | collective-permute-done | bytes 688160 | tf_op jit(solution)/shard_map/ppermute | solution.py:506
  493.1 15.6 %collective-permute-done.37.refs_3_ = bf16[7,128,384]{2,1,0:T(8,128)(2,1)S(1)} collective-permute-done((bf16[7,128,384]{2,1,0:T(8,128)(2,1)S(1)}, bf16[7,128,384]{2,1,0:T(8,128)(2,1)S(1)}, u32[]{:S(2)}, u32[]{:S(2)}) %collective-permute-start.37) | collective-permute-done | bytes 688160 | tf_op jit(solution)/shard_map/ppermute | solution.py:506
  511.6 8.7 %convolution_convert_fusion = bf16[2048,1536]{1,0:T(8,128)(2,1)} fusion(bf16[896,2048]{1,0:T(8,128)(2,1)S(1)} %copy-done.59, bf16[896,1536]{1,0:T(8,128)(2,1)S(1)} %gather_grads.1), kind=kOutput, calls=%fused_computation.3 | convolution fusion | flops 5640290304 | bytes 12713984 | tf_op jit(solution)/shard_map/dot_general | solution.py:33
  555.6 22.6 %collective-permute-start.47 = (bf16[64,2048]{1,0:T(8,128)(2,1)S(1)}, bf16[64,2048]{1,0:T(8,128)(2,1)S(1)}, u32[]{:S(2)}, u32[]{:S(2)}) collective-permute-start(bf16[64,2048]{1,0:T(8,128)(2,1)S(1)} %get-tuple-element.278), channel_id=1, source_target_pairs={{0,2},{1,3},{2,0},{3,1},{4,6},{5,7},{6,4},{7,5},{8,10},{9,11},{10,... | collective-permute-start | bytes 786440 | tf_op jit(solution)/shard_map/ppermute | solution.py:506
  581.7 14.0 %collective-permute-done.47 = bf16[64,2048]{1,0:T(8,128)(2,1)S(1)} collective-permute-done((bf16[64,2048]{1,0:T(8,128)(2,1)S(1)}, bf16[64,2048]{1,0:T(8,128)(2,1)S(1)}, u32[]{:S(2)}, u32[]{:S(2)}) %collective-permute-start.47) | collective-permute-done | bytes 262176 | tf_op jit(solution)/shard_map/ppermute | solution.py:506
  598.5 13.5 %collective-permute-done.48 = bf16[64,2048]{1,0:T(8,128)(2,1)} collective-permute-done((bf16[64,2048]{1,0:T(8,128)(2,1)}, bf16[64,2048]{1,0:T(8,128)(2,1)}, u32[]{:S(2)}, u32[]{:S(2)}) %collective-permute-start.48) | collective-permute-done | bytes 262176 | tf_op jit(solution)/shard_map/ppermute | solution.py:506
  631.4 8.0 %collective-permute-start.56 = (bf16[64,2048]{1,0:T(8,128)(2,1)S(1)}, bf16[64,2048]{1,0:T(8,128)(2,1)S(1)}, u32[]{:S(2)}, u32[]{:S(2)}) collective-permute-start(bf16[64,2048]{1,0:T(8,128)(2,1)S(1)} %add_convert_fusion.3), channel_id=1, source_target_pairs={{0,2},{1,3},{2,0},{3,1},{4,6},{5,7},{6,4},{7,5},{8,10},{9,11},{10,... | collective-permute-start | bytes 786440 | tf_op jit(solution)/shard_map/ppermute | solution.py:506
  649.8 29.7 %collective-permute-done.57 = bf16[64,2048]{1,0:T(8,128)(2,1)S(1)} collective-permute-done((bf16[64,2048]{1,0:T(8,128)(2,1)S(1)}, bf16[64,2048]{1,0:T(8,128)(2,1)S(1)}, u32[]{:S(2)}, u32[]{:S(2)}) %collective-permute-start.57) | collective-permute-done | bytes 262176 | tf_op jit(solution)/shard_map/ppermute | solution.py:506
  687.9 15.9 %collective-permute-start.61 = (f32[2,2048]{1,0:T(2,128)S(1)}, f32[2,2048]{1,0:T(2,128)S(1)}, u32[]{:S(2)}, u32[]{:S(2)}) collective-permute-start(f32[2,2048]{1,0:T(2,128)S(1)} %add.394), channel_id=1, source_target_pairs={{0,2},{1,3},{2,0},{3,1},{4,6},{5,7},{6,4},{7,5},{8,10},{9,11},{10,... | collective-permute-start | bytes 49160 | tf_op jit(solution)/shard_map/ppermute | solution.py:55
  (384 shorter events, 245.9 us)
Async XLA Ops:
  7.2 208.7 %all-gather.5.cloned.1.call-start = ((), (), s32[]{:S(2)}) async-start(), calls=%async_computation.3 | async-start | bytes 4718592 | tf_op jit(solution)/shard_map/all_gather | solution.py:590
  9.5 206.4 %all-gather.7.cloned.1.call-start = ((), (), s32[]{:S(2)}) async-start(), calls=%async_computation.4 | async-start | bytes 4718592 | tf_op jit(solution)/shard_map/all_gather | solution.py:645
  9.6 97.6 %collective-permute-start.7 = (bf16[512,2048]{1,0:T(8,128)(2,1)}, bf16[512,2048]{1,0:T(8,128)(2,1)}, u32[]{:S(2)}, u32[]{:S(2)}) collective-permute-start(bf16[512,2048]{1,0:T(8,128)(2,1)} %param.14), channel_id=1, source_target_pairs={{0,8},{8,0},{16,24},{24,16},{1,9},{9,1},{17,25},{25,17},{2,10},{10... | collective-permute-start | bytes 6291464 | tf_op jit(solution)/shard_map/ppermute | solution.py:55
  12.6 94.8 %collective-permute-start.8 = (bf16[512,2048]{1,0:T(8,128)(2,1)}, bf16[512,2048]{1,0:T(8,128)(2,1)}, u32[]{:S(2)}, u32[]{:S(2)}) collective-permute-start(bf16[512,2048]{1,0:T(8,128)(2,1)} %param.14), channel_id=1, source_target_pairs={{0,16},{8,24},{16,0},{24,8},{1,17},{9,25},{17,1},{25,9},{2,18},{10... | collective-permute-start | bytes 6291464 | tf_op jit(solution)/shard_map/ppermute | solution.py:55
  33.4 53.2 %collective-permute-start = (bf16[7,128,384]{2,1,0:T(8,128)(2,1)}, bf16[7,128,384]{2,1,0:T(8,128)(2,1)}, u32[]{:S(2)}, u32[]{:S(2)}) collective-permute-start(bf16[7,128,384]{2,1,0:T(8,128)(2,1)} %get-tuple-element.131), channel_id=1, source_target_pairs={{0,2},{1,3},{2,0},{3,1},{4,6},{5,7},{6,4},{7,5},{8,10},{9,11},{10,... | collective-permute-start | bytes 2064392 | tf_op jit(solution)/shard_map/ppermute | solution.py:506
  35.0 53.3 %collective-permute-start.1 = (bf16[7,128,384]{2,1,0:T(8,128)(2,1)S(1)}, bf16[7,128,384]{2,1,0:T(8,128)(2,1)}, u32[]{:S(2)}, u32[]{:S(2)}) collective-permute-start(bf16[7,128,384]{2,1,0:T(8,128)(2,1)S(1)} %get-tuple-element.132), channel_id=1, source_target_pairs={{0,4},{1,5},{2,6},{3,7},{4,0},{5,1},{6,2},{7,3},{8,12},{9,13},{10,... | collective-permute-start | bytes 2064392 | tf_op jit(solution)/shard_map/ppermute | solution.py:506
  42.6 60.6 %collective-permute-start.2 = (bf16[7,128,384]{2,1,0:T(8,128)(2,1)S(1)}, bf16[7,128,384]{2,1,0:T(8,128)(2,1)S(1)}, u32[]{:S(2)}, u32[]{:S(2)}) collective-permute-start(bf16[7,128,384]{2,1,0:T(8,128)(2,1)S(1)} %get-tuple-element.133), channel_id=1, source_target_pairs={{0,6},{1,7},{2,4},{3,5},{4,2},{5,3},{6,0},{7,1},{8,14},{9,15},{10,... | collective-permute-start | bytes 2064392 | tf_op jit(solution)/shard_map/ppermute | solution.py:506
  108.1 166.1 %all-gather.9.cloned.1.call-start = ((), (), s32[]{:S(2)}) async-start(), calls=%async_computation.5 | async-start | bytes 9437184 | tf_op jit(solution)/shard_map/all_gather | solution.py:646
  108.8 411.4 %reduce-scatter.4.cloned.1.call-start = ((), (), s32[]{:S(2)}) async-start(), calls=%async_computation.6 | async-start | bytes 9437184 | tf_op jit(solution)/shard_map/reduce_scatter | solution.py:679
  109.1 70.2 %collective-permute-start.17 = (bf16[512,2048]{1,0:T(8,128)(2,1)S(1)}, bf16[512,2048]{1,0:T(8,128)(2,1)}, u32[]{:S(2)}, u32[]{:S(2)}) collective-permute-start(bf16[512,2048]{1,0:T(8,128)(2,1)S(1)} %copy-done.20), channel_id=1, source_target_pairs={{0,24},{8,16},{16,8},{24,0},{1,25},{9,17},{17,9},{25,1},{2,26},{10... | collective-permute-start | bytes 6291464 | tf_op jit(solution)/shard_map/ppermute | solution.py:55
  127.0 48.3 %collective-permute-start.10 = (bf16[7,128,128]{2,1,0:T(8,128)(2,1)}, bf16[7,128,128]{2,1,0:T(8,128)(2,1)S(1)}, u32[]{:S(2)}, u32[]{:S(2)}) collective-permute-start(bf16[7,128,128]{2,1,0:T(8,128)(2,1)} %get-tuple-element.144), channel_id=1, source_target_pairs={{0,2},{1,3},{2,0},{3,1},{4,6},{5,7},{6,4},{7,5},{8,10},{9,11},{10,... | collective-permute-start | bytes 688136 | tf_op jit(solution)/shard_map/ppermute | solution.py:506
  193.5 38.1 %collective-permute-start.19 = (bf16[224,2048]{1,0:T(8,128)(2,1)S(1)}, bf16[224,2048]{1,0:T(8,128)(2,1)}, u32[]{:S(2)}, u32[]{:S(2)}) collective-permute-start(bf16[224,2048]{1,0:T(8,128)(2,1)S(1)} %multiply_convert_fusion), channel_id=1, source_target_pairs={{0,16},{8,24},{16,0},{24,8},{1,17},{9,25},{17,1},{25,9},{2,18},{10... | collective-permute-start | bytes 2752520 | tf_op jit(solution)/shard_map/ppermute | solution.py:55
  194.0 39.2 %collective-permute-start.20 = (bf16[224,2048]{1,0:T(8,128)(2,1)S(1)}, bf16[224,2048]{1,0:T(8,128)(2,1)}, u32[]{:S(2)}, u32[]{:S(2)}) collective-permute-start(bf16[224,2048]{1,0:T(8,128)(2,1)S(1)} %multiply_convert_fusion), channel_id=1, source_target_pairs={{0,24},{8,16},{16,8},{24,0},{1,25},{9,17},{17,9},{25,1},{2,26},{10... | collective-permute-start | bytes 2752520 | tf_op jit(solution)/shard_map/ppermute | solution.py:55
  264.6 255.6 %reduce-scatter.6.cloned.1.call-start = ((), (), s32[]{:S(2)}) async-start(), calls=%async_computation.7 | async-start | bytes 9437184 | tf_op jit(solution)/shard_map/reduce_scatter | solution.py:708
  305.6 33.7 %collective-permute-start.23 = (bf16[224,2048]{1,0:T(8,128)(2,1)}, bf16[224,2048]{1,0:T(8,128)(2,1)}, u32[]{:S(2)}, u32[]{:S(2)}) collective-permute-start(bf16[224,2048]{1,0:T(8,128)(2,1)} %convolution_convert_fusion.8), channel_id=1, source_target_pairs={{0,16},{8,24},{16,0},{24,8},{1,17},{9,25},{17,1},{25,9},{2,18},{10... | collective-permute-start | bytes 2752520 | tf_op jit(solution)/shard_map/ppermute | solution.py:55
  339.7 291.6 %reduce-scatter.8.cloned.1.call-start = ((), (), s32[]{:S(2)}) async-start(), calls=%async_computation.8 | async-start | bytes 7077888 | tf_op jit(solution)/shard_map/reduce_scatter | solution.py:763
  376.9 44.1 %collective-permute-start.31 = (bf16[224,2048]{1,0:T(8,128)(2,1)}, bf16[224,2048]{1,0:T(8,128)(2,1)S(1)}, u32[]{:S(2)}, u32[]{:S(2)}) collective-permute-start(bf16[224,2048]{1,0:T(8,128)(2,1)} %get-tuple-element.189), channel_id=1, source_target_pairs={{0,8},{8,0},{16,24},{24,16},{1,9},{9,1},{17,25},{25,17},{2,10},{10... | collective-permute-start | bytes 2752520 | tf_op jit(solution)/shard_map/ppermute | solution.py:55
  378.5 42.6 %collective-permute-start.32 = (bf16[224,2048]{1,0:T(8,128)(2,1)}, bf16[224,2048]{1,0:T(8,128)(2,1)}, u32[]{:S(2)}, u32[]{:S(2)}) collective-permute-start(bf16[224,2048]{1,0:T(8,128)(2,1)} %get-tuple-element.189), channel_id=1, source_target_pairs={{0,16},{8,24},{16,0},{24,8},{1,17},{9,25},{17,1},{25,9},{2,18},{10... | collective-permute-start | bytes 2752520 | tf_op jit(solution)/shard_map/ppermute | solution.py:55
  429.7 79.0 %collective-permute-start.38 = (bf16[224,2048]{1,0:T(8,128)(2,1)S(1)}, bf16[224,2048]{1,0:T(8,128)(2,1)S(1)}, u32[]{:S(2)}, u32[]{:S(2)}) collective-permute-start(bf16[224,2048]{1,0:T(8,128)(2,1)S(1)} %convolution_convert_fusion.5), channel_id=1, source_target_pairs={{0,8},{8,0},{16,24},{24,16},{1,9},{9,1},{17,25},{25,17},{2,10},{10... | collective-permute-start | bytes 2752520 | tf_op jit(solution)/shard_map/ppermute | solution.py:55
  431.5 77.2 %collective-permute-start.39 = (bf16[224,2048]{1,0:T(8,128)(2,1)S(1)}, bf16[224,2048]{1,0:T(8,128)(2,1)S(1)}, u32[]{:S(2)}, u32[]{:S(2)}) collective-permute-start(bf16[224,2048]{1,0:T(8,128)(2,1)S(1)} %convolution_convert_fusion.4), channel_id=1, source_target_pairs={{0,16},{8,24},{16,0},{24,8},{1,17},{9,25},{17,1},{25,9},{2,18},{10... | collective-permute-start | bytes 2752520 | tf_op jit(solution)/shard_map/ppermute | solution.py:55
  431.5 59.6 %collective-permute-start.35 = (bf16[7,128,384]{2,1,0:T(8,128)(2,1)S(1)}, bf16[7,128,384]{2,1,0:T(8,128)(2,1)S(1)}, u32[]{:S(2)}, u32[]{:S(2)}) collective-permute-start(bf16[7,128,384]{2,1,0:T(8,128)(2,1)S(1)} %get-tuple-element.202), channel_id=1, source_target_pairs={{0,2},{1,3},{2,0},{3,1},{4,6},{5,7},{6,4},{7,5},{8,10},{9,11},{10,... | collective-permute-start | bytes 2064392 | tf_op jit(solution)/shard_map/ppermute | solution.py:506
  442.8 50.3 %collective-permute-start.36 = (bf16[7,128,384]{2,1,0:T(8,128)(2,1)S(1)}, bf16[7,128,384]{2,1,0:T(8,128)(2,1)S(1)}, u32[]{:S(2)}, u32[]{:S(2)}) collective-permute-start(bf16[7,128,384]{2,1,0:T(8,128)(2,1)S(1)} %get-tuple-element.203), channel_id=1, source_target_pairs={{0,4},{1,5},{2,6},{3,7},{4,0},{5,1},{6,2},{7,3},{8,12},{9,13},{10,... | collective-permute-start | bytes 2064392 | tf_op jit(solution)/shard_map/ppermute | solution.py:506
  445.6 63.1 %collective-permute-start.37 = (bf16[7,128,384]{2,1,0:T(8,128)(2,1)S(1)}, bf16[7,128,384]{2,1,0:T(8,128)(2,1)S(1)}, u32[]{:S(2)}, u32[]{:S(2)}) collective-permute-start(bf16[7,128,384]{2,1,0:T(8,128)(2,1)S(1)} %get-tuple-element.204), channel_id=1, source_target_pairs={{0,6},{1,7},{2,4},{3,5},{4,2},{5,3},{6,0},{7,1},{8,14},{9,15},{10,... | collective-permute-start | bytes 2064392 | tf_op jit(solution)/shard_map/ppermute | solution.py:506
  520.3 199.3 %all-gather.11.cloned.1.call-start = ((), (), s32[]{:S(2)}) async-start(), calls=%async_computation.9 | async-start | bytes 7077888 | tf_op jit(solution)/shard_map/all_gather | solution.py:797
  555.6 40.1 %collective-permute-start.47 = (bf16[64,2048]{1,0:T(8,128)(2,1)S(1)}, bf16[64,2048]{1,0:T(8,128)(2,1)S(1)}, u32[]{:S(2)}, u32[]{:S(2)}) collective-permute-start(bf16[64,2048]{1,0:T(8,128)(2,1)S(1)} %get-tuple-element.278), channel_id=1, source_target_pairs={{0,2},{1,3},{2,0},{3,1},{4,6},{5,7},{6,4},{7,5},{8,10},{9,11},{10,... | collective-permute-start | bytes 786440 | tf_op jit(solution)/shard_map/ppermute | solution.py:506
  578.2 36.6 %collective-permute-start.44 = (bf16[224,2048]{1,0:T(8,128)(2,1)}, bf16[224,2048]{1,0:T(8,128)(2,1)S(1)}, u32[]{:S(2)}, u32[]{:S(2)}) collective-permute-start(bf16[224,2048]{1,0:T(8,128)(2,1)} %fusion.15), channel_id=1, source_target_pairs={{0,8},{8,0},{16,24},{24,16},{1,9},{9,1},{17,25},{25,17},{2,10},{10... | collective-permute-start | bytes 2752520 | tf_op jit(solution)/shard_map/ppermute | solution.py:55
  578.8 41.1 %collective-permute-start.45 = (bf16[224,2048]{1,0:T(8,128)(2,1)}, bf16[224,2048]{1,0:T(8,128)(2,1)}, u32[]{:S(2)}, u32[]{:S(2)}) collective-permute-start(bf16[224,2048]{1,0:T(8,128)(2,1)} %fusion.16), channel_id=1, source_target_pairs={{0,16},{8,24},{16,0},{24,8},{1,17},{9,25},{17,1},{25,9},{2,18},{10... | collective-permute-start | bytes 2752520 | tf_op jit(solution)/shard_map/ppermute | solution.py:55
  580.2 39.6 %collective-permute-start.46 = (bf16[224,2048]{1,0:T(8,128)(2,1)}, bf16[224,2048]{1,0:T(8,128)(2,1)}, u32[]{:S(2)}, u32[]{:S(2)}) collective-permute-start(bf16[224,2048]{1,0:T(8,128)(2,1)} %fusion.17), channel_id=1, source_target_pairs={{0,24},{8,16},{16,8},{24,0},{1,25},{9,17},{17,9},{25,1},{2,26},{10... | collective-permute-start | bytes 2752520 | tf_op jit(solution)/shard_map/ppermute | solution.py:55
  643.6 36.4 %collective-permute-start.52 = (bf16[224,2048]{1,0:T(8,128)(2,1)S(1)}, bf16[224,2048]{1,0:T(8,128)(2,1)S(1)}, u32[]{:S(2)}, u32[]{:S(2)}) collective-permute-start(bf16[224,2048]{1,0:T(8,128)(2,1)S(1)} %add_convert_fusion.1), channel_id=1, source_target_pairs={{0,8},{8,0},{16,24},{24,16},{1,9},{9,1},{17,25},{25,17},{2,10},{10... | collective-permute-start | bytes 2752520 | tf_op jit(solution)/shard_map/ppermute | solution.py:55
  644.7 36.3 %collective-permute-start.53 = (bf16[224,2048]{1,0:T(8,128)(2,1)S(1)}, bf16[224,2048]{1,0:T(8,128)(2,1)S(1)}, u32[]{:S(2)}, u32[]{:S(2)}) collective-permute-start(bf16[224,2048]{1,0:T(8,128)(2,1)S(1)} %add_convert_fusion.1), channel_id=1, source_target_pairs={{0,16},{8,24},{16,0},{24,8},{1,17},{9,25},{17,1},{25,9},{2,18},{10... | collective-permute-start | bytes 2752520 | tf_op jit(solution)/shard_map/ppermute | solution.py:55
  646.2 34.9 %collective-permute-start.54 = (bf16[224,2048]{1,0:T(8,128)(2,1)S(1)}, bf16[224,2048]{1,0:T(8,128)(2,1)S(1)}, u32[]{:S(2)}, u32[]{:S(2)}) collective-permute-start(bf16[224,2048]{1,0:T(8,128)(2,1)S(1)} %add_convert_fusion.1), channel_id=1, source_target_pairs={{0,24},{8,16},{16,8},{24,0},{1,25},{9,17},{17,9},{25,1},{2,26},{10... | collective-permute-start | bytes 2752520 | tf_op jit(solution)/shard_map/ppermute | solution.py:55
  681.0 34.9 %collective-permute-start.55 = (bf16[224,2048]{1,0:T(8,128)(2,1)S(1)}, bf16[224,2048]{1,0:T(8,128)(2,1)S(1)}, u32[]{:S(2)}, u32[]{:S(2)}) collective-permute-start(bf16[224,2048]{1,0:T(8,128)(2,1)S(1)} %copy-done.19), channel_id=1, source_target_pairs={{0,24},{8,16},{16,8},{24,0},{1,25},{9,17},{17,9},{25,1},{2,26},{10... | collective-permute-start | bytes 2752520 | tf_op jit(solution)/shard_map/ppermute | solution.py:55
  (104 other events, 2208.9 us)
Sparse Core Ops, SparseCore 0:
  10.2 73.0 all-gather.4
  108.2 78.8 all-gather.6
  188.7 85.3 all-gather.8
  276.3 89.7 reduce-scatter.3
  368.2 117.5 reduce-scatter.5
  520.4 105.1 reduce-scatter.7
  631.5 88.0 all-gather.10

commit v7 on v6

--- a/solution.py
+++ b/solution.py
@@ -517,15 +517,38 @@
         ]
         return lax.ppermute(values, "seq", pairs)
 
+    block = D // seq_count
+    z_groups = [[h * members + m for h in range(heads)] for m in range(members)]
+
+    def member_columns(values):
+        parts = []
+        for step in range(members):
+            whose = (member + members - step) % members
+            columns = [
+                lax.dynamic_slice_in_dim(values, (h * members + whose) * block, block, 1)
+                for h in range(heads)
+            ]
+            parts.append(jnp.concatenate(columns, axis=1))
+        return parts
+
+    def member_sum(parts, product):
+        sent = [among(product(parts[step]).astype(bf16), step) for step in range(1, members)]
+        return sum([v.astype(f32) for v in sent], product(parts[0]).astype(f32)).astype(bf16)
+
+    def scatter_z(values, axis):
+        return lax.psum_scatter(
+            values, "seq", scatter_dimension=axis, tiled=True, axis_index_groups=z_groups
+        )
+
     def scatter_members(values):
         size = values.shape[0] // members
 
-        def block(number):
+        def piece(number):
             return lax.dynamic_slice_in_dim(values, number * size, size, 0)
 
-        total = block(member).astype(f32)
+        total = piece(member).astype(f32)
         for step in range(1, members):
-            sent = block((member + members - step) % members)
+            sent = piece((member + members - step) % members)
             total = total + among(sent, step).astype(f32)
         return total.astype(bf16)
 
@@ -636,15 +659,15 @@
             values = values + flip(values, "seq", seq_count, bit)
         return values
 
-    pooled = hop(pooled[:SEQS], hops[:-2])
+    pooled = pooled[:SEQS]
     early = (slots, other_slots, out_slots[:-1], w_up[:, half:], w_down)
-    early = early + (hat_own, inverse_own, cotangent_rel, pooled)
+    early = early + (hat_own, inverse_own, cotangent_rel, pooled, member_columns(cotangent_rel))
     early = lax.optimization_barrier(early)
     slots, other_slots, out_slots[:-1], own_up, own_down = early[:5]
-    hat_own, inverse_own, cotangent_rel, pooled = early[5:]
+    hat_own, inverse_own, cotangent_rel, pooled, cotangent_parts = early[5:]
     second_up = lax.all_gather(own_up, "seq", axis=0, tiled=True)
     full_down = lax.all_gather(own_down, "seq", axis=1, tiled=True)
-    pooled = hop(pooled, hops[-2:-1])
+    pooled = hop(pooled, hops[:-1])
     full_out = jnp.concatenate(out_slots, axis=0)
     mixed_slots, logs = attend_forward(scal, slots, other_slots, heads, members)
     mixed_slots = [across(v, slot) if slot else v for slot, v in enumerate(mixed_slots)]
@@ -670,19 +693,21 @@
     upward = dot(normed_two, full_up)
     kept = jnp.maximum(upward, 0.0)
     active = (jnp.square(kept) * ffn_live).astype(bf16)
-    grad_down_part = contract(active, cotangent_rel, 0, 0).astype(bf16)
+    grad_down_part = member_sum(cotangent_parts, lambda v: contract(active, v, 0, 0))
     cotangent_rel, kept, grad_down_part = lax.optimization_barrier(
         (cotangent_rel, kept, grad_down_part)
     )
     grad_active = contract(cotangent_rel, full_down, 1, 1).astype(bf16)
     grad_upward = (grad_active.astype(f32) * ffn_live * 2.0 * kept).astype(bf16)
-    grad_down = lax.psum_scatter(grad_down_part, "seq", scatter_dimension=1, tiled=True)
+    grad_down = scatter_z(grad_down_part, 1)
     two_parts = [
         contract(grad_upward[slot * share : (slot + 1) * share], full_up, 1, 1)
         for slot in range(head_count)
     ]
     two_parts = scatter_heads(two_parts)
-    grad_up_part = contract(normed_two, grad_upward, 0, 0).astype(bf16)
+    grad_up_parts = [
+        contract(v, grad_upward, 0, 0).astype(bf16) for v in member_columns(normed_two)
+    ]
 
     pooled = pooled * lax.rsqrt(seq_length)[:, None]
     logits = jnp.dot(pooled, w_router, precision=highest, preferred_element_type=f32)
@@ -702,10 +727,11 @@
     grad_pooled_own = jnp.dot(
         member_own, grad_pooled, precision=highest, preferred_element_type=f32
     )
-    two_parts, grad_up_part, grad_router, grad_pooled_own = lax.optimization_barrier(
-        (two_parts, grad_up_part, grad_router, grad_pooled_own)
-    )
-    grad_up = lax.psum_scatter(grad_up_part, "seq", scatter_dimension=0, tiled=True)
+    two_parts, grad_up_parts, grad_router, grad_pooled_own = lax.optimization_barrier(
+        (two_parts, grad_up_parts, grad_router, grad_pooled_own)
+    )
+    grad_up_part = member_sum(grad_up_parts, lambda v: v)
+    grad_up = scatter_z(grad_up_part, 0)
 
     grad_two = sum([v.astype(f32) for v in two_parts[1:]], two_parts[0])
     back_two, gain_two = normalize_back(grad_two, hat_two, inverse_two, gain_ffn)

time: 742 us -> 729 us (0.982)
  waiting for transfers between devices: 292 us -> 282 us
    dot_general x22 -> x24, matrix products: 98.5 us -> 87.9 us  [contract(): lax.dot_general(left, right, (((left_dim,), (right_dim,)), ((), ())), pre...]
    ppermute x18, waiting for transfers between devices: 189 us -> 179 us  [across(): return lax.ppermute(values, 'seq', pairs)]
    dot_general x6, matrix products: 28 us -> 36.4 us  [dot(): return jnp.dot(left, right, preferred_element_type=f32)]
  transfers between devices with their start and end apart: 70 -> 72, of which waited for: 35 -> 34; matrix products, arithmetic and copies ran while one was open for 27% -> 28% of each run, Pallas kernels for 8% -> 8%
where the time goes in v7:
time: 729 us; the launch traced here: 721 us
  waiting for transfers between devices  282 us (39%)
  starting transfers between devices  154 us (21%)
  matrix products  128 us (18%)
  Pallas kernels  55.4 us (8%)
  other arithmetic  52.1 us (7%)
  local copies, waits for them, and re-layouts  33 us (5%)
  between operations  16.1 us (2%)
    ppermute x18, waiting for transfers between devices, across(): return lax.ppermute(values, 'seq', pairs)  179 us
    dot_general x24, matrix products, contract(): lax.dot_general(left, right, (((left_dim,), (right_dim,)), ((), ())), pre...  87.9 us
    ppermute x38, waiting for transfers between devices, flip(): return lax.ppermute(values, axis, [(i, i ^ bit) for i in range(size)])  85.2 us
    ppermute x18, starting transfers between devices, across(): return lax.ppermute(values, 'seq', pairs)  77.8 us
    ppermute x38, starting transfers between devices, flip(): return lax.ppermute(values, axis, [(i, i ^ bit) for i in range(size)])  73.9 us
    dot_general x6, matrix products, dot(): return jnp.dot(left, right, preferred_element_type=f32)  36.4 us
    pallas_call x1, Pallas kernels, attend_backward(): pl.pallas_call(functools.partial(back_kernel, heads, members), out_shape=...  20.9 us
    pallas_call x1, Pallas kernels, project(): pl.pallas_call(functools.partial(project_kernel, heads), out_shape=[jax.S...  16.3 us
  transfers between devices with their start and end apart: 72, of which 34 were waited for; matrix products, arithmetic and copies ran while one was open for 28% of the time, Pallas kernels for 8%

profile of v7, /device:TPU:0, one launch (start us, length us, event | category | flops | bytes accessed | tf_op | source)
XLA Modules:
  0.0 721.1 jit_solution(8564561586185149973)
XLA Ops:
  17.0 16.3 %project.1 = (bf16[7,128,384]{2,1,0:T(8,128)(2,1)S(1)}, bf16[7,128,384]{2,1,0:T(8,128)(2,1)}, bf16[7,128,384]{2,1,0:T(8,128)(2,1)S(1)}, bf16[7,128,384]{2,1,0:T(...) custom-call(s32[7]{0:T(128)S(1)} %pad_add_fusion.scal, bf16[896,2048]{1,0:T(8,128)(2,1)} %tokens.1, ...), custom_call_target="tpu_custom_call" | custom-call | flops 5637144576 | bytes 16777216 | tf_op jit(solution)/shard_map/project/pallas_call | solution.py:402
  42.6 43.9 %collective-permute-done.refs_1_ = bf16[7,128,384]{2,1,0:T(8,128)(2,1)S(1)} collective-permute-done((bf16[7,128,384]{2,1,0:T(8,128)(2,1)}, bf16[7,128,384]{2,1,0:T(8,128)(2,1)S(1)}, u32[]{:S(2)}, u32[]{:S(2)}) %collective-permute-start) | collective-permute-done | bytes 688160 | tf_op jit(solution)/shard_map/ppermute | solution.py:506
  90.2 13.1 %collective-permute-done.2.refs_3_ = bf16[7,128,384]{2,1,0:T(8,128)(2,1)} collective-permute-done((bf16[7,128,384]{2,1,0:T(8,128)(2,1)S(1)}, bf16[7,128,384]{2,1,0:T(8,128)(2,1)}, u32[]{:S(2)}, u32[]{:S(2)}) %collective-permute-start.2) | collective-permute-done | bytes 688160 | tf_op jit(solution)/shard_map/ppermute | solution.py:506
  110.4 15.5 %attend_forward.1 = (bf16[7,128,128]{2,1,0:T(8,128)(2,1)}, bf16[7,128,128]{2,1,0:T(8,128)(2,1)}, bf16[7,128,128]{2,1,0:T(8,128)(2,1)}, bf16[7,128,128]{2,1,0:T(8,128)(2,1)}, f32[4,7,1,128]{3,2,1,0:T(1,128)}) custom-call(s32[7]{0:T(128)} %copy-done.6, bf16[7,128,384]{2,1,0:T(8,128)(2,1)} %copy-done.8, bf16[7,128,384]{2,1,0:T(8,128)(2,1)} %copy-done.55, ...), custom_call_target="tpu_custom_call" | custom-call | flops 4000000000 | bytes 7340032 | tf_op jit(solution)/shard_map/attend_forward/pallas_call | solution.py:185
  125.9 14.4 %collective-permute-start.10 = (bf16[7,128,128]{2,1,0:T(8,128)(2,1)}, bf16[7,128,128]{2,1,0:T(8,128)(2,1)S(1)}, u32[]{:S(2)}, u32[]{:S(2)}) collective-permute-start(bf16[7,128,128]{2,1,0:T(8,128)(2,1)} %get-tuple-element.148), channel_id=1, source_target_pairs={{0,4},{1,5},{2,6},{3,7},{4,0},{5,1},{6,2},{7,3},{8,12},{9,13},{10,... | collective-permute-start | bytes 688136 | tf_op jit(solution)/shard_map/ppermute | solution.py:506
  149.0 24.8 %collective-permute-done.13 = f32[5,2048]{1,0:T(8,128)S(1)} collective-permute-done((f32[5,2048]{1,0:T(8,128)S(1)}, f32[5,2048]{1,0:T(8,128)S(1)}, u32[]{:S(2)}, u32[]{:S(2)}) %collective-permute-start.13) | collective-permute-done | bytes 40992 | tf_op jit(solution)/shard_map/ppermute | solution.py:55
  194.3 11.0 %collective-permute-start.21 = (f32[5,2048]{1,0:T(8,128)S(1)}, f32[5,2048]{1,0:T(8,128)S(1)}, u32[]{:S(2)}, u32[]{:S(2)}) collective-permute-start(f32[5,2048]{1,0:T(8,128)S(1)} %add.433), channel_id=1, source_target_pairs={{0,4},{1,5},{2,6},{3,7},{4,0},{5,1},{6,2},{7,3},{8,12},{9,13},{10,... | collective-permute-start | bytes 122888 | tf_op jit(solution)/shard_map/ppermute | solution.py:55
  205.4 9.1 %collective-permute-done.21 = f32[5,2048]{1,0:T(8,128)S(1)} collective-permute-done((f32[5,2048]{1,0:T(8,128)S(1)}, f32[5,2048]{1,0:T(8,128)S(1)}, u32[]{:S(2)}, u32[]{:S(2)}) %collective-permute-start.21) | collective-permute-done | bytes 40992 | tf_op jit(solution)/shard_map/ppermute | solution.py:55
  214.5 8.3 %pad_maximum_fusion = bf16[2048,2048]{1,0:T(8,128)(2,1)} fusion(bf16[2048,1024]{1,0:T(8,128)(2,1)} %all-gather.7.cloned.1.call-done, bf16[2048,1024]{1,0:T(8,128)(2,1)} %all-gather.5.cloned.1.call-done), kind=kLoop, calls=%fused_computation.2 | loop fusion | flops 16777216 | bytes 16777216 | tf_op jit(solution)/shard_map/concatenate | solution.py:690
  222.9 7.5 %collective-permute-done.19 = bf16[224,2048]{1,0:T(8,128)(2,1)} collective-permute-done((bf16[224,2048]{1,0:T(8,128)(2,1)S(1)}, bf16[224,2048]{1,0:T(8,128)(2,1)}, u32[]{:S(2)}, u32[]{:S(2)}) %collective-permute-start.19) | collective-permute-done | bytes 917536 | tf_op jit(solution)/shard_map/ppermute | solution.py:55
  236.0 13.1 %fusion = (bf16[896,2048]{1,0:T(8,128)(2,1)S(1)}, f32[896,2048]{1,0:T(8,128)}) fusion(s32[2048]{0:T(1024)S(1)} %iota_add_fusion, s32[896]{0:T(1024)S(1)} %add_multiply_fusion, bf16[896,2048]{1,0:T(8,128)(2,1)S(1)} %constant_dynamic-update-slice_fusion.4, bf16[2048,2048]{1,0:T(8,128)(2,1)} %pad_maximum_fusion), kind=kOutput, calls=%fused_computation.6 | convolution fusion | flops 7525367808 | bytes 23080448 | tf_op jit(solution)/shard_map/dot_general | solution.py:29
  261.9 6.3 add_convert_fusion.1
  272.7 13.4 %fusion.3 = bf16[896,2048]{1,0:T(8,128)(2,1)S(1)} fusion(f32[896,2048]{1,0:T(8,128)} %get-tuple-element.170, s32[2048]{0:T(1024)S(1)} %iota_add_fusion, s32[896]{0:T(1024)S(1)} %add_multiply_fusion, bf16[896,2048]{1,0:T(8,128)(2,1)} %copy-done.12, bf16[2048,2048]{1,0:T(8,128)(2,1)} %all-gather.9.cloned.1.call-done), kind=kOutput, calls=%fused_computation.9 | convolution fusion | flops 7529037824 | bytes 23080448 | tf_op jit(solution)/shard_map/dot_general | solution.py:33
  286.1 6.2 convolution_convert_fusion.8
  305.0 6.7 convolution_convert_fusion.1
  319.9 15.6 %collective-permute-done.24 = bf16[224,2048]{1,0:T(8,128)(2,1)S(1)} collective-permute-done((bf16[224,2048]{1,0:T(8,128)(2,1)S(1)}, bf16[224,2048]{1,0:T(8,128)(2,1)S(1)}, u32[]{:S(2)}, u32[]{:S(2)}) %collective-permute-start.24) | collective-permute-done | bytes 917536 | tf_op jit(solution)/shard_map/ppermute | solution.py:55
  339.0 6.3 convolution_convert_fusion.7
  359.4 6.7 convolution_convert_fusion.6
  375.6 7.1 fusion.89
  383.4 8.6 %collective-permute-done.29.refs_9_ = bf16[7,128,128]{2,1,0:T(8,128)(2,1)S(1)} collective-permute-done((bf16[7,128,128]{2,1,0:T(8,128)(2,1)S(1)}, bf16[7,128,128]{2,1,0:T(8,128)(2,1)S(1)}, u32[]{:S(2)}, u32[]{:S(2)}) %collective-permute-start.29) | collective-permute-done | bytes 229408 | tf_op jit(solution)/shard_map/ppermute | solution.py:506
  391.9 13.9 %collective-permute-done.30.refs_10_ = bf16[7,128,128]{2,1,0:T(8,128)(2,1)S(1)} collective-permute-done((bf16[7,128,128]{2,1,0:T(8,128)(2,1)S(1)}, bf16[7,128,128]{2,1,0:T(8,128)(2,1)S(1)}, u32[]{:S(2)}, u32[]{:S(2)}) %collective-permute-start.30) | collective-permute-done | bytes 229408 | tf_op jit(solution)/shard_map/ppermute | solution.py:506
  406.6 20.9 %attend_backward.1 = (bf16[7,128,384]{2,1,0:T(8,128)(2,1)}, bf16[7,128,384]{2,1,0:T(8,128)(2,1)}, bf16[7,128,384]{2,1,0:T(8,128)(2,1)}, bf16[7,128,384]{2,1,0:T(8,128)(2,1)}, bf16[4,7,128,384]{3,2,1,0:T(8,128)(2,1)}) custom-call(s32[7]{0:T(128)} %copy-done.6, bf16[7,128,384]{2,1,0:T(8,128)(2,1)} %copy-done.8, bf16[7,128,384]{2,1,0:T(8,128)(2,1)} %copy-done.55, ...), custom_call_target="tpu_custom_call" | custom-call | flops 10000000000 | bytes 12582912 | tf_op jit(solution)/shard_map/attend_backward/pallas_call | solution.py:311
  436.2 18.2 %collective-permute-start.36 = (bf16[7,128,384]{2,1,0:T(8,128)(2,1)S(1)}, bf16[7,128,384]{2,1,0:T(8,128)(2,1)S(1)}, u32[]{:S(2)}, u32[]{:S(2)}) collective-permute-start(bf16[7,128,384]{2,1,0:T(8,128)(2,1)S(1)} %get-tuple-element.207), channel_id=1, source_target_pairs={{0,2},{1,3},{2,0},{3,1},{4,6},{5,7},{6,4},{7,5},{8,10},{9,11},{10,... | collective-permute-start | bytes 2064392 | tf_op jit(solution)/shard_map/ppermute | solution.py:506
  460.3 21.9 %collective-permute-done.36.refs_1_ = bf16[7,128,384]{2,1,0:T(8,128)(2,1)S(1)} collective-permute-done((bf16[7,128,384]{2,1,0:T(8,128)(2,1)S(1)}, bf16[7,128,384]{2,1,0:T(8,128)(2,1)S(1)}, u32[]{:S(2)}, u32[]{:S(2)}) %collective-permute-start.36) | collective-permute-done | bytes 688160 | tf_op jit(solution)/shard_map/ppermute | solution.py:506
  484.9 18.1 %collective-permute-done.37.refs_2_ = bf16[7,128,384]{2,1,0:T(8,128)(2,1)S(1)} collective-permute-done((bf16[7,128,384]{2,1,0:T(8,128)(2,1)S(1)}, bf16[7,128,384]{2,1,0:T(8,128)(2,1)S(1)}, u32[]{:S(2)}, u32[]{:S(2)}) %collective-permute-start.37) | collective-permute-done | bytes 688160 | tf_op jit(solution)/shard_map/ppermute | solution.py:506
  505.9 8.7 %convolution_convert_fusion = bf16[2048,1536]{1,0:T(8,128)(2,1)} fusion(bf16[896,2048]{1,0:T(8,128)(2,1)S(1)} %copy-done.65, bf16[896,1536]{1,0:T(8,128)(2,1)S(1)} %gather_grads.1), kind=kOutput, calls=%fused_computation.5 | convolution fusion | flops 5640290304 | bytes 12713984 | tf_op jit(solution)/shard_map/dot_general | solution.py:33
  550.6 13.8 %collective-permute-start.49 = (bf16[64,2048]{1,0:T(8,128)(2,1)S(1)}, bf16[64,2048]{1,0:T(8,128)(2,1)S(1)}, u32[]{:S(2)}, u32[]{:S(2)}) collective-permute-start(bf16[64,2048]{1,0:T(8,128)(2,1)S(1)} %get-tuple-element.300), channel_id=1, source_target_pairs={{0,2},{1,3},{2,0},{3,1},{4,6},{5,7},{6,4},{7,5},{8,10},{9,11},{10,... | collective-permute-start | bytes 786440 | tf_op jit(solution)/shard_map/ppermute | solution.py:506
  567.9 14.4 %collective-permute-done.49 = bf16[64,2048]{1,0:T(8,128)(2,1)S(1)} collective-permute-done((bf16[64,2048]{1,0:T(8,128)(2,1)S(1)}, bf16[64,2048]{1,0:T(8,128)(2,1)S(1)}, u32[]{:S(2)}, u32[]{:S(2)}) %collective-permute-start.49) | collective-permute-done | bytes 262176 | tf_op jit(solution)/shard_map/ppermute | solution.py:506
  584.8 12.8 %collective-permute-done.50 = bf16[64,2048]{1,0:T(8,128)(2,1)} collective-permute-done((bf16[64,2048]{1,0:T(8,128)(2,1)}, bf16[64,2048]{1,0:T(8,128)(2,1)}, u32[]{:S(2)}, u32[]{:S(2)}) %collective-permute-start.50) | collective-permute-done | bytes 262176 | tf_op jit(solution)/shard_map/ppermute | solution.py:506
  618.0 8.3 %collective-permute-start.58 = (bf16[64,2048]{1,0:T(8,128)(2,1)S(1)}, bf16[64,2048]{1,0:T(8,128)(2,1)S(1)}, u32[]{:S(2)}, u32[]{:S(2)}) collective-permute-start(bf16[64,2048]{1,0:T(8,128)(2,1)S(1)} %add_convert_fusion.5), channel_id=1, source_target_pairs={{0,2},{1,3},{2,0},{3,1},{4,6},{5,7},{6,4},{7,5},{8,10},{9,11},{10,... | collective-permute-start | bytes 786440 | tf_op jit(solution)/shard_map/ppermute | solution.py:506
  636.7 29.6 %collective-permute-done.59 = bf16[64,2048]{1,0:T(8,128)(2,1)S(1)} collective-permute-done((bf16[64,2048]{1,0:T(8,128)(2,1)S(1)}, bf16[64,2048]{1,0:T(8,128)(2,1)S(1)}, u32[]{:S(2)}, u32[]{:S(2)}) %collective-permute-start.59) | collective-permute-done | bytes 262176 | tf_op jit(solution)/shard_map/ppermute | solution.py:506
  674.7 15.8 %collective-permute-start.63 = (f32[2,2048]{1,0:T(2,128)S(1)}, f32[2,2048]{1,0:T(2,128)S(1)}, u32[]{:S(2)}, u32[]{:S(2)}) collective-permute-start(f32[2,2048]{1,0:T(2,128)S(1)} %add.486), channel_id=1, source_target_pairs={{0,2},{1,3},{2,0},{3,1},{4,6},{5,7},{6,4},{7,5},{8,10},{9,11},{10,... | collective-permute-start | bytes 49160 | tf_op jit(solution)/shard_map/ppermute | solution.py:55
  (406 shorter events, 255.1 us)
Async XLA Ops:
  7.2 207.3 %all-gather.5.cloned.1.call-start = ((), (), s32[]{:S(2)}) async-start(), calls=%async_computation.3 | async-start | bytes 4718592 | tf_op jit(solution)/shard_map/all_gather | solution.py:613
  9.5 205.0 %all-gather.7.cloned.1.call-start = ((), (), s32[]{:S(2)}) async-start(), calls=%async_computation.4 | async-start | bytes 4718592 | tf_op jit(solution)/shard_map/all_gather | solution.py:668
  9.6 97.2 %collective-permute-start.7 = (bf16[512,2048]{1,0:T(8,128)(2,1)}, bf16[512,2048]{1,0:T(8,128)(2,1)}, u32[]{:S(2)}, u32[]{:S(2)}) collective-permute-start(bf16[512,2048]{1,0:T(8,128)(2,1)} %param.14), channel_id=1, source_target_pairs={{0,8},{8,0},{16,24},{24,16},{1,9},{9,1},{17,25},{25,17},{2,10},{10... | collective-permute-start | bytes 6291464 | tf_op jit(solution)/shard_map/ppermute | solution.py:55
  12.6 94.2 %collective-permute-start.8 = (bf16[512,2048]{1,0:T(8,128)(2,1)}, bf16[512,2048]{1,0:T(8,128)(2,1)}, u32[]{:S(2)}, u32[]{:S(2)}) collective-permute-start(bf16[512,2048]{1,0:T(8,128)(2,1)} %param.14), channel_id=1, source_target_pairs={{0,16},{8,24},{16,0},{24,8},{1,17},{9,25},{17,1},{25,9},{2,18},{10... | collective-permute-start | bytes 6291464 | tf_op jit(solution)/shard_map/ppermute | solution.py:55
  33.3 53.2 %collective-permute-start = (bf16[7,128,384]{2,1,0:T(8,128)(2,1)}, bf16[7,128,384]{2,1,0:T(8,128)(2,1)S(1)}, u32[]{:S(2)}, u32[]{:S(2)}) collective-permute-start(bf16[7,128,384]{2,1,0:T(8,128)(2,1)} %get-tuple-element.134), channel_id=1, source_target_pairs={{0,2},{1,3},{2,0},{3,1},{4,6},{5,7},{6,4},{7,5},{8,10},{9,11},{10,... | collective-permute-start | bytes 2064392 | tf_op jit(solution)/shard_map/ppermute | solution.py:506
  35.0 54.6 %collective-permute-start.1 = (bf16[7,128,384]{2,1,0:T(8,128)(2,1)S(1)}, bf16[7,128,384]{2,1,0:T(8,128)(2,1)}, u32[]{:S(2)}, u32[]{:S(2)}) collective-permute-start(bf16[7,128,384]{2,1,0:T(8,128)(2,1)S(1)} %get-tuple-element.135), channel_id=1, source_target_pairs={{0,4},{1,5},{2,6},{3,7},{4,0},{5,1},{6,2},{7,3},{8,12},{9,13},{10,... | collective-permute-start | bytes 2064392 | tf_op jit(solution)/shard_map/ppermute | solution.py:506
  37.5 65.7 %collective-permute-start.2 = (bf16[7,128,384]{2,1,0:T(8,128)(2,1)S(1)}, bf16[7,128,384]{2,1,0:T(8,128)(2,1)}, u32[]{:S(2)}, u32[]{:S(2)}) collective-permute-start(bf16[7,128,384]{2,1,0:T(8,128)(2,1)S(1)} %get-tuple-element.136), channel_id=1, source_target_pairs={{0,6},{1,7},{2,4},{3,5},{4,2},{5,3},{6,0},{7,1},{8,14},{9,15},{10,... | collective-permute-start | bytes 2064392 | tf_op jit(solution)/shard_map/ppermute | solution.py:506
  106.8 166.0 %all-gather.9.cloned.1.call-start = ((), (), s32[]{:S(2)}) async-start(), calls=%async_computation.5 | async-start | bytes 9437184 | tf_op jit(solution)/shard_map/all_gather | solution.py:669
  107.5 407.1 %reduce-scatter.4.cloned.1.call-start = ((), (), s32[]{:S(2)}) async-start(), calls=%async_computation.6 | async-start | bytes 5242880 | tf_op jit(solution)/shard_map/reduce_scatter | solution.py:539
  107.8 70.1 %collective-permute-start.17 = (bf16[512,2048]{1,0:T(8,128)(2,1)}, bf16[512,2048]{1,0:T(8,128)(2,1)S(1)}, u32[]{:S(2)}, u32[]{:S(2)}) collective-permute-start(bf16[512,2048]{1,0:T(8,128)(2,1)} %param.14), channel_id=1, source_target_pairs={{0,24},{8,16},{16,8},{24,0},{1,25},{9,17},{17,9},{25,1},{2,26},{10... | collective-permute-start | bytes 6291464 | tf_op jit(solution)/shard_map/ppermute | solution.py:55
  110.3 34.7 %collective-permute-start.12 = (f32[5,2048]{1,0:T(8,128)S(1)}, f32[5,2048]{1,0:T(8,128)S(1)}, u32[]{:S(2)}, u32[]{:S(2)}) collective-permute-start(f32[5,2048]{1,0:T(8,128)S(1)} %bitcast.102), channel_id=1, source_target_pairs={{0,1},{1,0},{2,3},{3,2},{4,5},{5,4},{6,7},{7,6},{8,9},{9,8},{10,11... | collective-permute-start | bytes 122888 | tf_op jit(solution)/shard_map/ppermute | solution.py:55
  125.9 47.9 %collective-permute-start.10 = (bf16[7,128,128]{2,1,0:T(8,128)(2,1)}, bf16[7,128,128]{2,1,0:T(8,128)(2,1)S(1)}, u32[]{:S(2)}, u32[]{:S(2)}) collective-permute-start(bf16[7,128,128]{2,1,0:T(8,128)(2,1)} %get-tuple-element.148), channel_id=1, source_target_pairs={{0,4},{1,5},{2,6},{3,7},{4,0},{5,1},{6,2},{7,3},{8,12},{9,13},{10,... | collective-permute-start | bytes 688136 | tf_op jit(solution)/shard_map/ppermute | solution.py:506
  192.2 38.1 %collective-permute-start.19 = (bf16[224,2048]{1,0:T(8,128)(2,1)S(1)}, bf16[224,2048]{1,0:T(8,128)(2,1)}, u32[]{:S(2)}, u32[]{:S(2)}) collective-permute-start(bf16[224,2048]{1,0:T(8,128)(2,1)S(1)} %multiply_convert_fusion), channel_id=1, source_target_pairs={{0,16},{8,24},{16,0},{24,8},{1,17},{9,25},{17,1},{25,9},{2,18},{10... | collective-permute-start | bytes 2752520 | tf_op jit(solution)/shard_map/ppermute | solution.py:55
  192.8 39.3 %collective-permute-start.20 = (bf16[224,2048]{1,0:T(8,128)(2,1)S(1)}, bf16[224,2048]{1,0:T(8,128)(2,1)}, u32[]{:S(2)}, u32[]{:S(2)}) collective-permute-start(bf16[224,2048]{1,0:T(8,128)(2,1)S(1)} %multiply_convert_fusion), channel_id=1, source_target_pairs={{0,24},{8,16},{16,8},{24,0},{1,25},{9,17},{17,9},{25,1},{2,26},{10... | collective-permute-start | bytes 2752520 | tf_op jit(solution)/shard_map/ppermute | solution.py:55
  268.2 246.4 %reduce-scatter.6.cloned.1.call-start = ((), (), s32[]{:S(2)}) async-start(), calls=%async_computation.7 | async-start | bytes 5242880 | tf_op jit(solution)/shard_map/reduce_scatter | solution.py:539
  301.2 34.3 %collective-permute-start.24 = (bf16[224,2048]{1,0:T(8,128)(2,1)S(1)}, bf16[224,2048]{1,0:T(8,128)(2,1)S(1)}, u32[]{:S(2)}, u32[]{:S(2)}) collective-permute-start(bf16[224,2048]{1,0:T(8,128)(2,1)S(1)} %convolution_convert_fusion.9), channel_id=1, source_target_pairs={{0,16},{8,24},{16,0},{24,8},{1,17},{9,25},{17,1},{25,9},{2,18},{10... | collective-permute-start | bytes 2752520 | tf_op jit(solution)/shard_map/ppermute | solution.py:55
  359.1 258.8 %reduce-scatter.8.cloned.1.call-start = ((), (), s32[]{:S(2)}) async-start(), calls=%async_computation.8 | async-start | bytes 7077888 | tf_op jit(solution)/shard_map/reduce_scatter | solution.py:789
  382.7 44.8 %collective-permute-start.32 = (bf16[224,2048]{1,0:T(8,128)(2,1)S(1)}, bf16[224,2048]{1,0:T(8,128)(2,1)S(1)}, u32[]{:S(2)}, u32[]{:S(2)}) collective-permute-start(bf16[224,2048]{1,0:T(8,128)(2,1)S(1)} %get-tuple-element.194), channel_id=1, source_target_pairs={{0,8},{8,0},{16,24},{24,16},{1,9},{9,1},{17,25},{25,17},{2,10},{10... | collective-permute-start | bytes 2752520 | tf_op jit(solution)/shard_map/ppermute | solution.py:55
  382.7 44.8 %collective-permute-start.33 = (bf16[224,2048]{1,0:T(8,128)(2,1)S(1)}, bf16[224,2048]{1,0:T(8,128)(2,1)S(1)}, u32[]{:S(2)}, u32[]{:S(2)}) collective-permute-start(bf16[224,2048]{1,0:T(8,128)(2,1)S(1)} %get-tuple-element.194), channel_id=1, source_target_pairs={{0,16},{8,24},{16,0},{24,8},{1,17},{9,25},{17,1},{25,9},{2,18},{10... | collective-permute-start | bytes 2752520 | tf_op jit(solution)/shard_map/ppermute | solution.py:55
  435.7 67.3 %collective-permute-start.39 = (bf16[224,2048]{1,0:T(8,128)(2,1)S(1)}, bf16[224,2048]{1,0:T(8,128)(2,1)S(1)}, u32[]{:S(2)}, u32[]{:S(2)}) collective-permute-start(bf16[224,2048]{1,0:T(8,128)(2,1)S(1)} %copy-done.54), channel_id=1, source_target_pairs={{0,8},{8,0},{16,24},{24,16},{1,9},{9,1},{17,25},{25,17},{2,10},{10... | collective-permute-start | bytes 2752520 | tf_op jit(solution)/shard_map/ppermute | solution.py:55
  435.8 67.2 %collective-permute-start.40 = (bf16[224,2048]{1,0:T(8,128)(2,1)S(1)}, bf16[224,2048]{1,0:T(8,128)(2,1)S(1)}, u32[]{:S(2)}, u32[]{:S(2)}) collective-permute-start(bf16[224,2048]{1,0:T(8,128)(2,1)S(1)} %copy-done.53), channel_id=1, source_target_pairs={{0,16},{8,24},{16,0},{24,8},{1,17},{9,25},{17,1},{25,9},{2,18},{10... | collective-permute-start | bytes 2752520 | tf_op jit(solution)/shard_map/ppermute | solution.py:55
  436.2 46.0 %collective-permute-start.36 = (bf16[7,128,384]{2,1,0:T(8,128)(2,1)S(1)}, bf16[7,128,384]{2,1,0:T(8,128)(2,1)S(1)}, u32[]{:S(2)}, u32[]{:S(2)}) collective-permute-start(bf16[7,128,384]{2,1,0:T(8,128)(2,1)S(1)} %get-tuple-element.207), channel_id=1, source_target_pairs={{0,2},{1,3},{2,0},{3,1},{4,6},{5,7},{6,4},{7,5},{8,10},{9,11},{10,... | collective-permute-start | bytes 2064392 | tf_op jit(solution)/shard_map/ppermute | solution.py:506
  454.4 48.7 %collective-permute-start.37 = (bf16[7,128,384]{2,1,0:T(8,128)(2,1)S(1)}, bf16[7,128,384]{2,1,0:T(8,128)(2,1)S(1)}, u32[]{:S(2)}, u32[]{:S(2)}) collective-permute-start(bf16[7,128,384]{2,1,0:T(8,128)(2,1)S(1)} %get-tuple-element.208), channel_id=1, source_target_pairs={{0,4},{1,5},{2,6},{3,7},{4,0},{5,1},{6,2},{7,3},{8,12},{9,13},{10,... | collective-permute-start | bytes 2064392 | tf_op jit(solution)/shard_map/ppermute | solution.py:506
  454.4 48.7 %collective-permute-start.38 = (bf16[7,128,384]{2,1,0:T(8,128)(2,1)S(1)}, bf16[7,128,384]{2,1,0:T(8,128)(2,1)S(1)}, u32[]{:S(2)}, u32[]{:S(2)}) collective-permute-start(bf16[7,128,384]{2,1,0:T(8,128)(2,1)S(1)} %get-tuple-element.209), channel_id=1, source_target_pairs={{0,6},{1,7},{2,4},{3,5},{4,2},{5,3},{6,0},{7,1},{8,14},{9,15},{10,... | collective-permute-start | bytes 2064392 | tf_op jit(solution)/shard_map/ppermute | solution.py:506
  514.6 190.9 %all-gather.11.cloned.1.call-start = ((), (), s32[]{:S(2)}) async-start(), calls=%async_computation.9 | async-start | bytes 7077888 | tf_op jit(solution)/shard_map/all_gather | solution.py:823
  564.4 37.0 %collective-permute-start.46 = (bf16[224,2048]{1,0:T(8,128)(2,1)}, bf16[224,2048]{1,0:T(8,128)(2,1)S(1)}, u32[]{:S(2)}, u32[]{:S(2)}) collective-permute-start(bf16[224,2048]{1,0:T(8,128)(2,1)} %fusion.15), channel_id=1, source_target_pairs={{0,8},{8,0},{16,24},{24,16},{1,9},{9,1},{17,25},{25,17},{2,10},{10... | collective-permute-start | bytes 2752520 | tf_op jit(solution)/shard_map/ppermute | solution.py:55
  565.0 40.2 %collective-permute-start.47 = (bf16[224,2048]{1,0:T(8,128)(2,1)}, bf16[224,2048]{1,0:T(8,128)(2,1)}, u32[]{:S(2)}, u32[]{:S(2)}) collective-permute-start(bf16[224,2048]{1,0:T(8,128)(2,1)} %fusion.16), channel_id=1, source_target_pairs={{0,16},{8,24},{16,0},{24,8},{1,17},{9,25},{17,1},{25,9},{2,18},{10... | collective-permute-start | bytes 2752520 | tf_op jit(solution)/shard_map/ppermute | solution.py:55
  566.7 39.8 %collective-permute-start.48 = (bf16[224,2048]{1,0:T(8,128)(2,1)}, bf16[224,2048]{1,0:T(8,128)(2,1)}, u32[]{:S(2)}, u32[]{:S(2)}) collective-permute-start(bf16[224,2048]{1,0:T(8,128)(2,1)} %fusion.17), channel_id=1, source_target_pairs={{0,24},{8,16},{16,8},{24,0},{1,25},{9,17},{17,9},{25,1},{2,26},{10... | collective-permute-start | bytes 2752520 | tf_op jit(solution)/shard_map/ppermute | solution.py:55
  630.5 36.3 %collective-permute-start.54 = (bf16[224,2048]{1,0:T(8,128)(2,1)S(1)}, bf16[224,2048]{1,0:T(8,128)(2,1)S(1)}, u32[]{:S(2)}, u32[]{:S(2)}) collective-permute-start(bf16[224,2048]{1,0:T(8,128)(2,1)S(1)} %add_convert_fusion.3), channel_id=1, source_target_pairs={{0,8},{8,0},{16,24},{24,16},{1,9},{9,1},{17,25},{25,17},{2,10},{10... | collective-permute-start | bytes 2752520 | tf_op jit(solution)/shard_map/ppermute | solution.py:55
  631.7 35.1 %collective-permute-start.55 = (bf16[224,2048]{1,0:T(8,128)(2,1)S(1)}, bf16[224,2048]{1,0:T(8,128)(2,1)S(1)}, u32[]{:S(2)}, u32[]{:S(2)}) collective-permute-start(bf16[224,2048]{1,0:T(8,128)(2,1)S(1)} %add_convert_fusion.3), channel_id=1, source_target_pairs={{0,16},{8,24},{16,0},{24,8},{1,17},{9,25},{17,1},{25,9},{2,18},{10... | collective-permute-start | bytes 2752520 | tf_op jit(solution)/shard_map/ppermute | solution.py:55
  633.3 33.9 %collective-permute-start.56 = (bf16[224,2048]{1,0:T(8,128)(2,1)S(1)}, bf16[224,2048]{1,0:T(8,128)(2,1)S(1)}, u32[]{:S(2)}, u32[]{:S(2)}) collective-permute-start(bf16[224,2048]{1,0:T(8,128)(2,1)S(1)} %add_convert_fusion.3), channel_id=1, source_target_pairs={{0,24},{8,16},{16,8},{24,0},{1,25},{9,17},{17,9},{25,1},{2,26},{10... | collective-permute-start | bytes 2752520 | tf_op jit(solution)/shard_map/ppermute | solution.py:55
  667.4 35.3 %collective-permute-start.57 = (bf16[224,2048]{1,0:T(8,128)(2,1)S(1)}, bf16[224,2048]{1,0:T(8,128)(2,1)S(1)}, u32[]{:S(2)}, u32[]{:S(2)}) collective-permute-start(bf16[224,2048]{1,0:T(8,128)(2,1)S(1)} %copy-done.19), channel_id=1, source_target_pairs={{0,24},{8,16},{16,8},{24,0},{1,25},{9,17},{17,9},{25,1},{2,26},{10... | collective-permute-start | bytes 2752520 | tf_op jit(solution)/shard_map/ppermute | solution.py:55
  (112 other events, 2308.2 us)
Sparse Core Ops, SparseCore 0:
  10.2 73.1 all-gather.4
  106.9 78.7 all-gather.6
  187.3 85.4 all-gather.8
  274.9 76.9 reduce-scatter.3
  359.3 93.2 reduce-scatter.5
  514.8 98.6 reduce-scatter.7
  618.1 87.4 all-gather.10

commit v8 on v7

--- a/solution.py
+++ b/solution.py
@@ -554,14 +554,32 @@
 
     def scatter_places(values):
         size = values.shape[0] // heads
-        pieces = [
-            lax.dynamic_slice_in_dim(values, (place ^ slot) * size, size, 0) for slot in range(heads)
-        ]
-        pieces = [v.astype(f32) for v in exchange(pieces)]
-        return sum(pieces[1:], pieces[0]).astype(bf16)
+        held = {
+            slot: lax.dynamic_slice_in_dim(values, (place ^ slot) * size, size, 0)
+            for slot in range(heads)
+        }
+        bit = 1
+        while bit < heads:
+            slots = [slot for slot in sorted(held) if slot & bit]
+            joined = jnp.concatenate([held[slot] for slot in slots], axis=0)
+            joined = jnp.split(across(joined, bit), len(slots), axis=0)
+            held = {
+                slot ^ bit: (held[slot ^ bit].astype(f32) + v.astype(f32)).astype(bf16)
+                for slot, v in zip(slots, joined)
+            }
+            bit *= 2
+        return held[0]
 
     def gather_seq(values):
-        values = placed(exchange([values] * heads), place, 0)
+        held = {0: values}
+        bit = heads // 2
+        while bit:
+            slots = sorted(held)
+            joined = jnp.concatenate([held[slot] for slot in slots], axis=0)
+            joined = jnp.split(across(joined, bit), len(slots), axis=0)
+            held.update({slot ^ bit: v for slot, v in zip(slots, joined)})
+            bit //= 2
+        values = placed([held[slot] for slot in range(heads)], place, 0)
         size = values.shape[0]
         full = jnp.zeros((size * members,) + values.shape[1:], values.dtype)
         for step in range(members):
@@ -741,12 +759,13 @@
     grad_mixed = [
         grad_mixed[:, slot * head_width : (slot + 1) * head_width] for slot in range(head_count)
     ]
-    active, grad_mixed = lax.optimization_barrier((active, grad_mixed))
     grad_mixed = [grad_mixed[0]] + [
         swap(grad_mixed[slot], slot) for slot in range(1, head_count)
     ]
     grad_heads = placed(grad_mixed, head_rank, 0)
-    grad_heads, grad_attn_own = lax.optimization_barrier((grad_heads, grad_attn_own))
+    grad_heads, grad_attn_own, active = lax.optimization_barrier(
+        (grad_heads, grad_attn_own, active)
+    )
     grad_attn = gather_heads(grad_attn_own)
     grad_slots = []
     for slot in range(heads):

time: 729 us -> 732 us (level)
  waiting for transfers between devices: 282 us -> 316 us
  starting transfers between devices: 154 us -> 122 us
    ppermute x38, waiting for transfers between devices: 85.2 us -> 116 us  [flip(): return lax.ppermute(values, axis, [(i, i ^ bit) for i in range(size)])]
    ppermute x18 -> x16, starting transfers between devices: 77.8 us -> 49.4 us  [across(): return lax.ppermute(values, 'seq', pairs)]
    ppermute x38, starting transfers between devices: 73.9 us -> 57.8 us  [flip(): return lax.ppermute(values, axis, [(i, i ^ bit) for i in range(size)])]
    reduce_scatter x1, starting transfers between devices: 0.21 us -> 12.9 us  [local(): lax.psum_scatter(grad_qkv_part, 'seq', scatter_dimension=0, tiled=True)]
    ppermute x18 -> x16, waiting for transfers between devices: 179 us -> 184 us  [across(): return lax.ppermute(values, 'seq', pairs)]
  transfers between devices with their start and end apart: 72 -> 70, of which waited for: 34 -> 32; matrix products, arithmetic and copies ran while one was open for 28% -> 28% of each run, Pallas kernels for 8% -> 8%
where the time goes in v8:
time: 732 us; the launch traced here: 725 us
  waiting for transfers between devices  316 us (43%)
  matrix products  130 us (18%)
  starting transfers between devices  122 us (17%)
  Pallas kernels  55.6 us (8%)
  other arithmetic  54.8 us (7%)
  local copies, waits for them, and re-layouts  29.6 us (4%)
  between operations  16.3 us (2%)
    ppermute x16, waiting for transfers between devices, across(): return lax.ppermute(values, 'seq', pairs)  184 us
    ppermute x38, waiting for transfers between devices, flip(): return lax.ppermute(values, axis, [(i, i ^ bit) for i in range(size)])  116 us
    dot_general x24, matrix products, contract(): lax.dot_general(left, right, (((left_dim,), (right_dim,)), ((), ())), pre...  89.2 us
    ppermute x38, starting transfers between devices, flip(): return lax.ppermute(values, axis, [(i, i ^ bit) for i in range(size)])  57.8 us
    ppermute x16, starting transfers between devices, across(): return lax.ppermute(values, 'seq', pairs)  49.4 us
    dot_general x6, matrix products, dot(): return jnp.dot(left, right, preferred_element_type=f32)  37.5 us
    pallas_call x1, Pallas kernels, attend_backward(): pl.pallas_call(functools.partial(back_kernel, heads, members), out_shape=...  21 us
    pallas_call x1, Pallas kernels, project(): pl.pallas_call(functools.partial(project_kernel, heads), out_shape=[jax.S...  16.3 us
  transfers between devices with their start and end apart: 70, of which 32 were waited for; matrix products, arithmetic and copies ran while one was open for 28% of the time, Pallas kernels for 8%

profile of v8, /device:TPU:0, one launch (start us, length us, event | category | flops | bytes accessed | tf_op | source)
XLA Modules:
  0.0 724.5 jit_solution(14694477698455297885)
XLA Ops:
  17.0 16.3 %project.1 = (bf16[7,128,384]{2,1,0:T(8,128)(2,1)S(1)}, bf16[7,128,384]{2,1,0:T(8,128)(2,1)}, bf16[7,128,384]{2,1,0:T(8,128)(2,1)S(1)}, bf16[7,128,384]{2,1,0:T(...) custom-call(s32[7]{0:T(128)S(1)} %pad_add_fusion.scal, bf16[896,2048]{1,0:T(8,128)(2,1)} %tokens.1, ...), custom_call_target="tpu_custom_call" | custom-call | flops 5637144576 | bytes 16777216 | tf_op jit(solution)/shard_map/project/pallas_call | solution.py:402
  42.6 43.9 %collective-permute-done.refs_1_ = bf16[7,128,384]{2,1,0:T(8,128)(2,1)S(1)} collective-permute-done((bf16[7,128,384]{2,1,0:T(8,128)(2,1)}, bf16[7,128,384]{2,1,0:T(8,128)(2,1)S(1)}, u32[]{:S(2)}, u32[]{:S(2)}) %collective-permute-start) | collective-permute-done | bytes 688160 | tf_op jit(solution)/shard_map/ppermute | solution.py:506
  90.1 13.1 %collective-permute-done.2.refs_3_ = bf16[7,128,384]{2,1,0:T(8,128)(2,1)} collective-permute-done((bf16[7,128,384]{2,1,0:T(8,128)(2,1)S(1)}, bf16[7,128,384]{2,1,0:T(8,128)(2,1)}, u32[]{:S(2)}, u32[]{:S(2)}) %collective-permute-start.2) | collective-permute-done | bytes 688160 | tf_op jit(solution)/shard_map/ppermute | solution.py:506
  110.4 15.5 %attend_forward.1 = (bf16[7,128,128]{2,1,0:T(8,128)(2,1)}, bf16[7,128,128]{2,1,0:T(8,128)(2,1)}, bf16[7,128,128]{2,1,0:T(8,128)(2,1)}, bf16[7,128,128]{2,1,0:T(8,128)(2,1)}, f32[4,7,1,128]{3,2,1,0:T(1,128)}) custom-call(s32[7]{0:T(128)} %copy-done.6, bf16[7,128,384]{2,1,0:T(8,128)(2,1)} %copy-done.8, bf16[7,128,384]{2,1,0:T(8,128)(2,1)} %copy-done.56, ...), custom_call_target="tpu_custom_call" | custom-call | flops 4000000000 | bytes 7340032 | tf_op jit(solution)/shard_map/attend_forward/pallas_call | solution.py:185
  125.9 14.4 %collective-permute-start.10 = (bf16[7,128,128]{2,1,0:T(8,128)(2,1)}, bf16[7,128,128]{2,1,0:T(8,128)(2,1)S(1)}, u32[]{:S(2)}, u32[]{:S(2)}) collective-permute-start(bf16[7,128,128]{2,1,0:T(8,128)(2,1)} %get-tuple-element.144), channel_id=1, source_target_pairs={{0,4},{1,5},{2,6},{3,7},{4,0},{5,1},{6,2},{7,3},{8,12},{9,13},{10,... | collective-permute-start | bytes 688136 | tf_op jit(solution)/shard_map/ppermute | solution.py:506
  149.0 24.8 %collective-permute-done.13 = f32[5,2048]{1,0:T(8,128)S(1)} collective-permute-done((f32[5,2048]{1,0:T(8,128)S(1)}, f32[5,2048]{1,0:T(8,128)S(1)}, u32[]{:S(2)}, u32[]{:S(2)}) %collective-permute-start.13) | collective-permute-done | bytes 40992 | tf_op jit(solution)/shard_map/ppermute | solution.py:55
  194.3 11.0 %collective-permute-start.21 = (f32[5,2048]{1,0:T(8,128)S(1)}, f32[5,2048]{1,0:T(8,128)S(1)}, u32[]{:S(2)}, u32[]{:S(2)}) collective-permute-start(f32[5,2048]{1,0:T(8,128)S(1)} %add.433), channel_id=1, source_target_pairs={{0,4},{1,5},{2,6},{3,7},{4,0},{5,1},{6,2},{7,3},{8,12},{9,13},{10,... | collective-permute-start | bytes 122888 | tf_op jit(solution)/shard_map/ppermute | solution.py:55
  205.4 9.1 %collective-permute-done.21 = f32[5,2048]{1,0:T(8,128)S(1)} collective-permute-done((f32[5,2048]{1,0:T(8,128)S(1)}, f32[5,2048]{1,0:T(8,128)S(1)}, u32[]{:S(2)}, u32[]{:S(2)}) %collective-permute-start.21) | collective-permute-done | bytes 40992 | tf_op jit(solution)/shard_map/ppermute | solution.py:55
  214.5 8.3 %pad_maximum_fusion = bf16[2048,2048]{1,0:T(8,128)(2,1)} fusion(bf16[2048,1024]{1,0:T(8,128)(2,1)} %all-gather.7.cloned.1.call-done, bf16[2048,1024]{1,0:T(8,128)(2,1)} %all-gather.5.cloned.1.call-done), kind=kLoop, calls=%fused_computation.2 | loop fusion | flops 16777216 | bytes 16777216 | tf_op jit(solution)/shard_map/concatenate | solution.py:708
  222.9 7.5 %collective-permute-done.19 = bf16[224,2048]{1,0:T(8,128)(2,1)} collective-permute-done((bf16[224,2048]{1,0:T(8,128)(2,1)S(1)}, bf16[224,2048]{1,0:T(8,128)(2,1)}, u32[]{:S(2)}, u32[]{:S(2)}) %collective-permute-start.19) | collective-permute-done | bytes 917536 | tf_op jit(solution)/shard_map/ppermute | solution.py:55
  236.0 13.1 %fusion = (bf16[896,2048]{1,0:T(8,128)(2,1)S(1)}, f32[896,2048]{1,0:T(8,128)}) fusion(s32[2048]{0:T(1024)S(1)} %iota_add_fusion, s32[896]{0:T(1024)S(1)} %add_multiply_fusion, bf16[896,2048]{1,0:T(8,128)(2,1)S(1)} %constant_dynamic-update-slice_fusion.4, bf16[2048,2048]{1,0:T(8,128)(2,1)} %pad_maximum_fusion), kind=kOutput, calls=%fused_computation.6 | convolution fusion | flops 7525367808 | bytes 23080448 | tf_op jit(solution)/shard_map/dot_general | solution.py:29
  261.9 6.3 add_convert_fusion.1
  272.7 13.4 %fusion.3 = bf16[896,2048]{1,0:T(8,128)(2,1)S(1)} fusion(f32[896,2048]{1,0:T(8,128)} %get-tuple-element.166, s32[2048]{0:T(1024)S(1)} %iota_add_fusion, s32[896]{0:T(1024)S(1)} %add_multiply_fusion, bf16[896,2048]{1,0:T(8,128)(2,1)} %copy-done.12, bf16[2048,2048]{1,0:T(8,128)(2,1)} %all-gather.9.cloned.1.call-done), kind=kOutput, calls=%fused_computation.9 | convolution fusion | flops 7529037824 | bytes 23080448 | tf_op jit(solution)/shard_map/dot_general | solution.py:33
  286.1 6.2 convolution_convert_fusion.8
  295.0 6.1 convolution_convert_fusion.9
  305.0 6.7 convolution_convert_fusion.1
  319.8 15.6 %collective-permute-done.24 = bf16[224,2048]{1,0:T(8,128)(2,1)S(1)} collective-permute-done((bf16[224,2048]{1,0:T(8,128)(2,1)S(1)}, bf16[224,2048]{1,0:T(8,128)(2,1)S(1)}, u32[]{:S(2)}, u32[]{:S(2)}) %collective-permute-start.24) | collective-permute-done | bytes 917536 | tf_op jit(solution)/shard_map/ppermute | solution.py:55
  338.9 6.3 convolution_convert_fusion.7
  378.2 12.9 %reduce-scatter.8.cloned.1.call-start = ((), (), s32[]{:S(2)}) async-start(), calls=%async_computation.8 | async-start | bytes 7077888 | tf_op jit(solution)/shard_map/reduce_scatter | solution.py:808
  391.1 6.9 convolution_convert_fusion.5
  398.0 6.5 convolution_convert_fusion.6
  408.7 21.0 %attend_backward.1 = (bf16[7,128,384]{2,1,0:T(8,128)(2,1)}, bf16[7,128,384]{2,1,0:T(8,128)(2,1)}, bf16[7,128,384]{2,1,0:T(8,128)(2,1)}, bf16[7,128,384]{2,1,0:T(8,128)(2,1)}, bf16[4,7,128,384]{3,2,1,0:T(8,128)(2,1)}) custom-call(s32[7]{0:T(128)} %copy-done.6, bf16[7,128,384]{2,1,0:T(8,128)(2,1)} %copy-done.8, bf16[7,128,384]{2,1,0:T(8,128)(2,1)} %copy-done.56, ...), custom_call_target="tpu_custom_call" | custom-call | flops 10000000000 | bytes 12582912 | tf_op jit(solution)/shard_map/attend_backward/pallas_call | solution.py:311
  441.9 12.2 %collective-permute-done.34 = bf16[224,2048]{1,0:T(8,128)(2,1)S(1)} collective-permute-done((bf16[224,2048]{1,0:T(8,128)(2,1)S(1)}, bf16[224,2048]{1,0:T(8,128)(2,1)S(1)}, u32[]{:S(2)}, u32[]{:S(2)}) %collective-permute-start.34) | collective-permute-done | bytes 917536 | tf_op jit(solution)/shard_map/ppermute | solution.py:55
  460.4 19.6 %collective-permute-done.36.refs_1_ = bf16[7,128,384]{2,1,0:T(8,128)(2,1)S(1)} collective-permute-done((bf16[7,128,384]{2,1,0:T(8,128)(2,1)S(1)}, bf16[7,128,384]{2,1,0:T(8,128)(2,1)S(1)}, u32[]{:S(2)}, u32[]{:S(2)}) %collective-permute-start.36) | collective-permute-done | bytes 688160 | tf_op jit(solution)/shard_map/ppermute | solution.py:506
  482.6 18.4 %collective-permute-done.37.refs_2_ = bf16[7,128,384]{2,1,0:T(8,128)(2,1)S(1)} collective-permute-done((bf16[7,128,384]{2,1,0:T(8,128)(2,1)S(1)}, bf16[7,128,384]{2,1,0:T(8,128)(2,1)S(1)}, u32[]{:S(2)}, u32[]{:S(2)}) %collective-permute-start.37) | collective-permute-done | bytes 688160 | tf_op jit(solution)/shard_map/ppermute | solution.py:506
  503.8 8.7 %convolution_convert_fusion = bf16[2048,1536]{1,0:T(8,128)(2,1)} fusion(bf16[896,2048]{1,0:T(8,128)(2,1)S(1)} %copy-done.65, bf16[896,1536]{1,0:T(8,128)(2,1)S(1)} %gather_grads.1), kind=kOutput, calls=%fused_computation.5 | convolution fusion | flops 5640290304 | bytes 12713984 | tf_op jit(solution)/shard_map/dot_general | solution.py:33
  548.1 15.7 %collective-permute-start.49 = (bf16[128,2048]{1,0:T(8,128)(2,1)}, bf16[128,2048]{1,0:T(8,128)(2,1)}, u32[]{:S(2)}, u32[]{:S(2)}) collective-permute-start(bf16[128,2048]{1,0:T(8,128)(2,1)} %pad_maximum_fusion.4), channel_id=1, source_target_pairs={{0,2},{1,3},{2,0},{3,1},{4,6},{5,7},{6,4},{7,5},{8,10},{9,11},{10,... | collective-permute-start | bytes 1572872 | tf_op jit(solution)/shard_map/ppermute | solution.py:506
  567.3 20.4 %collective-permute-done.49 = bf16[128,2048]{1,0:T(8,128)(2,1)} collective-permute-done((bf16[128,2048]{1,0:T(8,128)(2,1)}, bf16[128,2048]{1,0:T(8,128)(2,1)}, u32[]{:S(2)}, u32[]{:S(2)}) %collective-permute-start.49) | collective-permute-done | bytes 524320 | tf_op jit(solution)/shard_map/ppermute | solution.py:506
  589.8 20.2 %collective-permute-done.50 = bf16[64,2048]{1,0:T(8,128)(2,1)S(1)} collective-permute-done((bf16[64,2048]{1,0:T(8,128)(2,1)S(1)}, bf16[64,2048]{1,0:T(8,128)(2,1)S(1)}, u32[]{:S(2)}, u32[]{:S(2)}) %collective-permute-start.50) | collective-permute-done | bytes 262176 | tf_op jit(solution)/shard_map/ppermute | solution.py:506
  622.8 8.7 %collective-permute-done.57 = bf16[64,2048]{1,0:T(8,128)(2,1)S(1)} collective-permute-done((bf16[64,2048]{1,0:T(8,128)(2,1)S(1)}, bf16[64,2048]{1,0:T(8,128)(2,1)S(1)}, u32[]{:S(2)}, u32[]{:S(2)}) %collective-permute-start.57) | collective-permute-done | bytes 262176 | tf_op jit(solution)/shard_map/ppermute | solution.py:506
  640.3 39.7 %collective-permute-done.58 = bf16[128,2048]{1,0:T(8,128)(2,1)S(1)} collective-permute-done((bf16[128,2048]{1,0:T(8,128)(2,1)}, bf16[128,2048]{1,0:T(8,128)(2,1)S(1)}, u32[]{:S(2)}, u32[]{:S(2)}) %collective-permute-start.58) | collective-permute-done | bytes 524320 | tf_op jit(solution)/shard_map/ppermute | solution.py:506
  696.1 8.3 %collective-permute-done.56 = bf16[224,2048]{1,0:T(8,128)(2,1)S(1)} collective-permute-done((bf16[224,2048]{1,0:T(8,128)(2,1)S(1)}, bf16[224,2048]{1,0:T(8,128)(2,1)S(1)}, u32[]{:S(2)}, u32[]{:S(2)}) %collective-permute-start.56) | collective-permute-done | bytes 917536 | tf_op jit(solution)/shard_map/ppermute | solution.py:55
  (409 shorter events, 251.5 us)
Async XLA Ops:
  7.2 207.3 %all-gather.5.cloned.1.call-start = ((), (), s32[]{:S(2)}) async-start(), calls=%async_computation.3 | async-start | bytes 4718592 | tf_op jit(solution)/shard_map/all_gather | solution.py:631
  9.5 205.0 %all-gather.7.cloned.1.call-start = ((), (), s32[]{:S(2)}) async-start(), calls=%async_computation.4 | async-start | bytes 4718592 | tf_op jit(solution)/shard_map/all_gather | solution.py:686
  9.6 97.2 %collective-permute-start.7 = (bf16[512,2048]{1,0:T(8,128)(2,1)}, bf16[512,2048]{1,0:T(8,128)(2,1)}, u32[]{:S(2)}, u32[]{:S(2)}) collective-permute-start(bf16[512,2048]{1,0:T(8,128)(2,1)} %param.14), channel_id=1, source_target_pairs={{0,8},{8,0},{16,24},{24,16},{1,9},{9,1},{17,25},{25,17},{2,10},{10... | collective-permute-start | bytes 6291464 | tf_op jit(solution)/shard_map/ppermute | solution.py:55
  12.6 94.2 %collective-permute-start.8 = (bf16[512,2048]{1,0:T(8,128)(2,1)}, bf16[512,2048]{1,0:T(8,128)(2,1)}, u32[]{:S(2)}, u32[]{:S(2)}) collective-permute-start(bf16[512,2048]{1,0:T(8,128)(2,1)} %param.14), channel_id=1, source_target_pairs={{0,16},{8,24},{16,0},{24,8},{1,17},{9,25},{17,1},{25,9},{2,18},{10... | collective-permute-start | bytes 6291464 | tf_op jit(solution)/shard_map/ppermute | solution.py:55
  33.3 53.2 %collective-permute-start = (bf16[7,128,384]{2,1,0:T(8,128)(2,1)}, bf16[7,128,384]{2,1,0:T(8,128)(2,1)S(1)}, u32[]{:S(2)}, u32[]{:S(2)}) collective-permute-start(bf16[7,128,384]{2,1,0:T(8,128)(2,1)} %get-tuple-element.130), channel_id=1, source_target_pairs={{0,2},{1,3},{2,0},{3,1},{4,6},{5,7},{6,4},{7,5},{8,10},{9,11},{10,... | collective-permute-start | bytes 2064392 | tf_op jit(solution)/shard_map/ppermute | solution.py:506
  35.0 54.6 %collective-permute-start.1 = (bf16[7,128,384]{2,1,0:T(8,128)(2,1)S(1)}, bf16[7,128,384]{2,1,0:T(8,128)(2,1)}, u32[]{:S(2)}, u32[]{:S(2)}) collective-permute-start(bf16[7,128,384]{2,1,0:T(8,128)(2,1)S(1)} %get-tuple-element.131), channel_id=1, source_target_pairs={{0,4},{1,5},{2,6},{3,7},{4,0},{5,1},{6,2},{7,3},{8,12},{9,13},{10,... | collective-permute-start | bytes 2064392 | tf_op jit(solution)/shard_map/ppermute | solution.py:506
  37.5 65.7 %collective-permute-start.2 = (bf16[7,128,384]{2,1,0:T(8,128)(2,1)S(1)}, bf16[7,128,384]{2,1,0:T(8,128)(2,1)}, u32[]{:S(2)}, u32[]{:S(2)}) collective-permute-start(bf16[7,128,384]{2,1,0:T(8,128)(2,1)S(1)} %get-tuple-element.132), channel_id=1, source_target_pairs={{0,6},{1,7},{2,4},{3,5},{4,2},{5,3},{6,0},{7,1},{8,14},{9,15},{10,... | collective-permute-start | bytes 2064392 | tf_op jit(solution)/shard_map/ppermute | solution.py:506
  106.8 166.0 %all-gather.9.cloned.1.call-start = ((), (), s32[]{:S(2)}) async-start(), calls=%async_computation.5 | async-start | bytes 9437184 | tf_op jit(solution)/shard_map/all_gather | solution.py:687
  107.5 405.0 %reduce-scatter.4.cloned.1.call-start = ((), (), s32[]{:S(2)}) async-start(), calls=%async_computation.6 | async-start | bytes 5242880 | tf_op jit(solution)/shard_map/reduce_scatter | solution.py:539
  107.8 70.1 %collective-permute-start.17 = (bf16[512,2048]{1,0:T(8,128)(2,1)}, bf16[512,2048]{1,0:T(8,128)(2,1)S(1)}, u32[]{:S(2)}, u32[]{:S(2)}) collective-permute-start(bf16[512,2048]{1,0:T(8,128)(2,1)} %param.14), channel_id=1, source_target_pairs={{0,24},{8,16},{16,8},{24,0},{1,25},{9,17},{17,9},{25,1},{2,26},{10... | collective-permute-start | bytes 6291464 | tf_op jit(solution)/shard_map/ppermute | solution.py:55
  125.9 47.9 %collective-permute-start.10 = (bf16[7,128,128]{2,1,0:T(8,128)(2,1)}, bf16[7,128,128]{2,1,0:T(8,128)(2,1)S(1)}, u32[]{:S(2)}, u32[]{:S(2)}) collective-permute-start(bf16[7,128,128]{2,1,0:T(8,128)(2,1)} %get-tuple-element.144), channel_id=1, source_target_pairs={{0,4},{1,5},{2,6},{3,7},{4,0},{5,1},{6,2},{7,3},{8,12},{9,13},{10,... | collective-permute-start | bytes 688136 | tf_op jit(solution)/shard_map/ppermute | solution.py:506
  192.8 39.3 %collective-permute-start.20 = (bf16[224,2048]{1,0:T(8,128)(2,1)S(1)}, bf16[224,2048]{1,0:T(8,128)(2,1)}, u32[]{:S(2)}, u32[]{:S(2)}) collective-permute-start(bf16[224,2048]{1,0:T(8,128)(2,1)S(1)} %multiply_convert_fusion), channel_id=1, source_target_pairs={{0,24},{8,16},{16,8},{24,0},{1,25},{9,17},{17,9},{25,1},{2,26},{10... | collective-permute-start | bytes 2752520 | tf_op jit(solution)/shard_map/ppermute | solution.py:55
  268.2 244.3 %reduce-scatter.6.cloned.1.call-start = ((), (), s32[]{:S(2)}) async-start(), calls=%async_computation.7 | async-start | bytes 5242880 | tf_op jit(solution)/shard_map/reduce_scatter | solution.py:539
  359.5 70.2 %collective-permute-start.32 = (bf16[224,2048]{1,0:T(8,128)(2,1)S(1)}, bf16[224,2048]{1,0:T(8,128)(2,1)S(1)}, u32[]{:S(2)}, u32[]{:S(2)}) collective-permute-start(bf16[224,2048]{1,0:T(8,128)(2,1)S(1)} %get-tuple-element.186), channel_id=1, source_target_pairs={{0,8},{8,0},{16,24},{24,16},{1,9},{9,1},{17,25},{25,17},{2,10},{10... | collective-permute-start | bytes 2752520 | tf_op jit(solution)/shard_map/ppermute | solution.py:55
  360.7 69.0 %collective-permute-start.33 = (bf16[224,2048]{1,0:T(8,128)(2,1)S(1)}, bf16[224,2048]{1,0:T(8,128)(2,1)}, u32[]{:S(2)}, u32[]{:S(2)}) collective-permute-start(bf16[224,2048]{1,0:T(8,128)(2,1)S(1)} %get-tuple-element.186), channel_id=1, source_target_pairs={{0,16},{8,24},{16,0},{24,8},{1,17},{9,25},{17,1},{25,9},{2,18},{10... | collective-permute-start | bytes 2752520 | tf_op jit(solution)/shard_map/ppermute | solution.py:55
  362.4 45.5 %collective-permute-start.29 = (bf16[7,128,128]{2,1,0:T(8,128)(2,1)S(1)}, bf16[7,128,128]{2,1,0:T(8,128)(2,1)S(1)}, u32[]{:S(2)}, u32[]{:S(2)}) collective-permute-start(bf16[7,128,128]{2,1,0:T(8,128)(2,1)S(1)} %bitcast.117), channel_id=1, source_target_pairs={{0,2},{1,3},{2,0},{3,1},{4,6},{5,7},{6,4},{7,5},{8,10},{9,11},{10,... | collective-permute-start | bytes 688136 | tf_op jit(solution)/shard_map/ppermute | solution.py:506
  367.5 40.4 %collective-permute-start.30 = (bf16[7,128,128]{2,1,0:T(8,128)(2,1)S(1)}, bf16[7,128,128]{2,1,0:T(8,128)(2,1)S(1)}, u32[]{:S(2)}, u32[]{:S(2)}) collective-permute-start(bf16[7,128,128]{2,1,0:T(8,128)(2,1)S(1)} %bitcast.116), channel_id=1, source_target_pairs={{0,4},{1,5},{2,6},{3,7},{4,0},{5,1},{6,2},{7,3},{8,12},{9,13},{10,... | collective-permute-start | bytes 688136 | tf_op jit(solution)/shard_map/ppermute | solution.py:506
  378.2 244.4 %reduce-scatter.8.cloned.1.call-start = ((), (), s32[]{:S(2)}) async-start(), calls=%async_computation.8 | async-start | bytes 7077888 | tf_op jit(solution)/shard_map/reduce_scatter | solution.py:808
  438.0 63.0 %collective-permute-start.39 = (bf16[224,2048]{1,0:T(8,128)(2,1)S(1)}, bf16[224,2048]{1,0:T(8,128)(2,1)S(1)}, u32[]{:S(2)}, u32[]{:S(2)}) collective-permute-start(bf16[224,2048]{1,0:T(8,128)(2,1)S(1)} %copy-done.55), channel_id=1, source_target_pairs={{0,8},{8,0},{16,24},{24,16},{1,9},{9,1},{17,25},{25,17},{2,10},{10... | collective-permute-start | bytes 2752520 | tf_op jit(solution)/shard_map/ppermute | solution.py:55
  439.1 61.9 %collective-permute-start.40 = (bf16[224,2048]{1,0:T(8,128)(2,1)S(1)}, bf16[224,2048]{1,0:T(8,128)(2,1)S(1)}, u32[]{:S(2)}, u32[]{:S(2)}) collective-permute-start(bf16[224,2048]{1,0:T(8,128)(2,1)S(1)} %copy-done.54), channel_id=1, source_target_pairs={{0,16},{8,24},{16,0},{24,8},{1,17},{9,25},{17,1},{25,9},{2,18},{10... | collective-permute-start | bytes 2752520 | tf_op jit(solution)/shard_map/ppermute | solution.py:55
  439.8 40.2 %collective-permute-start.36 = (bf16[7,128,384]{2,1,0:T(8,128)(2,1)S(1)}, bf16[7,128,384]{2,1,0:T(8,128)(2,1)S(1)}, u32[]{:S(2)}, u32[]{:S(2)}) collective-permute-start(bf16[7,128,384]{2,1,0:T(8,128)(2,1)S(1)} %get-tuple-element.199), channel_id=1, source_target_pairs={{0,2},{1,3},{2,0},{3,1},{4,6},{5,7},{6,4},{7,5},{8,10},{9,11},{10,... | collective-permute-start | bytes 2064392 | tf_op jit(solution)/shard_map/ppermute | solution.py:506
  440.8 60.1 %collective-permute-start.37 = (bf16[7,128,384]{2,1,0:T(8,128)(2,1)S(1)}, bf16[7,128,384]{2,1,0:T(8,128)(2,1)S(1)}, u32[]{:S(2)}, u32[]{:S(2)}) collective-permute-start(bf16[7,128,384]{2,1,0:T(8,128)(2,1)S(1)} %get-tuple-element.200), channel_id=1, source_target_pairs={{0,4},{1,5},{2,6},{3,7},{4,0},{5,1},{6,2},{7,3},{8,12},{9,13},{10,... | collective-permute-start | bytes 2064392 | tf_op jit(solution)/shard_map/ppermute | solution.py:506
  454.1 46.8 %collective-permute-start.38 = (bf16[7,128,384]{2,1,0:T(8,128)(2,1)S(1)}, bf16[7,128,384]{2,1,0:T(8,128)(2,1)S(1)}, u32[]{:S(2)}, u32[]{:S(2)}) collective-permute-start(bf16[7,128,384]{2,1,0:T(8,128)(2,1)S(1)} %get-tuple-element.201), channel_id=1, source_target_pairs={{0,6},{1,7},{2,4},{3,5},{4,2},{5,3},{6,0},{7,1},{8,14},{9,15},{10,... | collective-permute-start | bytes 2064392 | tf_op jit(solution)/shard_map/ppermute | solution.py:506
  512.5 196.4 %all-gather.11.cloned.1.call-start = ((), (), s32[]{:S(2)}) async-start(), calls=%async_computation.9 | async-start | bytes 7077888 | tf_op jit(solution)/shard_map/all_gather | solution.py:842
  548.1 39.6 %collective-permute-start.49 = (bf16[128,2048]{1,0:T(8,128)(2,1)}, bf16[128,2048]{1,0:T(8,128)(2,1)}, u32[]{:S(2)}, u32[]{:S(2)}) collective-permute-start(bf16[128,2048]{1,0:T(8,128)(2,1)} %pad_maximum_fusion.4), channel_id=1, source_target_pairs={{0,2},{1,3},{2,0},{3,1},{4,6},{5,7},{6,4},{7,5},{8,10},{9,11},{10,... | collective-permute-start | bytes 1572872 | tf_op jit(solution)/shard_map/ppermute | solution.py:506
  563.8 47.4 %collective-permute-start.46 = (bf16[224,2048]{1,0:T(8,128)(2,1)}, bf16[224,2048]{1,0:T(8,128)(2,1)S(1)}, u32[]{:S(2)}, u32[]{:S(2)}) collective-permute-start(bf16[224,2048]{1,0:T(8,128)(2,1)} %fusion.15), channel_id=1, source_target_pairs={{0,8},{8,0},{16,24},{24,16},{1,9},{9,1},{17,25},{25,17},{2,10},{10... | collective-permute-start | bytes 2752520 | tf_op jit(solution)/shard_map/ppermute | solution.py:55
  564.4 46.8 %collective-permute-start.47 = (bf16[224,2048]{1,0:T(8,128)(2,1)}, bf16[224,2048]{1,0:T(8,128)(2,1)}, u32[]{:S(2)}, u32[]{:S(2)}) collective-permute-start(bf16[224,2048]{1,0:T(8,128)(2,1)} %fusion.16), channel_id=1, source_target_pairs={{0,16},{8,24},{16,0},{24,8},{1,17},{9,25},{17,1},{25,9},{2,18},{10... | collective-permute-start | bytes 2752520 | tf_op jit(solution)/shard_map/ppermute | solution.py:55
  565.9 45.3 %collective-permute-start.48 = (bf16[224,2048]{1,0:T(8,128)(2,1)}, bf16[224,2048]{1,0:T(8,128)(2,1)}, u32[]{:S(2)}, u32[]{:S(2)}) collective-permute-start(bf16[224,2048]{1,0:T(8,128)(2,1)} %fusion.17), channel_id=1, source_target_pairs={{0,24},{8,16},{16,8},{24,0},{1,25},{9,17},{17,9},{25,1},{2,26},{10... | collective-permute-start | bytes 2752520 | tf_op jit(solution)/shard_map/ppermute | solution.py:55
  632.3 47.6 %collective-permute-start.58 = (bf16[128,2048]{1,0:T(8,128)(2,1)}, bf16[128,2048]{1,0:T(8,128)(2,1)S(1)}, u32[]{:S(2)}, u32[]{:S(2)}) collective-permute-start(bf16[128,2048]{1,0:T(8,128)(2,1)} %pad_maximum_fusion.5), channel_id=1, source_target_pairs={{0,2},{1,3},{2,0},{3,1},{4,6},{5,7},{6,4},{7,5},{8,10},{9,11},{10,... | collective-permute-start | bytes 1572872 | tf_op jit(solution)/shard_map/ppermute | solution.py:506
  636.6 43.9 %collective-permute-start.53 = (bf16[224,2048]{1,0:T(8,128)(2,1)S(1)}, bf16[224,2048]{1,0:T(8,128)(2,1)S(1)}, u32[]{:S(2)}, u32[]{:S(2)}) collective-permute-start(bf16[224,2048]{1,0:T(8,128)(2,1)S(1)} %add_convert_fusion.3), channel_id=1, source_target_pairs={{0,8},{8,0},{16,24},{24,16},{1,9},{9,1},{17,25},{25,17},{2,10},{10... | collective-permute-start | bytes 2752520 | tf_op jit(solution)/shard_map/ppermute | solution.py:55
  638.3 42.2 %collective-permute-start.54 = (bf16[224,2048]{1,0:T(8,128)(2,1)S(1)}, bf16[224,2048]{1,0:T(8,128)(2,1)S(1)}, u32[]{:S(2)}, u32[]{:S(2)}) collective-permute-start(bf16[224,2048]{1,0:T(8,128)(2,1)S(1)} %add_convert_fusion.3), channel_id=1, source_target_pairs={{0,16},{8,24},{16,0},{24,8},{1,17},{9,25},{17,1},{25,9},{2,18},{10... | collective-permute-start | bytes 2752520 | tf_op jit(solution)/shard_map/ppermute | solution.py:55
  639.7 40.9 %collective-permute-start.55 = (bf16[224,2048]{1,0:T(8,128)(2,1)S(1)}, bf16[224,2048]{1,0:T(8,128)(2,1)S(1)}, u32[]{:S(2)}, u32[]{:S(2)}) collective-permute-start(bf16[224,2048]{1,0:T(8,128)(2,1)S(1)} %add_convert_fusion.3), channel_id=1, source_target_pairs={{0,24},{8,16},{16,8},{24,0},{1,25},{9,17},{17,9},{25,1},{2,26},{10... | collective-permute-start | bytes 2752520 | tf_op jit(solution)/shard_map/ppermute | solution.py:55
  (112 other events, 2161.5 us)
Sparse Core Ops, SparseCore 0:
  10.2 73.1 all-gather.4
  106.9 78.7 all-gather.6
  187.3 85.4 all-gather.8
  274.9 77.0 reduce-scatter.3
  378.4 93.0 reduce-scatter.5
  512.6 98.5 reduce-scatter.7
  622.8 72.9 all-gather.10

commit v9 on v8

--- a/solution.py
+++ b/solution.py
@@ -749,7 +749,6 @@
         (two_parts, grad_up_parts, grad_router, grad_pooled_own)
     )
     grad_up_part = member_sum(grad_up_parts, lambda v: v)
-    grad_up = scatter_z(grad_up_part, 0)
 
     grad_two = sum([v.astype(f32) for v in two_parts[1:]], two_parts[0])
     back_two, gain_two = normalize_back(grad_two, hat_two, inverse_two, gain_ffn)
@@ -763,9 +762,10 @@
         swap(grad_mixed[slot], slot) for slot in range(1, head_count)
     ]
     grad_heads = placed(grad_mixed, head_rank, 0)
-    grad_heads, grad_attn_own, active = lax.optimization_barrier(
-        (grad_heads, grad_attn_own, active)
-    )
+    grad_heads, grad_attn_own, active, grad_up_part = lax.optimization_barrier(
+        (grad_heads, grad_attn_own, active, grad_up_part)
+    )
+    grad_up = scatter_z(grad_up_part, 0)
     grad_attn = gather_heads(grad_attn_own)
     grad_slots = []
     for slot in range(heads):
@@ -832,13 +832,16 @@
     one_parts = scatter_heads(one_parts)
     total_out = scatter_places(total_out)
 
+    one_parts, total_qkv, total_out, output_slots = lax.optimization_barrier(
+        (one_parts, total_qkv, total_out, output_slots)
+    )
+    output_slots.append(swap(output_slots[0], head_count - 1))
+
     grad_one = sum([v.astype(f32) for v in one_parts[1:]], one_parts[0]) + grad_pooled_own
     back_one, gain_one = normalize_back(grad_one, hat_own, inverse_own, gain_attn)
     tokens_back = (grad_hidden + back_one).astype(bf16)
     gains = butterfly(jnp.stack([gain_one, gain_two]), "heads", head_count)
-    tokens_back, total_qkv, total_out, gains = lax.optimization_barrier(
-        (tokens_back, total_qkv, total_out, gains)
-    )
+    tokens_back, gains = lax.optimization_barrier((tokens_back, gains))
     total_qkv = lax.all_gather(total_qkv, "seq", axis=0, tiled=True)
     token_slots = gather_heads(tokens_back)
     grad_out = gather_seq(total_out).astype(f32)
@@ -849,10 +852,7 @@
         ],
         axis=1,
     )
-    token_slots, gains, output_slots = lax.optimization_barrier(
-        (token_slots, gains, output_slots)
-    )
-    output_slots.append(swap(output_slots[0], head_count - 1))
+    token_slots, gains = lax.optimization_barrier((token_slots, gains))
     output = in_order(output_slots, bf16)
     gains = butterfly(gains, "seq", seq_count)
     grad_tokens = in_order(token_slots, f32)

time: 732 us -> 742 us (1.014)
    ppermute x16, waiting for transfers between devices: 184 us -> 211 us  [across(): return lax.ppermute(values, 'seq', pairs)]
    ppermute x38, waiting for transfers between devices: 116 us -> 95.6 us  [flip(): return lax.ppermute(values, axis, [(i, i ^ bit) for i in range(size)])]
    ppermute x16, starting transfers between devices: 49.4 us -> 65.7 us  [across(): return lax.ppermute(values, 'seq', pairs)]
    reduce_scatter x1, starting transfers between devices: 12.9 us -> 0.51 us  [local(): lax.psum_scatter(grad_qkv_part, 'seq', scatter_dimension=0, tiled=True)]
  transfers between devices with their start and end apart: 70 -> 70, of which waited for: 32 -> 31; matrix products, arithmetic and copies ran while one was open for 28% -> 27% of each run, Pallas kernels for 8% -> 8%
where the time goes in v9:
time: 742 us; the launch traced here: 734 us
  waiting for transfers between devices  322 us (43%)
  matrix products  134 us (18%)
  starting transfers between devices  124 us (17%)
  Pallas kernels  55.7 us (8%)
  other arithmetic  52.7 us (7%)
  local copies, waits for them, and re-layouts  29.7 us (4%)
  between operations  16.3 us (2%)
    ppermute x16, waiting for transfers between devices, across(): return lax.ppermute(values, 'seq', pairs)  211 us
    ppermute x38, waiting for transfers between devices, flip(): return lax.ppermute(values, axis, [(i, i ^ bit) for i in range(size)])  95.6 us
    dot_general x24, matrix products, contract(): lax.dot_general(left, right, (((left_dim,), (right_dim,)), ((), ())), pre...  94.3 us
    ppermute x16, starting transfers between devices, across(): return lax.ppermute(values, 'seq', pairs)  65.7 us
    ppermute x38, starting transfers between devices, flip(): return lax.ppermute(values, axis, [(i, i ^ bit) for i in range(size)])  55.8 us
    dot_general x6, matrix products, dot(): return jnp.dot(left, right, preferred_element_type=f32)  35.7 us
    pallas_call x1, Pallas kernels, attend_backward(): pl.pallas_call(functools.partial(back_kernel, heads, members), out_shape=...  21.1 us
    pallas_call x1, Pallas kernels, project(): pl.pallas_call(functools.partial(project_kernel, heads), out_shape=[jax.S...  16.3 us
  transfers between devices with their start and end apart: 70, of which 31 were waited for; matrix products, arithmetic and copies ran while one was open for 27% of the time, Pallas kernels for 8%

profile of v9, /device:TPU:0, one launch (start us, length us, event | category | flops | bytes accessed | tf_op | source)
XLA Modules:
  0.0 734.0 jit_solution(4915871606911841466)
XLA Ops:
  17.0 16.3 %project.1 = (bf16[7,128,384]{2,1,0:T(8,128)(2,1)S(1)}, bf16[7,128,384]{2,1,0:T(8,128)(2,1)}, bf16[7,128,384]{2,1,0:T(8,128)(2,1)S(1)}, bf16[7,128,384]{2,1,0:T(...) custom-call(s32[7]{0:T(128)S(1)} %pad_add_fusion.scal, bf16[896,2048]{1,0:T(8,128)(2,1)} %tokens.1, ...), custom_call_target="tpu_custom_call" | custom-call | flops 5637144576 | bytes 16777216 | tf_op jit(solution)/shard_map/project/pallas_call | solution.py:402
  42.6 43.9 %collective-permute-done.refs_1_ = bf16[7,128,384]{2,1,0:T(8,128)(2,1)S(1)} collective-permute-done((bf16[7,128,384]{2,1,0:T(8,128)(2,1)}, bf16[7,128,384]{2,1,0:T(8,128)(2,1)S(1)}, u32[]{:S(2)}, u32[]{:S(2)}) %collective-permute-start) | collective-permute-done | bytes 688160 | tf_op jit(solution)/shard_map/ppermute | solution.py:506
  90.2 13.1 %collective-permute-done.2.refs_3_ = bf16[7,128,384]{2,1,0:T(8,128)(2,1)} collective-permute-done((bf16[7,128,384]{2,1,0:T(8,128)(2,1)S(1)}, bf16[7,128,384]{2,1,0:T(8,128)(2,1)}, u32[]{:S(2)}, u32[]{:S(2)}) %collective-permute-start.2) | collective-permute-done | bytes 688160 | tf_op jit(solution)/shard_map/ppermute | solution.py:506
  110.4 15.5 %attend_forward.1 = (bf16[7,128,128]{2,1,0:T(8,128)(2,1)}, bf16[7,128,128]{2,1,0:T(8,128)(2,1)}, bf16[7,128,128]{2,1,0:T(8,128)(2,1)}, bf16[7,128,128]{2,1,0:T(8,128)(2,1)}, f32[4,7,1,128]{3,2,1,0:T(1,128)}) custom-call(s32[7]{0:T(128)} %copy-done.6, bf16[7,128,384]{2,1,0:T(8,128)(2,1)} %copy-done.8, bf16[7,128,384]{2,1,0:T(8,128)(2,1)} %copy-done.59, ...), custom_call_target="tpu_custom_call" | custom-call | flops 4000000000 | bytes 7340032 | tf_op jit(solution)/shard_map/attend_forward/pallas_call | solution.py:185
  125.9 14.4 %collective-permute-start.10 = (bf16[7,128,128]{2,1,0:T(8,128)(2,1)}, bf16[7,128,128]{2,1,0:T(8,128)(2,1)S(1)}, u32[]{:S(2)}, u32[]{:S(2)}) collective-permute-start(bf16[7,128,128]{2,1,0:T(8,128)(2,1)} %get-tuple-element.149), channel_id=1, source_target_pairs={{0,4},{1,5},{2,6},{3,7},{4,0},{5,1},{6,2},{7,3},{8,12},{9,13},{10,... | collective-permute-start | bytes 688136 | tf_op jit(solution)/shard_map/ppermute | solution.py:506
  149.0 24.8 %collective-permute-done.13 = f32[5,2048]{1,0:T(8,128)S(1)} collective-permute-done((f32[5,2048]{1,0:T(8,128)S(1)}, f32[5,2048]{1,0:T(8,128)S(1)}, u32[]{:S(2)}, u32[]{:S(2)}) %collective-permute-start.13) | collective-permute-done | bytes 40992 | tf_op jit(solution)/shard_map/ppermute | solution.py:55
  194.3 11.0 %collective-permute-start.21 = (f32[5,2048]{1,0:T(8,128)S(1)}, f32[5,2048]{1,0:T(8,128)S(1)}, u32[]{:S(2)}, u32[]{:S(2)}) collective-permute-start(f32[5,2048]{1,0:T(8,128)S(1)} %add.433), channel_id=1, source_target_pairs={{0,4},{1,5},{2,6},{3,7},{4,0},{5,1},{6,2},{7,3},{8,12},{9,13},{10,... | collective-permute-start | bytes 122888 | tf_op jit(solution)/shard_map/ppermute | solution.py:55
  205.4 9.1 %collective-permute-done.21 = f32[5,2048]{1,0:T(8,128)S(1)} collective-permute-done((f32[5,2048]{1,0:T(8,128)S(1)}, f32[5,2048]{1,0:T(8,128)S(1)}, u32[]{:S(2)}, u32[]{:S(2)}) %collective-permute-start.21) | collective-permute-done | bytes 40992 | tf_op jit(solution)/shard_map/ppermute | solution.py:55
  214.5 8.3 %pad_maximum_fusion = bf16[2048,2048]{1,0:T(8,128)(2,1)} fusion(bf16[2048,1024]{1,0:T(8,128)(2,1)} %all-gather.7.cloned.1.call-done, bf16[2048,1024]{1,0:T(8,128)(2,1)} %all-gather.5.cloned.1.call-done), kind=kLoop, calls=%fused_computation.2 | loop fusion | flops 16777216 | bytes 16777216 | tf_op jit(solution)/shard_map/concatenate | solution.py:708
  222.9 7.5 %collective-permute-done.19 = bf16[224,2048]{1,0:T(8,128)(2,1)} collective-permute-done((bf16[224,2048]{1,0:T(8,128)(2,1)S(1)}, bf16[224,2048]{1,0:T(8,128)(2,1)}, u32[]{:S(2)}, u32[]{:S(2)}) %collective-permute-start.19) | collective-permute-done | bytes 917536 | tf_op jit(solution)/shard_map/ppermute | solution.py:55
  236.0 13.1 %fusion = (bf16[896,2048]{1,0:T(8,128)(2,1)S(1)}, f32[896,2048]{1,0:T(8,128)}) fusion(s32[2048]{0:T(1024)S(1)} %iota_add_fusion, s32[896]{0:T(1024)S(1)} %add_multiply_fusion, bf16[896,2048]{1,0:T(8,128)(2,1)S(1)} %constant_dynamic-update-slice_fusion.4, bf16[2048,2048]{1,0:T(8,128)(2,1)} %pad_maximum_fusion), kind=kOutput, calls=%fused_computation.6 | convolution fusion | flops 7525367808 | bytes 23080448 | tf_op jit(solution)/shard_map/dot_general | solution.py:29
  261.9 6.3 add_convert_fusion.1
  272.7 13.4 %fusion.3 = bf16[896,2048]{1,0:T(8,128)(2,1)S(1)} fusion(f32[896,2048]{1,0:T(8,128)} %get-tuple-element.171, s32[2048]{0:T(1024)S(1)} %iota_add_fusion, s32[896]{0:T(1024)S(1)} %add_multiply_fusion, bf16[896,2048]{1,0:T(8,128)(2,1)} %copy-done.12, bf16[2048,2048]{1,0:T(8,128)(2,1)} %all-gather.9.cloned.1.call-done), kind=kOutput, calls=%fused_computation.9 | convolution fusion | flops 7529037824 | bytes 23080448 | tf_op jit(solution)/shard_map/dot_general | solution.py:33
  286.2 7.4 %convolution_convert_fusion.8 = bf16[224,2048]{1,0:T(8,128)(2,1)S(1)} fusion(bf16[2048,2048]{1,0:T(8,128)(2,1)} %pad_maximum_fusion, bf16[896,2048]{1,0:T(8,128)(2,1)S(1)} %fusion.3), kind=kOutput, calls=%fused_computation.43 | convolution fusion | flops 1879506944 | bytes 10223616 | tf_op jit(solution)/shard_map/dot_general | solution.py:33
  293.6 6.3 convolution_convert_fusion.9
  306.2 7.3 convolution_convert_fusion.1
  317.4 7.3 convolution_convert_fusion.2
  324.7 18.3 %collective-permute-done.24 = bf16[224,2048]{1,0:T(8,128)(2,1)S(1)} collective-permute-done((bf16[224,2048]{1,0:T(8,128)(2,1)S(1)}, bf16[224,2048]{1,0:T(8,128)(2,1)S(1)}, u32[]{:S(2)}, u32[]{:S(2)}) %collective-permute-start.24) | collective-permute-done | bytes 917536 | tf_op jit(solution)/shard_map/ppermute | solution.py:55
  346.5 6.0 convolution_convert_fusion.7
  361.3 5.6 collective-permute-done.27
  382.0 7.3 convolution_convert_fusion.4
  401.3 8.0 %collective-permute-done.31.refs_10_ = bf16[7,128,128]{2,1,0:T(8,128)(2,1)S(1)} collective-permute-done((bf16[7,128,128]{2,1,0:T(8,128)(2,1)S(1)}, bf16[7,128,128]{2,1,0:T(8,128)(2,1)S(1)}, u32[]{:S(2)}, u32[]{:S(2)}) %collective-permute-start.31) | collective-permute-done | bytes 229408 | tf_op jit(solution)/shard_map/ppermute | solution.py:506
  410.1 21.1 %attend_backward.1 = (bf16[7,128,384]{2,1,0:T(8,128)(2,1)}, bf16[7,128,384]{2,1,0:T(8,128)(2,1)}, bf16[7,128,384]{2,1,0:T(8,128)(2,1)}, bf16[7,128,384]{2,1,0:T(8,128)(2,1)}, bf16[4,7,128,384]{3,2,1,0:T(8,128)(2,1)}) custom-call(s32[7]{0:T(128)} %copy-done.6, bf16[7,128,384]{2,1,0:T(8,128)(2,1)} %copy-done.8, bf16[7,128,384]{2,1,0:T(8,128)(2,1)} %copy-done.59, ...), custom_call_target="tpu_custom_call" | custom-call | flops 10000000000 | bytes 12582912 | tf_op jit(solution)/shard_map/attend_backward/pallas_call | solution.py:311
  441.1 17.1 %collective-permute-start.37 = (bf16[7,128,384]{2,1,0:T(8,128)(2,1)S(1)}, bf16[7,128,384]{2,1,0:T(8,128)(2,1)S(1)}, u32[]{:S(2)}, u32[]{:S(2)}) collective-permute-start(bf16[7,128,384]{2,1,0:T(8,128)(2,1)S(1)} %get-tuple-element.205), channel_id=1, source_target_pairs={{0,2},{1,3},{2,0},{3,1},{4,6},{5,7},{6,4},{7,5},{8,10},{9,11},{10,... | collective-permute-start | bytes 2064392 | tf_op jit(solution)/shard_map/ppermute | solution.py:506
  465.8 19.7 %collective-permute-done.37.refs_1_ = bf16[7,128,384]{2,1,0:T(8,128)(2,1)S(1)} collective-permute-done((bf16[7,128,384]{2,1,0:T(8,128)(2,1)S(1)}, bf16[7,128,384]{2,1,0:T(8,128)(2,1)S(1)}, u32[]{:S(2)}, u32[]{:S(2)}) %collective-permute-start.37) | collective-permute-done | bytes 688160 | tf_op jit(solution)/shard_map/ppermute | solution.py:506
  486.6 25.4 %collective-permute-done.38.refs_2_ = bf16[7,128,384]{2,1,0:T(8,128)(2,1)S(1)} collective-permute-done((bf16[7,128,384]{2,1,0:T(8,128)(2,1)S(1)}, bf16[7,128,384]{2,1,0:T(8,128)(2,1)S(1)}, u32[]{:S(2)}, u32[]{:S(2)}) %collective-permute-start.38) | collective-permute-done | bytes 688160 | tf_op jit(solution)/shard_map/ppermute | solution.py:506
  514.9 8.7 %convolution_convert_fusion = bf16[2048,1536]{1,0:T(8,128)(2,1)} fusion(bf16[896,2048]{1,0:T(8,128)(2,1)S(1)} %copy-done.70, bf16[896,1536]{1,0:T(8,128)(2,1)S(1)} %gather_grads.1), kind=kOutput, calls=%fused_computation.5 | convolution fusion | flops 5640290304 | bytes 12713984 | tf_op jit(solution)/shard_map/dot_general | solution.py:33
  558.9 15.1 %collective-permute-start.49 = (bf16[128,2048]{1,0:T(8,128)(2,1)}, bf16[128,2048]{1,0:T(8,128)(2,1)S(1)}, u32[]{:S(2)}, u32[]{:S(2)}) collective-permute-start(bf16[128,2048]{1,0:T(8,128)(2,1)} %pad_maximum_fusion.4), channel_id=1, source_target_pairs={{0,2},{1,3},{2,0},{3,1},{4,6},{5,7},{6,4},{7,5},{8,10},{9,11},{10,... | collective-permute-start | bytes 1572872 | tf_op jit(solution)/shard_map/ppermute | solution.py:506
  577.5 20.4 %collective-permute-done.49 = bf16[128,2048]{1,0:T(8,128)(2,1)S(1)} collective-permute-done((bf16[128,2048]{1,0:T(8,128)(2,1)}, bf16[128,2048]{1,0:T(8,128)(2,1)S(1)}, u32[]{:S(2)}, u32[]{:S(2)}) %collective-permute-start.49) | collective-permute-done | bytes 524320 | tf_op jit(solution)/shard_map/ppermute | solution.py:506
  601.6 19.9 %collective-permute-done.50 = bf16[64,2048]{1,0:T(8,128)(2,1)} collective-permute-done((bf16[64,2048]{1,0:T(8,128)(2,1)}, bf16[64,2048]{1,0:T(8,128)(2,1)}, u32[]{:S(2)}, u32[]{:S(2)}) %collective-permute-start.50) | collective-permute-done | bytes 262176 | tf_op jit(solution)/shard_map/ppermute | solution.py:506
  637.0 25.1 %collective-permute-done.57 = bf16[64,2048]{1,0:T(8,128)(2,1)S(1)} collective-permute-done((bf16[64,2048]{1,0:T(8,128)(2,1)S(1)}, bf16[64,2048]{1,0:T(8,128)(2,1)S(1)}, u32[]{:S(2)}, u32[]{:S(2)}) %collective-permute-start.57) | collective-permute-done | bytes 262176 | tf_op jit(solution)/shard_map/ppermute | solution.py:506
  665.9 35.3 %collective-permute-done.58 = bf16[128,2048]{1,0:T(8,128)(2,1)S(1)} collective-permute-done((bf16[128,2048]{1,0:T(8,128)(2,1)S(1)}, bf16[128,2048]{1,0:T(8,128)(2,1)S(1)}, u32[]{:S(2)}, u32[]{:S(2)}) %collective-permute-start.58) | collective-permute-done | bytes 524320 | tf_op jit(solution)/shard_map/ppermute | solution.py:506
  (414 shorter events, 239.8 us)
Async XLA Ops:
  7.2 207.3 %all-gather.5.cloned.1.call-start = ((), (), s32[]{:S(2)}) async-start(), calls=%async_computation.3 | async-start | bytes 4718592 | tf_op jit(solution)/shard_map/all_gather | solution.py:631
  9.5 205.0 %all-gather.7.cloned.1.call-start = ((), (), s32[]{:S(2)}) async-start(), calls=%async_computation.4 | async-start | bytes 4718592 | tf_op jit(solution)/shard_map/all_gather | solution.py:686
  9.6 97.2 %collective-permute-start.7 = (bf16[512,2048]{1,0:T(8,128)(2,1)}, bf16[512,2048]{1,0:T(8,128)(2,1)}, u32[]{:S(2)}, u32[]{:S(2)}) collective-permute-start(bf16[512,2048]{1,0:T(8,128)(2,1)} %param.14), channel_id=1, source_target_pairs={{0,8},{8,0},{16,24},{24,16},{1,9},{9,1},{17,25},{25,17},{2,10},{10... | collective-permute-start | bytes 6291464 | tf_op jit(solution)/shard_map/ppermute | solution.py:55
  12.6 94.2 %collective-permute-start.8 = (bf16[512,2048]{1,0:T(8,128)(2,1)}, bf16[512,2048]{1,0:T(8,128)(2,1)}, u32[]{:S(2)}, u32[]{:S(2)}) collective-permute-start(bf16[512,2048]{1,0:T(8,128)(2,1)} %param.14), channel_id=1, source_target_pairs={{0,16},{8,24},{16,0},{24,8},{1,17},{9,25},{17,1},{25,9},{2,18},{10... | collective-permute-start | bytes 6291464 | tf_op jit(solution)/shard_map/ppermute | solution.py:55
  33.3 53.2 %collective-permute-start = (bf16[7,128,384]{2,1,0:T(8,128)(2,1)}, bf16[7,128,384]{2,1,0:T(8,128)(2,1)S(1)}, u32[]{:S(2)}, u32[]{:S(2)}) collective-permute-start(bf16[7,128,384]{2,1,0:T(8,128)(2,1)} %get-tuple-element.135), channel_id=1, source_target_pairs={{0,2},{1,3},{2,0},{3,1},{4,6},{5,7},{6,4},{7,5},{8,10},{9,11},{10,... | collective-permute-start | bytes 2064392 | tf_op jit(solution)/shard_map/ppermute | solution.py:506
  35.0 54.6 %collective-permute-start.1 = (bf16[7,128,384]{2,1,0:T(8,128)(2,1)S(1)}, bf16[7,128,384]{2,1,0:T(8,128)(2,1)}, u32[]{:S(2)}, u32[]{:S(2)}) collective-permute-start(bf16[7,128,384]{2,1,0:T(8,128)(2,1)S(1)} %get-tuple-element.136), channel_id=1, source_target_pairs={{0,4},{1,5},{2,6},{3,7},{4,0},{5,1},{6,2},{7,3},{8,12},{9,13},{10,... | collective-permute-start | bytes 2064392 | tf_op jit(solution)/shard_map/ppermute | solution.py:506
  37.5 65.7 %collective-permute-start.2 = (bf16[7,128,384]{2,1,0:T(8,128)(2,1)S(1)}, bf16[7,128,384]{2,1,0:T(8,128)(2,1)}, u32[]{:S(2)}, u32[]{:S(2)}) collective-permute-start(bf16[7,128,384]{2,1,0:T(8,128)(2,1)S(1)} %get-tuple-element.137), channel_id=1, source_target_pairs={{0,6},{1,7},{2,4},{3,5},{4,2},{5,3},{6,0},{7,1},{8,14},{9,15},{10,... | collective-permute-start | bytes 2064392 | tf_op jit(solution)/shard_map/ppermute | solution.py:506
  106.8 166.0 %all-gather.9.cloned.1.call-start = ((), (), s32[]{:S(2)}) async-start(), calls=%async_computation.5 | async-start | bytes 9437184 | tf_op jit(solution)/shard_map/all_gather | solution.py:687
  107.5 416.1 %reduce-scatter.4.cloned.1.call-start = ((), (), s32[]{:S(2)}) async-start(), calls=%async_computation.6 | async-start | bytes 5242880 | tf_op jit(solution)/shard_map/reduce_scatter | solution.py:539
  107.8 70.1 %collective-permute-start.17 = (bf16[512,2048]{1,0:T(8,128)(2,1)}, bf16[512,2048]{1,0:T(8,128)(2,1)S(1)}, u32[]{:S(2)}, u32[]{:S(2)}) collective-permute-start(bf16[512,2048]{1,0:T(8,128)(2,1)} %param.14), channel_id=1, source_target_pairs={{0,24},{8,16},{16,8},{24,0},{1,25},{9,17},{17,9},{25,1},{2,26},{10... | collective-permute-start | bytes 6291464 | tf_op jit(solution)/shard_map/ppermute | solution.py:55
  125.9 47.9 %collective-permute-start.10 = (bf16[7,128,128]{2,1,0:T(8,128)(2,1)}, bf16[7,128,128]{2,1,0:T(8,128)(2,1)S(1)}, u32[]{:S(2)}, u32[]{:S(2)}) collective-permute-start(bf16[7,128,128]{2,1,0:T(8,128)(2,1)} %get-tuple-element.149), channel_id=1, source_target_pairs={{0,4},{1,5},{2,6},{3,7},{4,0},{5,1},{6,2},{7,3},{8,12},{9,13},{10,... | collective-permute-start | bytes 688136 | tf_op jit(solution)/shard_map/ppermute | solution.py:506
  192.8 39.3 %collective-permute-start.20 = (bf16[224,2048]{1,0:T(8,128)(2,1)S(1)}, bf16[224,2048]{1,0:T(8,128)(2,1)}, u32[]{:S(2)}, u32[]{:S(2)}) collective-permute-start(bf16[224,2048]{1,0:T(8,128)(2,1)S(1)} %multiply_convert_fusion), channel_id=1, source_target_pairs={{0,24},{8,16},{16,8},{24,0},{1,25},{9,17},{17,9},{25,1},{2,26},{10... | collective-permute-start | bytes 2752520 | tf_op jit(solution)/shard_map/ppermute | solution.py:55
  268.2 255.4 %reduce-scatter.6.cloned.1.call-start = ((), (), s32[]{:S(2)}) async-start(), calls=%async_computation.7 | async-start | bytes 5242880 | tf_op jit(solution)/shard_map/reduce_scatter | solution.py:539
  302.6 40.5 %collective-permute-start.24 = (bf16[224,2048]{1,0:T(8,128)(2,1)S(1)}, bf16[224,2048]{1,0:T(8,128)(2,1)S(1)}, u32[]{:S(2)}, u32[]{:S(2)}) collective-permute-start(bf16[224,2048]{1,0:T(8,128)(2,1)S(1)} %convolution_convert_fusion.9), channel_id=1, source_target_pairs={{0,16},{8,24},{16,0},{24,8},{1,17},{9,25},{17,1},{25,9},{2,18},{10... | collective-permute-start | bytes 2752520 | tf_op jit(solution)/shard_map/ppermute | solution.py:55
  371.0 60.2 %collective-permute-start.33 = (bf16[224,2048]{1,0:T(8,128)(2,1)S(1)}, bf16[224,2048]{1,0:T(8,128)(2,1)}, u32[]{:S(2)}, u32[]{:S(2)}) collective-permute-start(bf16[224,2048]{1,0:T(8,128)(2,1)S(1)} %get-tuple-element.192), channel_id=1, source_target_pairs={{0,8},{8,0},{16,24},{24,16},{1,9},{9,1},{17,25},{25,17},{2,10},{10... | collective-permute-start | bytes 2752520 | tf_op jit(solution)/shard_map/ppermute | solution.py:55
  371.6 59.7 %collective-permute-start.34 = (bf16[224,2048]{1,0:T(8,128)(2,1)S(1)}, bf16[224,2048]{1,0:T(8,128)(2,1)}, u32[]{:S(2)}, u32[]{:S(2)}) collective-permute-start(bf16[224,2048]{1,0:T(8,128)(2,1)S(1)} %get-tuple-element.192), channel_id=1, source_target_pairs={{0,16},{8,24},{16,0},{24,8},{1,17},{9,25},{17,1},{25,9},{2,18},{10... | collective-permute-start | bytes 2752520 | tf_op jit(solution)/shard_map/ppermute | solution.py:55
  381.4 241.4 %reduce-scatter.8.cloned.1.call-start = ((), (), s32[]{:S(2)}) async-start(), calls=%async_computation.8 | async-start | bytes 7077888 | tf_op jit(solution)/shard_map/reduce_scatter | solution.py:808
  439.5 72.6 %collective-permute-start.40 = (bf16[224,2048]{1,0:T(8,128)(2,1)S(1)}, bf16[224,2048]{1,0:T(8,128)(2,1)S(1)}, u32[]{:S(2)}, u32[]{:S(2)}) collective-permute-start(bf16[224,2048]{1,0:T(8,128)(2,1)S(1)} %copy-done.58), channel_id=1, source_target_pairs={{0,8},{8,0},{16,24},{24,16},{1,9},{9,1},{17,25},{25,17},{2,10},{10... | collective-permute-start | bytes 2752520 | tf_op jit(solution)/shard_map/ppermute | solution.py:55
  439.8 72.2 %collective-permute-start.41 = (bf16[224,2048]{1,0:T(8,128)(2,1)S(1)}, bf16[224,2048]{1,0:T(8,128)(2,1)S(1)}, u32[]{:S(2)}, u32[]{:S(2)}) collective-permute-start(bf16[224,2048]{1,0:T(8,128)(2,1)S(1)} %convolution_convert_fusion.5), channel_id=1, source_target_pairs={{0,16},{8,24},{16,0},{24,8},{1,17},{9,25},{17,1},{25,9},{2,18},{10... | collective-permute-start | bytes 2752520 | tf_op jit(solution)/shard_map/ppermute | solution.py:55
  441.1 44.3 %collective-permute-start.37 = (bf16[7,128,384]{2,1,0:T(8,128)(2,1)S(1)}, bf16[7,128,384]{2,1,0:T(8,128)(2,1)S(1)}, u32[]{:S(2)}, u32[]{:S(2)}) collective-permute-start(bf16[7,128,384]{2,1,0:T(8,128)(2,1)S(1)} %get-tuple-element.205), channel_id=1, source_target_pairs={{0,2},{1,3},{2,0},{3,1},{4,6},{5,7},{6,4},{7,5},{8,10},{9,11},{10,... | collective-permute-start | bytes 2064392 | tf_op jit(solution)/shard_map/ppermute | solution.py:506
  458.2 53.8 %collective-permute-start.38 = (bf16[7,128,384]{2,1,0:T(8,128)(2,1)S(1)}, bf16[7,128,384]{2,1,0:T(8,128)(2,1)S(1)}, u32[]{:S(2)}, u32[]{:S(2)}) collective-permute-start(bf16[7,128,384]{2,1,0:T(8,128)(2,1)S(1)} %get-tuple-element.206), channel_id=1, source_target_pairs={{0,4},{1,5},{2,6},{3,7},{4,0},{5,1},{6,2},{7,3},{8,12},{9,13},{10,... | collective-permute-start | bytes 2064392 | tf_op jit(solution)/shard_map/ppermute | solution.py:506
  458.2 53.8 %collective-permute-start.39 = (bf16[7,128,384]{2,1,0:T(8,128)(2,1)S(1)}, bf16[7,128,384]{2,1,0:T(8,128)(2,1)S(1)}, u32[]{:S(2)}, u32[]{:S(2)}) collective-permute-start(bf16[7,128,384]{2,1,0:T(8,128)(2,1)S(1)} %get-tuple-element.207), channel_id=1, source_target_pairs={{0,6},{1,7},{2,4},{3,5},{4,2},{5,3},{6,0},{7,1},{8,14},{9,15},{10,... | collective-permute-start | bytes 2064392 | tf_op jit(solution)/shard_map/ppermute | solution.py:506
  523.6 194.8 %all-gather.11.cloned.1.call-start = ((), (), s32[]{:S(2)}) async-start(), calls=%async_computation.9 | async-start | bytes 7077888 | tf_op jit(solution)/shard_map/all_gather | solution.py:845
  558.9 39.0 %collective-permute-start.49 = (bf16[128,2048]{1,0:T(8,128)(2,1)}, bf16[128,2048]{1,0:T(8,128)(2,1)S(1)}, u32[]{:S(2)}, u32[]{:S(2)}) collective-permute-start(bf16[128,2048]{1,0:T(8,128)(2,1)} %pad_maximum_fusion.4), channel_id=1, source_target_pairs={{0,2},{1,3},{2,0},{3,1},{4,6},{5,7},{6,4},{7,5},{8,10},{9,11},{10,... | collective-permute-start | bytes 1572872 | tf_op jit(solution)/shard_map/ppermute | solution.py:506
  574.0 48.8 %collective-permute-start.46 = (bf16[224,2048]{1,0:T(8,128)(2,1)}, bf16[224,2048]{1,0:T(8,128)(2,1)S(1)}, u32[]{:S(2)}, u32[]{:S(2)}) collective-permute-start(bf16[224,2048]{1,0:T(8,128)(2,1)} %fusion.15), channel_id=1, source_target_pairs={{0,8},{8,0},{16,24},{24,16},{1,9},{9,1},{17,25},{25,17},{2,10},{10... | collective-permute-start | bytes 2752520 | tf_op jit(solution)/shard_map/ppermute | solution.py:55
  575.0 47.8 %collective-permute-start.47 = (bf16[224,2048]{1,0:T(8,128)(2,1)}, bf16[224,2048]{1,0:T(8,128)(2,1)}, u32[]{:S(2)}, u32[]{:S(2)}) collective-permute-start(bf16[224,2048]{1,0:T(8,128)(2,1)} %fusion.16), channel_id=1, source_target_pairs={{0,16},{8,24},{16,0},{24,8},{1,17},{9,25},{17,1},{25,9},{2,18},{10... | collective-permute-start | bytes 2752520 | tf_op jit(solution)/shard_map/ppermute | solution.py:55
  576.0 46.8 %collective-permute-start.48 = (bf16[224,2048]{1,0:T(8,128)(2,1)}, bf16[224,2048]{1,0:T(8,128)(2,1)}, u32[]{:S(2)}, u32[]{:S(2)}) collective-permute-start(bf16[224,2048]{1,0:T(8,128)(2,1)} %fusion.17), channel_id=1, source_target_pairs={{0,24},{8,16},{16,8},{24,0},{1,25},{9,17},{17,9},{25,1},{2,26},{10... | collective-permute-start | bytes 2752520 | tf_op jit(solution)/shard_map/ppermute | solution.py:55
  631.2 70.7 %collective-permute-start.51 = (bf16[224,2048]{1,0:T(8,128)(2,1)S(1)}, bf16[224,2048]{1,0:T(8,128)(2,1)S(1)}, u32[]{:S(2)}, u32[]{:S(2)}) collective-permute-start(bf16[224,2048]{1,0:T(8,128)(2,1)S(1)} %copy-done.21), channel_id=1, source_target_pairs={{0,24},{8,16},{16,8},{24,0},{1,25},{9,17},{17,9},{25,1},{2,26},{10... | collective-permute-start | bytes 2752520 | tf_op jit(solution)/shard_map/ppermute | solution.py:55
  662.1 39.1 %collective-permute-start.58 = (bf16[128,2048]{1,0:T(8,128)(2,1)S(1)}, bf16[128,2048]{1,0:T(8,128)(2,1)S(1)}, u32[]{:S(2)}, u32[]{:S(2)}) collective-permute-start(bf16[128,2048]{1,0:T(8,128)(2,1)S(1)} %pad_maximum_fusion.5), channel_id=1, source_target_pairs={{0,2},{1,3},{2,0},{3,1},{4,6},{5,7},{6,4},{7,5},{8,10},{9,11},{10,... | collective-permute-start | bytes 1572872 | tf_op jit(solution)/shard_map/ppermute | solution.py:506
  662.4 39.7 %collective-permute-start.54 = (bf16[224,2048]{1,0:T(8,128)(2,1)S(1)}, bf16[224,2048]{1,0:T(8,128)(2,1)S(1)}, u32[]{:S(2)}, u32[]{:S(2)}) collective-permute-start(bf16[224,2048]{1,0:T(8,128)(2,1)S(1)} %add_convert_fusion.3), channel_id=1, source_target_pairs={{0,8},{8,0},{16,24},{24,16},{1,9},{9,1},{17,25},{25,17},{2,10},{10... | collective-permute-start | bytes 2752520 | tf_op jit(solution)/shard_map/ppermute | solution.py:55
  662.7 40.8 %collective-permute-start.55 = (bf16[224,2048]{1,0:T(8,128)(2,1)S(1)}, bf16[224,2048]{1,0:T(8,128)(2,1)S(1)}, u32[]{:S(2)}, u32[]{:S(2)}) collective-permute-start(bf16[224,2048]{1,0:T(8,128)(2,1)S(1)} %add_convert_fusion.3), channel_id=1, source_target_pairs={{0,16},{8,24},{16,0},{24,8},{1,17},{9,25},{17,1},{25,9},{2,18},{10... | collective-permute-start | bytes 2752520 | tf_op jit(solution)/shard_map/ppermute | solution.py:55
  664.4 40.7 %collective-permute-start.56 = (bf16[224,2048]{1,0:T(8,128)(2,1)S(1)}, bf16[224,2048]{1,0:T(8,128)(2,1)S(1)}, u32[]{:S(2)}, u32[]{:S(2)}) collective-permute-start(bf16[224,2048]{1,0:T(8,128)(2,1)S(1)} %add_convert_fusion.3), channel_id=1, source_target_pairs={{0,24},{8,16},{16,8},{24,0},{1,25},{9,17},{17,9},{25,1},{2,26},{10... | collective-permute-start | bytes 2752520 | tf_op jit(solution)/shard_map/ppermute | solution.py:55
  (115 other events, 2159.4 us)
Sparse Core Ops, SparseCore 0:
  10.2 73.1 all-gather.4
  106.9 78.7 all-gather.6
  187.3 85.4 all-gather.8
  274.9 77.0 reduce-scatter.3
  381.5 82.1 reduce-scatter.5
  523.7 98.8 reduce-scatter.7
  624.3 75.5 all-gather.10

commit v10 on v8

--- a/solution.py
+++ b/solution.py
@@ -830,14 +830,15 @@
         (one_parts, total_out, output_slots)
     )
     one_parts = scatter_heads(one_parts)
+    output_slots.append(swap(output_slots[0], head_count - 1))
     total_out = scatter_places(total_out)
 
     grad_one = sum([v.astype(f32) for v in one_parts[1:]], one_parts[0]) + grad_pooled_own
     back_one, gain_one = normalize_back(grad_one, hat_own, inverse_own, gain_attn)
     tokens_back = (grad_hidden + back_one).astype(bf16)
     gains = butterfly(jnp.stack([gain_one, gain_two]), "heads", head_count)
-    tokens_back, total_qkv, total_out, gains = lax.optimization_barrier(
-        (tokens_back, total_qkv, total_out, gains)
+    tokens_back, total_qkv, total_out, gains, output_slots = lax.optimization_barrier(
+        (tokens_back, total_qkv, total_out, gains, output_slots)
     )
     total_qkv = lax.all_gather(total_qkv, "seq", axis=0, tiled=True)
     token_slots = gather_heads(tokens_back)
@@ -849,10 +850,7 @@
         ],
         axis=1,
     )
-    token_slots, gains, output_slots = lax.optimization_barrier(
-        (token_slots, gains, output_slots)
-    )
-    output_slots.append(swap(output_slots[0], head_count - 1))
+    token_slots, gains = lax.optimization_barrier((token_slots, gains))
     output = in_order(output_slots, bf16)
     gains = butterfly(gains, "seq", seq_count)
     grad_tokens = in_order(token_slots, f32)

time: 732 us -> 744 us (1.016)
  waiting for transfers between devices: 316 us -> 330 us
    ppermute x16, waiting for transfers between devices: 184 us -> 192 us  [across(): return lax.ppermute(values, 'seq', pairs)]
  transfers between devices with their start and end apart: 70 -> 70, of which waited for: 32 -> 33; matrix products, arithmetic and copies ran while one was open for 28% -> 27% of each run, Pallas kernels for 8% -> 8%
where the time goes in v10:
time: 744 us; the launch traced here: 736 us
  waiting for transfers between devices  330 us (44%)
  matrix products  130 us (17%)
  starting transfers between devices  121 us (16%)
  Pallas kernels  55.5 us (7%)
  other arithmetic  55.2 us (7%)
  local copies, waits for them, and re-layouts  28 us (4%)
  between operations  16.3 us (2%)
    ppermute x16, waiting for transfers between devices, across(): return lax.ppermute(values, 'seq', pairs)  192 us
    ppermute x38, waiting for transfers between devices, flip(): return lax.ppermute(values, axis, [(i, i ^ bit) for i in range(size)])  122 us
    dot_general x24, matrix products, contract(): lax.dot_general(left, right, (((left_dim,), (right_dim,)), ((), ())), pre...  89.2 us
    ppermute x38, starting transfers between devices, flip(): return lax.ppermute(values, axis, [(i, i ^ bit) for i in range(size)])  56.5 us
    ppermute x16, starting transfers between devices, across(): return lax.ppermute(values, 'seq', pairs)  49.4 us
    dot_general x6, matrix products, dot(): return jnp.dot(left, right, preferred_element_type=f32)  37.5 us
    pallas_call x1, Pallas kernels, attend_backward(): pl.pallas_call(functools.partial(back_kernel, heads, members), out_shape=...  21 us
    pallas_call x1, Pallas kernels, project(): pl.pallas_call(functools.partial(project_kernel, heads), out_shape=[jax.S...  16.3 us
  transfers between devices with their start and end apart: 70, of which 33 were waited for; matrix products, arithmetic and copies ran while one was open for 27% of the time, Pallas kernels for 8%

profile of v10, /device:TPU:0, one launch (start us, length us, event | category | flops | bytes accessed | tf_op | source)
XLA Modules:
  0.0 736.0 jit_solution(2354182258246450110)
XLA Ops:
  17.0 16.3 %project.1 = (bf16[7,128,384]{2,1,0:T(8,128)(2,1)S(1)}, bf16[7,128,384]{2,1,0:T(8,128)(2,1)}, bf16[7,128,384]{2,1,0:T(8,128)(2,1)S(1)}, bf16[7,128,384]{2,1,0:T(...) custom-call(s32[7]{0:T(128)S(1)} %pad_add_fusion.scal, bf16[896,2048]{1,0:T(8,128)(2,1)} %tokens.1, ...), custom_call_target="tpu_custom_call" | custom-call | flops 5637144576 | bytes 16777216 | tf_op jit(solution)/shard_map/project/pallas_call | solution.py:402
  42.6 43.9 %collective-permute-done.refs_1_ = bf16[7,128,384]{2,1,0:T(8,128)(2,1)S(1)} collective-permute-done((bf16[7,128,384]{2,1,0:T(8,128)(2,1)}, bf16[7,128,384]{2,1,0:T(8,128)(2,1)S(1)}, u32[]{:S(2)}, u32[]{:S(2)}) %collective-permute-start) | collective-permute-done | bytes 688160 | tf_op jit(solution)/shard_map/ppermute | solution.py:506
  90.2 13.1 %collective-permute-done.2.refs_3_ = bf16[7,128,384]{2,1,0:T(8,128)(2,1)} collective-permute-done((bf16[7,128,384]{2,1,0:T(8,128)(2,1)S(1)}, bf16[7,128,384]{2,1,0:T(8,128)(2,1)}, u32[]{:S(2)}, u32[]{:S(2)}) %collective-permute-start.2) | collective-permute-done | bytes 688160 | tf_op jit(solution)/shard_map/ppermute | solution.py:506
  110.4 15.4 %attend_forward.1 = (bf16[7,128,128]{2,1,0:T(8,128)(2,1)}, bf16[7,128,128]{2,1,0:T(8,128)(2,1)}, bf16[7,128,128]{2,1,0:T(8,128)(2,1)}, bf16[7,128,128]{2,1,0:T(8,128)(2,1)}, f32[4,7,1,128]{3,2,1,0:T(1,128)}) custom-call(s32[7]{0:T(128)} %copy-done.6, bf16[7,128,384]{2,1,0:T(8,128)(2,1)} %copy-done.8, bf16[7,128,384]{2,1,0:T(8,128)(2,1)} %copy-done.57, ...), custom_call_target="tpu_custom_call" | custom-call | flops 4000000000 | bytes 7340032 | tf_op jit(solution)/shard_map/attend_forward/pallas_call | solution.py:185
  125.9 14.4 %collective-permute-start.10 = (bf16[7,128,128]{2,1,0:T(8,128)(2,1)}, bf16[7,128,128]{2,1,0:T(8,128)(2,1)S(1)}, u32[]{:S(2)}, u32[]{:S(2)}) collective-permute-start(bf16[7,128,128]{2,1,0:T(8,128)(2,1)} %get-tuple-element.145), channel_id=1, source_target_pairs={{0,4},{1,5},{2,6},{3,7},{4,0},{5,1},{6,2},{7,3},{8,12},{9,13},{10,... | collective-permute-start | bytes 688136 | tf_op jit(solution)/shard_map/ppermute | solution.py:506
  149.0 24.8 %collective-permute-done.13 = f32[5,2048]{1,0:T(8,128)S(1)} collective-permute-done((f32[5,2048]{1,0:T(8,128)S(1)}, f32[5,2048]{1,0:T(8,128)S(1)}, u32[]{:S(2)}, u32[]{:S(2)}) %collective-permute-start.13) | collective-permute-done | bytes 40992 | tf_op jit(solution)/shard_map/ppermute | solution.py:55
  194.3 11.0 %collective-permute-start.21 = (f32[5,2048]{1,0:T(8,128)S(1)}, f32[5,2048]{1,0:T(8,128)S(1)}, u32[]{:S(2)}, u32[]{:S(2)}) collective-permute-start(f32[5,2048]{1,0:T(8,128)S(1)} %add.433), channel_id=1, source_target_pairs={{0,4},{1,5},{2,6},{3,7},{4,0},{5,1},{6,2},{7,3},{8,12},{9,13},{10,... | collective-permute-start | bytes 122888 | tf_op jit(solution)/shard_map/ppermute | solution.py:55
  205.4 9.1 %collective-permute-done.21 = f32[5,2048]{1,0:T(8,128)S(1)} collective-permute-done((f32[5,2048]{1,0:T(8,128)S(1)}, f32[5,2048]{1,0:T(8,128)S(1)}, u32[]{:S(2)}, u32[]{:S(2)}) %collective-permute-start.21) | collective-permute-done | bytes 40992 | tf_op jit(solution)/shard_map/ppermute | solution.py:55
  214.5 8.3 %pad_maximum_fusion = bf16[2048,2048]{1,0:T(8,128)(2,1)} fusion(bf16[2048,1024]{1,0:T(8,128)(2,1)} %all-gather.7.cloned.1.call-done, bf16[2048,1024]{1,0:T(8,128)(2,1)} %all-gather.5.cloned.1.call-done), kind=kLoop, calls=%fused_computation.2 | loop fusion | flops 16777216 | bytes 16777216 | tf_op jit(solution)/shard_map/concatenate | solution.py:708
  222.9 7.5 %collective-permute-done.19 = bf16[224,2048]{1,0:T(8,128)(2,1)} collective-permute-done((bf16[224,2048]{1,0:T(8,128)(2,1)S(1)}, bf16[224,2048]{1,0:T(8,128)(2,1)}, u32[]{:S(2)}, u32[]{:S(2)}) %collective-permute-start.19) | collective-permute-done | bytes 917536 | tf_op jit(solution)/shard_map/ppermute | solution.py:55
  235.9 13.1 %fusion = (bf16[896,2048]{1,0:T(8,128)(2,1)S(1)}, f32[896,2048]{1,0:T(8,128)}) fusion(s32[2048]{0:T(1024)S(1)} %iota_add_fusion, s32[896]{0:T(1024)S(1)} %add_multiply_fusion, bf16[896,2048]{1,0:T(8,128)(2,1)S(1)} %constant_dynamic-update-slice_fusion.4, bf16[2048,2048]{1,0:T(8,128)(2,1)} %pad_maximum_fusion), kind=kOutput, calls=%fused_computation.6 | convolution fusion | flops 7525367808 | bytes 23080448 | tf_op jit(solution)/shard_map/dot_general | solution.py:29
  261.9 6.3 add_convert_fusion.1
  272.8 13.4 %fusion.3 = bf16[896,2048]{1,0:T(8,128)(2,1)S(1)} fusion(f32[896,2048]{1,0:T(8,128)} %get-tuple-element.167, s32[2048]{0:T(1024)S(1)} %iota_add_fusion, s32[896]{0:T(1024)S(1)} %add_multiply_fusion, bf16[896,2048]{1,0:T(8,128)(2,1)} %copy-done.12, bf16[2048,2048]{1,0:T(8,128)(2,1)} %all-gather.9.cloned.1.call-done), kind=kOutput, calls=%fused_computation.9 | convolution fusion | flops 7529037824 | bytes 23080448 | tf_op jit(solution)/shard_map/dot_general | solution.py:33
  286.2 6.2 convolution_convert_fusion.8
  295.0 6.1 convolution_convert_fusion.9
  305.0 6.7 convolution_convert_fusion.1
  319.8 15.6 %collective-permute-done.24 = bf16[224,2048]{1,0:T(8,128)(2,1)S(1)} collective-permute-done((bf16[224,2048]{1,0:T(8,128)(2,1)S(1)}, bf16[224,2048]{1,0:T(8,128)(2,1)S(1)}, u32[]{:S(2)}, u32[]{:S(2)}) %collective-permute-start.24) | collective-permute-done | bytes 917536 | tf_op jit(solution)/shard_map/ppermute | solution.py:55
  339.0 6.3 convolution_convert_fusion.7
  378.3 12.9 %reduce-scatter.8.cloned.1.call-start = ((), (), s32[]{:S(2)}) async-start(), calls=%async_computation.8 | async-start | bytes 7077888 | tf_op jit(solution)/shard_map/reduce_scatter | solution.py:808
  391.2 6.9 convolution_convert_fusion.5
  398.1 6.5 convolution_convert_fusion.6
  408.8 21.0 %attend_backward.1 = (bf16[7,128,384]{2,1,0:T(8,128)(2,1)}, bf16[7,128,384]{2,1,0:T(8,128)(2,1)}, bf16[7,128,384]{2,1,0:T(8,128)(2,1)}, bf16[7,128,384]{2,1,0:T(8,128)(2,1)}, bf16[4,7,128,384]{3,2,1,0:T(8,128)(2,1)}) custom-call(s32[7]{0:T(128)} %copy-done.6, bf16[7,128,384]{2,1,0:T(8,128)(2,1)} %copy-done.8, bf16[7,128,384]{2,1,0:T(8,128)(2,1)} %copy-done.57, ...), custom_call_target="tpu_custom_call" | custom-call | flops 10000000000 | bytes 12582912 | tf_op jit(solution)/shard_map/attend_backward/pallas_call | solution.py:311
  442.0 12.2 %collective-permute-done.34 = bf16[224,2048]{1,0:T(8,128)(2,1)S(1)} collective-permute-done((bf16[224,2048]{1,0:T(8,128)(2,1)S(1)}, bf16[224,2048]{1,0:T(8,128)(2,1)S(1)}, u32[]{:S(2)}, u32[]{:S(2)}) %collective-permute-start.34) | collective-permute-done | bytes 917536 | tf_op jit(solution)/shard_map/ppermute | solution.py:55
  460.5 19.6 %collective-permute-done.36.refs_1_ = bf16[7,128,384]{2,1,0:T(8,128)(2,1)S(1)} collective-permute-done((bf16[7,128,384]{2,1,0:T(8,128)(2,1)S(1)}, bf16[7,128,384]{2,1,0:T(8,128)(2,1)S(1)}, u32[]{:S(2)}, u32[]{:S(2)}) %collective-permute-start.36) | collective-permute-done | bytes 688160 | tf_op jit(solution)/shard_map/ppermute | solution.py:506
  482.6 18.3 %collective-permute-done.37.refs_2_ = bf16[7,128,384]{2,1,0:T(8,128)(2,1)S(1)} collective-permute-done((bf16[7,128,384]{2,1,0:T(8,128)(2,1)S(1)}, bf16[7,128,384]{2,1,0:T(8,128)(2,1)S(1)}, u32[]{:S(2)}, u32[]{:S(2)}) %collective-permute-start.37) | collective-permute-done | bytes 688160 | tf_op jit(solution)/shard_map/ppermute | solution.py:506
  503.8 8.7 %convolution_convert_fusion = bf16[2048,1536]{1,0:T(8,128)(2,1)} fusion(bf16[896,2048]{1,0:T(8,128)(2,1)S(1)} %copy-done.66, bf16[896,1536]{1,0:T(8,128)(2,1)S(1)} %gather_grads.1), kind=kOutput, calls=%fused_computation.5 | convolution fusion | flops 5640290304 | bytes 12713984 | tf_op jit(solution)/shard_map/dot_general | solution.py:33
  548.2 15.7 %collective-permute-start.49 = (bf16[128,2048]{1,0:T(8,128)(2,1)}, bf16[128,2048]{1,0:T(8,128)(2,1)}, u32[]{:S(2)}, u32[]{:S(2)}) collective-permute-start(bf16[128,2048]{1,0:T(8,128)(2,1)} %pad_maximum_fusion.4), channel_id=1, source_target_pairs={{0,2},{1,3},{2,0},{3,1},{4,6},{5,7},{6,4},{7,5},{8,10},{9,11},{10,... | collective-permute-start | bytes 1572872 | tf_op jit(solution)/shard_map/ppermute | solution.py:506
  567.3 20.4 %collective-permute-done.49 = bf16[128,2048]{1,0:T(8,128)(2,1)} collective-permute-done((bf16[128,2048]{1,0:T(8,128)(2,1)}, bf16[128,2048]{1,0:T(8,128)(2,1)}, u32[]{:S(2)}, u32[]{:S(2)}) %collective-permute-start.49) | collective-permute-done | bytes 524320 | tf_op jit(solution)/shard_map/ppermute | solution.py:506
  591.3 18.8 %collective-permute-done.50 = bf16[64,2048]{1,0:T(8,128)(2,1)S(1)} collective-permute-done((bf16[64,2048]{1,0:T(8,128)(2,1)S(1)}, bf16[64,2048]{1,0:T(8,128)(2,1)S(1)}, u32[]{:S(2)}, u32[]{:S(2)}) %collective-permute-start.50) | collective-permute-done | bytes 262176 | tf_op jit(solution)/shard_map/ppermute | solution.py:506
  611.2 14.0 %collective-permute-done.47 = bf16[224,2048]{1,0:T(8,128)(2,1)} collective-permute-done((bf16[224,2048]{1,0:T(8,128)(2,1)}, bf16[224,2048]{1,0:T(8,128)(2,1)}, u32[]{:S(2)}, u32[]{:S(2)}) %collective-permute-start.47) | collective-permute-done | bytes 917536 | tf_op jit(solution)/shard_map/ppermute | solution.py:55
  645.7 22.3 %collective-permute-done.57 = bf16[64,2048]{1,0:T(8,128)(2,1)S(1)} collective-permute-done((bf16[64,2048]{1,0:T(8,128)(2,1)S(1)}, bf16[64,2048]{1,0:T(8,128)(2,1)S(1)}, u32[]{:S(2)}, u32[]{:S(2)}) %collective-permute-start.57) | collective-permute-done | bytes 262176 | tf_op jit(solution)/shard_map/ppermute | solution.py:506
  669.8 35.7 %collective-permute-done.58 = bf16[128,2048]{1,0:T(8,128)(2,1)S(1)} collective-permute-done((bf16[128,2048]{1,0:T(8,128)(2,1)S(1)}, bf16[128,2048]{1,0:T(8,128)(2,1)S(1)}, u32[]{:S(2)}, u32[]{:S(2)}) %collective-permute-start.58) | collective-permute-done | bytes 524320 | tf_op jit(solution)/shard_map/ppermute | solution.py:506
  (411 shorter events, 249.4 us)
Async XLA Ops:
  7.2 207.3 %all-gather.5.cloned.1.call-start = ((), (), s32[]{:S(2)}) async-start(), calls=%async_computation.3 | async-start | bytes 4718592 | tf_op jit(solution)/shard_map/all_gather | solution.py:631
  9.5 205.0 %all-gather.7.cloned.1.call-start = ((), (), s32[]{:S(2)}) async-start(), calls=%async_computation.4 | async-start | bytes 4718592 | tf_op jit(solution)/shard_map/all_gather | solution.py:686
  9.6 97.2 %collective-permute-start.7 = (bf16[512,2048]{1,0:T(8,128)(2,1)}, bf16[512,2048]{1,0:T(8,128)(2,1)}, u32[]{:S(2)}, u32[]{:S(2)}) collective-permute-start(bf16[512,2048]{1,0:T(8,128)(2,1)} %param.14), channel_id=1, source_target_pairs={{0,8},{8,0},{16,24},{24,16},{1,9},{9,1},{17,25},{25,17},{2,10},{10... | collective-permute-start | bytes 6291464 | tf_op jit(solution)/shard_map/ppermute | solution.py:55
  12.6 94.2 %collective-permute-start.8 = (bf16[512,2048]{1,0:T(8,128)(2,1)}, bf16[512,2048]{1,0:T(8,128)(2,1)}, u32[]{:S(2)}, u32[]{:S(2)}) collective-permute-start(bf16[512,2048]{1,0:T(8,128)(2,1)} %param.14), channel_id=1, source_target_pairs={{0,16},{8,24},{16,0},{24,8},{1,17},{9,25},{17,1},{25,9},{2,18},{10... | collective-permute-start | bytes 6291464 | tf_op jit(solution)/shard_map/ppermute | solution.py:55
  33.3 53.2 %collective-permute-start = (bf16[7,128,384]{2,1,0:T(8,128)(2,1)}, bf16[7,128,384]{2,1,0:T(8,128)(2,1)S(1)}, u32[]{:S(2)}, u32[]{:S(2)}) collective-permute-start(bf16[7,128,384]{2,1,0:T(8,128)(2,1)} %get-tuple-element.131), channel_id=1, source_target_pairs={{0,2},{1,3},{2,0},{3,1},{4,6},{5,7},{6,4},{7,5},{8,10},{9,11},{10,... | collective-permute-start | bytes 2064392 | tf_op jit(solution)/shard_map/ppermute | solution.py:506
  35.0 54.6 %collective-permute-start.1 = (bf16[7,128,384]{2,1,0:T(8,128)(2,1)S(1)}, bf16[7,128,384]{2,1,0:T(8,128)(2,1)}, u32[]{:S(2)}, u32[]{:S(2)}) collective-permute-start(bf16[7,128,384]{2,1,0:T(8,128)(2,1)S(1)} %get-tuple-element.132), channel_id=1, source_target_pairs={{0,4},{1,5},{2,6},{3,7},{4,0},{5,1},{6,2},{7,3},{8,12},{9,13},{10,... | collective-permute-start | bytes 2064392 | tf_op jit(solution)/shard_map/ppermute | solution.py:506
  37.5 65.7 %collective-permute-start.2 = (bf16[7,128,384]{2,1,0:T(8,128)(2,1)S(1)}, bf16[7,128,384]{2,1,0:T(8,128)(2,1)}, u32[]{:S(2)}, u32[]{:S(2)}) collective-permute-start(bf16[7,128,384]{2,1,0:T(8,128)(2,1)S(1)} %get-tuple-element.133), channel_id=1, source_target_pairs={{0,6},{1,7},{2,4},{3,5},{4,2},{5,3},{6,0},{7,1},{8,14},{9,15},{10,... | collective-permute-start | bytes 2064392 | tf_op jit(solution)/shard_map/ppermute | solution.py:506
  106.8 166.0 %all-gather.9.cloned.1.call-start = ((), (), s32[]{:S(2)}) async-start(), calls=%async_computation.5 | async-start | bytes 9437184 | tf_op jit(solution)/shard_map/all_gather | solution.py:687
  107.5 405.0 %reduce-scatter.4.cloned.1.call-start = ((), (), s32[]{:S(2)}) async-start(), calls=%async_computation.6 | async-start | bytes 5242880 | tf_op jit(solution)/shard_map/reduce_scatter | solution.py:539
  107.8 70.1 %collective-permute-start.17 = (bf16[512,2048]{1,0:T(8,128)(2,1)}, bf16[512,2048]{1,0:T(8,128)(2,1)S(1)}, u32[]{:S(2)}, u32[]{:S(2)}) collective-permute-start(bf16[512,2048]{1,0:T(8,128)(2,1)} %param.14), channel_id=1, source_target_pairs={{0,24},{8,16},{16,8},{24,0},{1,25},{9,17},{17,9},{25,1},{2,26},{10... | collective-permute-start | bytes 6291464 | tf_op jit(solution)/shard_map/ppermute | solution.py:55
  125.9 47.9 %collective-permute-start.10 = (bf16[7,128,128]{2,1,0:T(8,128)(2,1)}, bf16[7,128,128]{2,1,0:T(8,128)(2,1)S(1)}, u32[]{:S(2)}, u32[]{:S(2)}) collective-permute-start(bf16[7,128,128]{2,1,0:T(8,128)(2,1)} %get-tuple-element.145), channel_id=1, source_target_pairs={{0,4},{1,5},{2,6},{3,7},{4,0},{5,1},{6,2},{7,3},{8,12},{9,13},{10,... | collective-permute-start | bytes 688136 | tf_op jit(solution)/shard_map/ppermute | solution.py:506
  192.8 39.3 %collective-permute-start.20 = (bf16[224,2048]{1,0:T(8,128)(2,1)S(1)}, bf16[224,2048]{1,0:T(8,128)(2,1)}, u32[]{:S(2)}, u32[]{:S(2)}) collective-permute-start(bf16[224,2048]{1,0:T(8,128)(2,1)S(1)} %multiply_convert_fusion), channel_id=1, source_target_pairs={{0,24},{8,16},{16,8},{24,0},{1,25},{9,17},{17,9},{25,1},{2,26},{10... | collective-permute-start | bytes 2752520 | tf_op jit(solution)/shard_map/ppermute | solution.py:55
  268.2 244.3 %reduce-scatter.6.cloned.1.call-start = ((), (), s32[]{:S(2)}) async-start(), calls=%async_computation.7 | async-start | bytes 5242880 | tf_op jit(solution)/shard_map/reduce_scatter | solution.py:539
  359.6 70.2 %collective-permute-start.32 = (bf16[224,2048]{1,0:T(8,128)(2,1)S(1)}, bf16[224,2048]{1,0:T(8,128)(2,1)S(1)}, u32[]{:S(2)}, u32[]{:S(2)}) collective-permute-start(bf16[224,2048]{1,0:T(8,128)(2,1)S(1)} %get-tuple-element.187), channel_id=1, source_target_pairs={{0,8},{8,0},{16,24},{24,16},{1,9},{9,1},{17,25},{25,17},{2,10},{10... | collective-permute-start | bytes 2752520 | tf_op jit(solution)/shard_map/ppermute | solution.py:55
  360.7 69.1 %collective-permute-start.33 = (bf16[224,2048]{1,0:T(8,128)(2,1)S(1)}, bf16[224,2048]{1,0:T(8,128)(2,1)}, u32[]{:S(2)}, u32[]{:S(2)}) collective-permute-start(bf16[224,2048]{1,0:T(8,128)(2,1)S(1)} %get-tuple-element.187), channel_id=1, source_target_pairs={{0,16},{8,24},{16,0},{24,8},{1,17},{9,25},{17,1},{25,9},{2,18},{10... | collective-permute-start | bytes 2752520 | tf_op jit(solution)/shard_map/ppermute | solution.py:55
  362.5 45.5 %collective-permute-start.29 = (bf16[7,128,128]{2,1,0:T(8,128)(2,1)S(1)}, bf16[7,128,128]{2,1,0:T(8,128)(2,1)S(1)}, u32[]{:S(2)}, u32[]{:S(2)}) collective-permute-start(bf16[7,128,128]{2,1,0:T(8,128)(2,1)S(1)} %bitcast.117), channel_id=1, source_target_pairs={{0,2},{1,3},{2,0},{3,1},{4,6},{5,7},{6,4},{7,5},{8,10},{9,11},{10,... | collective-permute-start | bytes 688136 | tf_op jit(solution)/shard_map/ppermute | solution.py:506
  367.6 40.4 %collective-permute-start.30 = (bf16[7,128,128]{2,1,0:T(8,128)(2,1)S(1)}, bf16[7,128,128]{2,1,0:T(8,128)(2,1)S(1)}, u32[]{:S(2)}, u32[]{:S(2)}) collective-permute-start(bf16[7,128,128]{2,1,0:T(8,128)(2,1)S(1)} %bitcast.116), channel_id=1, source_target_pairs={{0,4},{1,5},{2,6},{3,7},{4,0},{5,1},{6,2},{7,3},{8,12},{9,13},{10,... | collective-permute-start | bytes 688136 | tf_op jit(solution)/shard_map/ppermute | solution.py:506
  378.3 258.8 %reduce-scatter.8.cloned.1.call-start = ((), (), s32[]{:S(2)}) async-start(), calls=%async_computation.8 | async-start | bytes 7077888 | tf_op jit(solution)/shard_map/reduce_scatter | solution.py:808
  438.0 62.9 %collective-permute-start.39 = (bf16[224,2048]{1,0:T(8,128)(2,1)S(1)}, bf16[224,2048]{1,0:T(8,128)(2,1)S(1)}, u32[]{:S(2)}, u32[]{:S(2)}) collective-permute-start(bf16[224,2048]{1,0:T(8,128)(2,1)S(1)} %copy-done.56), channel_id=1, source_target_pairs={{0,8},{8,0},{16,24},{24,16},{1,9},{9,1},{17,25},{25,17},{2,10},{10... | collective-permute-start | bytes 2752520 | tf_op jit(solution)/shard_map/ppermute | solution.py:55
  439.2 61.8 %collective-permute-start.40 = (bf16[224,2048]{1,0:T(8,128)(2,1)S(1)}, bf16[224,2048]{1,0:T(8,128)(2,1)S(1)}, u32[]{:S(2)}, u32[]{:S(2)}) collective-permute-start(bf16[224,2048]{1,0:T(8,128)(2,1)S(1)} %copy-done.55), channel_id=1, source_target_pairs={{0,16},{8,24},{16,0},{24,8},{1,17},{9,25},{17,1},{25,9},{2,18},{10... | collective-permute-start | bytes 2752520 | tf_op jit(solution)/shard_map/ppermute | solution.py:55
  439.8 40.3 %collective-permute-start.36 = (bf16[7,128,384]{2,1,0:T(8,128)(2,1)S(1)}, bf16[7,128,384]{2,1,0:T(8,128)(2,1)S(1)}, u32[]{:S(2)}, u32[]{:S(2)}) collective-permute-start(bf16[7,128,384]{2,1,0:T(8,128)(2,1)S(1)} %get-tuple-element.200), channel_id=1, source_target_pairs={{0,2},{1,3},{2,0},{3,1},{4,6},{5,7},{6,4},{7,5},{8,10},{9,11},{10,... | collective-permute-start | bytes 2064392 | tf_op jit(solution)/shard_map/ppermute | solution.py:506
  440.9 60.1 %collective-permute-start.37 = (bf16[7,128,384]{2,1,0:T(8,128)(2,1)S(1)}, bf16[7,128,384]{2,1,0:T(8,128)(2,1)S(1)}, u32[]{:S(2)}, u32[]{:S(2)}) collective-permute-start(bf16[7,128,384]{2,1,0:T(8,128)(2,1)S(1)} %get-tuple-element.201), channel_id=1, source_target_pairs={{0,4},{1,5},{2,6},{3,7},{4,0},{5,1},{6,2},{7,3},{8,12},{9,13},{10,... | collective-permute-start | bytes 2064392 | tf_op jit(solution)/shard_map/ppermute | solution.py:506
  454.2 46.8 %collective-permute-start.38 = (bf16[7,128,384]{2,1,0:T(8,128)(2,1)S(1)}, bf16[7,128,384]{2,1,0:T(8,128)(2,1)S(1)}, u32[]{:S(2)}, u32[]{:S(2)}) collective-permute-start(bf16[7,128,384]{2,1,0:T(8,128)(2,1)S(1)} %get-tuple-element.202), channel_id=1, source_target_pairs={{0,6},{1,7},{2,4},{3,5},{4,2},{5,3},{6,0},{7,1},{8,14},{9,15},{10,... | collective-permute-start | bytes 2064392 | tf_op jit(solution)/shard_map/ppermute | solution.py:506
  512.5 207.9 %all-gather.11.cloned.1.call-start = ((), (), s32[]{:S(2)}) async-start(), calls=%async_computation.9 | async-start | bytes 7077888 | tf_op jit(solution)/shard_map/all_gather | solution.py:843
  548.2 39.6 %collective-permute-start.49 = (bf16[128,2048]{1,0:T(8,128)(2,1)}, bf16[128,2048]{1,0:T(8,128)(2,1)}, u32[]{:S(2)}, u32[]{:S(2)}) collective-permute-start(bf16[128,2048]{1,0:T(8,128)(2,1)} %pad_maximum_fusion.4), channel_id=1, source_target_pairs={{0,2},{1,3},{2,0},{3,1},{4,6},{5,7},{6,4},{7,5},{8,10},{9,11},{10,... | collective-permute-start | bytes 1572872 | tf_op jit(solution)/shard_map/ppermute | solution.py:506
  563.8 47.4 %collective-permute-start.46 = (bf16[224,2048]{1,0:T(8,128)(2,1)}, bf16[224,2048]{1,0:T(8,128)(2,1)}, u32[]{:S(2)}, u32[]{:S(2)}) collective-permute-start(bf16[224,2048]{1,0:T(8,128)(2,1)} %fusion.15), channel_id=1, source_target_pairs={{0,8},{8,0},{16,24},{24,16},{1,9},{9,1},{17,25},{25,17},{2,10},{10... | collective-permute-start | bytes 2752520 | tf_op jit(solution)/shard_map/ppermute | solution.py:55
  564.4 60.8 %collective-permute-start.47 = (bf16[224,2048]{1,0:T(8,128)(2,1)}, bf16[224,2048]{1,0:T(8,128)(2,1)}, u32[]{:S(2)}, u32[]{:S(2)}) collective-permute-start(bf16[224,2048]{1,0:T(8,128)(2,1)} %fusion.16), channel_id=1, source_target_pairs={{0,16},{8,24},{16,0},{24,8},{1,17},{9,25},{17,1},{25,9},{2,18},{10... | collective-permute-start | bytes 2752520 | tf_op jit(solution)/shard_map/ppermute | solution.py:55
  565.9 59.3 %collective-permute-start.48 = (bf16[224,2048]{1,0:T(8,128)(2,1)}, bf16[224,2048]{1,0:T(8,128)(2,1)}, u32[]{:S(2)}, u32[]{:S(2)}) collective-permute-start(bf16[224,2048]{1,0:T(8,128)(2,1)} %fusion.17), channel_id=1, source_target_pairs={{0,24},{8,16},{16,8},{24,0},{1,25},{9,17},{17,9},{25,1},{2,26},{10... | collective-permute-start | bytes 2752520 | tf_op jit(solution)/shard_map/ppermute | solution.py:55
  589.8 47.2 %collective-permute-start.53 = (bf16[224,2048]{1,0:T(8,128)(2,1)S(1)}, bf16[224,2048]{1,0:T(8,128)(2,1)}, u32[]{:S(2)}, u32[]{:S(2)}) collective-permute-start(bf16[224,2048]{1,0:T(8,128)(2,1)S(1)} %copy-done.19), channel_id=1, source_target_pairs={{0,24},{8,16},{16,8},{24,0},{1,25},{9,17},{17,9},{25,1},{2,26},{10... | collective-permute-start | bytes 2752520 | tf_op jit(solution)/shard_map/ppermute | solution.py:55
  641.5 64.7 %collective-permute-start.54 = (bf16[224,2048]{1,0:T(8,128)(2,1)S(1)}, bf16[224,2048]{1,0:T(8,128)(2,1)S(1)}, u32[]{:S(2)}, u32[]{:S(2)}) collective-permute-start(bf16[224,2048]{1,0:T(8,128)(2,1)S(1)} %copy-done.20), channel_id=1, source_target_pairs={{0,8},{8,0},{16,24},{24,16},{1,9},{9,1},{17,25},{25,17},{2,10},{10... | collective-permute-start | bytes 2752520 | tf_op jit(solution)/shard_map/ppermute | solution.py:55
  642.7 63.5 %collective-permute-start.55 = (bf16[224,2048]{1,0:T(8,128)(2,1)S(1)}, bf16[224,2048]{1,0:T(8,128)(2,1)S(1)}, u32[]{:S(2)}, u32[]{:S(2)}) collective-permute-start(bf16[224,2048]{1,0:T(8,128)(2,1)S(1)} %copy-done.20), channel_id=1, source_target_pairs={{0,16},{8,24},{16,0},{24,8},{1,17},{9,25},{17,1},{25,9},{2,18},{10... | collective-permute-start | bytes 2752520 | tf_op jit(solution)/shard_map/ppermute | solution.py:55
  643.6 62.7 %collective-permute-start.56 = (bf16[224,2048]{1,0:T(8,128)(2,1)S(1)}, bf16[224,2048]{1,0:T(8,128)(2,1)S(1)}, u32[]{:S(2)}, u32[]{:S(2)}) collective-permute-start(bf16[224,2048]{1,0:T(8,128)(2,1)S(1)} %copy-done.20), channel_id=1, source_target_pairs={{0,24},{8,16},{16,8},{24,0},{1,25},{9,17},{17,9},{25,1},{2,26},{10... | collective-permute-start | bytes 2752520 | tf_op jit(solution)/shard_map/ppermute | solution.py:55
  (113 other events, 2312.3 us)
Sparse Core Ops, SparseCore 0:
  10.2 73.1 all-gather.4
  106.9 78.7 all-gather.6
  187.3 85.4 all-gather.8
  274.9 76.9 reduce-scatter.3
  378.4 93.0 reduce-scatter.5
  512.6 98.5 reduce-scatter.7
  637.3 73.4 all-gather.10

commit v11 on v7

--- a/solution.py
+++ b/solution.py
@@ -470,6 +470,28 @@
     )(scal, cosine, sine, *slots)
 
 
+def widen_kernel(source, target):
+    width = target.shape[2]
+    for part in range(3):
+        target[part] = source[:, part * width : (part + 1) * width].astype(f32)
+
+
+def widen(values):
+    rows, width = values.shape[0], values.shape[1] // 3
+    tile = rows // 8
+    return pl.pallas_call(
+        widen_kernel,
+        grid=(8,),
+        out_shape=jax.ShapeDtypeStruct((3, rows, width), f32),
+        in_specs=[pl.BlockSpec((tile, 3 * width), lambda i: (i, 0))],
+        out_specs=pl.BlockSpec((3, tile, width), lambda i: (0, i, 0)),
+        cost_estimate=pl.CostEstimate(
+            flops=3 * rows * width, bytes_accessed=18 * rows * width, transcendentals=0
+        ),
+        name="widen",
+    )(values)
+
+
 def local(
     tokens,
     w_qkv,
@@ -823,13 +845,7 @@
     total_qkv = lax.all_gather(total_qkv, "seq", axis=0, tiled=True)
     token_slots = gather_heads(tokens_back)
     grad_out = gather_seq(total_out).astype(f32)
-    grad_qkv = jnp.stack(
-        [
-            total_qkv[:, part * head_width : (part + 1) * head_width].astype(f32)
-            for part in range(3)
-        ],
-        axis=1,
-    )
+    grad_qkv = widen(total_qkv).transpose(1, 0, 2)
     token_slots, gains, output_slots = lax.optimization_barrier(
         (token_slots, gains, output_slots)
     )

time: 729 us -> 729 us (level)
  Pallas kernels: 55.4 us -> 64.2 us
    pallas_call x0 -> x1, Pallas kernels: none -> 8.79 us  [widen(): pl.pallas_call(widen_kernel, grid=(8,), out_shape=jax.ShapeDtypeStruct((3...]
where the time goes in v11:
time: 729 us; the launch traced here: 721 us
  waiting for transfers between devices  283 us (39%)
  starting transfers between devices  154 us (21%)
  matrix products  128 us (18%)
  Pallas kernels  64.2 us (9%)
  other arithmetic  47.1 us (6%)
  local copies, waits for them, and re-layouts  29.5 us (4%)
  between operations  16.1 us (2%)
    ppermute x18, waiting for transfers between devices, across(): return lax.ppermute(values, 'seq', pairs)  179 us
    dot_general x24, matrix products, contract(): lax.dot_general(left, right, (((left_dim,), (right_dim,)), ((), ())), pre...  87.9 us
    ppermute x38, waiting for transfers between devices, flip(): return lax.ppermute(values, axis, [(i, i ^ bit) for i in range(size)])  85.4 us
    ppermute x18, starting transfers between devices, across(): return lax.ppermute(values, 'seq', pairs)  77.7 us
    ppermute x38, starting transfers between devices, flip(): return lax.ppermute(values, axis, [(i, i ^ bit) for i in range(size)])  74 us
    dot_general x6, matrix products, dot(): return jnp.dot(left, right, preferred_element_type=f32)  36.3 us
    pallas_call x1, Pallas kernels, attend_backward(): pl.pallas_call(functools.partial(back_kernel, heads, members), out_shape=...  20.9 us
    pallas_call x1, Pallas kernels, project(): pl.pallas_call(functools.partial(project_kernel, heads), out_shape=[jax.S...  16.3 us
  transfers between devices with their start and end apart: 72, of which 34 were waited for; matrix products, arithmetic and copies ran while one was open for 28% of the time, Pallas kernels for 8%

profile of v11, /device:TPU:0, one launch (start us, length us, event | category | flops | bytes accessed | tf_op | source)
XLA Modules:
  0.0 721.4 jit_solution(2473400385907654661)
XLA Ops:
  17.0 16.3 %project.1 = (bf16[7,128,384]{2,1,0:T(8,128)(2,1)S(1)}, bf16[7,128,384]{2,1,0:T(8,128)(2,1)}, bf16[7,128,384]{2,1,0:T(8,128)(2,1)S(1)}, bf16[7,128,384]{2,1,0:T(...) custom-call(s32[7]{0:T(128)S(1)} %pad_add_fusion.scal, bf16[896,2048]{1,0:T(8,128)(2,1)} %tokens.1, ...), custom_call_target="tpu_custom_call" | custom-call | flops 5637144576 | bytes 16777216 | tf_op jit(solution)/shard_map/project/pallas_call | solution.py:402
  42.6 43.9 %collective-permute-done.refs_1_ = bf16[7,128,384]{2,1,0:T(8,128)(2,1)S(1)} collective-permute-done((bf16[7,128,384]{2,1,0:T(8,128)(2,1)}, bf16[7,128,384]{2,1,0:T(8,128)(2,1)S(1)}, u32[]{:S(2)}, u32[]{:S(2)}) %collective-permute-start) | collective-permute-done | bytes 688160 | tf_op jit(solution)/shard_map/ppermute | solution.py:528
  90.1 13.1 %collective-permute-done.2.refs_3_ = bf16[7,128,384]{2,1,0:T(8,128)(2,1)} collective-permute-done((bf16[7,128,384]{2,1,0:T(8,128)(2,1)S(1)}, bf16[7,128,384]{2,1,0:T(8,128)(2,1)}, u32[]{:S(2)}, u32[]{:S(2)}) %collective-permute-start.2) | collective-permute-done | bytes 688160 | tf_op jit(solution)/shard_map/ppermute | solution.py:528
  110.4 15.5 %attend_forward.1 = (bf16[7,128,128]{2,1,0:T(8,128)(2,1)}, bf16[7,128,128]{2,1,0:T(8,128)(2,1)}, bf16[7,128,128]{2,1,0:T(8,128)(2,1)}, bf16[7,128,128]{2,1,0:T(8,128)(2,1)}, f32[4,7,1,128]{3,2,1,0:T(1,128)}) custom-call(s32[7]{0:T(128)} %copy-done.6, bf16[7,128,384]{2,1,0:T(8,128)(2,1)} %copy-done.8, bf16[7,128,384]{2,1,0:T(8,128)(2,1)} %copy-done.55, ...), custom_call_target="tpu_custom_call" | custom-call | flops 4000000000 | bytes 7340032 | tf_op jit(solution)/shard_map/attend_forward/pallas_call | solution.py:185
  125.9 14.4 %collective-permute-start.10 = (bf16[7,128,128]{2,1,0:T(8,128)(2,1)}, bf16[7,128,128]{2,1,0:T(8,128)(2,1)S(1)}, u32[]{:S(2)}, u32[]{:S(2)}) collective-permute-start(bf16[7,128,128]{2,1,0:T(8,128)(2,1)} %get-tuple-element.148), channel_id=1, source_target_pairs={{0,4},{1,5},{2,6},{3,7},{4,0},{5,1},{6,2},{7,3},{8,12},{9,13},{10,... | collective-permute-start | bytes 688136 | tf_op jit(solution)/shard_map/ppermute | solution.py:528
  149.0 24.8 %collective-permute-done.13 = f32[5,2048]{1,0:T(8,128)S(1)} collective-permute-done((f32[5,2048]{1,0:T(8,128)S(1)}, f32[5,2048]{1,0:T(8,128)S(1)}, u32[]{:S(2)}, u32[]{:S(2)}) %collective-permute-start.13) | collective-permute-done | bytes 40992 | tf_op jit(solution)/shard_map/ppermute | solution.py:55
  194.3 11.0 %collective-permute-start.21 = (f32[5,2048]{1,0:T(8,128)S(1)}, f32[5,2048]{1,0:T(8,128)S(1)}, u32[]{:S(2)}, u32[]{:S(2)}) collective-permute-start(f32[5,2048]{1,0:T(8,128)S(1)} %add.433), channel_id=1, source_target_pairs={{0,4},{1,5},{2,6},{3,7},{4,0},{5,1},{6,2},{7,3},{8,12},{9,13},{10,... | collective-permute-start | bytes 122888 | tf_op jit(solution)/shard_map/ppermute | solution.py:55
  205.4 9.1 %collective-permute-done.21 = f32[5,2048]{1,0:T(8,128)S(1)} collective-permute-done((f32[5,2048]{1,0:T(8,128)S(1)}, f32[5,2048]{1,0:T(8,128)S(1)}, u32[]{:S(2)}, u32[]{:S(2)}) %collective-permute-start.21) | collective-permute-done | bytes 40992 | tf_op jit(solution)/shard_map/ppermute | solution.py:55
  214.5 8.3 %pad_maximum_fusion = bf16[2048,2048]{1,0:T(8,128)(2,1)} fusion(bf16[2048,1024]{1,0:T(8,128)(2,1)} %all-gather.7.cloned.1.call-done, bf16[2048,1024]{1,0:T(8,128)(2,1)} %all-gather.5.cloned.1.call-done), kind=kLoop, calls=%fused_computation.2 | loop fusion | flops 16777216 | bytes 16777216 | tf_op jit(solution)/shard_map/concatenate | solution.py:712
  222.9 7.5 %collective-permute-done.19 = bf16[224,2048]{1,0:T(8,128)(2,1)} collective-permute-done((bf16[224,2048]{1,0:T(8,128)(2,1)S(1)}, bf16[224,2048]{1,0:T(8,128)(2,1)}, u32[]{:S(2)}, u32[]{:S(2)}) %collective-permute-start.19) | collective-permute-done | bytes 917536 | tf_op jit(solution)/shard_map/ppermute | solution.py:55
  236.0 13.1 %fusion = (bf16[896,2048]{1,0:T(8,128)(2,1)S(1)}, f32[896,2048]{1,0:T(8,128)}) fusion(s32[2048]{0:T(1024)S(1)} %iota_add_fusion, s32[896]{0:T(1024)S(1)} %add_multiply_fusion, bf16[896,2048]{1,0:T(8,128)(2,1)S(1)} %constant_dynamic-update-slice_fusion.4, bf16[2048,2048]{1,0:T(8,128)(2,1)} %pad_maximum_fusion), kind=kOutput, calls=%fused_computation.6 | convolution fusion | flops 7525367808 | bytes 23080448 | tf_op jit(solution)/shard_map/dot_general | solution.py:29
  261.9 6.3 add_convert_fusion.1
  272.7 13.4 %fusion.3 = bf16[896,2048]{1,0:T(8,128)(2,1)S(1)} fusion(f32[896,2048]{1,0:T(8,128)} %get-tuple-element.170, s32[2048]{0:T(1024)S(1)} %iota_add_fusion, s32[896]{0:T(1024)S(1)} %add_multiply_fusion, bf16[896,2048]{1,0:T(8,128)(2,1)} %copy-done.12, bf16[2048,2048]{1,0:T(8,128)(2,1)} %all-gather.9.cloned.1.call-done), kind=kOutput, calls=%fused_computation.9 | convolution fusion | flops 7529037824 | bytes 23080448 | tf_op jit(solution)/shard_map/dot_general | solution.py:33
  305.0 6.7 convolution_convert_fusion.1
  319.9 15.6 %collective-permute-done.24 = bf16[224,2048]{1,0:T(8,128)(2,1)S(1)} collective-permute-done((bf16[224,2048]{1,0:T(8,128)(2,1)S(1)}, bf16[224,2048]{1,0:T(8,128)(2,1)S(1)}, u32[]{:S(2)}, u32[]{:S(2)}) %collective-permute-start.24) | collective-permute-done | bytes 917536 | tf_op jit(solution)/shard_map/ppermute | solution.py:55
  339.0 6.3 convolution_convert_fusion.7
  359.3 6.7 convolution_convert_fusion.6
  375.6 7.1 fusion.89
  383.3 8.5 %collective-permute-done.29.refs_9_ = bf16[7,128,128]{2,1,0:T(8,128)(2,1)S(1)} collective-permute-done((bf16[7,128,128]{2,1,0:T(8,128)(2,1)S(1)}, bf16[7,128,128]{2,1,0:T(8,128)(2,1)S(1)}, u32[]{:S(2)}, u32[]{:S(2)}) %collective-permute-start.29) | collective-permute-done | bytes 229408 | tf_op jit(solution)/shard_map/ppermute | solution.py:528
  391.8 13.9 %collective-permute-done.30.refs_10_ = bf16[7,128,128]{2,1,0:T(8,128)(2,1)S(1)} collective-permute-done((bf16[7,128,128]{2,1,0:T(8,128)(2,1)S(1)}, bf16[7,128,128]{2,1,0:T(8,128)(2,1)S(1)}, u32[]{:S(2)}, u32[]{:S(2)}) %collective-permute-start.30) | collective-permute-done | bytes 229408 | tf_op jit(solution)/shard_map/ppermute | solution.py:528
  406.5 20.9 %attend_backward.1 = (bf16[7,128,384]{2,1,0:T(8,128)(2,1)}, bf16[7,128,384]{2,1,0:T(8,128)(2,1)}, bf16[7,128,384]{2,1,0:T(8,128)(2,1)}, bf16[7,128,384]{2,1,0:T(8,128)(2,1)}, bf16[4,7,128,384]{3,2,1,0:T(8,128)(2,1)}) custom-call(s32[7]{0:T(128)} %copy-done.6, bf16[7,128,384]{2,1,0:T(8,128)(2,1)} %copy-done.8, bf16[7,128,384]{2,1,0:T(8,128)(2,1)} %copy-done.55, ...), custom_call_target="tpu_custom_call" | custom-call | flops 10000000000 | bytes 12582912 | tf_op jit(solution)/shard_map/attend_backward/pallas_call | solution.py:311
  436.2 18.1 %collective-permute-start.36 = (bf16[7,128,384]{2,1,0:T(8,128)(2,1)S(1)}, bf16[7,128,384]{2,1,0:T(8,128)(2,1)S(1)}, u32[]{:S(2)}, u32[]{:S(2)}) collective-permute-start(bf16[7,128,384]{2,1,0:T(8,128)(2,1)S(1)} %get-tuple-element.207), channel_id=1, source_target_pairs={{0,2},{1,3},{2,0},{3,1},{4,6},{5,7},{6,4},{7,5},{8,10},{9,11},{10,... | collective-permute-start | bytes 2064392 | tf_op jit(solution)/shard_map/ppermute | solution.py:528
  460.2 21.9 %collective-permute-done.36.refs_1_ = bf16[7,128,384]{2,1,0:T(8,128)(2,1)S(1)} collective-permute-done((bf16[7,128,384]{2,1,0:T(8,128)(2,1)S(1)}, bf16[7,128,384]{2,1,0:T(8,128)(2,1)S(1)}, u32[]{:S(2)}, u32[]{:S(2)}) %collective-permute-start.36) | collective-permute-done | bytes 688160 | tf_op jit(solution)/shard_map/ppermute | solution.py:528
  484.9 18.1 %collective-permute-done.37.refs_2_ = bf16[7,128,384]{2,1,0:T(8,128)(2,1)S(1)} collective-permute-done((bf16[7,128,384]{2,1,0:T(8,128)(2,1)S(1)}, bf16[7,128,384]{2,1,0:T(8,128)(2,1)S(1)}, u32[]{:S(2)}, u32[]{:S(2)}) %collective-permute-start.37) | collective-permute-done | bytes 688160 | tf_op jit(solution)/shard_map/ppermute | solution.py:528
  505.9 8.7 %convolution_convert_fusion = bf16[2048,1536]{1,0:T(8,128)(2,1)} fusion(bf16[896,2048]{1,0:T(8,128)(2,1)S(1)} %copy-done.65, bf16[896,1536]{1,0:T(8,128)(2,1)S(1)} %gather_grads.1), kind=kOutput, calls=%fused_computation.5 | convolution fusion | flops 5640290304 | bytes 12713984 | tf_op jit(solution)/shard_map/dot_general | solution.py:33
  550.6 13.8 %collective-permute-start.49 = (bf16[64,2048]{1,0:T(8,128)(2,1)S(1)}, bf16[64,2048]{1,0:T(8,128)(2,1)S(1)}, u32[]{:S(2)}, u32[]{:S(2)}) collective-permute-start(bf16[64,2048]{1,0:T(8,128)(2,1)S(1)} %get-tuple-element.297), channel_id=1, source_target_pairs={{0,2},{1,3},{2,0},{3,1},{4,6},{5,7},{6,4},{7,5},{8,10},{9,11},{10,... | collective-permute-start | bytes 786440 | tf_op jit(solution)/shard_map/ppermute | solution.py:528
  567.9 14.4 %collective-permute-done.49 = bf16[64,2048]{1,0:T(8,128)(2,1)S(1)} collective-permute-done((bf16[64,2048]{1,0:T(8,128)(2,1)S(1)}, bf16[64,2048]{1,0:T(8,128)(2,1)S(1)}, u32[]{:S(2)}, u32[]{:S(2)}) %collective-permute-start.49) | collective-permute-done | bytes 262176 | tf_op jit(solution)/shard_map/ppermute | solution.py:528
  584.7 12.6 %collective-permute-done.50 = bf16[64,2048]{1,0:T(8,128)(2,1)} collective-permute-done((bf16[64,2048]{1,0:T(8,128)(2,1)}, bf16[64,2048]{1,0:T(8,128)(2,1)}, u32[]{:S(2)}, u32[]{:S(2)}) %collective-permute-start.50) | collective-permute-done | bytes 262176 | tf_op jit(solution)/shard_map/ppermute | solution.py:528
  617.9 8.3 %collective-permute-start.58 = (bf16[64,2048]{1,0:T(8,128)(2,1)S(1)}, bf16[64,2048]{1,0:T(8,128)(2,1)S(1)}, u32[]{:S(2)}, u32[]{:S(2)}) collective-permute-start(bf16[64,2048]{1,0:T(8,128)(2,1)S(1)} %add_convert_fusion.5), channel_id=1, source_target_pairs={{0,2},{1,3},{2,0},{3,1},{4,6},{5,7},{6,4},{7,5},{8,10},{9,11},{10,... | collective-permute-start | bytes 786440 | tf_op jit(solution)/shard_map/ppermute | solution.py:528
  636.6 29.6 %collective-permute-done.59 = bf16[64,2048]{1,0:T(8,128)(2,1)S(1)} collective-permute-done((bf16[64,2048]{1,0:T(8,128)(2,1)S(1)}, bf16[64,2048]{1,0:T(8,128)(2,1)S(1)}, u32[]{:S(2)}, u32[]{:S(2)}) %collective-permute-start.59) | collective-permute-done | bytes 262176 | tf_op jit(solution)/shard_map/ppermute | solution.py:528
  674.4 15.8 %collective-permute-start.63 = (f32[2,2048]{1,0:T(2,128)S(1)}, f32[2,2048]{1,0:T(2,128)S(1)}, u32[]{:S(2)}, u32[]{:S(2)}) collective-permute-start(f32[2,2048]{1,0:T(2,128)S(1)} %add.486), channel_id=1, source_target_pairs={{0,2},{1,3},{2,0},{3,1},{4,6},{5,7},{6,4},{7,5},{8,10},{9,11},{10,... | collective-permute-start | bytes 49160 | tf_op jit(solution)/shard_map/ppermute | solution.py:55
  705.4 8.8 %widen.1 = f32[3,2048,512]{2,1,0:T(8,128)} custom-call(bf16[2048,1536]{1,0:T(8,128)(2,1)} %all-gather.11.cloned.1.call-done.source), custom_call_target="tpu_custom_call" | custom-call | flops 3145728 | bytes 18874368 | tf_op jit(solution)/shard_map/widen/pallas_call | solution.py:482
  (405 shorter events, 253.0 us)
Async XLA Ops:
  7.2 207.3 %all-gather.5.cloned.1.call-start = ((), (), s32[]{:S(2)}) async-start(), calls=%async_computation.3 | async-start | bytes 4718592 | tf_op jit(solution)/shard_map/all_gather | solution.py:635
  9.5 205.0 %all-gather.7.cloned.1.call-start = ((), (), s32[]{:S(2)}) async-start(), calls=%async_computation.4 | async-start | bytes 4718592 | tf_op jit(solution)/shard_map/all_gather | solution.py:690
  9.6 97.2 %collective-permute-start.7 = (bf16[512,2048]{1,0:T(8,128)(2,1)}, bf16[512,2048]{1,0:T(8,128)(2,1)}, u32[]{:S(2)}, u32[]{:S(2)}) collective-permute-start(bf16[512,2048]{1,0:T(8,128)(2,1)} %param.14), channel_id=1, source_target_pairs={{0,8},{8,0},{16,24},{24,16},{1,9},{9,1},{17,25},{25,17},{2,10},{10... | collective-permute-start | bytes 6291464 | tf_op jit(solution)/shard_map/ppermute | solution.py:55
  12.6 94.2 %collective-permute-start.8 = (bf16[512,2048]{1,0:T(8,128)(2,1)}, bf16[512,2048]{1,0:T(8,128)(2,1)}, u32[]{:S(2)}, u32[]{:S(2)}) collective-permute-start(bf16[512,2048]{1,0:T(8,128)(2,1)} %param.14), channel_id=1, source_target_pairs={{0,16},{8,24},{16,0},{24,8},{1,17},{9,25},{17,1},{25,9},{2,18},{10... | collective-permute-start | bytes 6291464 | tf_op jit(solution)/shard_map/ppermute | solution.py:55
  33.3 53.2 %collective-permute-start = (bf16[7,128,384]{2,1,0:T(8,128)(2,1)}, bf16[7,128,384]{2,1,0:T(8,128)(2,1)S(1)}, u32[]{:S(2)}, u32[]{:S(2)}) collective-permute-start(bf16[7,128,384]{2,1,0:T(8,128)(2,1)} %get-tuple-element.134), channel_id=1, source_target_pairs={{0,2},{1,3},{2,0},{3,1},{4,6},{5,7},{6,4},{7,5},{8,10},{9,11},{10,... | collective-permute-start | bytes 2064392 | tf_op jit(solution)/shard_map/ppermute | solution.py:528
  35.0 54.6 %collective-permute-start.1 = (bf16[7,128,384]{2,1,0:T(8,128)(2,1)S(1)}, bf16[7,128,384]{2,1,0:T(8,128)(2,1)}, u32[]{:S(2)}, u32[]{:S(2)}) collective-permute-start(bf16[7,128,384]{2,1,0:T(8,128)(2,1)S(1)} %get-tuple-element.135), channel_id=1, source_target_pairs={{0,4},{1,5},{2,6},{3,7},{4,0},{5,1},{6,2},{7,3},{8,12},{9,13},{10,... | collective-permute-start | bytes 2064392 | tf_op jit(solution)/shard_map/ppermute | solution.py:528
  37.5 65.7 %collective-permute-start.2 = (bf16[7,128,384]{2,1,0:T(8,128)(2,1)S(1)}, bf16[7,128,384]{2,1,0:T(8,128)(2,1)}, u32[]{:S(2)}, u32[]{:S(2)}) collective-permute-start(bf16[7,128,384]{2,1,0:T(8,128)(2,1)S(1)} %get-tuple-element.136), channel_id=1, source_target_pairs={{0,6},{1,7},{2,4},{3,5},{4,2},{5,3},{6,0},{7,1},{8,14},{9,15},{10,... | collective-permute-start | bytes 2064392 | tf_op jit(solution)/shard_map/ppermute | solution.py:528
  106.8 166.0 %all-gather.9.cloned.1.call-start = ((), (), s32[]{:S(2)}) async-start(), calls=%async_computation.5 | async-start | bytes 9437184 | tf_op jit(solution)/shard_map/all_gather | solution.py:691
  107.5 407.0 %reduce-scatter.4.cloned.1.call-start = ((), (), s32[]{:S(2)}) async-start(), calls=%async_computation.6 | async-start | bytes 5242880 | tf_op jit(solution)/shard_map/reduce_scatter | solution.py:561
  107.8 70.1 %collective-permute-start.17 = (bf16[512,2048]{1,0:T(8,128)(2,1)}, bf16[512,2048]{1,0:T(8,128)(2,1)S(1)}, u32[]{:S(2)}, u32[]{:S(2)}) collective-permute-start(bf16[512,2048]{1,0:T(8,128)(2,1)} %param.14), channel_id=1, source_target_pairs={{0,24},{8,16},{16,8},{24,0},{1,25},{9,17},{17,9},{25,1},{2,26},{10... | collective-permute-start | bytes 6291464 | tf_op jit(solution)/shard_map/ppermute | solution.py:55
  110.3 34.7 %collective-permute-start.12 = (f32[5,2048]{1,0:T(8,128)S(1)}, f32[5,2048]{1,0:T(8,128)S(1)}, u32[]{:S(2)}, u32[]{:S(2)}) collective-permute-start(f32[5,2048]{1,0:T(8,128)S(1)} %bitcast.97), channel_id=1, source_target_pairs={{0,1},{1,0},{2,3},{3,2},{4,5},{5,4},{6,7},{7,6},{8,9},{9,8},{10,11... | collective-permute-start | bytes 122888 | tf_op jit(solution)/shard_map/ppermute | solution.py:55
  125.9 48.0 %collective-permute-start.10 = (bf16[7,128,128]{2,1,0:T(8,128)(2,1)}, bf16[7,128,128]{2,1,0:T(8,128)(2,1)S(1)}, u32[]{:S(2)}, u32[]{:S(2)}) collective-permute-start(bf16[7,128,128]{2,1,0:T(8,128)(2,1)} %get-tuple-element.148), channel_id=1, source_target_pairs={{0,4},{1,5},{2,6},{3,7},{4,0},{5,1},{6,2},{7,3},{8,12},{9,13},{10,... | collective-permute-start | bytes 688136 | tf_op jit(solution)/shard_map/ppermute | solution.py:528
  192.2 38.1 %collective-permute-start.19 = (bf16[224,2048]{1,0:T(8,128)(2,1)S(1)}, bf16[224,2048]{1,0:T(8,128)(2,1)}, u32[]{:S(2)}, u32[]{:S(2)}) collective-permute-start(bf16[224,2048]{1,0:T(8,128)(2,1)S(1)} %multiply_convert_fusion), channel_id=1, source_target_pairs={{0,16},{8,24},{16,0},{24,8},{1,17},{9,25},{17,1},{25,9},{2,18},{10... | collective-permute-start | bytes 2752520 | tf_op jit(solution)/shard_map/ppermute | solution.py:55
  192.8 39.3 %collective-permute-start.20 = (bf16[224,2048]{1,0:T(8,128)(2,1)S(1)}, bf16[224,2048]{1,0:T(8,128)(2,1)}, u32[]{:S(2)}, u32[]{:S(2)}) collective-permute-start(bf16[224,2048]{1,0:T(8,128)(2,1)S(1)} %multiply_convert_fusion), channel_id=1, source_target_pairs={{0,24},{8,16},{16,8},{24,0},{1,25},{9,17},{17,9},{25,1},{2,26},{10... | collective-permute-start | bytes 2752520 | tf_op jit(solution)/shard_map/ppermute | solution.py:55
  268.2 246.4 %reduce-scatter.6.cloned.1.call-start = ((), (), s32[]{:S(2)}) async-start(), calls=%async_computation.7 | async-start | bytes 5242880 | tf_op jit(solution)/shard_map/reduce_scatter | solution.py:561
  301.2 34.3 %collective-permute-start.24 = (bf16[224,2048]{1,0:T(8,128)(2,1)S(1)}, bf16[224,2048]{1,0:T(8,128)(2,1)S(1)}, u32[]{:S(2)}, u32[]{:S(2)}) collective-permute-start(bf16[224,2048]{1,0:T(8,128)(2,1)S(1)} %convolution_convert_fusion.9), channel_id=1, source_target_pairs={{0,16},{8,24},{16,0},{24,8},{1,17},{9,25},{17,1},{25,9},{2,18},{10... | collective-permute-start | bytes 2752520 | tf_op jit(solution)/shard_map/ppermute | solution.py:55
  359.1 258.8 %reduce-scatter.8.cloned.1.call-start = ((), (), s32[]{:S(2)}) async-start(), calls=%async_computation.8 | async-start | bytes 7077888 | tf_op jit(solution)/shard_map/reduce_scatter | solution.py:811
  382.6 44.8 %collective-permute-start.32 = (bf16[224,2048]{1,0:T(8,128)(2,1)S(1)}, bf16[224,2048]{1,0:T(8,128)(2,1)S(1)}, u32[]{:S(2)}, u32[]{:S(2)}) collective-permute-start(bf16[224,2048]{1,0:T(8,128)(2,1)S(1)} %get-tuple-element.194), channel_id=1, source_target_pairs={{0,8},{8,0},{16,24},{24,16},{1,9},{9,1},{17,25},{25,17},{2,10},{10... | collective-permute-start | bytes 2752520 | tf_op jit(solution)/shard_map/ppermute | solution.py:55
  382.6 44.8 %collective-permute-start.33 = (bf16[224,2048]{1,0:T(8,128)(2,1)S(1)}, bf16[224,2048]{1,0:T(8,128)(2,1)S(1)}, u32[]{:S(2)}, u32[]{:S(2)}) collective-permute-start(bf16[224,2048]{1,0:T(8,128)(2,1)S(1)} %get-tuple-element.194), channel_id=1, source_target_pairs={{0,16},{8,24},{16,0},{24,8},{1,17},{9,25},{17,1},{25,9},{2,18},{10... | collective-permute-start | bytes 2752520 | tf_op jit(solution)/shard_map/ppermute | solution.py:55
  435.7 67.3 %collective-permute-start.39 = (bf16[224,2048]{1,0:T(8,128)(2,1)S(1)}, bf16[224,2048]{1,0:T(8,128)(2,1)S(1)}, u32[]{:S(2)}, u32[]{:S(2)}) collective-permute-start(bf16[224,2048]{1,0:T(8,128)(2,1)S(1)} %copy-done.54), channel_id=1, source_target_pairs={{0,8},{8,0},{16,24},{24,16},{1,9},{9,1},{17,25},{25,17},{2,10},{10... | collective-permute-start | bytes 2752520 | tf_op jit(solution)/shard_map/ppermute | solution.py:55
  435.8 67.3 %collective-permute-start.40 = (bf16[224,2048]{1,0:T(8,128)(2,1)S(1)}, bf16[224,2048]{1,0:T(8,128)(2,1)S(1)}, u32[]{:S(2)}, u32[]{:S(2)}) collective-permute-start(bf16[224,2048]{1,0:T(8,128)(2,1)S(1)} %copy-done.53), channel_id=1, source_target_pairs={{0,16},{8,24},{16,0},{24,8},{1,17},{9,25},{17,1},{25,9},{2,18},{10... | collective-permute-start | bytes 2752520 | tf_op jit(solution)/shard_map/ppermute | solution.py:55
  436.2 45.9 %collective-permute-start.36 = (bf16[7,128,384]{2,1,0:T(8,128)(2,1)S(1)}, bf16[7,128,384]{2,1,0:T(8,128)(2,1)S(1)}, u32[]{:S(2)}, u32[]{:S(2)}) collective-permute-start(bf16[7,128,384]{2,1,0:T(8,128)(2,1)S(1)} %get-tuple-element.207), channel_id=1, source_target_pairs={{0,2},{1,3},{2,0},{3,1},{4,6},{5,7},{6,4},{7,5},{8,10},{9,11},{10,... | collective-permute-start | bytes 2064392 | tf_op jit(solution)/shard_map/ppermute | solution.py:528
  454.3 48.7 %collective-permute-start.37 = (bf16[7,128,384]{2,1,0:T(8,128)(2,1)S(1)}, bf16[7,128,384]{2,1,0:T(8,128)(2,1)S(1)}, u32[]{:S(2)}, u32[]{:S(2)}) collective-permute-start(bf16[7,128,384]{2,1,0:T(8,128)(2,1)S(1)} %get-tuple-element.208), channel_id=1, source_target_pairs={{0,4},{1,5},{2,6},{3,7},{4,0},{5,1},{6,2},{7,3},{8,12},{9,13},{10,... | collective-permute-start | bytes 2064392 | tf_op jit(solution)/shard_map/ppermute | solution.py:528
  454.3 48.7 %collective-permute-start.38 = (bf16[7,128,384]{2,1,0:T(8,128)(2,1)S(1)}, bf16[7,128,384]{2,1,0:T(8,128)(2,1)S(1)}, u32[]{:S(2)}, u32[]{:S(2)}) collective-permute-start(bf16[7,128,384]{2,1,0:T(8,128)(2,1)S(1)} %get-tuple-element.209), channel_id=1, source_target_pairs={{0,6},{1,7},{2,4},{3,5},{4,2},{5,3},{6,0},{7,1},{8,14},{9,15},{10,... | collective-permute-start | bytes 2064392 | tf_op jit(solution)/shard_map/ppermute | solution.py:528
  514.6 190.8 %all-gather.11.cloned.1.call-start = ((), (), s32[]{:S(2)}) async-start(), calls=%async_computation.9 | async-start | bytes 7077888 | tf_op jit(solution)/shard_map/all_gather | solution.py:845
  564.4 37.1 %collective-permute-start.46 = (bf16[224,2048]{1,0:T(8,128)(2,1)}, bf16[224,2048]{1,0:T(8,128)(2,1)S(1)}, u32[]{:S(2)}, u32[]{:S(2)}) collective-permute-start(bf16[224,2048]{1,0:T(8,128)(2,1)} %fusion.15), channel_id=1, source_target_pairs={{0,8},{8,0},{16,24},{24,16},{1,9},{9,1},{17,25},{25,17},{2,10},{10... | collective-permute-start | bytes 2752520 | tf_op jit(solution)/shard_map/ppermute | solution.py:55
  565.0 40.2 %collective-permute-start.47 = (bf16[224,2048]{1,0:T(8,128)(2,1)}, bf16[224,2048]{1,0:T(8,128)(2,1)}, u32[]{:S(2)}, u32[]{:S(2)}) collective-permute-start(bf16[224,2048]{1,0:T(8,128)(2,1)} %fusion.16), channel_id=1, source_target_pairs={{0,16},{8,24},{16,0},{24,8},{1,17},{9,25},{17,1},{25,9},{2,18},{10... | collective-permute-start | bytes 2752520 | tf_op jit(solution)/shard_map/ppermute | solution.py:55
  566.6 39.8 %collective-permute-start.48 = (bf16[224,2048]{1,0:T(8,128)(2,1)}, bf16[224,2048]{1,0:T(8,128)(2,1)}, u32[]{:S(2)}, u32[]{:S(2)}) collective-permute-start(bf16[224,2048]{1,0:T(8,128)(2,1)} %fusion.17), channel_id=1, source_target_pairs={{0,24},{8,16},{16,8},{24,0},{1,25},{9,17},{17,9},{25,1},{2,26},{10... | collective-permute-start | bytes 2752520 | tf_op jit(solution)/shard_map/ppermute | solution.py:55
  630.5 36.3 %collective-permute-start.54 = (bf16[224,2048]{1,0:T(8,128)(2,1)S(1)}, bf16[224,2048]{1,0:T(8,128)(2,1)S(1)}, u32[]{:S(2)}, u32[]{:S(2)}) collective-permute-start(bf16[224,2048]{1,0:T(8,128)(2,1)S(1)} %add_convert_fusion.3), channel_id=1, source_target_pairs={{0,8},{8,0},{16,24},{24,16},{1,9},{9,1},{17,25},{25,17},{2,10},{10... | collective-permute-start | bytes 2752520 | tf_op jit(solution)/shard_map/ppermute | solution.py:55
  631.6 35.1 %collective-permute-start.55 = (bf16[224,2048]{1,0:T(8,128)(2,1)S(1)}, bf16[224,2048]{1,0:T(8,128)(2,1)S(1)}, u32[]{:S(2)}, u32[]{:S(2)}) collective-permute-start(bf16[224,2048]{1,0:T(8,128)(2,1)S(1)} %add_convert_fusion.3), channel_id=1, source_target_pairs={{0,16},{8,24},{16,0},{24,8},{1,17},{9,25},{17,1},{25,9},{2,18},{10... | collective-permute-start | bytes 2752520 | tf_op jit(solution)/shard_map/ppermute | solution.py:55
  633.2 33.9 %collective-permute-start.56 = (bf16[224,2048]{1,0:T(8,128)(2,1)S(1)}, bf16[224,2048]{1,0:T(8,128)(2,1)S(1)}, u32[]{:S(2)}, u32[]{:S(2)}) collective-permute-start(bf16[224,2048]{1,0:T(8,128)(2,1)S(1)} %add_convert_fusion.3), channel_id=1, source_target_pairs={{0,24},{8,16},{16,8},{24,0},{1,25},{9,17},{17,9},{25,1},{2,26},{10... | collective-permute-start | bytes 2752520 | tf_op jit(solution)/shard_map/ppermute | solution.py:55
  667.3 35.2 %collective-permute-start.57 = (bf16[224,2048]{1,0:T(8,128)(2,1)S(1)}, bf16[224,2048]{1,0:T(8,128)(2,1)S(1)}, u32[]{:S(2)}, u32[]{:S(2)}) collective-permute-start(bf16[224,2048]{1,0:T(8,128)(2,1)S(1)} %copy-done.19), channel_id=1, source_target_pairs={{0,24},{8,16},{16,8},{24,0},{1,25},{9,17},{17,9},{25,1},{2,26},{10... | collective-permute-start | bytes 2752520 | tf_op jit(solution)/shard_map/ppermute | solution.py:55
  (112 other events, 2311.9 us)
Sparse Core Ops, SparseCore 0:
  10.2 73.1 all-gather.4
  106.9 78.7 all-gather.6
  187.3 85.4 all-gather.8
  274.9 77.0 reduce-scatter.3
  359.2 93.3 reduce-scatter.5
  514.7 98.5 reduce-scatter.7
  618.0 87.3 all-gather.10
